TPU v7x, 32 devices: a whole 2x2x4 slice. The times are simulated.
32 devices in a mesh: chan: 2 (over y), seq: 8 (over z, core), dp: 2 (over x).
Axes of the slice: x: 2, y: 2, z: 4, core: 2. Of those that a mesh axis runs over, the one named last changes fastest.
Arguments:
- queries: bfloat16 [2, 2, 1024, 2048], P('dp', 'chan', 'seq'), may hold values from -8 to 8
- keys: bfloat16 [2, 2, 1024, 2048], P('dp', 'chan', 'seq'), may hold values from -8 to 8
- values: bfloat16 [2, 2, 1024, 2048], P('dp', 'chan', 'seq'), may hold values from -6 to 6
- out_grad: bfloat16 [2, 2, 1024, 2048], P('dp', 'chan', 'seq'), may hold values from -6 to 6
- cross_bias: float32 [16], replicated, may hold values from -2 to 2
- lengths: int32 [2], P('dp'), may hold values from 256 to 1024
Outputs:
- query_grad: bfloat16 [2, 2, 1024, 2048], P('dp', 'chan', 'seq')
- key_grad: bfloat16 [2, 2, 1024, 2048], P('dp', 'chan', 'seq')
- value_grad: bfloat16 [2, 2, 1024, 2048], P('dp', 'chan', 'seq')
- bias_grad: float32 [16], replicated
Inputs may be any that keep to these rules, and one draw needn't show every extreme that they name: Frames of conversation b from lengths[b] on are padding in both channels.
All inputs are finite; a program needn't handle non-finite values.
Results may differ from a plain program's by a relative error of at most 0.011.
Values may be sent and summed in bfloat16 or wider, within the bound.
No kernel may reach another device: no remote copies, remote signals or barrier semaphores. Data moves between devices by JAX's collectives and lax.ppermute only.
A program may use at most 128 MiB of HBM per device.

v0:
```python
import math

import jax
import jax.numpy as jnp
from jax import lax
from jax.sharding import PartitionSpec as P

LOOKBACK = 6


NEG_FILL = -1e30


def swapped(value, axis, apart):
    mask = 2**apart
    pairs = [(source, source ^ mask) for source in range(lax.axis_size(axis))]
    return lax.ppermute(value, axis, pairs)


def from_behind(value, axis, steps):
    count = lax.axis_size(axis)
    first, last = (max(0, -steps), min(count, count - steps))
    return lax.ppermute(value, axis, [(source, source + steps) for source in range(first, last)])


def local_scores(query_part, key_part, bias_part, allowed, root_scale):
    scores = jnp.einsum("pgd,sgd->gps", query_part, key_part, preferred_element_type=jnp.float32)
    scores = scores * root_scale + bias_part
    return jnp.where(allowed[None], scores, NEG_FILL)


def forward_stats(query_heads, grad_heads, key_heads, value_heads, bias_heads, allowed, root_scale):
    row_count, head_count, head_width = query_heads.shape

    def forward_group_step(head_group, carried):
        row_max, row_total, row_moment = carried
        offset = head_group * 2
        query_part = lax.dynamic_slice_in_dim(query_heads, offset, 2, 1)
        grad_part = lax.dynamic_slice_in_dim(grad_heads, offset, 2, 1)
        key_part = lax.dynamic_slice_in_dim(key_heads, offset, 2, 1)
        value_part = lax.dynamic_slice_in_dim(value_heads, offset, 2, 1)
        bias_part = lax.dynamic_slice_in_dim(bias_heads, offset, 2, 0)[:, :, None]
        scores = local_scores(query_part, key_part, bias_part, allowed, root_scale)
        group_max = jnp.max(scores, axis=2)
        weights = jnp.where(allowed[None], jnp.exp(scores - group_max[:, :, None]), 0.0)
        weight_grad = jnp.einsum(
            "pgd,sgd->gps", grad_part, value_part, preferred_element_type=jnp.float32
        )
        group_total = jnp.sum(weights, axis=2)
        group_moment = jnp.sum(weights * weight_grad, axis=2)
        row_max = lax.dynamic_update_slice_in_dim(row_max, group_max, offset, 0)
        row_total = lax.dynamic_update_slice_in_dim(row_total, group_total, offset, 0)
        row_moment = lax.dynamic_update_slice_in_dim(row_moment, group_moment, offset, 0)
        return (row_max, row_total, row_moment)

    initial = (
        jnp.zeros((head_count, row_count), jnp.float32),
        jnp.zeros((head_count, row_count), jnp.float32),
        jnp.zeros((head_count, row_count), jnp.float32),
    )
    return lax.fori_loop(0, head_count // 2, forward_group_step, initial)


def backward_local(
    query_heads,
    grad_heads,
    key_heads,
    value_heads,
    bias_heads,
    partner_flag,
    allowed,
    log_norm,
    row_delta,
    root_scale,
):
    row_count, head_count, head_width = query_heads.shape
    key_count = key_heads.shape[0]

    def backward_group_step(head_group, carried):
        query_sum, key_sum, value_sum, bias_sum = carried
        offset = head_group * 2
        query_part = lax.dynamic_slice_in_dim(query_heads, offset, 2, 1)
        grad_part = lax.dynamic_slice_in_dim(grad_heads, offset, 2, 1)
        key_part = lax.dynamic_slice_in_dim(key_heads, offset, 2, 1)
        value_part = lax.dynamic_slice_in_dim(value_heads, offset, 2, 1)
        bias_part = lax.dynamic_slice_in_dim(bias_heads, offset, 2, 0)[:, :, None]
        norm_part = lax.dynamic_slice_in_dim(log_norm, offset, 2, 0)[:, :, None]
        delta_part = lax.dynamic_slice_in_dim(row_delta, offset, 2, 0)[:, :, None]
        scores = local_scores(query_part, key_part, bias_part, allowed, root_scale)
        weights = jnp.where(allowed[None], jnp.exp(scores - norm_part), 0.0)
        weight_grad = jnp.einsum(
            "pgd,sgd->gps", grad_part, value_part, preferred_element_type=jnp.float32
        )
        score_grad = weights * (weight_grad - delta_part)
        weight_low = weights.astype(jnp.bfloat16)
        score_low = score_grad.astype(jnp.bfloat16)
        query_term = (
            jnp.einsum("gps,sgd->pgd", score_low, key_part, preferred_element_type=jnp.float32)
            * root_scale
        )
        key_term = (
            jnp.einsum("gps,pgd->sgd", score_low, query_part, preferred_element_type=jnp.float32)
            * root_scale
        )
        value_term = jnp.einsum(
            "gps,pgd->sgd", weight_low, grad_part, preferred_element_type=jnp.float32
        )
        bias_term = jnp.sum(score_grad * partner_flag[None, :, None], axis=(1, 2))
        query_sum = lax.dynamic_update_slice_in_dim(query_sum, query_term, offset, 1)
        key_sum = lax.dynamic_update_slice_in_dim(key_sum, key_term, offset, 1)
        value_sum = lax.dynamic_update_slice_in_dim(value_sum, value_term, offset, 1)
        bias_sum = lax.dynamic_update_slice_in_dim(bias_sum, bias_term, offset, 0)
        return (query_sum, key_sum, value_sum, bias_sum)

    initial = (
        jnp.zeros((row_count, head_count, head_width), jnp.float32),
        jnp.zeros((key_count, head_count, head_width), jnp.float32),
        jnp.zeros((key_count, head_count, head_width), jnp.float32),
        jnp.zeros((head_count,), jnp.float32),
    )
    return lax.fori_loop(0, head_count // 2, backward_group_step, initial)


def shards(queries, keys, values, out_grad, cross_bias, lengths):
    frames = queries.shape[2]
    feature_width = queries.shape[3]
    head_count = cross_bias.shape[0]
    head_width = feature_width // head_count
    root_scale = 1.0 / math.sqrt(head_width)
    channel = lax.axis_index("chan")
    block_index = lax.axis_index("seq")
    dialog_length = lengths[0]
    own_query = queries[0, 0]
    own_grad = out_grad[0, 0]
    own_keys = keys[0, 0]
    own_values = values[0, 0]
    partner_query, partner_grad = swapped((own_query, own_grad), "chan", 0)
    leading = channel == 0
    query_rows = jnp.where(
        leading,
        jnp.concatenate([own_query, partner_query], axis=0),
        jnp.concatenate([partner_query, own_query], axis=0),
    )
    grad_rows = jnp.where(
        leading,
        jnp.concatenate([own_grad, partner_grad], axis=0),
        jnp.concatenate([partner_grad, own_grad], axis=0),
    )
    tower_index = jnp.arange(2 * frames, dtype=jnp.int32) // frames
    partner_flag = (tower_index != channel).astype(jnp.float32)
    pieces = [None] * LOOKBACK + [(own_keys, own_values)]
    moving = (own_keys, own_values)
    for distance in range(1, LOOKBACK + 1):
        moving = from_behind((moving[0], moving[1]), "seq", 1)
        pieces[LOOKBACK - distance] = moving
    key_window = jnp.concatenate([shard_pair[0] for shard_pair in pieces], axis=0)
    value_window = jnp.concatenate([shard_pair[1] for shard_pair in pieces], axis=0)
    window_rows = key_window.shape[0]
    reach_frames = LOOKBACK * frames
    own_frames = block_index * frames + jnp.arange(frames, dtype=jnp.int32)
    query_frame = jnp.concatenate([own_frames, own_frames])
    key_frame = (block_index - LOOKBACK) * frames + jnp.arange(window_rows, dtype=jnp.int32)
    allowed = (key_frame[None, :] > query_frame[:, None] - reach_frames) & (
        key_frame[None, :] <= query_frame[:, None]
    )
    allowed = allowed & (key_frame[None, :] >= 0) & (key_frame[None, :] < dialog_length)
    allowed = allowed & (query_frame[:, None] < dialog_length)
    query_heads = query_rows.reshape(2 * frames, head_count, head_width)
    grad_heads = grad_rows.reshape(2 * frames, head_count, head_width)
    key_heads = key_window.reshape(window_rows, head_count, head_width)
    value_heads = value_window.reshape(window_rows, head_count, head_width)
    bias_heads = cross_bias[:, None] * partner_flag[None, :]
    row_max, row_total, row_moment = forward_stats(
        query_heads, grad_heads, key_heads, value_heads, bias_heads, allowed, root_scale
    )
    merged_peak = lax.pmax(row_max, "chan")
    rescale = jnp.exp(row_max - merged_peak)
    merged_total, merged_moment = lax.psum((row_total * rescale, row_moment * rescale), "chan")
    safe_total = jnp.where(merged_total > 0.0, merged_total, 1.0)
    log_norm = merged_peak + jnp.log(safe_total)
    row_delta = merged_moment / safe_total
    query_sum, key_sum, value_sum, bias_sum = backward_local(
        query_heads,
        grad_heads,
        key_heads,
        value_heads,
        bias_heads,
        partner_flag,
        allowed,
        log_norm,
        row_delta,
        root_scale,
    )
    query_flat = query_sum.reshape(2 * frames, feature_width)
    own_part = jnp.where(leading, query_flat[:frames], query_flat[frames:])
    other_part = jnp.where(leading, query_flat[frames:], query_flat[:frames])
    arrived_query = swapped(other_part.astype(jnp.bfloat16), "chan", 0).astype(other_part.dtype)
    query_out = (own_part + arrived_query).astype(jnp.bfloat16)
    key_flat = key_sum.reshape(window_rows, feature_width)
    value_flat = value_sum.reshape(window_rows, feature_width)

    def key_block(position):
        return key_flat[position * frames : (position + 1) * frames]

    def value_block(position):
        return value_flat[position * frames : (position + 1) * frames]

    running = (key_block(0), value_block(0))
    for distance in range(1, LOOKBACK + 1):
        arrived = (
            from_behind(running[0].astype(jnp.bfloat16), "seq", -1).astype(jnp.float32),
            from_behind(running[1].astype(jnp.bfloat16), "seq", -1).astype(jnp.float32),
        )
        running = (arrived[0] + key_block(distance), arrived[1] + value_block(distance))
    bias_out = lax.psum(bias_sum, ("chan", "seq", "dp"))
    return (
        query_out[None, None],
        running[0].astype(jnp.bfloat16)[None, None],
        running[1].astype(jnp.bfloat16)[None, None],
        bias_out,
    )


def solution(mesh):
    placed = (
        P("dp", "chan", "seq", None),
        P("dp", "chan", "seq", None),
        P("dp", "chan", "seq", None),
        P("dp", "chan", "seq", None),
        P(),
        P("dp"),
    )
    return jax.shard_map(
        shards,
        mesh=mesh,
        in_specs=placed,
        out_specs=(
            P("dp", "chan", "seq", None),
            P("dp", "chan", "seq", None),
            P("dp", "chan", "seq", None),
            P(),
        ),
        check_vma=False,
    )
```

profile of v0, /device:TPU:1, one launch (start us, length us, event | category | flops | bytes accessed | tf_op | source)
XLA Modules:
  0.0 400.4 jit_solution(14205888204503150751)
XLA Ops:
  2.0 4.6 %collective-permute-start = (bf16[128,2048]{0,1:T(8,128)(2,1)S(1)}, bf16[128,2048]{0,1:T(8,128)(2,1)S(1)}, u32[]{:S(2)}, u32[]{:S(2)}) collective-permute-start(bf16[128,2048]{0,1:T(8,128)(2,1)S(1)} %bitcast.90), channel_id=1, source_target_pairs={{0,2},{2,4},{4,6},{6,8},{8,10},{10,12},{12,14},{1,3},{3,5},{5,7},{... | collective-permute-start | bytes 1572872 | tf_op jit(solution)/shard_map/ppermute | solution.py:23
  9.8 2.9 collective-permute-done
  12.7 4.4 %collective-permute-start.1 = (bf16[128,2048]{0,1:T(8,128)(2,1)S(1)}, bf16[128,2048]{0,1:T(8,128)(2,1)S(1)}, u32[]{:S(2)}, u32[]{:S(2)}) collective-permute-start(bf16[128,2048]{0,1:T(8,128)(2,1)S(1)} %collective-permute-done), channel_id=1, source_target_pairs={{0,2},{2,4},{4,6},{6,8},{8,10},{10,12},{12,14},{1,3},{3,5},{5,7},{... | collective-permute-start | bytes 1572872 | tf_op jit(solution)/shard_map/ppermute | solution.py:23
  18.3 4.4 %collective-permute-start.9 = (bf16[128,2048]{0,1:T(8,128)(2,1)S(1)}, bf16[128,2048]{0,1:T(8,128)(2,1)S(1)}, u32[]{:S(2)}, u32[]{:S(2)}) collective-permute-start(bf16[128,2048]{0,1:T(8,128)(2,1)S(1)} %collective-permute-done.8), channel_id=1, source_target_pairs={{0,2},{2,4},{4,6},{6,8},{8,10},{10,12},{12,14},{1,3},{3,5},{5,7},{... | collective-permute-start | bytes 1572872 | tf_op jit(solution)/shard_map/ppermute | solution.py:23
  23.9 4.4 %collective-permute-start.2 = (bf16[128,2048]{0,1:T(8,128)(2,1)S(1)}, bf16[128,2048]{0,1:T(8,128)(2,1)}, u32[]{:S(2)}, u32[]{:S(2)}) collective-permute-start(bf16[128,2048]{0,1:T(8,128)(2,1)S(1)} %collective-permute-done.1), channel_id=1, source_target_pairs={{0,2},{2,4},{4,6},{6,8},{8,10},{10,12},{12,14},{1,3},{3,5},{5,7},{... | collective-permute-start | bytes 1572872 | tf_op jit(solution)/shard_map/ppermute | solution.py:23
  29.5 4.4 %collective-permute-start.10 = (bf16[128,2048]{0,1:T(8,128)(2,1)S(1)}, bf16[128,2048]{0,1:T(8,128)(2,1)}, u32[]{:S(2)}, u32[]{:S(2)}) collective-permute-start(bf16[128,2048]{0,1:T(8,128)(2,1)S(1)} %collective-permute-done.9), channel_id=1, source_target_pairs={{0,2},{2,4},{4,6},{6,8},{8,10},{10,12},{12,14},{1,3},{3,5},{5,7},{... | collective-permute-start | bytes 1572872 | tf_op jit(solution)/shard_map/ppermute | solution.py:23
  35.1 4.5 %collective-permute-start.3 = (bf16[128,2048]{0,1:T(8,128)(2,1)}, bf16[128,2048]{0,1:T(8,128)(2,1)}, u32[]{:S(2)}, u32[]{:S(2)}) collective-permute-start(bf16[128,2048]{0,1:T(8,128)(2,1)} %collective-permute-done.2), channel_id=1, source_target_pairs={{0,2},{2,4},{4,6},{6,8},{8,10},{10,12},{12,14},{1,3},{3,5},{5,7},{... | collective-permute-start | bytes 1572872 | tf_op jit(solution)/shard_map/ppermute | solution.py:23
  47.0 3.8 collective-permute-start.4
  53.4 4.4 %collective-permute-start.12 = (bf16[128,2048]{0,1:T(8,128)(2,1)}, bf16[128,2048]{0,1:T(8,128)(2,1)}, u32[]{:S(2)}, u32[]{:S(2)}) collective-permute-start(bf16[128,2048]{0,1:T(8,128)(2,1)} %collective-permute-done.11), channel_id=1, source_target_pairs={{0,2},{2,4},{4,6},{6,8},{8,10},{10,12},{12,14},{1,3},{3,5},{5,7},{... | collective-permute-start | bytes 1572872 | tf_op jit(solution)/shard_map/ppermute | solution.py:23
  59.1 4.4 %collective-permute-start.5 = (bf16[128,2048]{0,1:T(8,128)(2,1)}, bf16[128,2048]{0,1:T(8,128)(2,1)}, u32[]{:S(2)}, u32[]{:S(2)}) collective-permute-start(bf16[128,2048]{0,1:T(8,128)(2,1)} %collective-permute-done.4), channel_id=1, source_target_pairs={{0,2},{2,4},{4,6},{6,8},{8,10},{10,12},{12,14},{1,3},{3,5},{5,7},{... | collective-permute-start | bytes 1572872 | tf_op jit(solution)/shard_map/ppermute | solution.py:23
  82.7 6.1 %copy.44 = bf16[896,16,128]{2,0,1:T(8,128)(2,1)} copy(bf16[896,16,128]{0,2,1:T(8,128)(2,1)} %constant_dynamic-update-slice_fusion.3) | data formatting | bytes 7340032
  98.2 6.1 %copy.43 = bf16[896,16,128]{2,0,1:T(8,128)(2,1)} copy(bf16[896,16,128]{0,2,1:T(8,128)(2,1)} %constant_dynamic-update-slice_fusion.10) | data formatting | bytes 7340032
  104.3 37.3 %while.38 = (s32[]{:T(128)}, f32[16,256]{1,0:T(8,128)S(1)}, f32[16,256]{1,0:T(8,128)S(1)}, f32[16,256]{1,0:T(8,128)S(1)}, bf16[256,16,128]{2,0,1:T(8,128)(2,1)},...) while((s32[]{:T(128)}, f32[16,256]{1,0:T(8,128)S(1)}, ...), condition=%wide.region_4.5_spmd.clone, body=%wide.region_0.4_spmd.clone.sunk | while | flops 241302016 | bytes 7640807 | solution.py:61
  141.6 6.2 %pmax.7 = f32[16,256]{1,0:T(8,128)S(1)} all-reduce(f32[16,256]{1,0:T(8,128)S(1)} %get-tuple-element.407), channel_id=1, replica_groups=mesh['chan'=2,'seq'=8,'dp'=2] {'chan'}, use_global_device_ids=true, to_apply=%region_5.6 | all-reduce | flops 4096 | bytes 32768 | tf_op jit(solution)/shard_map/pmax | solution.py:176
  147.7 5.4 %all-reduce = (f32[16,256]{1,0:T(8,128)S(1)}, f32[16,256]{1,0:T(8,128)S(1)}) all-reduce(f32[16,256]{1,0:T(8,128)S(1)} %get-tuple-element.625, f32[16,256]{1,0:T(8,128)S(1)} %get-tuple-element.624), channel_id=1, replica_groups=mesh['chan'=2,'seq'=8,'dp'=2] {'chan'}, use_global_device_ids=true, to_apply=%region_6.7 | all-reduce | flops 8192 | bytes 65536 | tf_op jit(solution)/shard_map/psum | solution.py:178
  154.7 3.8 broadcast.129.clone
  158.4 3.7 broadcast.129
  162.1 85.7 %while.39 = (s32[]{:T(128)}, f32[256,16,128]{0,2,1:T(8,128)}, f32[896,16,128]{0,2,1:T(8,128)}, f32[896,16,128]{0,2,1:T(8,128)}, f32[16]{0:T(128)S(1)}, /*index=5...) while((s32[]{:T(128)}, f32[256,16,128]{0,2,1:T(8,128)}, ...), condition=%wide.region_10.11_spmd.clone, body=%wide.region_8.10_spmd.clone.sunk | while | flops 593922560 | bytes 12747555 | solution.py:121
  250.2 6.6 %collective-permute-start.21 = (bf16[128,2048]{1,0:T(8,128)(2,1)}, bf16[128,2048]{1,0:T(8,128)(2,1)}, u32[]{:S(2)}, u32[]{:S(2)}) collective-permute-start(bf16[128,2048]{1,0:T(8,128)(2,1)} %copy.76), channel_id=1, source_target_pairs={{2,0},{4,2},{6,4},{8,6},{10,8},{12,10},{14,12},{3,1},{5,3},{7,5},{... | collective-permute-start | bytes 1572872 | tf_op jit(solution)/shard_map/ppermute | solution.py:23
  256.8 5.2 %fusion.43 = (f32[128,16,128]{0,2,1:T(8,128)}, f32[128,16,128]{0,2,1:T(8,128)}, f32[128,16,128]{0,2,1:T(8,128)}, f32[128,16,128]{0,2,1:T(8,128)}, f32[128,16,128]{0,2,1:T(8,128)S(1)}, /*index=5*/f32[128,16,128]{0,2,1:T(8,128)S(1)}) fusion(f32[896,16,128]{0,2,1:T(8,128)} %get-tuple-element.411), kind=kLoop, calls=%fused_computation.110 | loop fusion | bytes 12582912 | tf_op jit(solution)/shard_map/slice | solution.py:203
  266.2 5.2 %fusion.42 = (f32[128,16,128]{0,2,1:T(8,128)}, f32[128,16,128]{0,2,1:T(8,128)}, f32[128,16,128]{0,2,1:T(8,128)}, f32[128,16,128]{0,2,1:T(8,128)S(1)}, f32[128,16,128]{0,2,1:T(8,128)}, /*index=5*/f32[128,16,128]{0,2,1:T(8,128)}) fusion(f32[896,16,128]{0,2,1:T(8,128)} %get-tuple-element.412), kind=kLoop, calls=%fused_computation.109 | loop fusion | bytes 12582912 | tf_op jit(solution)/shard_map/slice | solution.py:206
  274.0 2.5 copy.77
  284.9 2.5 copy.78
  300.8 2.7 copy.72
  313.6 2.5 copy.80
  316.2 2.5 copy.73
  328.0 40.2 %psum.23 = f32[16]{0:T(128)} all-reduce(f32[16]{0:T(128)S(1)} %get-tuple-element.413), channel_id=1, replica_groups=mesh['chan'=2,'seq'=8,'dp'=2] {'chan','seq','dp'}, use_global_device_ids=true, to_apply=%region_11.12 | all-reduce | flops 16 | bytes 128 | tf_op jit(solution)/shard_map/psum | solution.py:215
  371.9 2.5 copy.74
  374.4 2.5 copy.81
  381.2 4.7 %collective-permute-start.26 = (bf16[128,2048]{1,0:T(8,128)(2,1)S(1)}, bf16[128,2048]{1,0:T(8,128)(2,1)S(1)}, u32[]{:S(2)}, u32[]{:S(2)}) collective-permute-start(bf16[128,2048]{1,0:T(8,128)(2,1)S(1)} %add_convert_fusion.1), channel_id=1, source_target_pairs={{2,0},{4,2},{6,4},{8,6},{10,8},{12,10},{14,12},{3,1},{5,3},{7,5},{... | collective-permute-start | bytes 1572872 | tf_op jit(solution)/shard_map/ppermute | solution.py:23
  391.3 2.6 collective-permute-done.26
  394.8 4.7 %collective-permute-done.20 = bf16[128,2048]{1,0:T(8,128)(2,1)S(1)} collective-permute-done((bf16[128,2048]{1,0:T(8,128)(2,1)S(1)}, bf16[128,2048]{1,0:T(8,128)(2,1)S(1)}, u32[]{:S(2)}, u32[]{:S(2)}) %collective-permute-start.20) | collective-permute-done | bytes 524320 | tf_op jit(solution)/shard_map/ppermute | solution.py:23
  (264 shorter events, 237.6 us)
Async XLA Ops:
  0.6 62.8 %copy-start.12 = (f32[16]{0:T(128)S(1)}, f32[16]{0:T(128)}, u32[]{:S(2)}) copy-start(f32[16]{0:T(128)} %param.14) | copy-start | bytes 196
  2.0 10.7 %collective-permute-start = (bf16[128,2048]{0,1:T(8,128)(2,1)S(1)}, bf16[128,2048]{0,1:T(8,128)(2,1)S(1)}, u32[]{:S(2)}, u32[]{:S(2)}) collective-permute-start(bf16[128,2048]{0,1:T(8,128)(2,1)S(1)} %bitcast.90), channel_id=1, source_target_pairs={{0,2},{2,4},{4,6},{6,8},{8,10},{10,12},{12,14},{1,3},{3,5},{5,7},{... | collective-permute-start | bytes 1572872 | tf_op jit(solution)/shard_map/ppermute | solution.py:23
  7.9 10.4 %collective-permute-start.8 = (bf16[128,2048]{0,1:T(8,128)(2,1)S(1)}, bf16[128,2048]{0,1:T(8,128)(2,1)S(1)}, u32[]{:S(2)}, u32[]{:S(2)}) collective-permute-start(bf16[128,2048]{0,1:T(8,128)(2,1)S(1)} %bitcast.88), channel_id=1, source_target_pairs={{0,2},{2,4},{4,6},{6,8},{8,10},{10,12},{12,14},{1,3},{3,5},{5,7},{... | collective-permute-start | bytes 1572872 | tf_op jit(solution)/shard_map/ppermute | solution.py:23
  12.7 28.3 %copy-start.8 = (bf16[128,2048]{0,1:T(8,128)(2,1)}, bf16[128,2048]{0,1:T(8,128)(2,1)S(1)}, u32[]{:S(2)}) copy-start(bf16[128,2048]{0,1:T(8,128)(2,1)S(1)} %collective-permute-done) | copy-start | bytes 1572868
  12.7 11.2 %collective-permute-start.1 = (bf16[128,2048]{0,1:T(8,128)(2,1)S(1)}, bf16[128,2048]{0,1:T(8,128)(2,1)S(1)}, u32[]{:S(2)}, u32[]{:S(2)}) collective-permute-start(bf16[128,2048]{0,1:T(8,128)(2,1)S(1)} %collective-permute-done), channel_id=1, source_target_pairs={{0,2},{2,4},{4,6},{6,8},{8,10},{10,12},{12,14},{1,3},{3,5},{5,7},{... | collective-permute-start | bytes 1572872 | tf_op jit(solution)/shard_map/ppermute | solution.py:23
  18.3 16.9 %copy-start.4 = (bf16[128,2048]{0,1:T(8,128)(2,1)}, bf16[128,2048]{0,1:T(8,128)(2,1)S(1)}, u32[]{:S(2)}) copy-start(bf16[128,2048]{0,1:T(8,128)(2,1)S(1)} %collective-permute-done.8) | copy-start | bytes 1572868
  18.3 11.2 %collective-permute-start.9 = (bf16[128,2048]{0,1:T(8,128)(2,1)S(1)}, bf16[128,2048]{0,1:T(8,128)(2,1)S(1)}, u32[]{:S(2)}, u32[]{:S(2)}) collective-permute-start(bf16[128,2048]{0,1:T(8,128)(2,1)S(1)} %collective-permute-done.8), channel_id=1, source_target_pairs={{0,2},{2,4},{4,6},{6,8},{8,10},{10,12},{12,14},{1,3},{3,5},{5,7},{... | collective-permute-start | bytes 1572872 | tf_op jit(solution)/shard_map/ppermute | solution.py:23
  23.9 17.1 %copy-start.10 = (bf16[128,2048]{0,1:T(8,128)(2,1)}, bf16[128,2048]{0,1:T(8,128)(2,1)S(1)}, u32[]{:S(2)}) copy-start(bf16[128,2048]{0,1:T(8,128)(2,1)S(1)} %collective-permute-done.1) | copy-start | bytes 1572868
  23.9 11.2 %collective-permute-start.2 = (bf16[128,2048]{0,1:T(8,128)(2,1)S(1)}, bf16[128,2048]{0,1:T(8,128)(2,1)}, u32[]{:S(2)}, u32[]{:S(2)}) collective-permute-start(bf16[128,2048]{0,1:T(8,128)(2,1)S(1)} %collective-permute-done.1), channel_id=1, source_target_pairs={{0,2},{2,4},{4,6},{6,8},{8,10},{10,12},{12,14},{1,3},{3,5},{5,7},{... | collective-permute-start | bytes 1572872 | tf_op jit(solution)/shard_map/ppermute | solution.py:23
  29.5 34.1 %copy-start.6 = (bf16[128,2048]{0,1:T(8,128)(2,1)}, bf16[128,2048]{0,1:T(8,128)(2,1)S(1)}, u32[]{:S(2)}) copy-start(bf16[128,2048]{0,1:T(8,128)(2,1)S(1)} %collective-permute-done.9) | copy-start | bytes 1572868
  29.5 15.0 %collective-permute-start.10 = (bf16[128,2048]{0,1:T(8,128)(2,1)S(1)}, bf16[128,2048]{0,1:T(8,128)(2,1)}, u32[]{:S(2)}, u32[]{:S(2)}) collective-permute-start(bf16[128,2048]{0,1:T(8,128)(2,1)S(1)} %collective-permute-done.9), channel_id=1, source_target_pairs={{0,2},{2,4},{4,6},{6,8},{8,10},{10,12},{12,14},{1,3},{3,5},{5,7},{... | collective-permute-start | bytes 1572872 | tf_op jit(solution)/shard_map/ppermute | solution.py:23
  35.1 11.9 %collective-permute-start.3 = (bf16[128,2048]{0,1:T(8,128)(2,1)}, bf16[128,2048]{0,1:T(8,128)(2,1)}, u32[]{:S(2)}, u32[]{:S(2)}) collective-permute-start(bf16[128,2048]{0,1:T(8,128)(2,1)} %collective-permute-done.2), channel_id=1, source_target_pairs={{0,2},{2,4},{4,6},{6,8},{8,10},{10,12},{12,14},{1,3},{3,5},{5,7},{... | collective-permute-start | bytes 1572872 | tf_op jit(solution)/shard_map/ppermute | solution.py:23
  41.0 22.6 %collective-permute-start.7 = (bf16[128,2048]{0,1:T(8,128)(2,1)S(1)}, bf16[128,2048]{0,1:T(8,128)(2,1)S(1)}, u32[]{:S(2)}, u32[]{:S(2)}) collective-permute-start(bf16[128,2048]{0,1:T(8,128)(2,1)S(1)} %bitcast.86), channel_id=1, source_target_pairs={{0,16},{16,0},{1,17},{17,1},{2,18},{18,2},{3,19},{19,3},{4,20},{20... | collective-permute-start | bytes 1572872 | tf_op jit(solution)/shard_map/ppermute | solution.py:17
  43.6 23.8 %collective-permute-start.6 = (bf16[128,2048]{0,1:T(8,128)(2,1)S(1)}, bf16[128,2048]{0,1:T(8,128)(2,1)}, u32[]{:S(2)}, u32[]{:S(2)}) collective-permute-start(bf16[128,2048]{0,1:T(8,128)(2,1)S(1)} %bitcast.84), channel_id=1, source_target_pairs={{0,16},{16,0},{1,17},{17,1},{2,18},{18,2},{3,19},{19,3},{4,20},{20... | collective-permute-start | bytes 1572872 | tf_op jit(solution)/shard_map/ppermute | solution.py:17
  44.5 8.9 %collective-permute-start.11 = (bf16[128,2048]{0,1:T(8,128)(2,1)}, bf16[128,2048]{0,1:T(8,128)(2,1)}, u32[]{:S(2)}, u32[]{:S(2)}) collective-permute-start(bf16[128,2048]{0,1:T(8,128)(2,1)} %collective-permute-done.10), channel_id=1, source_target_pairs={{0,2},{2,4},{4,6},{6,8},{8,10},{10,12},{12,14},{1,3},{3,5},{5,7},{... | collective-permute-start | bytes 1572872 | tf_op jit(solution)/shard_map/ppermute | solution.py:23
  47.0 12.0 %collective-permute-start.4 = (bf16[128,2048]{0,1:T(8,128)(2,1)}, bf16[128,2048]{0,1:T(8,128)(2,1)}, u32[]{:S(2)}, u32[]{:S(2)}) collective-permute-start(bf16[128,2048]{0,1:T(8,128)(2,1)} %collective-permute-done.3), channel_id=1, source_target_pairs={{0,2},{2,4},{4,6},{6,8},{8,10},{10,12},{12,14},{1,3},{3,5},{5,7},{... | collective-permute-start | bytes 1572872 | tf_op jit(solution)/shard_map/ppermute | solution.py:23
  53.4 16.8 %collective-permute-start.12 = (bf16[128,2048]{0,1:T(8,128)(2,1)}, bf16[128,2048]{0,1:T(8,128)(2,1)}, u32[]{:S(2)}, u32[]{:S(2)}) collective-permute-start(bf16[128,2048]{0,1:T(8,128)(2,1)} %collective-permute-done.11), channel_id=1, source_target_pairs={{0,2},{2,4},{4,6},{6,8},{8,10},{10,12},{12,14},{1,3},{3,5},{5,7},{... | collective-permute-start | bytes 1572872 | tf_op jit(solution)/shard_map/ppermute | solution.py:23
  59.1 13.1 %collective-permute-start.5 = (bf16[128,2048]{0,1:T(8,128)(2,1)}, bf16[128,2048]{0,1:T(8,128)(2,1)}, u32[]{:S(2)}, u32[]{:S(2)}) collective-permute-start(bf16[128,2048]{0,1:T(8,128)(2,1)} %collective-permute-done.4), channel_id=1, source_target_pairs={{0,2},{2,4},{4,6},{6,8},{8,10},{10,12},{12,14},{1,3},{3,5},{5,7},{... | collective-permute-start | bytes 1572872 | tf_op jit(solution)/shard_map/ppermute | solution.py:23
  70.3 18.5 %collective-permute-start.13 = (bf16[128,2048]{0,1:T(8,128)(2,1)}, bf16[128,2048]{0,1:T(8,128)(2,1)S(1)}, u32[]{:S(2)}, u32[]{:S(2)}) collective-permute-start(bf16[128,2048]{0,1:T(8,128)(2,1)} %collective-permute-done.12), channel_id=1, source_target_pairs={{0,2},{2,4},{4,6},{6,8},{8,10},{10,12},{12,14},{1,3},{3,5},{5,7},{... | collective-permute-start | bytes 1572872 | tf_op jit(solution)/shard_map/ppermute | solution.py:23
  250.2 26.4 %collective-permute-start.21 = (bf16[128,2048]{1,0:T(8,128)(2,1)}, bf16[128,2048]{1,0:T(8,128)(2,1)}, u32[]{:S(2)}, u32[]{:S(2)}) collective-permute-start(bf16[128,2048]{1,0:T(8,128)(2,1)} %copy.76), channel_id=1, source_target_pairs={{2,0},{4,2},{6,4},{8,6},{10,8},{12,10},{14,12},{3,1},{5,3},{7,5},{... | collective-permute-start | bytes 1572872 | tf_op jit(solution)/shard_map/ppermute | solution.py:23
  264.3 16.4 %collective-permute-start.15 = (bf16[128,2048]{1,0:T(8,128)(2,1)}, bf16[128,2048]{1,0:T(8,128)(2,1)}, u32[]{:S(2)}, u32[]{:S(2)}) collective-permute-start(bf16[128,2048]{1,0:T(8,128)(2,1)} %copy.69), channel_id=1, source_target_pairs={{2,0},{4,2},{6,4},{8,6},{10,8},{12,10},{14,12},{3,1},{5,3},{7,5},{... | collective-permute-start | bytes 1572872 | tf_op jit(solution)/shard_map/ppermute | solution.py:23
  278.8 10.8 %collective-permute-start.22 = (bf16[128,2048]{1,0:T(8,128)(2,1)}, bf16[128,2048]{1,0:T(8,128)(2,1)}, u32[]{:S(2)}, u32[]{:S(2)}) collective-permute-start(bf16[128,2048]{1,0:T(8,128)(2,1)} %add_convert_fusion.5), channel_id=1, source_target_pairs={{2,0},{4,2},{6,4},{8,6},{10,8},{12,10},{14,12},{3,1},{5,3},{7,5},{... | collective-permute-start | bytes 1572872 | tf_op jit(solution)/shard_map/ppermute | solution.py:23
  283.0 12.2 %collective-permute-start.16 = (bf16[128,2048]{1,0:T(8,128)(2,1)}, bf16[128,2048]{1,0:T(8,128)(2,1)}, u32[]{:S(2)}, u32[]{:S(2)}) collective-permute-start(bf16[128,2048]{1,0:T(8,128)(2,1)} %add_convert_fusion.11), channel_id=1, source_target_pairs={{2,0},{4,2},{6,4},{8,6},{10,8},{12,10},{14,12},{3,1},{5,3},{7,5},{... | collective-permute-start | bytes 1572872 | tf_op jit(solution)/shard_map/ppermute | solution.py:23
  291.9 11.6 %collective-permute-start.23 = (bf16[128,2048]{1,0:T(8,128)(2,1)}, bf16[128,2048]{1,0:T(8,128)(2,1)}, u32[]{:S(2)}, u32[]{:S(2)}) collective-permute-start(bf16[128,2048]{1,0:T(8,128)(2,1)} %add_convert_fusion.4), channel_id=1, source_target_pairs={{2,0},{4,2},{6,4},{8,6},{10,8},{12,10},{14,12},{3,1},{5,3},{7,5},{... | collective-permute-start | bytes 1572872 | tf_op jit(solution)/shard_map/ppermute | solution.py:23
  297.5 10.8 %collective-permute-start.17 = (bf16[128,2048]{1,0:T(8,128)(2,1)}, bf16[128,2048]{1,0:T(8,128)(2,1)}, u32[]{:S(2)}, u32[]{:S(2)}) collective-permute-start(bf16[128,2048]{1,0:T(8,128)(2,1)} %add_convert_fusion.10), channel_id=1, source_target_pairs={{2,0},{4,2},{6,4},{8,6},{10,8},{12,10},{14,12},{3,1},{5,3},{7,5},{... | collective-permute-start | bytes 1572872 | tf_op jit(solution)/shard_map/ppermute | solution.py:23
  305.7 13.0 %collective-permute-start.24 = (bf16[128,2048]{1,0:T(8,128)(2,1)}, bf16[128,2048]{1,0:T(8,128)(2,1)}, u32[]{:S(2)}, u32[]{:S(2)}) collective-permute-start(bf16[128,2048]{1,0:T(8,128)(2,1)} %add_convert_fusion.3), channel_id=1, source_target_pairs={{2,0},{4,2},{6,4},{8,6},{10,8},{12,10},{14,12},{3,1},{5,3},{7,5},{... | collective-permute-start | bytes 1572872 | tf_op jit(solution)/shard_map/ppermute | solution.py:23
  310.6 12.3 %collective-permute-start.18 = (bf16[128,2048]{1,0:T(8,128)(2,1)}, bf16[128,2048]{1,0:T(8,128)(2,1)}, u32[]{:S(2)}, u32[]{:S(2)}) collective-permute-start(bf16[128,2048]{1,0:T(8,128)(2,1)} %add_convert_fusion.9), channel_id=1, source_target_pairs={{2,0},{4,2},{6,4},{8,6},{10,8},{12,10},{14,12},{3,1},{5,3},{7,5},{... | collective-permute-start | bytes 1572872 | tf_op jit(solution)/shard_map/ppermute | solution.py:23
  321.0 58.7 %collective-permute-start.25 = (bf16[128,2048]{1,0:T(8,128)(2,1)}, bf16[128,2048]{1,0:T(8,128)(2,1)}, u32[]{:S(2)}, u32[]{:S(2)}) collective-permute-start(bf16[128,2048]{1,0:T(8,128)(2,1)} %add_convert_fusion.2), channel_id=1, source_target_pairs={{2,0},{4,2},{6,4},{8,6},{10,8},{12,10},{14,12},{3,1},{5,3},{7,5},{... | collective-permute-start | bytes 1572872 | tf_op jit(solution)/shard_map/ppermute | solution.py:23
  325.2 60.7 %collective-permute-start.19 = (bf16[128,2048]{1,0:T(8,128)(2,1)}, bf16[128,2048]{1,0:T(8,128)(2,1)}, u32[]{:S(2)}, u32[]{:S(2)}) collective-permute-start(bf16[128,2048]{1,0:T(8,128)(2,1)} %add_convert_fusion.8), channel_id=1, source_target_pairs={{2,0},{4,2},{6,4},{8,6},{10,8},{12,10},{14,12},{3,1},{5,3},{7,5},{... | collective-permute-start | bytes 1572872 | tf_op jit(solution)/shard_map/ppermute | solution.py:23
  377.0 12.3 %collective-permute-start.14 = (bf16[128,2048]{1,0:T(8,128)(2,1)}, bf16[128,2048]{1,0:T(8,128)(2,1)}, u32[]{:S(2)}, u32[]{:S(2)}) collective-permute-start(bf16[128,2048]{1,0:T(8,128)(2,1)} %copy.68), channel_id=1, source_target_pairs={{0,16},{16,0},{1,17},{17,1},{2,18},{18,2},{3,19},{19,3},{4,20},{20... | collective-permute-start | bytes 1572872 | tf_op jit(solution)/shard_map/ppermute | solution.py:17
  381.2 12.6 %collective-permute-start.26 = (bf16[128,2048]{1,0:T(8,128)(2,1)S(1)}, bf16[128,2048]{1,0:T(8,128)(2,1)S(1)}, u32[]{:S(2)}, u32[]{:S(2)}) collective-permute-start(bf16[128,2048]{1,0:T(8,128)(2,1)S(1)} %add_convert_fusion.1), channel_id=1, source_target_pairs={{2,0},{4,2},{6,4},{8,6},{10,8},{12,10},{14,12},{3,1},{5,3},{7,5},{... | collective-permute-start | bytes 1572872 | tf_op jit(solution)/shard_map/ppermute | solution.py:23
  387.4 12.1 %collective-permute-start.20 = (bf16[128,2048]{1,0:T(8,128)(2,1)S(1)}, bf16[128,2048]{1,0:T(8,128)(2,1)S(1)}, u32[]{:S(2)}, u32[]{:S(2)}) collective-permute-start(bf16[128,2048]{1,0:T(8,128)(2,1)S(1)} %add_convert_fusion.7), channel_id=1, source_target_pairs={{2,0},{4,2},{6,4},{8,6},{10,8},{12,10},{14,12},{3,1},{5,3},{7,5},{... | collective-permute-start | bytes 1572872 | tf_op jit(solution)/shard_map/ppermute | solution.py:23
  (8 other events, 74.0 us)
where the time goes:
time: 404 us; the launch traced here: 400 us
  matrix products  110 us (27%)
  local copies, waits for them, and re-layouts  95.4 us (24%)
  starting transfers between devices  78.4 us (19%)
  blocking collectives  51.7 us (13%)
  other arithmetic  40.6 us (10%)
  waiting for transfers between devices  21.8 us (5%)
    ppermute x24, starting transfers between devices, from_behind(): lax.ppermute(value, axis, [(source, source + steps) for source in range(f...  75.8 us
    psum x1, blocking collectives, shards(): bias_out = lax.psum(bias_sum, ('chan', 'seq', 'dp'))  40.2 us
    unnamed x46, local copies, waits for them, and re-layouts  39.1 us
    dot_general x16, matrix products, local_scores(): jnp.einsum('pgd,sgd->gps', query_part, key_part, preferred_element_type=j...  28.7 us
    ppermute x24, waiting for transfers between devices, from_behind(): lax.ppermute(value, axis, [(source, source + steps) for source in range(f...  21.8 us
    slice x8, local copies, waits for them, and re-layouts, value_block(): return value_flat[position * frames:(position + 1) * frames]  19.4 us
    slice x8, local copies, waits for them, and re-layouts, key_block(): return key_flat[position * frames:(position + 1) * frames]  18.5 us
    dot_general x8, matrix products, backward_group_step(): jnp.einsum('gps,pgd->sgd', weight_low, grad_part, preferred_element_type=...  17.7 us
  transfers between devices with their start and end apart: 27, of which 12 were waited for; matrix products, arithmetic and copies ran while one was open for 23% of the time, Pallas kernels for 0%

commit v1 on v0

v1 whole, which is shorter than its diff:
```python
import functools
import math

import jax
import jax.numpy as jnp
from jax import lax
from jax.experimental import pallas as pl
from jax.experimental.pallas import tpu as pltpu
from jax.sharding import PartitionSpec as P

LOOKBACK = 6
NEG_FILL = -1e30
EXTRA = 8


def pack_kernel(copies, q_ref, k_ref, v_ref, g_ref, send_ref, sems):
    width = send_ref.shape[3]
    sources = (q_ref, k_ref, v_ref, g_ref)
    started = []
    for dest in range(send_ref.shape[0]):
        head = dest // copies
        for kind, source in enumerate(sources):
            copy = pltpu.make_async_copy(
                source.at[:, pl.ds(head * width, width)], send_ref.at[dest, kind], sems.at[dest, kind]
            )
            copy.start()
            started.append(copy)
    for copy in started:
        copy.wait()


def unpack_kernel(home_ref, q_ref, k_ref, v_ref, sems):
    heads = home_ref.shape[0]
    rows, width = q_ref.shape[0], home_ref.shape[2]
    started = []
    for head in range(heads):
        for kind, target in enumerate((q_ref, k_ref, v_ref)):
            copy = pltpu.make_async_copy(
                home_ref.at[head, pl.ds(kind * rows, rows)],
                target.at[:, pl.ds(head * width, width)],
                sems.at[head, kind],
            )
            copy.start()
            started.append(copy)
    for copy in started:
        copy.wait()


def head_kernel(copies, length_ref, place_ref, bias_ref, got_ref, out_ref, kt_ref, s_ref, d_ref, dk_ref, dv_ref, bias_acc):
    devices, _, rows, width = got_ref.shape
    blocks = devices // 2
    both = 2 * rows
    root_scale = 1.0 / math.sqrt(width)
    log2_scale = root_scale * math.log2(math.e)
    length = length_ref[0]
    bias = bias_ref[place_ref[0]] * math.log2(math.e)
    part = place_ref[1]

    def pair(kind, block):
        return jnp.concatenate([got_ref[block, kind], got_ref[blocks + block, kind]], axis=0)

    def dot(left, right, contract):
        return lax.dot_general(left, right, (contract, ((), ())), preferred_element_type=jnp.float32)

    column = lax.broadcasted_iota(jnp.int32, (1, both), 1)
    own = [jnp.where((column // rows) == c, 0.0, bias) for c in range(2)]
    key_row = lax.broadcasted_iota(jnp.int32, (rows, both), 0)
    query_column = lax.broadcasted_iota(jnp.int32, (rows, both), 1) % rows
    causal = key_row <= query_column
    in_reach = key_row > query_column

    out_ref[...] = jnp.zeros_like(out_ref)
    dk_ref[...] = jnp.zeros_like(dk_ref)
    dv_ref[...] = jnp.zeros_like(dv_ref)
    bias_acc[...] = jnp.zeros_like(bias_acc)

    def fold(tile, op):
        return op(tile.reshape(tile.shape[0] // 8, 8, tile.shape[1]), axis=0)

    def row_block(block, tiles):
        queries = pair(0, block)
        grads = pair(3, block)
        first = block - (tiles - 1)
        peak = jnp.full((8, both), NEG_FILL, jnp.float32)
        for t in range(tiles):
            raw = dot(pair(1, first + t), queries, ((1,), (1,)))
            for c in range(2):
                tile = raw[c * rows : (c + 1) * rows] * log2_scale + own[c]
                if t == tiles - 1:
                    tile = jnp.where(causal, tile, NEG_FILL)
                if tiles == LOOKBACK + 1 and t == 0:
                    tile = jnp.where(in_reach, tile, NEG_FILL)
                s_ref[t, c * rows : (c + 1) * rows] = tile
                peak = jnp.maximum(peak, fold(tile, jnp.max))
        peak = jnp.max(peak, axis=0, keepdims=True)
        total = jnp.zeros((8, both), jnp.float32)
        moment = jnp.zeros((8, both), jnp.float32)
        for t in range(tiles):
            weight_grad = dot(pair(2, first + t), grads, ((1,), (1,)))
            d_ref[t] = weight_grad
            power = jnp.exp2(s_ref[t] - peak)
            s_ref[t] = power
            total = total + fold(power, jnp.sum)
            moment = moment + fold(power * weight_grad, jnp.sum)
        total = jnp.sum(total, axis=0, keepdims=True)
        moment = jnp.sum(moment, axis=0, keepdims=True)
        frame = block * rows + column % rows
        live = frame < length
        if copies > 1:
            live = live & ((column * copies) // both == part)
        inverse = jnp.where(live, 1.0 / total, 0.0)
        delta = moment * inverse
        query_sum = jnp.zeros((width, both), jnp.float32)
        cross = jnp.zeros((8, rows), jnp.float32)
        for t in range(tiles):
            weights = s_ref[t] * inverse
            score_grad = weights * (d_ref[t] - delta)
            cross = cross + fold(score_grad[:rows, rows:], jnp.sum) + fold(score_grad[rows:, :rows], jnp.sum)
            weight_low = weights.astype(jnp.bfloat16)
            score_low = score_grad.astype(jnp.bfloat16)
            dv_ref[first + t] += dot(weight_low, grads, ((1,), (0,)))
            dk_ref[first + t] += dot(score_low, queries, ((1,), (0,)))
            query_sum = query_sum + dot(kt_ref[first + t], score_low, ((1,), (0,)))
        bias_acc[...] += cross
        query_grad = (query_sum.T * root_scale).astype(jnp.bfloat16)
        out_ref[block, 0:rows] = query_grad[:rows]
        out_ref[blocks + block, 0:rows] = query_grad[rows:]

    for block in range(blocks):
        kt_ref[block] = pair(1, block).T

    live_blocks = jnp.minimum((length + rows - 1) // rows, blocks)
    for block in range(min(LOOKBACK, blocks)):
        @pl.when(block < live_blocks)
        def _():
            row_block(block, block + 1)

    if blocks > LOOKBACK:
        def step(block, carried):
            row_block(block, LOOKBACK + 1)
            return carried

        lax.fori_loop(LOOKBACK, live_blocks, step, 0)

    for block in range(blocks):
        key_grad = (dk_ref[block] * root_scale).astype(jnp.bfloat16)
        value_grad = dv_ref[block].astype(jnp.bfloat16)
        for c in range(2):
            out_ref[c * blocks + block, rows : 2 * rows] = key_grad[c * rows : (c + 1) * rows]
            out_ref[c * blocks + block, 2 * rows : 3 * rows] = value_grad[c * rows : (c + 1) * rows]

    whole = jnp.sum(jnp.sum(bias_acc[...], axis=0, keepdims=True), axis=1, keepdims=True)
    whole = jnp.broadcast_to(whole, (1, width))
    high = whole.astype(jnp.bfloat16)
    rest = whole - high.astype(jnp.float32)
    middle = rest.astype(jnp.bfloat16)
    low = (rest - middle.astype(jnp.float32)).astype(jnp.bfloat16)
    lane = lax.broadcasted_iota(jnp.int32, (1, width), 1)
    pieces = jnp.where(
        lane == 0,
        high.astype(jnp.float32),
        jnp.where(lane == 1, middle.astype(jnp.float32), jnp.where(lane == 2, low.astype(jnp.float32), 0.0)),
    ).astype(jnp.bfloat16)
    pieces = jnp.broadcast_to(pieces, (EXTRA, width))
    for dest in range(devices):
        out_ref[dest, 3 * rows : 3 * rows + EXTRA] = pieces


def summed_over(value, axis):
    count = lax.axis_size(axis)
    if count & (count - 1):
        return lax.psum(value, axis)
    step = 1
    while step < count:
        pairs = [(source, source ^ step) for source in range(count)]
        value = value + lax.ppermute(value, axis, pairs)
        step *= 2
    return value


def shards(queries, keys, values, out_grad, cross_bias, lengths):
    rows, features = queries.shape[2:]
    heads = cross_bias.shape[0]
    width = features // heads
    blocks = lax.axis_size("seq")
    devices = lax.axis_size("chan") * blocks
    copies = devices // heads
    place = lax.axis_index("chan") * blocks + lax.axis_index("seq")
    vmem = pl.BlockSpec(memory_space=pltpu.VMEM)
    smem = pl.BlockSpec(memory_space=pltpu.SMEM)
    anywhere = pl.BlockSpec(memory_space=pl.ANY)

    send = pl.pallas_call(
        functools.partial(pack_kernel, copies),
        out_shape=jax.ShapeDtypeStruct((devices, 4, rows, width), queries.dtype),
        in_specs=[anywhere] * 4,
        out_specs=vmem,
        scratch_shapes=[pltpu.SemaphoreType.DMA((devices, 4))],
        name="pack",
    )(queries[0, 0], keys[0, 0], values[0, 0], out_grad[0, 0])
    got = lax.all_to_all(send, ("chan", "seq"), 0, 0, tiled=True)

    payload = 3 * rows + EXTRA
    both = 2 * rows
    tiles = min(LOOKBACK + 1, blocks)
    back = pl.pallas_call(
        functools.partial(head_kernel, copies),
        out_shape=jax.ShapeDtypeStruct((devices, payload, width), queries.dtype),
        in_specs=[smem, smem, smem, vmem],
        out_specs=vmem,
        scratch_shapes=[
            pltpu.VMEM((blocks, width, both), jnp.bfloat16),
            pltpu.VMEM((tiles, both, both), jnp.float32),
            pltpu.VMEM((tiles, both, both), jnp.float32),
            pltpu.VMEM((blocks, both, width), jnp.float32),
            pltpu.VMEM((blocks, both, width), jnp.float32),
            pltpu.VMEM((8, rows), jnp.float32),
        ],
        name="head",
    )(lengths, jnp.stack([place // copies, place % copies]).astype(jnp.int32), cross_bias, got)
    home = lax.all_to_all(back, ("chan", "seq"), 0, 0, tiled=True)

    pieces = home[:, 3 * rows, :3].astype(jnp.float32)
    if copies > 1:
        pieces = jnp.sum(pieces.reshape(heads, copies, 3), axis=1)
        home = jnp.sum(home.reshape(heads, copies, payload, width).astype(jnp.float32), axis=1).astype(queries.dtype)
    bias_out = summed_over(pieces[:, 0] + pieces[:, 1] + pieces[:, 2], "dp")
    flat = jax.ShapeDtypeStruct((rows, features), queries.dtype)
    grads = pl.pallas_call(
        unpack_kernel,
        out_shape=(flat, flat, flat),
        in_specs=[vmem],
        out_specs=(anywhere, anywhere, anywhere),
        scratch_shapes=[pltpu.SemaphoreType.DMA((heads, 3))],
        name="unpack",
    )(home)
    return tuple(grad[None, None] for grad in grads) + (bias_out,)


def solution(mesh):
    placed = P("dp", "chan", "seq", None)
    return jax.shard_map(
        shards,
        mesh=mesh,
        in_specs=(placed, placed, placed, placed, P(), P("dp")),
        out_specs=(placed, placed, placed, P()),
        check_vma=False,
    )
```

time: 404 us -> 120 us (0.30); the launches traced: 400 us -> 122 us
  matrix products: 110 us -> 0 us
  local copies, waits for them, and re-layouts: 95.4 us -> 2.45 us
  starting transfers between devices: 78.4 us -> 7.37 us
  other arithmetic: 40.6 us -> 1.12 us
  waiting for transfers between devices: 21.8 us -> 44.9 us
  Pallas kernels: 0 us -> 20 us
  blocking collectives: 51.7 us -> 44.6 us
    dot_general x56 -> x0, matrix products: 110 us -> none  [the longest x16 28.7 us: local_scores(): jnp.einsum('pgd,sgd->gps', query_part, key_part, preferred_element_type=j...]
    ppermute x27 -> x1, starting transfers between devices: 78.4 us -> 0.02 us  [summed_over(): value = value + lax.ppermute(value, axis, pairs)]
    psum x2 -> x0, blocking collectives: 45.6 us -> none  [the longest x1 40.2 us: shards(): bias_out = lax.psum(bias_sum, ('chan', 'seq', 'dp'))]
    all_to_all x0 -> x1, waiting for transfers between devices: none -> 44.9 us  [shards(): got = lax.all_to_all(send, ('chan', 'seq'), 0, 0, tiled=True)]
    all_to_all x0 -> x1, blocking collectives: none -> 44.6 us  [shards(): home = lax.all_to_all(back, ('chan', 'seq'), 0, 0, tiled=True)]
    slice x16 -> x0, local copies, waits for them, and re-layouts: 37.9 us -> none  [the longest x8 19.4 us: value_block(): return value_flat[position * frames:(position + 1) * frames]]
    unnamed x46 -> x4, local copies, waits for them, and re-layouts: 39.1 us -> 2.37 us
    convert_element_type x20 -> x1, other arithmetic: 22 us -> 0.01 us  [shards(): pieces = home[:, 3 * rows, :3].astype(jnp.float32)]
  transfers between devices with their start and end apart: 27 -> 2, of which waited for: 12 -> 1; matrix products, arithmetic and copies ran while one was open for 23% -> 0% of each run, Pallas kernels for 0% -> 2%
where the time goes in v1:
time: 120 us; the launch traced here: 122 us
  waiting for transfers between devices  44.9 us (37%)
  blocking collectives  44.6 us (37%)
  Pallas kernels  20 us (17%)
  starting transfers between devices  7.37 us (6%)
  local copies, waits for them, and re-layouts  2.45 us (2%)
  between operations  1.33 us (1%)
    all_to_all x1, waiting for transfers between devices, shards(): got = lax.all_to_all(send, ('chan', 'seq'), 0, 0, tiled=True)  44.9 us
    all_to_all x1, blocking collectives, shards(): home = lax.all_to_all(back, ('chan', 'seq'), 0, 0, tiled=True)  44.6 us
    pallas_call x1, Pallas kernels, shards(): pl.pallas_call(functools.partial(head_kernel, copies), out_shape=jax.Shap...  13.6 us
    all_to_all x1, starting transfers between devices, shards(): got = lax.all_to_all(send, ('chan', 'seq'), 0, 0, tiled=True)  7.35 us
    pallas_call x1, Pallas kernels, shards(): pl.pallas_call(functools.partial(pack_kernel, copies), out_shape=jax.Shap...  3.45 us
    pallas_call x1, Pallas kernels, shards(): pl.pallas_call(unpack_kernel, out_shape=(flat, flat, flat), in_specs=[vme...  2.96 us
  transfers between devices with their start and end apart: 2, of which 1 were waited for; matrix products, arithmetic and copies ran while one was open for 0% of the time, Pallas kernels for 2%

profile of v1, /device:TPU:1, one launch (start us, length us, event | category | flops | bytes accessed | tf_op | source)
XLA Modules:
  0.0 121.7 jit_solution(4936933443046835050)
XLA Ops:
  0.6 3.4 %pack.1 = bf16[16,4,128,128]{3,2,1,0:T(8,128)(2,1)} custom-call(bf16[128,2048]{1,0:T(8,128)(2,1)} %bitcast.13, bf16[128,2048]{1,0:T(8,128)(2,1)} %bitcast.14, bf16[128,2048]{1,0:T(8,128)(2,1)} %bitcast.15, bf16[128,2048]{1,0:T(8,128)(2,1)} %bitcast.16), custom_call_target="tpu_custom_call" | custom-call | tf_op jit(solution)/shard_map/pack/pallas_call | solution.py:193
  4.1 7.4 %all-to-all-start = ((bf16[16,4,128,128]{3,2,1,0:T(8,128)(2,1)}), bf16[16,4,128,128]{3,2,1,0:T(8,128)(2,1)S(1)}, u32[]{:S(2)}, u32[]{:S(2)}) async-start(bf16[16,4,128,128]{3,2,1,0:T(8,128)(2,1)} %pack.1), calls=%async_computation | async-start | bytes 4194304 | tf_op jit(solution)/shard_map/all_to_all | solution.py:201
  12.1 0.6 pad_add_fusion.place_ref
  12.7 44.9 %all-to-all-done.got_ref = bf16[16,4,128,128]{3,2,1,0:T(8,128)(2,1)S(1)} async-done(((bf16[16,4,128,128]{3,2,1,0:T(8,128)(2,1)}), bf16[16,4,128,128]{3,2,1,0:T(8,128)(2,1)S(1)}, u32[]{:S(2)}, u32[]{:S(2)}) %all-to-all-start) | async-done | bytes 2097184 | tf_op jit(solution)/shard_map/all_to_all | solution.py:201
  57.5 0.0 copy-start
  57.5 1.3 %copy-done = bf16[16,4,128,128]{3,2,1,0:T(8,128)(2,1)} copy-done((bf16[16,4,128,128]{3,2,1,0:T(8,128)(2,1)}, bf16[16,4,128,128]{3,2,1,0:T(8,128)(2,1)S(1)}, u32[]{:S(2)}) %copy-start) | copy-done | bytes 2097176
  58.9 13.6 %head.1 = bf16[16,392,128]{2,1,0:T(8,128)(2,1)} custom-call(s32[1]{0:T(128)S(6)} %copy.12.length_ref, s32[2]{0:T(128)} %pad_add_fusion.place_ref, f32[16]{0:T(128)} %bias_ref.1, bf16[16,4,128,128]{3,2,1,0:T(8,128)(2,1)} %copy-done), custom_call_target="tpu_custom_call" | custom-call | tf_op jit(solution)/shard_map/head/pallas_call | solution.py:206
  72.4 44.6 %all_to_all.10.home_ref = bf16[16,392,128]{2,1,0:T(8,128)(2,1)S(1)} all-to-all(bf16[16,392,128]{2,1,0:T(8,128)(2,1)} %head.1), channel_id=1, replica_groups=mesh['chan'=2,'seq'=8,'dp'=2] {'chan','seq'}, dimensions={0} | all-to-all | bytes 3211264 | tf_op jit(solution)/shard_map/all_to_all | solution.py:221
  117.0 0.0 copy-start.1
  117.0 0.1 copy.11
  117.1 0.0 collective-permute-start
  117.1 1.0 copy-done.1
  118.2 3.0 %unpack.1 = (bf16[128,2048]{1,0:T(8,128)(2,1)}, bf16[128,2048]{1,0:T(8,128)(2,1)}, bf16[128,2048]{1,0:T(8,128)(2,1)}) custom-call(bf16[16,392,128]{2,1,0:T(8,128)(2,1)} %copy-done.1), custom_call_target="tpu_custom_call" | custom-call | tf_op jit(solution)/shard_map/unpack/pallas_call | solution.py:229
  121.1 0.0 collective-permute-done
  121.1 0.5 fusion
  (2 shorter events, 0.0 us)
Async XLA Ops:
  4.1 53.5 %all-to-all-start = ((bf16[16,4,128,128]{3,2,1,0:T(8,128)(2,1)}), bf16[16,4,128,128]{3,2,1,0:T(8,128)(2,1)S(1)}, u32[]{:S(2)}, u32[]{:S(2)}) async-start(bf16[16,4,128,128]{3,2,1,0:T(8,128)(2,1)} %pack.1), calls=%async_computation | async-start | bytes 4194304 | tf_op jit(solution)/shard_map/all_to_all | solution.py:201
  57.5 1.3 %copy-start = (bf16[16,4,128,128]{3,2,1,0:T(8,128)(2,1)}, bf16[16,4,128,128]{3,2,1,0:T(8,128)(2,1)S(1)}, u32[]{:S(2)}) copy-start(bf16[16,4,128,128]{3,2,1,0:T(8,128)(2,1)S(1)} %all-to-all-done.got_ref) | copy-start | bytes 6291460
  117.0 1.2 copy-start.1
  117.1 4.0 %collective-permute-start = (f32[16]{0:T(128)S(1)}, f32[16]{0:T(128)S(1)}, u32[]{:S(2)}, u32[]{:S(2)}) collective-permute-start(f32[16]{0:T(128)S(1)} %add_bitcast_fusion), channel_id=1, source_target_pairs={{0,1},{1,0},{2,3},{3,2},{4,5},{5,4},{6,7},{7,6},{8,9},{9,8},{10,11... | collective-permute-start | bytes 200 | tf_op jit(solution)/shard_map/ppermute | solution.py:176

commit v2 on v1

v2 whole, which is shorter than its diff:
```python
import functools
import math

import jax
import jax.numpy as jnp
from jax import lax
from jax.experimental import pallas as pl
from jax.experimental.pallas import tpu as pltpu
from jax.sharding import PartitionSpec as P


LOOKBACK = 6
NEG_FILL = -1e30
EXTRA = 8
LOG2_E = math.log2(math.e)
SLACK_BYTES = 6 << 20


def stages(devices):
    seats = [0, 1, devices // 2, devices // 2 + 1]
    lanes = [2 * step for step in range(devices // 4)]
    return seats, lanes


def places_of(devices):
    seats, lanes = stages(devices)
    return [(i, j, lane + seat) for i, lane in enumerate(lanes) for j, seat in enumerate(seats)]


def run_all(copies):
    for copy in copies:
        copy.start()
    for copy in copies:
        copy.wait()


def piece(pieces, lanes_first, i, j, devices):
    seats, lanes = stages(devices)
    firsts = len(lanes) if lanes_first else len(seats)
    near, far = (i, j) if lanes_first else (j, i)
    return pieces[near].at[0] if far == 0 else pieces[firsts + far - 1].at[near]


def gathered(place, pieces, lanes_first, target, sems):
    devices = target.shape[0]
    return [
        pltpu.make_async_copy(piece(pieces, lanes_first, i, j, devices), target.at[place ^ mask], sems.at[index])
        for index, (i, j, mask) in enumerate(places_of(devices))
    ]


def scattered(place, source, refs, lanes_first, sems):
    return [
        pltpu.make_async_copy(
            source.at[place ^ mask], (refs[i].at[j] if lanes_first else refs[j].at[i]), sems.at[index]
        )
        for index, (i, j, mask) in enumerate(places_of(source.shape[0]))
    ]


def pack_kernel(copies, lanes_first, place_ref, first_ref, second_ref, *refs):
    sems = refs[-1]
    width = refs[0].shape[-1]
    started = []
    for index, (i, j, mask) in enumerate(places_of(sems.shape[0])):
        head = (place_ref[0] ^ mask) // copies
        columns = pl.ds(pl.multiple_of(head * width, width), width)
        target = refs[i].at[j] if lanes_first else refs[j].at[i]
        for kind, source in enumerate((first_ref, second_ref)):
            started.append(pltpu.make_async_copy(source.at[:, columns], target.at[kind], sems.at[index, kind]))
    run_all(started)


def unpack_kernel(copies, lanes_first, place_ref, *refs):
    pieces, (out, sums, home, sems) = refs[:-4], refs[-4:]
    devices = sems.shape[0]
    rows = out.shape[0]
    width = home.shape[-1]
    started = []
    for index, (i, j, mask) in enumerate(places_of(devices)):
        other = place_ref[0] ^ mask
        source = piece(pieces, lanes_first, i, j, devices).at[pl.ds(0, rows)]
        target = home.at[other]
        if copies == 1:
            target = out.at[:, pl.ds(pl.multiple_of(other * width, width), width)]
        started.append(pltpu.make_async_copy(source, target, sems.at[index]))
    run_all(started)
    if copies > 1:
        for head in range(devices // copies):
            value = home[head * copies].astype(jnp.float32)
            for other in range(1, copies):
                value = value + home[head * copies + other].astype(jnp.float32)
            sums[:, head * width : (head + 1) * width] = value.astype(sums.dtype)
        run_all([pltpu.make_async_copy(sums, out, sems.at[0])])


def dot(left, right, contract):
    return lax.dot_general(left, right, (contract, ((), ())), preferred_element_type=jnp.float32)


def fold(tile, op):
    return op(tile.reshape(tile.shape[0] // 8, 8, tile.shape[1]), axis=0)


def pair(ref, kind, block):
    blocks = ref.shape[0] // 2
    return jnp.concatenate([ref[block, kind], ref[blocks + block, kind]], axis=0)


def tile_count(blocks):
    return sum(min(block, LOOKBACK) + 1 for block in range(blocks))


def for_blocks(length, rows, blocks, row_block):
    live_blocks = jnp.minimum((length + rows - 1) // rows, blocks)
    for block in range(min(LOOKBACK, blocks)):
        @pl.when(block < live_blocks)
        def _():
            row_block(block, tile_count(block), block + 1)

    if blocks > LOOKBACK:
        def step(block, carried):
            row_block(block, tile_count(LOOKBACK) + (block - LOOKBACK) * (LOOKBACK + 1), LOOKBACK + 1)
            return carried

        lax.fori_loop(LOOKBACK, live_blocks, step, 0)


def stats_kernel(copies, length_ref, place_ref, bias_ref, *refs):
    pieces, (qk_ref, weight_ref, sems) = refs[:-3], refs[-3:]
    devices, _, rows, width = qk_ref.shape
    both = 2 * rows
    log2_scale = LOG2_E / math.sqrt(width)
    place = place_ref[0]
    bias = bias_ref[place // copies] * LOG2_E
    part = place % copies
    length = length_ref[0]
    arriving = gathered(place, pieces, True, qk_ref, sems)
    run_all(arriving)

    column = lax.broadcasted_iota(jnp.int32, (1, both), 1)
    own = [jnp.where((column // rows) == c, 0.0, bias) for c in range(2)]
    key_row = lax.broadcasted_iota(jnp.int32, (rows, both), 0)
    query_column = lax.broadcasted_iota(jnp.int32, (rows, both), 1) % rows
    causal = key_row <= query_column
    in_reach = key_row > query_column

    def row_block(block, base, tiles):
        queries = pair(qk_ref, 0, block)
        first = block - (tiles - 1)
        peak = jnp.full((8, both), NEG_FILL, jnp.float32)
        for t in range(tiles):
            raw = dot(pair(qk_ref, 1, first + t), queries, ((1,), (1,)))
            for c in range(2):
                tile = raw[c * rows : (c + 1) * rows] * log2_scale + own[c]
                if t == tiles - 1:
                    tile = jnp.where(causal, tile, NEG_FILL)
                if tiles == LOOKBACK + 1 and t == 0:
                    tile = jnp.where(in_reach, tile, NEG_FILL)
                weight_ref[base + t, c * rows : (c + 1) * rows] = tile
                peak = jnp.maximum(peak, fold(tile, jnp.max))
        peak = jnp.max(peak, axis=0, keepdims=True)
        total = jnp.zeros((8, both), jnp.float32)
        for t in range(tiles):
            power = jnp.exp2(weight_ref[base + t] - peak)
            weight_ref[base + t] = power
            total = total + fold(power, jnp.sum)
        total = jnp.sum(total, axis=0, keepdims=True)
        live = block * rows + column % rows < length
        if copies > 1:
            live = live & ((column * copies) // both == part)
        inverse = jnp.where(live, 1.0 / total, 0.0)
        for t in range(tiles):
            weight_ref[base + t] = weight_ref[base + t] * inverse

    for_blocks(length, rows, devices // 2, row_block)


def values_kernel(length_ref, place_ref, weight_ref, *refs):
    arrays, (low_ref, sum_ref, got_sems, send_sems) = refs[:-4], refs[-4:]
    devices, rows, _ = low_ref.shape
    seats, lanes = stages(devices)
    blocks = devices // 2
    count = len(seats) + len(lanes) - 1
    vg_ref = arrays[count]
    place = place_ref[0]
    arriving = gathered(place, arrays[:count], False, vg_ref, got_sems)
    for copy in arriving:
        copy.start()
    sum_ref[...] = jnp.zeros_like(sum_ref)
    for copy in arriving:
        copy.wait()

    def row_block(block, base, tiles):
        grads = pair(vg_ref, 1, block)
        first = block - (tiles - 1)
        for t in range(tiles):
            sum_ref[first + t] += dot(weight_ref[base + t].astype(jnp.bfloat16), grads, ((1,), (0,)))

    for_blocks(length_ref[0], rows, blocks, row_block)
    for block in range(blocks):
        value_grad = sum_ref[block].astype(low_ref.dtype)
        low_ref[block] = value_grad[:rows]
        low_ref[blocks + block] = value_grad[rows:]
    run_all(scattered(place, low_ref, arrays[count + 1 :], True, send_sems))


def scores_kernel(length_ref, place_ref, qk_ref, vg_ref, weight_ref, *refs):
    outputs, (key_low, query_low, kt_ref, d_ref, dk_ref, bias_acc, key_sems, query_sems) = refs[:-8], refs[-8:]
    devices, _, rows, width = qk_ref.shape
    _, lanes = stages(devices)
    blocks = devices // 2
    both = 2 * rows
    root_scale = 1.0 / math.sqrt(width)
    place = place_ref[0]
    query_low[...] = jnp.zeros_like(query_low)
    dk_ref[...] = jnp.zeros_like(dk_ref)
    bias_acc[...] = jnp.zeros_like(bias_acc)
    for block in range(blocks):
        kt_ref[block] = pair(qk_ref, 1, block).T

    def row_block(block, base, tiles):
        queries = pair(qk_ref, 0, block)
        grads = pair(vg_ref, 1, block)
        first = block - (tiles - 1)
        delta = jnp.zeros((8, both), jnp.float32)
        for t in range(tiles):
            weight_grad = dot(pair(vg_ref, 0, first + t), grads, ((1,), (1,)))
            d_ref[t] = weight_grad
            delta = delta + fold(weight_ref[base + t] * weight_grad, jnp.sum)
        delta = jnp.sum(delta, axis=0, keepdims=True)
        query_sum = jnp.zeros((width, both), jnp.float32)
        cross = jnp.zeros((8, rows), jnp.float32)
        for t in range(tiles):
            score_grad = weight_ref[base + t] * (d_ref[t] - delta)
            cross = cross + fold(score_grad[:rows, rows:], jnp.sum) + fold(score_grad[rows:, :rows], jnp.sum)
            score_low = score_grad.astype(jnp.bfloat16)
            dk_ref[first + t] += dot(score_low, queries, ((1,), (0,)))
            query_sum = query_sum + dot(kt_ref[first + t], score_low, ((1,), (0,)))
        bias_acc[...] += cross
        query_grad = (query_sum.T * root_scale).astype(query_low.dtype)
        query_low[block] = query_grad[:rows]
        query_low[blocks + block] = query_grad[rows:]

    for_blocks(length_ref[0], rows, blocks, row_block)

    leaving = scattered(place, query_low, outputs[len(lanes) :], False, query_sems)
    for copy in leaving:
        copy.start()
    whole = jnp.sum(jnp.sum(bias_acc[...], axis=0, keepdims=True), axis=1, keepdims=True)
    whole = jnp.broadcast_to(whole, (1, width))
    high = whole.astype(jnp.bfloat16).astype(jnp.float32)
    middle = (whole - high).astype(jnp.bfloat16).astype(jnp.float32)
    low = (whole - high - middle).astype(jnp.bfloat16).astype(jnp.float32)
    lane = lax.broadcasted_iota(jnp.int32, (1, width), 1)
    pieces = jnp.where(lane == 0, high, jnp.where(lane == 1, middle, jnp.where(lane == 2, low, 0.0)))
    pieces = jnp.broadcast_to(pieces, (EXTRA, width)).astype(key_low.dtype)
    for block in range(blocks):
        key_grad = (dk_ref[block] * root_scale).astype(key_low.dtype)
        for c in range(2):
            key_low[c * blocks + block, :rows] = key_grad[c * rows : (c + 1) * rows]
            key_low[c * blocks + block, rows : rows + EXTRA] = pieces
    run_all(scattered(place, key_low, outputs[: len(lanes)], True, key_sems))
    for copy in leaving:
        copy.wait()


def summed_over(value, axis):
    count = lax.axis_size(axis)
    if count & (count - 1):
        return lax.psum(value, axis)
    step = 1
    while step < count:
        pairs = [(source, source ^ step) for source in range(count)]
        value = value + lax.ppermute(value, axis, pairs)
        step *= 2
    return value


def in_hbm(value):
    return pltpu.with_memory_space_constraint(value, pltpu.HBM)


def moved(value, mask):
    devices = lax.axis_size("chan") * lax.axis_size("seq")
    return lax.ppermute(value, ("chan", "seq"), [(source, source ^ mask) for source in range(devices)])


def both_after(value, earlier):
    return lax.optimization_barrier((value, earlier))


def over_lanes_first(by_lane, devices, earlier=None):
    _, lanes = stages(devices)
    first = [by_lane[0]]
    for i in range(1, len(lanes)):
        value = by_lane[i]
        if earlier is not None:
            value, earlier[i] = both_after(value, earlier[i])
        first.append(moved(value, lanes[i]))
    return first


def then_seats(first, devices):
    seats, _ = stages(devices)
    return [moved(jnp.stack([value[j] for value in first]), seats[j]) for j in range(1, len(seats))]


def over_seats_first(by_seat, devices, earlier):
    seats, lanes = stages(devices)
    first = [by_seat[0]] + [moved(by_seat[j], seats[j]) for j in range(1, len(seats))]
    last = []
    for i in range(1, len(lanes)):
        waiting, earlier[i] = both_after(jnp.stack([value[i] for value in first]), earlier[i])
        last.append(moved(waiting, lanes[i]))
    return first + last


def layer(queries, keys, values, out_grad, cross_bias, lengths):
    rows, features = queries.shape[2:]
    heads = cross_bias.shape[0]
    width = features // heads
    blocks = lax.axis_size("seq")
    devices = lax.axis_size("chan") * blocks
    copies = devices // heads
    seats, lanes = stages(devices)
    place = lax.axis_index("chan") * blocks + lax.axis_index("seq")
    places = place.astype(jnp.int32)[None]
    kind = queries.dtype
    both = 2 * rows
    tiles = min(LOOKBACK + 1, blocks)
    vmem = pl.BlockSpec(memory_space=pltpu.VMEM)
    smem = pl.BlockSpec(memory_space=pltpu.SMEM)
    anywhere = pl.BlockSpec(memory_space=pl.ANY)
    hbm = pl.BlockSpec(memory_space=pltpu.HBM)

    def by_lane(*block):
        return [jax.ShapeDtypeStruct((len(seats),) + block, kind)] * len(lanes)

    def by_seat(*block):
        return [jax.ShapeDtypeStruct((len(lanes),) + block, kind)] * len(seats)

    def size(*shapes):
        return sum(math.prod(shape.shape) * shape.dtype.itemsize for shape in shapes)

    def call(kernel, out_shape, in_specs, out_specs, scratch, grant, matmuls, args):
        flops = 2 * matmuls * tile_count(blocks) * both * both * width
        return pl.pallas_call(
            kernel,
            out_shape=out_shape,
            in_specs=in_specs,
            out_specs=out_specs,
            scratch_shapes=scratch,
            compiler_params=pltpu.CompilerParams(vmem_limit_bytes=grant + SLACK_BYTES),
            cost_estimate=pl.CostEstimate(flops=flops, bytes_accessed=2 << 20, transcendentals=0),
        )(*args)

    def pack(lanes_first, first, second):
        sends = by_lane(2, rows, width) if lanes_first else by_seat(2, rows, width)
        return call(
            functools.partial(pack_kernel, copies, lanes_first),
            sends,
            [smem, hbm, hbm],
            [vmem] * len(sends),
            [pltpu.SemaphoreType.DMA((devices, 2))],
            0,
            0,
            (places, in_hbm(first[0, 0]), in_hbm(second[0, 0])),
        )

    sent_a = pack(True, queries, keys)
    values, out_grad, sent_a = lax.optimization_barrier((values, out_grad, sent_a))
    sent_b = pack(False, values, out_grad)
    lane_a = over_lanes_first(sent_a, devices)
    arrived_b = over_seats_first(sent_b, devices, lane_a)
    arrived_a = lane_a + then_seats(lane_a, devices)

    gathered_shape = jax.ShapeDtypeStruct((devices, 2, rows, width), kind)
    weights_shape = jax.ShapeDtypeStruct((tile_count(blocks), both, both), jnp.float32)
    sums_shape = jax.ShapeDtypeStruct((blocks, both, width), jnp.float32)
    dma = pltpu.SemaphoreType.DMA((devices,))
    qk, weights = call(
        functools.partial(stats_kernel, copies),
        (gathered_shape, weights_shape),
        [smem, smem, smem] + [anywhere] * len(arrived_a),
        (vmem, vmem),
        [dma],
        size(gathered_shape, weights_shape),
        1,
        (lengths, places, cross_bias, *arrived_a),
    )
    sends = by_lane(rows, width)
    vg, *sent_v = call(
        values_kernel,
        [gathered_shape] + sends,
        [smem, smem, vmem] + [anywhere] * len(arrived_b),
        [vmem] + [anywhere] * len(sends),
        [
            pltpu.VMEM((devices, rows, width), kind),
            pltpu.VMEM(sums_shape.shape, jnp.float32),
            dma,
            dma,
        ],
        size(gathered_shape, weights_shape, sums_shape, gathered_shape),
        1,
        (lengths, places, weights, *arrived_b),
    )
    lane_v = over_lanes_first(sent_v, devices)
    sends = by_lane(rows + EXTRA, width) + by_seat(rows, width)
    sent = call(
        scores_kernel,
        sends,
        [smem, smem, vmem, vmem, vmem],
        [anywhere] * len(sends),
        [
            pltpu.VMEM((devices, rows + EXTRA, width), kind),
            pltpu.VMEM((devices, rows, width), kind),
            pltpu.VMEM((blocks, width, both), kind),
            pltpu.VMEM((tiles, both, both), jnp.float32),
            pltpu.VMEM(sums_shape.shape, jnp.float32),
            pltpu.VMEM((8, rows), jnp.float32),
            dma,
            dma,
        ],
        size(gathered_shape, gathered_shape, gathered_shape, gathered_shape, weights_shape, sums_shape),
        3,
        (lengths, places, qk, vg, weights),
    )
    lane_k = over_lanes_first(sent[: len(lanes)], devices, lane_v)
    arrived_q = over_seats_first(sent[len(lanes) :], devices, lane_k)
    arrived_v = lane_v + then_seats(lane_v, devices)
    arrived_k = lane_k + then_seats(lane_k, devices)

    pieces = [
        (arrived_k[i][0] if j == 0 else arrived_k[len(lanes) + j - 1][i])[rows] for i, j, _ in places_of(devices)
    ]
    masks = jnp.array([mask for _, _, mask in places_of(devices)], jnp.int32)
    chosen = (masks ^ place)[None] // copies == jnp.arange(heads, dtype=jnp.int32)[:, None]
    sums = jnp.sum(jnp.stack(pieces).astype(jnp.float32), axis=1)
    bias_out = summed_over(jnp.sum(jnp.where(chosen, sums[None], 0.0), axis=1), "dp")

    def unpack(lanes_first, arrived):
        sums_rows, homes = (16, 1) if copies == 1 else (rows, devices)
        return call(
            functools.partial(unpack_kernel, copies, lanes_first),
            jax.ShapeDtypeStruct((rows, features), kind),
            [smem] + [anywhere] * len(arrived),
            hbm,
            [
                pltpu.VMEM((sums_rows, features), kind),
                pltpu.VMEM((homes, rows, width), kind),
                dma,
            ],
            size(gathered_shape),
            0,
            (places, *arrived),
        )[None, None]

    value_out = unpack(True, arrived_v)
    key_out = unpack(True, arrived_k)
    query_out = unpack(False, arrived_q)
    return query_out, key_out, value_out, bias_out


def solution(mesh):
    placed = P("dp", "chan", "seq", None)
    return jax.shard_map(
        layer,
        mesh=mesh,
        in_specs=(placed, placed, placed, placed, P(), P("dp")),
        out_specs=(placed, placed, placed, P()),
        check_vma=False,
    )
```

time: 120 us -> 121 us (level); the launches traced: 122 us -> 119 us
  blocking collectives: 44.6 us -> 0 us
  starting transfers between devices: 7.37 us -> 33.4 us
  waiting for transfers between devices: 44.9 us -> 57.3 us
  Pallas kernels: 20 us -> 24.1 us
  local copies, waits for them, and re-layouts: 2.45 us -> 0.97 us
    ppermute x0 -> x30, waiting for transfers between devices: none -> 57 us  [moved(): lax.ppermute(value, ('chan', 'seq'), [(source, source ^ mask) for source...]
    all_to_all x1 -> x0, waiting for transfers between devices: 44.9 us -> none  [shards(): got = lax.all_to_all(send, ('chan', 'seq'), 0, 0, tiled=True)]
    all_to_all x1 -> x0, blocking collectives: 44.6 us -> none  [shards(): home = lax.all_to_all(back, ('chan', 'seq'), 0, 0, tiled=True)]
    ppermute x0 -> x30, starting transfers between devices: none -> 32.1 us  [moved(): lax.ppermute(value, ('chan', 'seq'), [(source, source ^ mask) for source...]
    all_to_all x1 -> x0, starting transfers between devices: 7.35 us -> none  [shards(): got = lax.all_to_all(send, ('chan', 'seq'), 0, 0, tiled=True)]
    pallas_call x3 -> x8, Pallas kernels: 20 us -> 24.1 us  [call(): pl.pallas_call(kernel, out_shape=out_shape, in_specs=in_specs, out_specs=...]
    unnamed x4 -> x2, local copies, waits for them, and re-layouts: 2.37 us -> 0.66 us
    ppermute x1, starting transfers between devices: 0.02 us -> 1.27 us  [summed_over(): value = value + lax.ppermute(value, axis, pairs)]
  transfers between devices with their start and end apart: 2 -> 31, of which waited for: 1 -> 14; matrix products, arithmetic and copies ran while one was open for 0% -> 1% of each run, Pallas kernels for 2% -> 14%
where the time goes in v2:
time: 121 us; the launch traced here: 119 us
  waiting for transfers between devices  57.3 us (47%)
  starting transfers between devices  33.4 us (28%)
  Pallas kernels  24.1 us (20%)
  other arithmetic  1.81 us (1%)
  between operations  1.73 us (1%)
    ppermute x30, waiting for transfers between devices, moved(): lax.ppermute(value, ('chan', 'seq'), [(source, source ^ mask) for source...  57 us
    ppermute x30, starting transfers between devices, moved(): lax.ppermute(value, ('chan', 'seq'), [(source, source ^ mask) for source...  32.1 us
    pallas_call x8, Pallas kernels, call(): pl.pallas_call(kernel, out_shape=out_shape, in_specs=in_specs, out_specs=...  24.1 us
  transfers between devices with their start and end apart: 31, of which 14 were waited for; matrix products, arithmetic and copies ran while one was open for 1% of the time, Pallas kernels for 14%

profile of v2, /device:TPU:1, one launch (start us, length us, event | category | flops | bytes accessed | tf_op | source)
XLA Modules:
  0.0 119.3 jit_solution(13657067379323792612)
XLA Ops:
  0.6 1.5 %shard_map.102 = (bf16[4,2,128,128]{3,2,1,0:T(8,128)(2,1)S(1)}, bf16[4,2,128,128]{3,2,1,0:T(8,128)(2,1)S(1)}, bf16[4,2,128,128]{3,2,1,0:T(8,128)(2,1)S(1)}, bf16[4,2,128,128]{3,2,1,0:T(8,128)(2,1)S(1)}) custom-call(s32[1]{0:T(128)} %bitcast.place_ref, bf16[128,2048]{1,0:T(8,128)(2,1)} %bitcast.43, bf16[128,2048]{1,0:T(8,128)(2,1)} %bitcast.44), custom_call_target="tpu_custom_call" | custom-call | bytes 2097152 | tf_op jit(solution)/shard_map/pallas_call | solution.py:348
  2.1 1.5 %shard_map.103 = (bf16[4,2,128,128]{3,2,1,0:T(8,128)(2,1)S(1)}, bf16[4,2,128,128]{3,2,1,0:T(8,128)(2,1)S(1)}, bf16[4,2,128,128]{3,2,1,0:T(8,128)(2,1)S(1)}, bf16[4,2,128,128]{3,2,1,0:T(8,128)(2,1)S(1)}) custom-call(s32[1]{0:T(128)} %bitcast.place_ref, bf16[128,2048]{1,0:T(8,128)(2,1)} %bitcast.45, bf16[128,2048]{1,0:T(8,128)(2,1)} %bitcast.46), custom_call_target="tpu_custom_call" | custom-call | bytes 2097152 | tf_op jit(solution)/shard_map/pallas_call | solution.py:348
  3.7 2.7 %collective-permute-start.1 = (bf16[4,2,128,128]{3,2,1,0:T(8,128)(2,1)S(1)}, bf16[4,2,128,128]{3,2,1,0:T(8,128)(2,1)S(1)}, u32[]{:S(2)}, u32[]{:S(2)}) collective-permute-start(bf16[4,2,128,128]{3,2,1,0:T(8,128)(2,1)S(1)} %get-tuple-element.60), channel_id=1, source_target_pairs={{0,16},{2,18},{4,20},{6,22},{8,24},{10,26},{12,28},{14,30},{16,0},... | collective-permute-start | bytes 786440 | tf_op jit(solution)/shard_map/ppermute | solution.py:286
  6.5 3.7 %collective-permute-start.5 = (bf16[4,2,128,128]{3,2,1,0:T(8,128)(2,1)S(1)}, bf16[4,2,128,128]{3,2,1,0:T(8,128)(2,1)S(1)}, u32[]{:S(2)}, u32[]{:S(2)}) collective-permute-start(bf16[4,2,128,128]{3,2,1,0:T(8,128)(2,1)S(1)} %get-tuple-element.66), channel_id=1, source_target_pairs={{0,12},{2,14},{4,8},{6,10},{8,4},{10,6},{12,0},{14,2},{16,28},{18,... | collective-permute-start | bytes 786440 | tf_op jit(solution)/shard_map/ppermute | solution.py:286
  10.6 2.4 %collective-permute-done.1.refs_2_ = bf16[4,2,128,128]{3,2,1,0:T(8,128)(2,1)S(1)} collective-permute-done((bf16[4,2,128,128]{3,2,1,0:T(8,128)(2,1)S(1)}, bf16[4,2,128,128]{3,2,1,0:T(8,128)(2,1)S(1)}, u32[]{:S(2)}, u32[]{:S(2)}) %collective-permute-start.1) | collective-permute-done | bytes 262176 | tf_op jit(solution)/shard_map/ppermute | solution.py:286
  13.0 5.9 %collective-permute-done.2.refs_3_ = bf16[4,2,128,128]{3,2,1,0:T(8,128)(2,1)S(1)} collective-permute-done((bf16[4,2,128,128]{3,2,1,0:T(8,128)(2,1)S(1)}, bf16[4,2,128,128]{3,2,1,0:T(8,128)(2,1)S(1)}, u32[]{:S(2)}, u32[]{:S(2)}) %collective-permute-start.2) | collective-permute-done | bytes 262176 | tf_op jit(solution)/shard_map/ppermute | solution.py:286
  19.1 13.4 %collective-permute-done.4.refs_2_ = bf16[4,2,128,128]{3,2,1,0:T(8,128)(2,1)S(1)} collective-permute-done((bf16[4,2,128,128]{3,2,1,0:T(8,128)(2,1)S(1)}, bf16[4,2,128,128]{3,2,1,0:T(8,128)(2,1)S(1)}, u32[]{:S(2)}, u32[]{:S(2)}) %collective-permute-start.4) | collective-permute-done | bytes 262176 | tf_op jit(solution)/shard_map/ppermute | solution.py:286
  32.6 2.2 %collective-permute-start.8 = (bf16[4,2,128,128]{3,2,1,0:T(8,128)(2,1)S(1)}, bf16[4,2,128,128]{3,2,1,0:T(8,128)(2,1)S(1)}, u32[]{:S(2)}, u32[]{:S(2)}) collective-permute-start(bf16[4,2,128,128]{3,2,1,0:T(8,128)(2,1)S(1)} %pad_maximum_fusion.5), channel_id=1, source_target_pairs={{0,18},{2,16},{4,22},{6,20},{8,26},{10,24},{12,30},{14,28},{16,2},... | collective-permute-start | bytes 786440 | tf_op jit(solution)/shard_map/ppermute | solution.py:286
  36.0 2.3 %collective-permute-start.11 = (bf16[4,2,128,128]{3,2,1,0:T(8,128)(2,1)S(1)}, bf16[4,2,128,128]{3,2,1,0:T(8,128)(2,1)S(1)}, u32[]{:S(2)}, u32[]{:S(2)}) collective-permute-start(bf16[4,2,128,128]{3,2,1,0:T(8,128)(2,1)S(1)} %pad_maximum_fusion.2), channel_id=1, source_target_pairs={{0,12},{2,14},{4,8},{6,10},{8,4},{10,6},{12,0},{14,2},{16,28},{18,... | collective-permute-start | bytes 786440 | tf_op jit(solution)/shard_map/ppermute | solution.py:286
  38.3 3.6 %collective-permute-done.8.refs_6_ = bf16[4,2,128,128]{3,2,1,0:T(8,128)(2,1)S(1)} collective-permute-done((bf16[4,2,128,128]{3,2,1,0:T(8,128)(2,1)S(1)}, bf16[4,2,128,128]{3,2,1,0:T(8,128)(2,1)S(1)}, u32[]{:S(2)}, u32[]{:S(2)}) %collective-permute-start.8) | collective-permute-done | bytes 262176 | tf_op jit(solution)/shard_map/ppermute | solution.py:286
  42.6 4.8 %collective-permute-done.7.refs_5_ = bf16[4,2,128,128]{3,2,1,0:T(8,128)(2,1)S(1)} collective-permute-done((bf16[4,2,128,128]{3,2,1,0:T(8,128)(2,1)S(1)}, bf16[4,2,128,128]{3,2,1,0:T(8,128)(2,1)S(1)}, u32[]{:S(2)}, u32[]{:S(2)}) %collective-permute-start.7) | collective-permute-done | bytes 262176 | tf_op jit(solution)/shard_map/ppermute | solution.py:286
  48.0 6.0 %shard_map.104 = (bf16[16,2,128,128]{3,2,1,0:T(8,128)(2,1)S(1)}, f32[35,256,256]{2,1,0:T(8,128)S(1)}) custom-call(s32[1]{0:T(128)S(6)} %copy.11.length_ref, s32[1]{0:T(128)} %bitcast.place_ref, f32[16]{0:T(128)S(1)} %copy-done, bf16[4,2,128,128]{3,2,1,0:T(8,128)(2,1)S(1)} %get-tuple-element.55.refs_0_, ...), custom_call_target="tpu_custom_call" | custom-call | flops 587202560 | bytes 2097152 | tf_op jit(solution)/shard_map/pallas_call | solution.py:348
  54.0 5.6 %collective-permute-done.10.refs_5_ = bf16[4,2,128,128]{3,2,1,0:T(8,128)(2,1)S(1)} collective-permute-done((bf16[4,2,128,128]{3,2,1,0:T(8,128)(2,1)S(1)}, bf16[4,2,128,128]{3,2,1,0:T(8,128)(2,1)S(1)}, u32[]{:S(2)}, u32[]{:S(2)}) %collective-permute-start.10) | collective-permute-done | bytes 262176 | tf_op jit(solution)/shard_map/ppermute | solution.py:286
  59.6 4.5 %shard_map.105 = (bf16[16,2,128,128]{3,2,1,0:T(8,128)(2,1)S(1)}, bf16[4,128,128]{2,1,0:T(8,128)(2,1)S(1)}, bf16[4,128,128]{2,1,0:T(8,128)(2,1)S(1)}, bf16[4,128,...) custom-call(s32[1]{0:T(128)S(6)} %copy.11.length_ref, s32[1]{0:T(128)} %bitcast.place_ref, ...), custom_call_target="tpu_custom_call" | custom-call | flops 587202560 | bytes 2097152 | tf_op jit(solution)/shard_map/pallas_call | solution.py:348
  64.1 1.1 collective-permute-start.21
  65.3 7.9 %shard_map.106 = (bf16[4,136,128]{2,1,0:T(8,128)(2,1)S(1)}, bf16[4,136,128]{2,1,0:T(8,128)(2,1)S(1)}, bf16[4,136,128]{2,1,0:T(8,128)(2,1)S(1)}, bf16[4,136,128]{...) custom-call(s32[1]{0:T(128)S(6)} %copy.11.length_ref, ...), custom_call_target="tpu_custom_call" | custom-call | flops 1761607680 | bytes 2097152 | tf_op jit(solution)/shard_map/pallas_call | solution.py:348
  73.2 1.5 %collective-permute-start.12 = (bf16[4,128,128]{2,1,0:T(8,128)(2,1)S(1)}, bf16[4,128,128]{2,1,0:T(8,128)(2,1)S(1)}, u32[]{:S(2)}, u32[]{:S(2)}) collective-permute-start(bf16[4,128,128]{2,1,0:T(8,128)(2,1)S(1)} %get-tuple-element.75), channel_id=1, source_target_pairs={{0,2},{2,0},{4,6},{6,4},{8,10},{10,8},{12,14},{14,12},{16,18},{18,... | collective-permute-start | bytes 393224 | tf_op jit(solution)/shard_map/ppermute | solution.py:286
  75.8 2.5 %collective-permute-start.15 = (bf16[4,128,128]{2,1,0:T(8,128)(2,1)S(1)}, bf16[4,128,128]{2,1,0:T(8,128)(2,1)S(1)}, u32[]{:S(2)}, u32[]{:S(2)}) collective-permute-start(bf16[4,128,128]{2,1,0:T(8,128)(2,1)S(1)} %get-tuple-element.79), channel_id=1, source_target_pairs={{0,4},{2,6},{4,0},{6,2},{8,12},{10,14},{12,8},{14,10},{16,20},{18,... | collective-permute-start | bytes 393224 | tf_op jit(solution)/shard_map/ppermute | solution.py:286
  78.4 1.3 %collective-permute-start.14 = (bf16[4,128,128]{2,1,0:T(8,128)(2,1)S(1)}, bf16[4,128,128]{2,1,0:T(8,128)(2,1)S(1)}, u32[]{:S(2)}, u32[]{:S(2)}) collective-permute-start(bf16[4,128,128]{2,1,0:T(8,128)(2,1)S(1)} %get-tuple-element.77), channel_id=1, source_target_pairs={{0,18},{2,16},{4,22},{6,20},{8,26},{10,24},{12,30},{14,28},{16,2},... | collective-permute-start | bytes 393224 | tf_op jit(solution)/shard_map/ppermute | solution.py:286
  79.6 5.2 %collective-permute-done.18.refs_2_ = bf16[4,128,128]{2,1,0:T(8,128)(2,1)S(1)} collective-permute-done((bf16[4,128,128]{2,1,0:T(8,128)(2,1)S(1)}, bf16[4,128,128]{2,1,0:T(8,128)(2,1)S(1)}, u32[]{:S(2)}, u32[]{:S(2)}) %collective-permute-start.18) | collective-permute-done | bytes 131104 | tf_op jit(solution)/shard_map/ppermute | solution.py:286
  86.0 1.2 collective-permute-start.29
  87.2 1.1 collective-permute-start.28
  88.6 3.5 %collective-permute-done.29.refs_6_ = bf16[4,128,128]{2,1,0:T(8,128)(2,1)S(1)} collective-permute-done((bf16[4,128,128]{2,1,0:T(8,128)(2,1)S(1)}, bf16[4,128,128]{2,1,0:T(8,128)(2,1)S(1)}, u32[]{:S(2)}, u32[]{:S(2)}) %collective-permute-start.29) | collective-permute-done | bytes 131104 | tf_op jit(solution)/shard_map/ppermute | solution.py:286
  92.1 2.2 %collective-permute-start.16 = (bf16[4,136,128]{2,1,0:T(8,128)(2,1)S(1)}, bf16[4,136,128]{2,1,0:T(8,128)(2,1)S(1)}, u32[]{:S(2)}, u32[]{:S(2)}) collective-permute-start(bf16[4,136,128]{2,1,0:T(8,128)(2,1)S(1)} %get-tuple-element.80), channel_id=1, source_target_pairs={{0,4},{2,6},{4,0},{6,2},{8,12},{10,14},{12,8},{14,10},{16,20},{18,... | collective-permute-start | bytes 417800 | tf_op jit(solution)/shard_map/ppermute | solution.py:286
  95.8 2.4 %collective-permute-done.19.refs_2_ = bf16[4,136,128]{2,1,0:T(8,128)(2,1)S(1)} collective-permute-done((bf16[4,136,128]{2,1,0:T(8,128)(2,1)S(1)}, bf16[4,136,128]{2,1,0:T(8,128)(2,1)S(1)}, u32[]{:S(2)}, u32[]{:S(2)}) %collective-permute-start.19) | collective-permute-done | bytes 139296 | tf_op jit(solution)/shard_map/ppermute | solution.py:286
  98.3 2.9 %collective-permute-done.16.refs_1_ = bf16[4,136,128]{2,1,0:T(8,128)(2,1)S(1)} collective-permute-done((bf16[4,136,128]{2,1,0:T(8,128)(2,1)S(1)}, bf16[4,136,128]{2,1,0:T(8,128)(2,1)S(1)}, u32[]{:S(2)}, u32[]{:S(2)}) %collective-permute-start.16) | collective-permute-done | bytes 139296 | tf_op jit(solution)/shard_map/ppermute | solution.py:286
  102.1 1.4 %collective-permute-start.23 = (bf16[4,128,128]{2,1,0:T(8,128)(2,1)S(1)}, bf16[4,128,128]{2,1,0:T(8,128)(2,1)S(1)}, u32[]{:S(2)}, u32[]{:S(2)}) collective-permute-start(bf16[4,128,128]{2,1,0:T(8,128)(2,1)S(1)} %pad_maximum_fusion.11), channel_id=1, source_target_pairs={{0,12},{2,14},{4,8},{6,10},{8,4},{10,6},{12,0},{14,2},{16,28},{18,... | collective-permute-start | bytes 393224 | tf_op jit(solution)/shard_map/ppermute | solution.py:286
  103.5 2.2 %collective-permute-start.17 = (bf16[4,128,128]{2,1,0:T(8,128)(2,1)S(1)}, bf16[4,128,128]{2,1,0:T(8,128)(2,1)S(1)}, u32[]{:S(2)}, u32[]{:S(2)}) collective-permute-start(bf16[4,128,128]{2,1,0:T(8,128)(2,1)S(1)} %pad_maximum_fusion.9), channel_id=1, source_target_pairs={{0,4},{2,6},{4,0},{6,2},{8,12},{10,14},{12,8},{14,10},{16,20},{18,... | collective-permute-start | bytes 393224 | tf_op jit(solution)/shard_map/ppermute | solution.py:286
  106.8 2.1 %collective-permute-done.23.refs_6_ = bf16[4,128,128]{2,1,0:T(8,128)(2,1)S(1)} collective-permute-done((bf16[4,128,128]{2,1,0:T(8,128)(2,1)S(1)}, bf16[4,128,128]{2,1,0:T(8,128)(2,1)S(1)}, u32[]{:S(2)}, u32[]{:S(2)}) %collective-permute-start.23) | collective-permute-done | bytes 131104 | tf_op jit(solution)/shard_map/ppermute | solution.py:286
  109.0 1.5 %collective-permute-start.24 = (bf16[4,136,128]{2,1,0:T(8,128)(2,1)S(1)}, bf16[4,136,128]{2,1,0:T(8,128)(2,1)S(1)}, u32[]{:S(2)}, u32[]{:S(2)}) collective-permute-start(bf16[4,136,128]{2,1,0:T(8,128)(2,1)S(1)} %pad_maximum_fusion.6), channel_id=1, source_target_pairs={{0,2},{2,0},{4,6},{6,4},{8,10},{10,8},{12,14},{14,12},{16,18},{18,... | collective-permute-start | bytes 417800 | tf_op jit(solution)/shard_map/ppermute | solution.py:286
  110.5 4.6 %collective-permute-done.20.refs_5_ = bf16[4,128,128]{2,1,0:T(8,128)(2,1)S(1)} collective-permute-done((bf16[4,128,128]{2,1,0:T(8,128)(2,1)S(1)}, bf16[4,128,128]{2,1,0:T(8,128)(2,1)S(1)}, u32[]{:S(2)}, u32[]{:S(2)}) %collective-permute-start.20) | collective-permute-done | bytes 131104 | tf_op jit(solution)/shard_map/ppermute | solution.py:286
  116.3 1.3 %collective-permute-start.30 = (f32[16]{0:T(128)S(1)}, f32[16]{0:T(128)S(1)}, u32[]{:S(2)}, u32[]{:S(2)}) collective-permute-start(f32[16]{0:T(128)S(1)} %select_reduce_fusion), channel_id=1, source_target_pairs={{0,1},{1,0},{2,3},{3,2},{4,5},{5,4},{6,7},{7,6},{8,9},{9,8},{10,11... | collective-permute-start | bytes 200 | tf_op jit(solution)/shard_map/ppermute | solution.py:275
  (87 shorter events, 11.8 us)
Async XLA Ops:
  3.6 6.6 %collective-permute-start = (bf16[4,2,128,128]{3,2,1,0:T(8,128)(2,1)S(1)}, bf16[4,2,128,128]{3,2,1,0:T(8,128)(2,1)S(1)}, u32[]{:S(2)}, u32[]{:S(2)}) collective-permute-start(bf16[4,2,128,128]{3,2,1,0:T(8,128)(2,1)S(1)} %get-tuple-element.59), channel_id=1, source_target_pairs={{0,2},{2,0},{4,6},{6,4},{8,10},{10,8},{12,14},{14,12},{16,18},{18,... | collective-permute-start | bytes 786440 | tf_op jit(solution)/shard_map/ppermute | solution.py:286
  3.7 9.3 %collective-permute-start.1 = (bf16[4,2,128,128]{3,2,1,0:T(8,128)(2,1)S(1)}, bf16[4,2,128,128]{3,2,1,0:T(8,128)(2,1)S(1)}, u32[]{:S(2)}, u32[]{:S(2)}) collective-permute-start(bf16[4,2,128,128]{3,2,1,0:T(8,128)(2,1)S(1)} %get-tuple-element.60), channel_id=1, source_target_pairs={{0,16},{2,18},{4,20},{6,22},{8,24},{10,26},{12,28},{14,30},{16,0},... | collective-permute-start | bytes 786440 | tf_op jit(solution)/shard_map/ppermute | solution.py:286
  6.4 12.5 %collective-permute-start.2 = (bf16[4,2,128,128]{3,2,1,0:T(8,128)(2,1)S(1)}, bf16[4,2,128,128]{3,2,1,0:T(8,128)(2,1)S(1)}, u32[]{:S(2)}, u32[]{:S(2)}) collective-permute-start(bf16[4,2,128,128]{3,2,1,0:T(8,128)(2,1)S(1)} %get-tuple-element.61), channel_id=1, source_target_pairs={{0,18},{2,16},{4,22},{6,20},{8,26},{10,24},{12,30},{14,28},{16,2},... | collective-permute-start | bytes 786440 | tf_op jit(solution)/shard_map/ppermute | solution.py:286
  6.5 12.5 %collective-permute-start.5 = (bf16[4,2,128,128]{3,2,1,0:T(8,128)(2,1)S(1)}, bf16[4,2,128,128]{3,2,1,0:T(8,128)(2,1)S(1)}, u32[]{:S(2)}, u32[]{:S(2)}) collective-permute-start(bf16[4,2,128,128]{3,2,1,0:T(8,128)(2,1)S(1)} %get-tuple-element.66), channel_id=1, source_target_pairs={{0,12},{2,14},{4,8},{6,10},{8,4},{10,6},{12,0},{14,2},{16,28},{18,... | collective-permute-start | bytes 786440 | tf_op jit(solution)/shard_map/ppermute | solution.py:286
  10.2 22.3 %collective-permute-start.4 = (bf16[4,2,128,128]{3,2,1,0:T(8,128)(2,1)S(1)}, bf16[4,2,128,128]{3,2,1,0:T(8,128)(2,1)S(1)}, u32[]{:S(2)}, u32[]{:S(2)}) collective-permute-start(bf16[4,2,128,128]{3,2,1,0:T(8,128)(2,1)S(1)} %get-tuple-element.64), channel_id=1, source_target_pairs={{0,8},{2,10},{4,12},{6,14},{8,0},{10,2},{12,4},{14,6},{16,24},{18,... | collective-permute-start | bytes 786440 | tf_op jit(solution)/shard_map/ppermute | solution.py:286
  10.3 22.2 %collective-permute-start.3 = (bf16[4,2,128,128]{3,2,1,0:T(8,128)(2,1)S(1)}, bf16[4,2,128,128]{3,2,1,0:T(8,128)(2,1)S(1)}, u32[]{:S(2)}, u32[]{:S(2)}) collective-permute-start(bf16[4,2,128,128]{3,2,1,0:T(8,128)(2,1)S(1)} %get-tuple-element.62), channel_id=1, source_target_pairs={{0,4},{2,6},{4,0},{6,2},{8,12},{10,14},{12,8},{14,10},{16,20},{18,... | collective-permute-start | bytes 786440 | tf_op jit(solution)/shard_map/ppermute | solution.py:286
  32.6 9.4 %collective-permute-start.8 = (bf16[4,2,128,128]{3,2,1,0:T(8,128)(2,1)S(1)}, bf16[4,2,128,128]{3,2,1,0:T(8,128)(2,1)S(1)}, u32[]{:S(2)}, u32[]{:S(2)}) collective-permute-start(bf16[4,2,128,128]{3,2,1,0:T(8,128)(2,1)S(1)} %pad_maximum_fusion.5), channel_id=1, source_target_pairs={{0,18},{2,16},{4,22},{6,20},{8,26},{10,24},{12,30},{14,28},{16,2},... | collective-permute-start | bytes 786440 | tf_op jit(solution)/shard_map/ppermute | solution.py:286
  34.8 12.6 %collective-permute-start.7 = (bf16[4,2,128,128]{3,2,1,0:T(8,128)(2,1)S(1)}, bf16[4,2,128,128]{3,2,1,0:T(8,128)(2,1)S(1)}, u32[]{:S(2)}, u32[]{:S(2)}) collective-permute-start(bf16[4,2,128,128]{3,2,1,0:T(8,128)(2,1)S(1)} %pad_maximum_fusion.4), channel_id=1, source_target_pairs={{0,16},{2,18},{4,20},{6,22},{8,24},{10,26},{12,28},{14,30},{16,0},... | collective-permute-start | bytes 786440 | tf_op jit(solution)/shard_map/ppermute | solution.py:286
  35.1 12.3 %collective-permute-start.6 = (bf16[4,2,128,128]{3,2,1,0:T(8,128)(2,1)S(1)}, bf16[4,2,128,128]{3,2,1,0:T(8,128)(2,1)S(1)}, u32[]{:S(2)}, u32[]{:S(2)}) collective-permute-start(bf16[4,2,128,128]{3,2,1,0:T(8,128)(2,1)S(1)} %pad_maximum_fusion.3), channel_id=1, source_target_pairs={{0,2},{2,0},{4,6},{6,4},{8,10},{10,8},{12,14},{14,12},{16,18},{18,... | collective-permute-start | bytes 786440 | tf_op jit(solution)/shard_map/ppermute | solution.py:286
  36.0 18.0 %collective-permute-start.11 = (bf16[4,2,128,128]{3,2,1,0:T(8,128)(2,1)S(1)}, bf16[4,2,128,128]{3,2,1,0:T(8,128)(2,1)S(1)}, u32[]{:S(2)}, u32[]{:S(2)}) collective-permute-start(bf16[4,2,128,128]{3,2,1,0:T(8,128)(2,1)S(1)} %pad_maximum_fusion.2), channel_id=1, source_target_pairs={{0,12},{2,14},{4,8},{6,10},{8,4},{10,6},{12,0},{14,2},{16,28},{18,... | collective-permute-start | bytes 786440 | tf_op jit(solution)/shard_map/ppermute | solution.py:286
  38.3 21.3 %collective-permute-start.10 = (bf16[4,2,128,128]{3,2,1,0:T(8,128)(2,1)S(1)}, bf16[4,2,128,128]{3,2,1,0:T(8,128)(2,1)S(1)}, u32[]{:S(2)}, u32[]{:S(2)}) collective-permute-start(bf16[4,2,128,128]{3,2,1,0:T(8,128)(2,1)S(1)} %pad_maximum_fusion.1), channel_id=1, source_target_pairs={{0,8},{2,10},{4,12},{6,14},{8,0},{10,2},{12,4},{14,6},{16,24},{18,... | collective-permute-start | bytes 786440 | tf_op jit(solution)/shard_map/ppermute | solution.py:286
  41.9 17.7 %collective-permute-start.9 = (bf16[4,2,128,128]{3,2,1,0:T(8,128)(2,1)S(1)}, bf16[4,2,128,128]{3,2,1,0:T(8,128)(2,1)S(1)}, u32[]{:S(2)}, u32[]{:S(2)}) collective-permute-start(bf16[4,2,128,128]{3,2,1,0:T(8,128)(2,1)S(1)} %pad_maximum_fusion), channel_id=1, source_target_pairs={{0,4},{2,6},{4,0},{6,2},{8,12},{10,14},{12,8},{14,10},{16,20},{18,... | collective-permute-start | bytes 786440 | tf_op jit(solution)/shard_map/ppermute | solution.py:286
  47.4 0.7 copy-start
  64.1 14.2 %collective-permute-start.21 = (bf16[4,128,128]{2,1,0:T(8,128)(2,1)S(1)}, bf16[4,128,128]{2,1,0:T(8,128)(2,1)S(1)}, u32[]{:S(2)}, u32[]{:S(2)}) collective-permute-start(bf16[4,128,128]{2,1,0:T(8,128)(2,1)S(1)} %get-tuple-element.87), channel_id=1, source_target_pairs={{0,12},{2,14},{4,8},{6,10},{8,4},{10,6},{12,0},{14,2},{16,28},{18,... | collective-permute-start | bytes 393224 | tf_op jit(solution)/shard_map/ppermute | solution.py:286
  73.2 12.8 %collective-permute-start.12 = (bf16[4,128,128]{2,1,0:T(8,128)(2,1)S(1)}, bf16[4,128,128]{2,1,0:T(8,128)(2,1)S(1)}, u32[]{:S(2)}, u32[]{:S(2)}) collective-permute-start(bf16[4,128,128]{2,1,0:T(8,128)(2,1)S(1)} %get-tuple-element.75), channel_id=1, source_target_pairs={{0,2},{2,0},{4,6},{6,4},{8,10},{10,8},{12,14},{14,12},{16,18},{18,... | collective-permute-start | bytes 393224 | tf_op jit(solution)/shard_map/ppermute | solution.py:286
  74.7 12.5 %collective-permute-start.13 = (bf16[4,128,128]{2,1,0:T(8,128)(2,1)S(1)}, bf16[4,128,128]{2,1,0:T(8,128)(2,1)S(1)}, u32[]{:S(2)}, u32[]{:S(2)}) collective-permute-start(bf16[4,128,128]{2,1,0:T(8,128)(2,1)S(1)} %get-tuple-element.76), channel_id=1, source_target_pairs={{0,16},{2,18},{4,20},{6,22},{8,24},{10,26},{12,28},{14,30},{16,0},... | collective-permute-start | bytes 393224 | tf_op jit(solution)/shard_map/ppermute | solution.py:286
  75.8 9.1 %collective-permute-start.18 = (bf16[4,128,128]{2,1,0:T(8,128)(2,1)S(1)}, bf16[4,128,128]{2,1,0:T(8,128)(2,1)S(1)}, u32[]{:S(2)}, u32[]{:S(2)}) collective-permute-start(bf16[4,128,128]{2,1,0:T(8,128)(2,1)S(1)} %get-tuple-element.83), channel_id=1, source_target_pairs={{0,8},{2,10},{4,12},{6,14},{8,0},{10,2},{12,4},{14,6},{16,24},{18,... | collective-permute-start | bytes 393224 | tf_op jit(solution)/shard_map/ppermute | solution.py:286
  75.8 10.1 %collective-permute-start.15 = (bf16[4,128,128]{2,1,0:T(8,128)(2,1)S(1)}, bf16[4,128,128]{2,1,0:T(8,128)(2,1)S(1)}, u32[]{:S(2)}, u32[]{:S(2)}) collective-permute-start(bf16[4,128,128]{2,1,0:T(8,128)(2,1)S(1)} %get-tuple-element.79), channel_id=1, source_target_pairs={{0,4},{2,6},{4,0},{6,2},{8,12},{10,14},{12,8},{14,10},{16,20},{18,... | collective-permute-start | bytes 393224 | tf_op jit(solution)/shard_map/ppermute | solution.py:286
  78.4 10.0 %collective-permute-start.14 = (bf16[4,128,128]{2,1,0:T(8,128)(2,1)S(1)}, bf16[4,128,128]{2,1,0:T(8,128)(2,1)S(1)}, u32[]{:S(2)}, u32[]{:S(2)}) collective-permute-start(bf16[4,128,128]{2,1,0:T(8,128)(2,1)S(1)} %get-tuple-element.77), channel_id=1, source_target_pairs={{0,18},{2,16},{4,22},{6,20},{8,26},{10,24},{12,30},{14,28},{16,2},... | collective-permute-start | bytes 393224 | tf_op jit(solution)/shard_map/ppermute | solution.py:286
  84.9 10.9 %collective-permute-start.22 = (bf16[4,136,128]{2,1,0:T(8,128)(2,1)S(1)}, bf16[4,136,128]{2,1,0:T(8,128)(2,1)S(1)}, u32[]{:S(2)}, u32[]{:S(2)}) collective-permute-start(bf16[4,136,128]{2,1,0:T(8,128)(2,1)S(1)} %get-tuple-element.88), channel_id=1, source_target_pairs={{0,12},{2,14},{4,8},{6,10},{8,4},{10,6},{12,0},{14,2},{16,28},{18,... | collective-permute-start | bytes 417800 | tf_op jit(solution)/shard_map/ppermute | solution.py:286
  85.9 12.3 %collective-permute-start.19 = (bf16[4,136,128]{2,1,0:T(8,128)(2,1)S(1)}, bf16[4,136,128]{2,1,0:T(8,128)(2,1)S(1)}, u32[]{:S(2)}, u32[]{:S(2)}) collective-permute-start(bf16[4,136,128]{2,1,0:T(8,128)(2,1)S(1)} %get-tuple-element.84), channel_id=1, source_target_pairs={{0,8},{2,10},{4,12},{6,14},{8,0},{10,2},{12,4},{14,6},{16,24},{18,... | collective-permute-start | bytes 417800 | tf_op jit(solution)/shard_map/ppermute | solution.py:286
  86.0 6.0 %collective-permute-start.29 = (bf16[4,128,128]{2,1,0:T(8,128)(2,1)S(1)}, bf16[4,128,128]{2,1,0:T(8,128)(2,1)S(1)}, u32[]{:S(2)}, u32[]{:S(2)}) collective-permute-start(bf16[4,128,128]{2,1,0:T(8,128)(2,1)S(1)} %pad_maximum_fusion.14), channel_id=1, source_target_pairs={{0,18},{2,16},{4,22},{6,20},{8,26},{10,24},{12,30},{14,28},{16,2},... | collective-permute-start | bytes 393224 | tf_op jit(solution)/shard_map/ppermute | solution.py:286
  87.2 7.6 %collective-permute-start.28 = (bf16[4,128,128]{2,1,0:T(8,128)(2,1)S(1)}, bf16[4,128,128]{2,1,0:T(8,128)(2,1)S(1)}, u32[]{:S(2)}, u32[]{:S(2)}) collective-permute-start(bf16[4,128,128]{2,1,0:T(8,128)(2,1)S(1)} %pad_maximum_fusion.13), channel_id=1, source_target_pairs={{0,16},{2,18},{4,20},{6,22},{8,24},{10,26},{12,28},{14,30},{16,0},... | collective-permute-start | bytes 393224 | tf_op jit(solution)/shard_map/ppermute | solution.py:286
  88.4 6.5 %collective-permute-start.27 = (bf16[4,128,128]{2,1,0:T(8,128)(2,1)S(1)}, bf16[4,128,128]{2,1,0:T(8,128)(2,1)S(1)}, u32[]{:S(2)}, u32[]{:S(2)}) collective-permute-start(bf16[4,128,128]{2,1,0:T(8,128)(2,1)S(1)} %pad_maximum_fusion.12), channel_id=1, source_target_pairs={{0,2},{2,0},{4,6},{6,4},{8,10},{10,8},{12,14},{14,12},{16,18},{18,... | collective-permute-start | bytes 393224 | tf_op jit(solution)/shard_map/ppermute | solution.py:286
  92.1 9.1 %collective-permute-start.16 = (bf16[4,136,128]{2,1,0:T(8,128)(2,1)S(1)}, bf16[4,136,128]{2,1,0:T(8,128)(2,1)S(1)}, u32[]{:S(2)}, u32[]{:S(2)}) collective-permute-start(bf16[4,136,128]{2,1,0:T(8,128)(2,1)S(1)} %get-tuple-element.80), channel_id=1, source_target_pairs={{0,4},{2,6},{4,0},{6,2},{8,12},{10,14},{12,8},{14,10},{16,20},{18,... | collective-permute-start | bytes 417800 | tf_op jit(solution)/shard_map/ppermute | solution.py:286
  101.3 14.7 %collective-permute-start.26 = (bf16[4,136,128]{2,1,0:T(8,128)(2,1)S(1)}, bf16[4,136,128]{2,1,0:T(8,128)(2,1)S(1)}, u32[]{:S(2)}, u32[]{:S(2)}) collective-permute-start(bf16[4,136,128]{2,1,0:T(8,128)(2,1)S(1)} %pad_maximum_fusion.8), channel_id=1, source_target_pairs={{0,18},{2,16},{4,22},{6,20},{8,26},{10,24},{12,30},{14,28},{16,2},... | collective-permute-start | bytes 417800 | tf_op jit(solution)/shard_map/ppermute | solution.py:286
  102.1 6.9 %collective-permute-start.23 = (bf16[4,128,128]{2,1,0:T(8,128)(2,1)S(1)}, bf16[4,128,128]{2,1,0:T(8,128)(2,1)S(1)}, u32[]{:S(2)}, u32[]{:S(2)}) collective-permute-start(bf16[4,128,128]{2,1,0:T(8,128)(2,1)S(1)} %pad_maximum_fusion.11), channel_id=1, source_target_pairs={{0,12},{2,14},{4,8},{6,10},{8,4},{10,6},{12,0},{14,2},{16,28},{18,... | collective-permute-start | bytes 393224 | tf_op jit(solution)/shard_map/ppermute | solution.py:286
  103.5 11.6 %collective-permute-start.20 = (bf16[4,128,128]{2,1,0:T(8,128)(2,1)S(1)}, bf16[4,128,128]{2,1,0:T(8,128)(2,1)S(1)}, u32[]{:S(2)}, u32[]{:S(2)}) collective-permute-start(bf16[4,128,128]{2,1,0:T(8,128)(2,1)S(1)} %pad_maximum_fusion.10), channel_id=1, source_target_pairs={{0,8},{2,10},{4,12},{6,14},{8,0},{10,2},{12,4},{14,6},{16,24},{18,... | collective-permute-start | bytes 393224 | tf_op jit(solution)/shard_map/ppermute | solution.py:286
  103.5 11.6 %collective-permute-start.17 = (bf16[4,128,128]{2,1,0:T(8,128)(2,1)S(1)}, bf16[4,128,128]{2,1,0:T(8,128)(2,1)S(1)}, u32[]{:S(2)}, u32[]{:S(2)}) collective-permute-start(bf16[4,128,128]{2,1,0:T(8,128)(2,1)S(1)} %pad_maximum_fusion.9), channel_id=1, source_target_pairs={{0,4},{2,6},{4,0},{6,2},{8,12},{10,14},{12,8},{14,10},{16,20},{18,... | collective-permute-start | bytes 393224 | tf_op jit(solution)/shard_map/ppermute | solution.py:286
  105.7 10.3 %collective-permute-start.25 = (bf16[4,136,128]{2,1,0:T(8,128)(2,1)S(1)}, bf16[4,136,128]{2,1,0:T(8,128)(2,1)S(1)}, u32[]{:S(2)}, u32[]{:S(2)}) collective-permute-start(bf16[4,136,128]{2,1,0:T(8,128)(2,1)S(1)} %pad_maximum_fusion.7), channel_id=1, source_target_pairs={{0,16},{2,18},{4,20},{6,22},{8,24},{10,26},{12,28},{14,30},{16,0},... | collective-permute-start | bytes 417800 | tf_op jit(solution)/shard_map/ppermute | solution.py:286
  109.0 7.0 %collective-permute-start.24 = (bf16[4,136,128]{2,1,0:T(8,128)(2,1)S(1)}, bf16[4,136,128]{2,1,0:T(8,128)(2,1)S(1)}, u32[]{:S(2)}, u32[]{:S(2)}) collective-permute-start(bf16[4,136,128]{2,1,0:T(8,128)(2,1)S(1)} %pad_maximum_fusion.6), channel_id=1, source_target_pairs={{0,2},{2,0},{4,6},{6,4},{8,10},{10,8},{12,14},{14,12},{16,18},{18,... | collective-permute-start | bytes 417800 | tf_op jit(solution)/shard_map/ppermute | solution.py:286
  116.3 2.5 %collective-permute-start.30 = (f32[16]{0:T(128)S(1)}, f32[16]{0:T(128)S(1)}, u32[]{:S(2)}, u32[]{:S(2)}) collective-permute-start(f32[16]{0:T(128)S(1)} %select_reduce_fusion), channel_id=1, source_target_pairs={{0,1},{1,0},{2,3},{3,2},{4,5},{5,4},{6,7},{7,6},{8,9},{9,8},{10,11... | collective-permute-start | bytes 200 | tf_op jit(solution)/shard_map/ppermute | solution.py:275

commit v3 on v2

--- a/solution.py
+++ b/solution.py
@@ -11,7 +11,6 @@
 
 LOOKBACK = 6
 NEG_FILL = -1e30
-EXTRA = 8
 LOG2_E = math.log2(math.e)
 SLACK_BYTES = 6 << 20
 
@@ -34,27 +33,30 @@
         copy.wait()
 
 
-def piece(pieces, lanes_first, i, j, devices):
+def piece(pieces, lanes_first, i, j, devices, kind=None):
     seats, lanes = stages(devices)
     firsts = len(lanes) if lanes_first else len(seats)
     near, far = (i, j) if lanes_first else (j, i)
-    return pieces[near].at[0] if far == 0 else pieces[firsts + far - 1].at[near]
-
-
-def gathered(place, pieces, lanes_first, target, sems):
+    if far:
+        return pieces[firsts + far - 1].at[near]
+    return pieces[near].at[0] if kind is None else pieces[near].at[0, kind]
+
+
+def gathered(place, pieces, lanes_first, target, sems, kind=None):
     devices = target.shape[0]
     return [
-        pltpu.make_async_copy(piece(pieces, lanes_first, i, j, devices), target.at[place ^ mask], sems.at[index])
+        pltpu.make_async_copy(piece(pieces, lanes_first, i, j, devices, kind), target.at[place ^ mask], sems.at[index])
         for index, (i, j, mask) in enumerate(places_of(devices))
     ]
 
 
 def scattered(place, source, refs, lanes_first, sems):
+    devices = source.shape[0]
     return [
         pltpu.make_async_copy(
             source.at[place ^ mask], (refs[i].at[j] if lanes_first else refs[j].at[i]), sems.at[index]
         )
-        for index, (i, j, mask) in enumerate(places_of(source.shape[0]))
+        for index, (i, j, mask) in enumerate(places_of(devices))
     ]
 
 
@@ -74,12 +76,11 @@
 def unpack_kernel(copies, lanes_first, place_ref, *refs):
     pieces, (out, sums, home, sems) = refs[:-4], refs[-4:]
     devices = sems.shape[0]
-    rows = out.shape[0]
     width = home.shape[-1]
     started = []
     for index, (i, j, mask) in enumerate(places_of(devices)):
         other = place_ref[0] ^ mask
-        source = piece(pieces, lanes_first, i, j, devices).at[pl.ds(0, rows)]
+        source = piece(pieces, lanes_first, i, j, devices)
         target = home.at[other]
         if copies == 1:
             target = out.at[:, pl.ds(pl.multiple_of(other * width, width), width)]
@@ -102,9 +103,9 @@
     return op(tile.reshape(tile.shape[0] // 8, 8, tile.shape[1]), axis=0)
 
 
-def pair(ref, kind, block):
+def pair(ref, block, *kind):
     blocks = ref.shape[0] // 2
-    return jnp.concatenate([ref[block, kind], ref[blocks + block, kind]], axis=0)
+    return jnp.concatenate([ref[block, *kind], ref[blocks + block, *kind]], axis=0)
 
 
 def tile_count(blocks):
@@ -146,11 +147,11 @@
     in_reach = key_row > query_column
 
     def row_block(block, base, tiles):
-        queries = pair(qk_ref, 0, block)
+        queries = pair(qk_ref, block, 0)
         first = block - (tiles - 1)
         peak = jnp.full((8, both), NEG_FILL, jnp.float32)
         for t in range(tiles):
-            raw = dot(pair(qk_ref, 1, first + t), queries, ((1,), (1,)))
+            raw = dot(pair(qk_ref, first + t, 1), queries, ((1,), (1,)))
             for c in range(2):
                 tile = raw[c * rows : (c + 1) * rows] * log2_scale + own[c]
                 if t == tiles - 1:
@@ -182,9 +183,9 @@
     seats, lanes = stages(devices)
     blocks = devices // 2
     count = len(seats) + len(lanes) - 1
-    vg_ref = arrays[count]
+    grad_ref = arrays[count]
     place = place_ref[0]
-    arriving = gathered(place, arrays[:count], False, vg_ref, got_sems)
+    arriving = gathered(place, arrays[:count], False, grad_ref, got_sems, 0)
     for copy in arriving:
         copy.start()
     sum_ref[...] = jnp.zeros_like(sum_ref)
@@ -192,7 +193,7 @@
         copy.wait()
 
     def row_block(block, base, tiles):
-        grads = pair(vg_ref, 1, block)
+        grads = pair(grad_ref, block)
         first = block - (tiles - 1)
         for t in range(tiles):
             sum_ref[first + t] += dot(weight_ref[base + t].astype(jnp.bfloat16), grads, ((1,), (0,)))
@@ -205,27 +206,35 @@
     run_all(scattered(place, low_ref, arrays[count + 1 :], True, send_sems))
 
 
-def scores_kernel(length_ref, place_ref, qk_ref, vg_ref, weight_ref, *refs):
-    outputs, (key_low, query_low, kt_ref, d_ref, dk_ref, bias_acc, key_sems, query_sems) = refs[:-8], refs[-8:]
+def scores_kernel(copies, length_ref, place_ref, qk_ref, grad_ref, weight_ref, *refs):
+    arrays, scratch = refs[:-9], refs[-9:]
+    value_ref, low_ref, kt_ref, d_ref, dk_ref, bias_acc, got_sems, key_sems, query_sems = scratch
     devices, _, rows, width = qk_ref.shape
-    _, lanes = stages(devices)
+    seats, lanes = stages(devices)
+    count = len(seats) + len(lanes) - 1
     blocks = devices // 2
     both = 2 * rows
     root_scale = 1.0 / math.sqrt(width)
     place = place_ref[0]
-    query_low[...] = jnp.zeros_like(query_low)
+    arriving = gathered(place, arrays[:count], False, value_ref, got_sems, 1)
+    bias_ref, outputs = arrays[count], arrays[count + 1 :]
+    for copy in arriving:
+        copy.start()
+    low_ref[...] = jnp.zeros_like(low_ref)
     dk_ref[...] = jnp.zeros_like(dk_ref)
     bias_acc[...] = jnp.zeros_like(bias_acc)
     for block in range(blocks):
-        kt_ref[block] = pair(qk_ref, 1, block).T
+        kt_ref[block] = pair(qk_ref, block, 1).T
+    for copy in arriving:
+        copy.wait()
 
     def row_block(block, base, tiles):
-        queries = pair(qk_ref, 0, block)
-        grads = pair(vg_ref, 1, block)
+        queries = pair(qk_ref, block, 0)
+        grads = pair(grad_ref, block)
         first = block - (tiles - 1)
         delta = jnp.zeros((8, both), jnp.float32)
         for t in range(tiles):
-            weight_grad = dot(pair(vg_ref, 0, first + t), grads, ((1,), (1,)))
+            weight_grad = dot(pair(value_ref, first + t), grads, ((1,), (1,)))
             d_ref[t] = weight_grad
             delta = delta + fold(weight_ref[base + t] * weight_grad, jnp.sum)
         delta = jnp.sum(delta, axis=0, keepdims=True)
@@ -238,29 +247,23 @@
             dk_ref[first + t] += dot(score_low, queries, ((1,), (0,)))
             query_sum = query_sum + dot(kt_ref[first + t], score_low, ((1,), (0,)))
         bias_acc[...] += cross
-        query_grad = (query_sum.T * root_scale).astype(query_low.dtype)
-        query_low[block] = query_grad[:rows]
-        query_low[blocks + block] = query_grad[rows:]
+        query_grad = (query_sum.T * root_scale).astype(low_ref.dtype)
+        low_ref[0, block] = query_grad[:rows]
+        low_ref[0, blocks + block] = query_grad[rows:]
 
     for_blocks(length_ref[0], rows, blocks, row_block)
 
-    leaving = scattered(place, query_low, outputs[len(lanes) :], False, query_sems)
+    leaving = scattered(place, low_ref.at[0], outputs[len(lanes) :], False, query_sems)
     for copy in leaving:
         copy.start()
     whole = jnp.sum(jnp.sum(bias_acc[...], axis=0, keepdims=True), axis=1, keepdims=True)
-    whole = jnp.broadcast_to(whole, (1, width))
-    high = whole.astype(jnp.bfloat16).astype(jnp.float32)
-    middle = (whole - high).astype(jnp.bfloat16).astype(jnp.float32)
-    low = (whole - high - middle).astype(jnp.bfloat16).astype(jnp.float32)
-    lane = lax.broadcasted_iota(jnp.int32, (1, width), 1)
-    pieces = jnp.where(lane == 0, high, jnp.where(lane == 1, middle, jnp.where(lane == 2, low, 0.0)))
-    pieces = jnp.broadcast_to(pieces, (EXTRA, width)).astype(key_low.dtype)
+    lane = lax.broadcasted_iota(jnp.int32, bias_ref.shape, 1)
+    bias_ref[...] = jnp.where(lane == place // copies, whole, 0.0)
     for block in range(blocks):
-        key_grad = (dk_ref[block] * root_scale).astype(key_low.dtype)
+        key_grad = (dk_ref[block] * root_scale).astype(low_ref.dtype)
         for c in range(2):
-            key_low[c * blocks + block, :rows] = key_grad[c * rows : (c + 1) * rows]
-            key_low[c * blocks + block, rows : rows + EXTRA] = pieces
-    run_all(scattered(place, key_low, outputs[: len(lanes)], True, key_sems))
+            low_ref[1, c * blocks + block] = key_grad[c * rows : (c + 1) * rows]
+    run_all(scattered(place, low_ref.at[1], outputs[: len(lanes)], True, key_sems))
     for copy in leaving:
         copy.wait()
 
@@ -306,14 +309,20 @@
     return [moved(jnp.stack([value[j] for value in first]), seats[j]) for j in range(1, len(seats))]
 
 
-def over_seats_first(by_seat, devices, earlier):
-    seats, lanes = stages(devices)
-    first = [by_seat[0]] + [moved(by_seat[j], seats[j]) for j in range(1, len(seats))]
+def over_seats_first(by_seat, devices):
+    seats, _ = stages(devices)
+    return [by_seat[0]] + [moved(by_seat[j], seats[j]) for j in range(1, len(seats))]
+
+
+def then_lanes(first, devices, earlier, free=None):
+    _, lanes = stages(devices)
     last = []
     for i in range(1, len(lanes)):
-        waiting, earlier[i] = both_after(jnp.stack([value[i] for value in first]), earlier[i])
+        waiting = jnp.stack([value[i] for value in first])
+        if i != free:
+            waiting, earlier[i] = both_after(waiting, earlier[i])
         last.append(moved(waiting, lanes[i]))
-    return first + last
+    return last
 
 
 def layer(queries, keys, values, out_grad, cross_bias, lengths):
@@ -370,9 +379,13 @@
 
     sent_a = pack(True, queries, keys)
     values, out_grad, sent_a = lax.optimization_barrier((values, out_grad, sent_a))
-    sent_b = pack(False, values, out_grad)
+    sent_b = pack(False, out_grad, values)
     lane_a = over_lanes_first(sent_a, devices)
-    arrived_b = over_seats_first(sent_b, devices, lane_a)
+    seat_b = over_seats_first(sent_b, devices)
+    lane_g = then_lanes([value[:, 0] for value in seat_b], devices, lane_a, len(lanes) - 1)
+    gates = [None] + lane_g
+    lane_w = then_lanes([value[:, 1] for value in seat_b], devices, gates)
+    arrived_g, arrived_w = seat_b + gates[1:], seat_b + lane_w
     arrived_a = lane_a + then_seats(lane_a, devices)
 
     gathered_shape = jax.ShapeDtypeStruct((devices, 2, rows, width), kind)
@@ -389,11 +402,12 @@
         1,
         (lengths, places, cross_bias, *arrived_a),
     )
+    one_shape = jax.ShapeDtypeStruct((devices, rows, width), kind)
     sends = by_lane(rows, width)
-    vg, *sent_v = call(
+    grads, *sent_v = call(
         values_kernel,
-        [gathered_shape] + sends,
-        [smem, smem, vmem] + [anywhere] * len(arrived_b),
+        [one_shape] + sends,
+        [smem, smem, vmem] + [anywhere] * len(arrived_g),
         [vmem] + [anywhere] * len(sends),
         [
             pltpu.VMEM((devices, rows, width), kind),
@@ -403,41 +417,41 @@
         ],
         size(gathered_shape, weights_shape, sums_shape, gathered_shape),
         1,
-        (lengths, places, weights, *arrived_b),
+        (lengths, places, weights, *arrived_g),
     )
     lane_v = over_lanes_first(sent_v, devices)
-    sends = by_lane(rows + EXTRA, width) + by_seat(rows, width)
-    sent = call(
-        scores_kernel,
-        sends,
-        [smem, smem, vmem, vmem, vmem],
-        [anywhere] * len(sends),
+    sends = by_lane(rows, width) + by_seat(rows, width)
+    bias_sum, *sent = call(
+        functools.partial(scores_kernel, copies),
+        [jax.ShapeDtypeStruct((1, heads), jnp.float32)] + sends,
+        [smem, smem, vmem, vmem, vmem] + [anywhere] * len(arrived_w),
+        [vmem] + [anywhere] * len(sends),
         [
-            pltpu.VMEM((devices, rows + EXTRA, width), kind),
-            pltpu.VMEM((devices, rows, width), kind),
+            pltpu.VMEM(one_shape.shape, kind),
+            pltpu.VMEM((2,) + one_shape.shape, kind),
             pltpu.VMEM((blocks, width, both), kind),
             pltpu.VMEM((tiles, both, both), jnp.float32),
             pltpu.VMEM(sums_shape.shape, jnp.float32),
             pltpu.VMEM((8, rows), jnp.float32),
             dma,
             dma,
+            dma,
         ],
         size(gathered_shape, gathered_shape, gathered_shape, gathered_shape, weights_shape, sums_shape),
         3,
-        (lengths, places, qk, vg, weights),
+        (lengths, places, qk, grads, weights, *arrived_w),
     )
     lane_k = over_lanes_first(sent[: len(lanes)], devices, lane_v)
-    arrived_q = over_seats_first(sent[len(lanes) :], devices, lane_k)
+    seat_q = over_seats_first(sent[len(lanes) :], devices)
+    arrived_q = seat_q + then_lanes(seat_q, devices, lane_k)
     arrived_v = lane_v + then_seats(lane_v, devices)
     arrived_k = lane_k + then_seats(lane_k, devices)
 
-    pieces = [
-        (arrived_k[i][0] if j == 0 else arrived_k[len(lanes) + j - 1][i])[rows] for i, j, _ in places_of(devices)
-    ]
-    masks = jnp.array([mask for _, _, mask in places_of(devices)], jnp.int32)
-    chosen = (masks ^ place)[None] // copies == jnp.arange(heads, dtype=jnp.int32)[:, None]
-    sums = jnp.sum(jnp.stack(pieces).astype(jnp.float32), axis=1)
-    bias_out = summed_over(jnp.sum(jnp.where(chosen, sums[None], 0.0), axis=1), "dp")
+    bias_out = summed_over(bias_sum[0], "dp")
+    mask = 1
+    while mask < devices:
+        bias_out = bias_out + moved(bias_out, mask)
+        mask *= 2
 
     def unpack(lanes_first, arrived):
         sums_rows, homes = (16, 1) if copies == 1 else (rows, devices)

time: 121 us -> 125 us (1.033)
  starting transfers between devices: 33.4 us -> 69.2 us
  waiting for transfers between devices: 57.3 us -> 26.4 us
    ppermute x30 -> x37, starting transfers between devices: 32.1 us -> 68 us  [moved(): lax.ppermute(value, ('chan', 'seq'), [(source, source ^ mask) for source...]
    ppermute x30 -> x37, waiting for transfers between devices: 57 us -> 26.4 us  [moved(): lax.ppermute(value, ('chan', 'seq'), [(source, source ^ mask) for source...]
  transfers between devices with their start and end apart: 31 -> 38, of which waited for: 14 -> 9; matrix products, arithmetic and copies ran while one was open for 1% -> 1% of each run, Pallas kernels for 14% -> 11%
where the time goes in v3:
time: 125 us; the launch traced here: 124 us
  starting transfers between devices  69.2 us (55%)
  waiting for transfers between devices  26.4 us (21%)
  Pallas kernels  24.7 us (20%)
  between operations  1.87 us (1%)
    ppermute x37, starting transfers between devices, moved(): lax.ppermute(value, ('chan', 'seq'), [(source, source ^ mask) for source...  68 us
    ppermute x37, waiting for transfers between devices, moved(): lax.ppermute(value, ('chan', 'seq'), [(source, source ^ mask) for source...  26.4 us
    pallas_call x8, Pallas kernels, call(): pl.pallas_call(kernel, out_shape=out_shape, in_specs=in_specs, out_specs=...  24.7 us
  transfers between devices with their start and end apart: 38, of which 9 were waited for; matrix products, arithmetic and copies ran while one was open for 1% of the time, Pallas kernels for 11%

profile of v3, /device:TPU:1, one launch (start us, length us, event | category | flops | bytes accessed | tf_op | source)
XLA Modules:
  0.0 124.0 jit_solution(5677155141999436087)
XLA Ops:
  0.6 1.5 %shard_map.93 = (bf16[4,2,128,128]{3,2,1,0:T(8,128)(2,1)S(1)}, bf16[4,2,128,128]{3,2,1,0:T(8,128)(2,1)S(1)}, bf16[4,2,128,128]{3,2,1,0:T(8,128)(2,1)S(1)}, bf16[4,2,128,128]{3,2,1,0:T(8,128)(2,1)S(1)}) custom-call(s32[1]{0:T(128)} %bitcast.place_ref, bf16[128,2048]{1,0:T(8,128)(2,1)} %bitcast.62, bf16[128,2048]{1,0:T(8,128)(2,1)} %bitcast.63), custom_call_target="tpu_custom_call" | custom-call | bytes 2097152 | tf_op jit(solution)/shard_map/pallas_call | solution.py:357
  2.1 2.2 %collective-permute-start.3 = (bf16[4,2,128,128]{3,2,1,0:T(8,128)(2,1)S(1)}, bf16[4,2,128,128]{3,2,1,0:T(8,128)(2,1)S(1)}, u32[]{:S(2)}, u32[]{:S(2)}) collective-permute-start(bf16[4,2,128,128]{3,2,1,0:T(8,128)(2,1)S(1)} %get-tuple-element.67), channel_id=1, source_target_pairs={{0,4},{2,6},{4,0},{6,2},{8,12},{10,14},{12,8},{14,10},{16,20},{18,... | collective-permute-start | bytes 786440 | tf_op jit(solution)/shard_map/ppermute | solution.py:289
  4.3 2.3 %collective-permute-start.4 = (bf16[4,2,128,128]{3,2,1,0:T(8,128)(2,1)S(1)}, bf16[4,2,128,128]{3,2,1,0:T(8,128)(2,1)S(1)}, u32[]{:S(2)}, u32[]{:S(2)}) collective-permute-start(bf16[4,2,128,128]{3,2,1,0:T(8,128)(2,1)S(1)} %get-tuple-element.69), channel_id=1, source_target_pairs={{0,8},{2,10},{4,12},{6,14},{8,0},{10,2},{12,4},{14,6},{16,24},{18,... | collective-permute-start | bytes 786440 | tf_op jit(solution)/shard_map/ppermute | solution.py:289
  6.6 1.5 %shard_map.94 = (bf16[4,2,128,128]{3,2,1,0:T(8,128)(2,1)S(1)}, bf16[4,2,128,128]{3,2,1,0:T(8,128)(2,1)S(1)}, bf16[4,2,128,128]{3,2,1,0:T(8,128)(2,1)S(1)}, bf16[4,2,128,128]{3,2,1,0:T(8,128)(2,1)S(1)}) custom-call(s32[1]{0:T(128)} %bitcast.place_ref, bf16[128,2048]{1,0:T(8,128)(2,1)} %bitcast.64, bf16[128,2048]{1,0:T(8,128)(2,1)} %bitcast.65), custom_call_target="tpu_custom_call" | custom-call | bytes 2097152 | tf_op jit(solution)/shard_map/pallas_call | solution.py:357
  8.1 1.3 %collective-permute-start = (bf16[4,2,128,128]{3,2,1,0:T(8,128)(2,1)S(1)}, bf16[4,2,128,128]{3,2,1,0:T(8,128)(2,1)S(1)}, u32[]{:S(2)}, u32[]{:S(2)}) collective-permute-start(bf16[4,2,128,128]{3,2,1,0:T(8,128)(2,1)S(1)} %get-tuple-element.64), channel_id=1, source_target_pairs={{0,2},{2,0},{4,6},{6,4},{8,10},{10,8},{12,14},{14,12},{16,18},{18,... | collective-permute-start | bytes 786440 | tf_op jit(solution)/shard_map/ppermute | solution.py:289
  9.4 1.5 %collective-permute-start.1 = (bf16[4,2,128,128]{3,2,1,0:T(8,128)(2,1)S(1)}, bf16[4,2,128,128]{3,2,1,0:T(8,128)(2,1)S(1)}, u32[]{:S(2)}, u32[]{:S(2)}) collective-permute-start(bf16[4,2,128,128]{3,2,1,0:T(8,128)(2,1)S(1)} %get-tuple-element.65), channel_id=1, source_target_pairs={{0,16},{2,18},{4,20},{6,22},{8,24},{10,26},{12,28},{14,30},{16,0},... | collective-permute-start | bytes 786440 | tf_op jit(solution)/shard_map/ppermute | solution.py:289
  10.9 1.4 %collective-permute-start.2 = (bf16[4,2,128,128]{3,2,1,0:T(8,128)(2,1)S(1)}, bf16[4,2,128,128]{3,2,1,0:T(8,128)(2,1)S(1)}, u32[]{:S(2)}, u32[]{:S(2)}) collective-permute-start(bf16[4,2,128,128]{3,2,1,0:T(8,128)(2,1)S(1)} %get-tuple-element.66), channel_id=1, source_target_pairs={{0,18},{2,16},{4,22},{6,20},{8,26},{10,24},{12,30},{14,28},{16,2},... | collective-permute-start | bytes 786440 | tf_op jit(solution)/shard_map/ppermute | solution.py:289
  12.3 4.9 %collective-permute-done.1.refs_2_ = bf16[4,2,128,128]{3,2,1,0:T(8,128)(2,1)S(1)} collective-permute-done((bf16[4,2,128,128]{3,2,1,0:T(8,128)(2,1)S(1)}, bf16[4,2,128,128]{3,2,1,0:T(8,128)(2,1)S(1)}, u32[]{:S(2)}, u32[]{:S(2)}) %collective-permute-start.1) | collective-permute-done | bytes 262176 | tf_op jit(solution)/shard_map/ppermute | solution.py:289
  17.2 6.1 %collective-permute-done.2.refs_3_ = bf16[4,2,128,128]{3,2,1,0:T(8,128)(2,1)S(1)} collective-permute-done((bf16[4,2,128,128]{3,2,1,0:T(8,128)(2,1)S(1)}, bf16[4,2,128,128]{3,2,1,0:T(8,128)(2,1)S(1)}, u32[]{:S(2)}, u32[]{:S(2)}) %collective-permute-start.2) | collective-permute-done | bytes 262176 | tf_op jit(solution)/shard_map/ppermute | solution.py:289
  23.8 3.5 %collective-permute-start.10 = (bf16[4,128,128]{2,1,0:T(8,128)(2,1)S(1)}, bf16[4,128,128]{2,1,0:T(8,128)(2,1)S(1)}, u32[]{:S(2)}, u32[]{:S(2)}) collective-permute-start(bf16[4,128,128]{2,1,0:T(8,128)(2,1)S(1)} %pad_maximum_fusion.4), channel_id=1, source_target_pairs={{0,8},{2,10},{4,12},{6,14},{8,0},{10,2},{12,4},{14,6},{16,24},{18,... | collective-permute-start | bytes 393224 | tf_op jit(solution)/shard_map/ppermute | solution.py:289
  27.4 2.5 %collective-permute-start.6 = (bf16[4,2,128,128]{3,2,1,0:T(8,128)(2,1)S(1)}, bf16[4,2,128,128]{3,2,1,0:T(8,128)(2,1)S(1)}, u32[]{:S(2)}, u32[]{:S(2)}) collective-permute-start(bf16[4,2,128,128]{3,2,1,0:T(8,128)(2,1)S(1)} %pad_maximum_fusion), channel_id=1, source_target_pairs={{0,2},{2,0},{4,6},{6,4},{8,10},{10,8},{12,14},{14,12},{16,18},{18,... | collective-permute-start | bytes 786440 | tf_op jit(solution)/shard_map/ppermute | solution.py:289
  29.9 1.3 %collective-permute-start.7 = (bf16[4,2,128,128]{3,2,1,0:T(8,128)(2,1)S(1)}, bf16[4,2,128,128]{3,2,1,0:T(8,128)(2,1)S(1)}, u32[]{:S(2)}, u32[]{:S(2)}) collective-permute-start(bf16[4,2,128,128]{3,2,1,0:T(8,128)(2,1)S(1)} %pad_maximum_fusion.1), channel_id=1, source_target_pairs={{0,16},{2,18},{4,20},{6,22},{8,24},{10,26},{12,28},{14,30},{16,0},... | collective-permute-start | bytes 786440 | tf_op jit(solution)/shard_map/ppermute | solution.py:289
  33.0 1.7 %collective-permute-done.10.refs_5_ = bf16[4,128,128]{2,1,0:T(8,128)(2,1)S(1)} collective-permute-done((bf16[4,128,128]{2,1,0:T(8,128)(2,1)S(1)}, bf16[4,128,128]{2,1,0:T(8,128)(2,1)S(1)}, u32[]{:S(2)}, u32[]{:S(2)}) %collective-permute-start.10) | collective-permute-done | bytes 131104 | tf_op jit(solution)/shard_map/ppermute | solution.py:289
  34.7 4.1 %collective-permute-start.12 = (bf16[4,128,128]{2,1,0:T(8,128)(2,1)S(1)}, bf16[4,128,128]{2,1,0:T(8,128)(2,1)S(1)}, u32[]{:S(2)}, u32[]{:S(2)}) collective-permute-start(bf16[4,128,128]{2,1,0:T(8,128)(2,1)S(1)} %pad_maximum_fusion.5), channel_id=1, source_target_pairs={{0,4},{2,6},{4,0},{6,2},{8,12},{10,14},{12,8},{14,10},{16,20},{18,... | collective-permute-start | bytes 393224 | tf_op jit(solution)/shard_map/ppermute | solution.py:289
  38.8 4.4 %collective-permute-start.13 = (bf16[4,128,128]{2,1,0:T(8,128)(2,1)S(1)}, bf16[4,128,128]{2,1,0:T(8,128)(2,1)S(1)}, u32[]{:S(2)}, u32[]{:S(2)}) collective-permute-start(bf16[4,128,128]{2,1,0:T(8,128)(2,1)S(1)} %pad_maximum_fusion.6), channel_id=1, source_target_pairs={{0,8},{2,10},{4,12},{6,14},{8,0},{10,2},{12,4},{14,6},{16,24},{18,... | collective-permute-start | bytes 393224 | tf_op jit(solution)/shard_map/ppermute | solution.py:289
  45.7 6.0 %shard_map.95 = (bf16[16,2,128,128]{3,2,1,0:T(8,128)(2,1)S(1)}, f32[35,256,256]{2,1,0:T(8,128)S(1)}) custom-call(s32[1]{0:T(128)S(6)} %copy.10.length_ref, s32[1]{0:T(128)} %bitcast.place_ref, f32[16]{0:T(128)S(1)} %copy-done, bf16[4,2,128,128]{3,2,1,0:T(8,128)(2,1)S(1)} %get-tuple-element.60.refs_0_, ...), custom_call_target="tpu_custom_call" | custom-call | flops 587202560 | bytes 2097152 | tf_op jit(solution)/shard_map/pallas_call | solution.py:357
  51.6 3.9 %shard_map.96 = (bf16[16,128,128]{2,1,0:T(8,128)(2,1)S(1)}, bf16[4,128,128]{2,1,0:T(8,128)(2,1)S(1)}, bf16[4,128,128]{2,1,0:T(8,128)(2,1)S(1)}, bf16[4,128,128]{2,1,0:T(8,128)(2,1)S(1)}, bf16[4,128,128]{2,1,0:T(8,128)(2,1)S(1)}) custom-call(s32[1]{0:T(128)S(6)} %copy.10.length_ref, s32[1]{0:T(128)} %bitcast.place_ref, ...), custom_call_target="tpu_custom_call" | custom-call | flops 587202560 | bytes 2097152 | tf_op jit(solution)/shard_map/pallas_call | solution.py:357
  55.6 9.1 %shard_map.97 = (f32[1,16]{1,0:T(1,128)S(1)}, bf16[4,128,128]{2,1,0:T(8,128)(2,1)S(1)}, bf16[4,128,128]{2,1,0:T(8,128)(2,1)S(1)}, bf16[4,128,128]{2,1,0:T(8,128)...) custom-call(s32[1]{0:T(128)S(6)} %copy.10.length_ref, ...), custom_call_target="tpu_custom_call" | custom-call | flops 1761607680 | bytes 2097152 | tf_op jit(solution)/shard_map/pallas_call | solution.py:357
  64.7 1.3 %collective-permute-start.33 = (f32[16]{0:T(128)S(1)}, f32[16]{0:T(128)S(1)}, u32[]{:S(2)}, u32[]{:S(2)}) collective-permute-start(f32[16]{0:T(128)S(1)} %bitcast.58), channel_id=1, source_target_pairs={{0,1},{1,0},{2,3},{3,2},{4,5},{5,4},{6,7},{7,6},{8,9},{9,8},{10,11... | collective-permute-start | bytes 200 | tf_op jit(solution)/shard_map/ppermute | solution.py:278
  66.0 2.0 %collective-permute-start.15 = (bf16[4,128,128]{2,1,0:T(8,128)(2,1)S(1)}, bf16[4,128,128]{2,1,0:T(8,128)(2,1)S(1)}, u32[]{:S(2)}, u32[]{:S(2)}) collective-permute-start(bf16[4,128,128]{2,1,0:T(8,128)(2,1)S(1)} %get-tuple-element.84), channel_id=1, source_target_pairs={{0,2},{2,0},{4,6},{6,4},{8,10},{10,8},{12,14},{14,12},{16,18},{18,... | collective-permute-start | bytes 393224 | tf_op jit(solution)/shard_map/ppermute | solution.py:289
  71.1 2.7 %collective-permute-start.35 = (f32[16]{0:T(128)S(1)}, f32[16]{0:T(128)S(1)}, u32[]{:S(2)}, u32[]{:S(2)}) collective-permute-start(f32[16]{0:T(128)S(1)} %add.20), channel_id=1, source_target_pairs={{0,4},{2,6},{4,0},{6,2},{8,12},{10,14},{12,8},{14,10},{16,20},{18,... | collective-permute-start | bytes 200 | tf_op jit(solution)/shard_map/ppermute | solution.py:289
  75.1 2.5 %collective-permute-start.36 = (f32[16]{0:T(128)S(1)}, f32[16]{0:T(128)S(1)}, u32[]{:S(2)}, u32[]{:S(2)}) collective-permute-start(f32[16]{0:T(128)S(1)} %add.21), channel_id=1, source_target_pairs={{0,8},{2,10},{4,12},{6,14},{8,0},{10,2},{12,4},{14,6},{16,24},{18,... | collective-permute-start | bytes 200 | tf_op jit(solution)/shard_map/ppermute | solution.py:289
  78.5 2.4 %collective-permute-start.21 = (bf16[4,128,128]{2,1,0:T(8,128)(2,1)S(1)}, bf16[4,128,128]{2,1,0:T(8,128)(2,1)S(1)}, u32[]{:S(2)}, u32[]{:S(2)}) collective-permute-start(bf16[4,128,128]{2,1,0:T(8,128)(2,1)S(1)} %get-tuple-element.92), channel_id=1, source_target_pairs={{0,8},{2,10},{4,12},{6,14},{8,0},{10,2},{12,4},{14,6},{16,24},{18,... | collective-permute-start | bytes 393224 | tf_op jit(solution)/shard_map/ppermute | solution.py:289
  82.0 3.1 %collective-permute-done.21.refs_2_ = bf16[4,128,128]{2,1,0:T(8,128)(2,1)S(1)} collective-permute-done((bf16[4,128,128]{2,1,0:T(8,128)(2,1)S(1)}, bf16[4,128,128]{2,1,0:T(8,128)(2,1)S(1)}, u32[]{:S(2)}, u32[]{:S(2)}) %collective-permute-start.21) | collective-permute-done | bytes 131104 | tf_op jit(solution)/shard_map/ppermute | solution.py:289
  87.3 5.1 %collective-permute-start.19 = (bf16[4,128,128]{2,1,0:T(8,128)(2,1)S(1)}, bf16[4,128,128]{2,1,0:T(8,128)(2,1)S(1)}, u32[]{:S(2)}, u32[]{:S(2)}) collective-permute-start(bf16[4,128,128]{2,1,0:T(8,128)(2,1)S(1)} %get-tuple-element.89), channel_id=1, source_target_pairs={{0,4},{2,6},{4,0},{6,2},{8,12},{10,14},{12,8},{14,10},{16,20},{18,... | collective-permute-start | bytes 393224 | tf_op jit(solution)/shard_map/ppermute | solution.py:289
  93.4 3.2 %collective-permute-start.30 = (bf16[4,128,128]{2,1,0:T(8,128)(2,1)S(1)}, bf16[4,128,128]{2,1,0:T(8,128)(2,1)S(1)}, u32[]{:S(2)}, u32[]{:S(2)}) collective-permute-start(bf16[4,128,128]{2,1,0:T(8,128)(2,1)S(1)} %pad_maximum_fusion.15), channel_id=1, source_target_pairs={{0,2},{2,0},{4,6},{6,4},{8,10},{10,8},{12,14},{14,12},{16,18},{18,... | collective-permute-start | bytes 393224 | tf_op jit(solution)/shard_map/ppermute | solution.py:289
  98.7 7.8 %collective-permute-start.32 = (bf16[4,128,128]{2,1,0:T(8,128)(2,1)S(1)}, bf16[4,128,128]{2,1,0:T(8,128)(2,1)S(1)}, u32[]{:S(2)}, u32[]{:S(2)}) collective-permute-start(bf16[4,128,128]{2,1,0:T(8,128)(2,1)S(1)} %pad_maximum_fusion.17), channel_id=1, source_target_pairs={{0,18},{2,16},{4,22},{6,20},{8,26},{10,24},{12,30},{14,28},{16,2},... | collective-permute-start | bytes 393224 | tf_op jit(solution)/shard_map/ppermute | solution.py:289
  107.1 1.8 %collective-permute-start.29 = (bf16[4,128,128]{2,1,0:T(8,128)(2,1)S(1)}, bf16[4,128,128]{2,1,0:T(8,128)(2,1)S(1)}, u32[]{:S(2)}, u32[]{:S(2)}) collective-permute-start(bf16[4,128,128]{2,1,0:T(8,128)(2,1)S(1)} %pad_maximum_fusion.14), channel_id=1, source_target_pairs={{0,18},{2,16},{4,22},{6,20},{8,26},{10,24},{12,30},{14,28},{16,2},... | collective-permute-start | bytes 393224 | tf_op jit(solution)/shard_map/ppermute | solution.py:289
  108.9 2.3 %collective-permute-start.26 = (bf16[4,128,128]{2,1,0:T(8,128)(2,1)S(1)}, bf16[4,128,128]{2,1,0:T(8,128)(2,1)S(1)}, u32[]{:S(2)}, u32[]{:S(2)}) collective-permute-start(bf16[4,128,128]{2,1,0:T(8,128)(2,1)S(1)} %pad_maximum_fusion.11), channel_id=1, source_target_pairs={{0,12},{2,14},{4,8},{6,10},{8,4},{10,6},{12,0},{14,2},{16,28},{18,... | collective-permute-start | bytes 393224 | tf_op jit(solution)/shard_map/ppermute | solution.py:289
  111.3 2.0 %collective-permute-start.20 = (bf16[4,128,128]{2,1,0:T(8,128)(2,1)S(1)}, bf16[4,128,128]{2,1,0:T(8,128)(2,1)S(1)}, u32[]{:S(2)}, u32[]{:S(2)}) collective-permute-start(bf16[4,128,128]{2,1,0:T(8,128)(2,1)S(1)} %pad_maximum_fusion.9), channel_id=1, source_target_pairs={{0,4},{2,6},{4,0},{6,2},{8,12},{10,14},{12,8},{14,10},{16,20},{18,... | collective-permute-start | bytes 393224 | tf_op jit(solution)/shard_map/ppermute | solution.py:289
  114.7 1.8 %collective-permute-done.29.refs_6_ = bf16[4,128,128]{2,1,0:T(8,128)(2,1)S(1)} collective-permute-done((bf16[4,128,128]{2,1,0:T(8,128)(2,1)S(1)}, bf16[4,128,128]{2,1,0:T(8,128)(2,1)S(1)}, u32[]{:S(2)}, u32[]{:S(2)}) %collective-permute-start.29) | collective-permute-done | bytes 131104 | tf_op jit(solution)/shard_map/ppermute | solution.py:289
  117.4 5.5 %collective-permute-done.23.refs_5_ = bf16[4,128,128]{2,1,0:T(8,128)(2,1)S(1)} collective-permute-done((bf16[4,128,128]{2,1,0:T(8,128)(2,1)S(1)}, bf16[4,128,128]{2,1,0:T(8,128)(2,1)S(1)}, u32[]{:S(2)}, u32[]{:S(2)}) %collective-permute-start.23) | collective-permute-done | bytes 131104 | tf_op jit(solution)/shard_map/ppermute | solution.py:289
  (96 shorter events, 19.5 us)
Async XLA Ops:
  2.1 21.3 %collective-permute-start.3 = (bf16[4,2,128,128]{3,2,1,0:T(8,128)(2,1)S(1)}, bf16[4,2,128,128]{3,2,1,0:T(8,128)(2,1)S(1)}, u32[]{:S(2)}, u32[]{:S(2)}) collective-permute-start(bf16[4,2,128,128]{3,2,1,0:T(8,128)(2,1)S(1)} %get-tuple-element.67), channel_id=1, source_target_pairs={{0,4},{2,6},{4,0},{6,2},{8,12},{10,14},{12,8},{14,10},{16,20},{18,... | collective-permute-start | bytes 786440 | tf_op jit(solution)/shard_map/ppermute | solution.py:289
  4.3 19.1 %collective-permute-start.4 = (bf16[4,2,128,128]{3,2,1,0:T(8,128)(2,1)S(1)}, bf16[4,2,128,128]{3,2,1,0:T(8,128)(2,1)S(1)}, u32[]{:S(2)}, u32[]{:S(2)}) collective-permute-start(bf16[4,2,128,128]{3,2,1,0:T(8,128)(2,1)S(1)} %get-tuple-element.69), channel_id=1, source_target_pairs={{0,8},{2,10},{4,12},{6,14},{8,0},{10,2},{12,4},{14,6},{16,24},{18,... | collective-permute-start | bytes 786440 | tf_op jit(solution)/shard_map/ppermute | solution.py:289
  6.6 20.8 %collective-permute-start.5 = (bf16[4,2,128,128]{3,2,1,0:T(8,128)(2,1)S(1)}, bf16[4,2,128,128]{3,2,1,0:T(8,128)(2,1)S(1)}, u32[]{:S(2)}, u32[]{:S(2)}) collective-permute-start(bf16[4,2,128,128]{3,2,1,0:T(8,128)(2,1)S(1)} %get-tuple-element.71), channel_id=1, source_target_pairs={{0,12},{2,14},{4,8},{6,10},{8,4},{10,6},{12,0},{14,2},{16,28},{18,... | collective-permute-start | bytes 786440 | tf_op jit(solution)/shard_map/ppermute | solution.py:289
  9.4 7.8 %collective-permute-start.1 = (bf16[4,2,128,128]{3,2,1,0:T(8,128)(2,1)S(1)}, bf16[4,2,128,128]{3,2,1,0:T(8,128)(2,1)S(1)}, u32[]{:S(2)}, u32[]{:S(2)}) collective-permute-start(bf16[4,2,128,128]{3,2,1,0:T(8,128)(2,1)S(1)} %get-tuple-element.65), channel_id=1, source_target_pairs={{0,16},{2,18},{4,20},{6,22},{8,24},{10,26},{12,28},{14,30},{16,0},... | collective-permute-start | bytes 786440 | tf_op jit(solution)/shard_map/ppermute | solution.py:289
  10.9 12.4 %collective-permute-start.2 = (bf16[4,2,128,128]{3,2,1,0:T(8,128)(2,1)S(1)}, bf16[4,2,128,128]{3,2,1,0:T(8,128)(2,1)S(1)}, u32[]{:S(2)}, u32[]{:S(2)}) collective-permute-start(bf16[4,2,128,128]{3,2,1,0:T(8,128)(2,1)S(1)} %get-tuple-element.66), channel_id=1, source_target_pairs={{0,18},{2,16},{4,22},{6,20},{8,26},{10,24},{12,30},{14,28},{16,2},... | collective-permute-start | bytes 786440 | tf_op jit(solution)/shard_map/ppermute | solution.py:289
  23.4 8.4 %collective-permute-start.9 = (bf16[4,128,128]{2,1,0:T(8,128)(2,1)S(1)}, bf16[4,128,128]{2,1,0:T(8,128)(2,1)S(1)}, u32[]{:S(2)}, u32[]{:S(2)}) collective-permute-start(bf16[4,128,128]{2,1,0:T(8,128)(2,1)S(1)} %pad_maximum_fusion.3), channel_id=1, source_target_pairs={{0,4},{2,6},{4,0},{6,2},{8,12},{10,14},{12,8},{14,10},{16,20},{18,... | collective-permute-start | bytes 393224 | tf_op jit(solution)/shard_map/ppermute | solution.py:289
  23.8 10.9 %collective-permute-start.10 = (bf16[4,128,128]{2,1,0:T(8,128)(2,1)S(1)}, bf16[4,128,128]{2,1,0:T(8,128)(2,1)S(1)}, u32[]{:S(2)}, u32[]{:S(2)}) collective-permute-start(bf16[4,128,128]{2,1,0:T(8,128)(2,1)S(1)} %pad_maximum_fusion.4), channel_id=1, source_target_pairs={{0,8},{2,10},{4,12},{6,14},{8,0},{10,2},{12,4},{14,6},{16,24},{18,... | collective-permute-start | bytes 393224 | tf_op jit(solution)/shard_map/ppermute | solution.py:289
  27.4 15.8 %collective-permute-start.6 = (bf16[4,2,128,128]{3,2,1,0:T(8,128)(2,1)S(1)}, bf16[4,2,128,128]{3,2,1,0:T(8,128)(2,1)S(1)}, u32[]{:S(2)}, u32[]{:S(2)}) collective-permute-start(bf16[4,2,128,128]{3,2,1,0:T(8,128)(2,1)S(1)} %pad_maximum_fusion), channel_id=1, source_target_pairs={{0,2},{2,0},{4,6},{6,4},{8,10},{10,8},{12,14},{14,12},{16,18},{18,... | collective-permute-start | bytes 786440 | tf_op jit(solution)/shard_map/ppermute | solution.py:289
  29.9 15.0 %collective-permute-start.7 = (bf16[4,2,128,128]{3,2,1,0:T(8,128)(2,1)S(1)}, bf16[4,2,128,128]{3,2,1,0:T(8,128)(2,1)S(1)}, u32[]{:S(2)}, u32[]{:S(2)}) collective-permute-start(bf16[4,2,128,128]{3,2,1,0:T(8,128)(2,1)S(1)} %pad_maximum_fusion.1), channel_id=1, source_target_pairs={{0,16},{2,18},{4,20},{6,22},{8,24},{10,26},{12,28},{14,30},{16,0},... | collective-permute-start | bytes 786440 | tf_op jit(solution)/shard_map/ppermute | solution.py:289
  31.3 13.7 %collective-permute-start.8 = (bf16[4,2,128,128]{3,2,1,0:T(8,128)(2,1)S(1)}, bf16[4,2,128,128]{3,2,1,0:T(8,128)(2,1)S(1)}, u32[]{:S(2)}, u32[]{:S(2)}) collective-permute-start(bf16[4,2,128,128]{3,2,1,0:T(8,128)(2,1)S(1)} %pad_maximum_fusion.2), channel_id=1, source_target_pairs={{0,18},{2,16},{4,22},{6,20},{8,26},{10,24},{12,30},{14,28},{16,2},... | collective-permute-start | bytes 786440 | tf_op jit(solution)/shard_map/ppermute | solution.py:289
  31.8 7.0 %collective-permute-start.11 = (bf16[4,128,128]{2,1,0:T(8,128)(2,1)S(1)}, bf16[4,128,128]{2,1,0:T(8,128)(2,1)S(1)}, u32[]{:S(2)}, u32[]{:S(2)}) collective-permute-start(bf16[4,128,128]{2,1,0:T(8,128)(2,1)S(1)} %pad_maximum_fusion.8), channel_id=1, source_target_pairs={{0,12},{2,14},{4,8},{6,10},{8,4},{10,6},{12,0},{14,2},{16,28},{18,... | collective-permute-start | bytes 393224 | tf_op jit(solution)/shard_map/ppermute | solution.py:289
  34.7 20.9 %collective-permute-start.12 = (bf16[4,128,128]{2,1,0:T(8,128)(2,1)S(1)}, bf16[4,128,128]{2,1,0:T(8,128)(2,1)S(1)}, u32[]{:S(2)}, u32[]{:S(2)}) collective-permute-start(bf16[4,128,128]{2,1,0:T(8,128)(2,1)S(1)} %pad_maximum_fusion.5), channel_id=1, source_target_pairs={{0,4},{2,6},{4,0},{6,2},{8,12},{10,14},{12,8},{14,10},{16,20},{18,... | collective-permute-start | bytes 393224 | tf_op jit(solution)/shard_map/ppermute | solution.py:289
  38.8 16.7 %collective-permute-start.13 = (bf16[4,128,128]{2,1,0:T(8,128)(2,1)S(1)}, bf16[4,128,128]{2,1,0:T(8,128)(2,1)S(1)}, u32[]{:S(2)}, u32[]{:S(2)}) collective-permute-start(bf16[4,128,128]{2,1,0:T(8,128)(2,1)S(1)} %pad_maximum_fusion.6), channel_id=1, source_target_pairs={{0,8},{2,10},{4,12},{6,14},{8,0},{10,2},{12,4},{14,6},{16,24},{18,... | collective-permute-start | bytes 393224 | tf_op jit(solution)/shard_map/ppermute | solution.py:289
  43.3 12.3 %collective-permute-start.14 = (bf16[4,128,128]{2,1,0:T(8,128)(2,1)S(1)}, bf16[4,128,128]{2,1,0:T(8,128)(2,1)S(1)}, u32[]{:S(2)}, u32[]{:S(2)}) collective-permute-start(bf16[4,128,128]{2,1,0:T(8,128)(2,1)S(1)} %pad_maximum_fusion.7), channel_id=1, source_target_pairs={{0,12},{2,14},{4,8},{6,10},{8,4},{10,6},{12,0},{14,2},{16,28},{18,... | collective-permute-start | bytes 393224 | tf_op jit(solution)/shard_map/ppermute | solution.py:289
  66.0 26.4 %collective-permute-start.15 = (bf16[4,128,128]{2,1,0:T(8,128)(2,1)S(1)}, bf16[4,128,128]{2,1,0:T(8,128)(2,1)S(1)}, u32[]{:S(2)}, u32[]{:S(2)}) collective-permute-start(bf16[4,128,128]{2,1,0:T(8,128)(2,1)S(1)} %get-tuple-element.84), channel_id=1, source_target_pairs={{0,2},{2,0},{4,6},{6,4},{8,10},{10,8},{12,14},{14,12},{16,18},{18,... | collective-permute-start | bytes 393224 | tf_op jit(solution)/shard_map/ppermute | solution.py:289
  68.0 25.5 %collective-permute-start.16 = (bf16[4,128,128]{2,1,0:T(8,128)(2,1)S(1)}, bf16[4,128,128]{2,1,0:T(8,128)(2,1)S(1)}, u32[]{:S(2)}, u32[]{:S(2)}) collective-permute-start(bf16[4,128,128]{2,1,0:T(8,128)(2,1)S(1)} %get-tuple-element.85), channel_id=1, source_target_pairs={{0,16},{2,18},{4,20},{6,22},{8,24},{10,26},{12,28},{14,30},{16,0},... | collective-permute-start | bytes 393224 | tf_op jit(solution)/shard_map/ppermute | solution.py:289
  70.0 26.7 %collective-permute-start.17 = (bf16[4,128,128]{2,1,0:T(8,128)(2,1)S(1)}, bf16[4,128,128]{2,1,0:T(8,128)(2,1)S(1)}, u32[]{:S(2)}, u32[]{:S(2)}) collective-permute-start(bf16[4,128,128]{2,1,0:T(8,128)(2,1)S(1)} %get-tuple-element.86), channel_id=1, source_target_pairs={{0,18},{2,16},{4,22},{6,20},{8,26},{10,24},{12,30},{14,28},{16,2},... | collective-permute-start | bytes 393224 | tf_op jit(solution)/shard_map/ppermute | solution.py:289
  73.9 7.1 %collective-permute-start.18 = (bf16[4,128,128]{2,1,0:T(8,128)(2,1)S(1)}, bf16[4,128,128]{2,1,0:T(8,128)(2,1)S(1)}, u32[]{:S(2)}, u32[]{:S(2)}) collective-permute-start(bf16[4,128,128]{2,1,0:T(8,128)(2,1)S(1)} %get-tuple-element.88), channel_id=1, source_target_pairs={{0,4},{2,6},{4,0},{6,2},{8,12},{10,14},{12,8},{14,10},{16,20},{18,... | collective-permute-start | bytes 393224 | tf_op jit(solution)/shard_map/ppermute | solution.py:289
  78.5 6.5 %collective-permute-start.21 = (bf16[4,128,128]{2,1,0:T(8,128)(2,1)S(1)}, bf16[4,128,128]{2,1,0:T(8,128)(2,1)S(1)}, u32[]{:S(2)}, u32[]{:S(2)}) collective-permute-start(bf16[4,128,128]{2,1,0:T(8,128)(2,1)S(1)} %get-tuple-element.92), channel_id=1, source_target_pairs={{0,8},{2,10},{4,12},{6,14},{8,0},{10,2},{12,4},{14,6},{16,24},{18,... | collective-permute-start | bytes 393224 | tf_op jit(solution)/shard_map/ppermute | solution.py:289
  80.9 6.4 %collective-permute-start.24 = (bf16[4,128,128]{2,1,0:T(8,128)(2,1)S(1)}, bf16[4,128,128]{2,1,0:T(8,128)(2,1)S(1)}, u32[]{:S(2)}, u32[]{:S(2)}) collective-permute-start(bf16[4,128,128]{2,1,0:T(8,128)(2,1)S(1)} %get-tuple-element.96), channel_id=1, source_target_pairs={{0,12},{2,14},{4,8},{6,10},{8,4},{10,6},{12,0},{14,2},{16,28},{18,... | collective-permute-start | bytes 393224 | tf_op jit(solution)/shard_map/ppermute | solution.py:289
  85.1 21.6 %collective-permute-start.37 = (f32[16]{0:T(128)S(1)}, f32[16]{0:T(128)S(1)}, u32[]{:S(2)}, u32[]{:S(2)}) collective-permute-start(f32[16]{0:T(128)S(1)} %add.22), channel_id=1, source_target_pairs={{0,16},{2,18},{4,20},{6,22},{8,24},{10,26},{12,28},{14,30},{16,0},... | collective-permute-start | bytes 200 | tf_op jit(solution)/shard_map/ppermute | solution.py:289
  87.3 10.7 %collective-permute-start.19 = (bf16[4,128,128]{2,1,0:T(8,128)(2,1)S(1)}, bf16[4,128,128]{2,1,0:T(8,128)(2,1)S(1)}, u32[]{:S(2)}, u32[]{:S(2)}) collective-permute-start(bf16[4,128,128]{2,1,0:T(8,128)(2,1)S(1)} %get-tuple-element.89), channel_id=1, source_target_pairs={{0,4},{2,6},{4,0},{6,2},{8,12},{10,14},{12,8},{14,10},{16,20},{18,... | collective-permute-start | bytes 393224 | tf_op jit(solution)/shard_map/ppermute | solution.py:289
  92.4 6.3 %collective-permute-start.22 = (bf16[4,128,128]{2,1,0:T(8,128)(2,1)S(1)}, bf16[4,128,128]{2,1,0:T(8,128)(2,1)S(1)}, u32[]{:S(2)}, u32[]{:S(2)}) collective-permute-start(bf16[4,128,128]{2,1,0:T(8,128)(2,1)S(1)} %get-tuple-element.93), channel_id=1, source_target_pairs={{0,8},{2,10},{4,12},{6,14},{8,0},{10,2},{12,4},{14,6},{16,24},{18,... | collective-permute-start | bytes 393224 | tf_op jit(solution)/shard_map/ppermute | solution.py:289
  93.4 13.7 %collective-permute-start.30 = (bf16[4,128,128]{2,1,0:T(8,128)(2,1)S(1)}, bf16[4,128,128]{2,1,0:T(8,128)(2,1)S(1)}, u32[]{:S(2)}, u32[]{:S(2)}) collective-permute-start(bf16[4,128,128]{2,1,0:T(8,128)(2,1)S(1)} %pad_maximum_fusion.15), channel_id=1, source_target_pairs={{0,2},{2,0},{4,6},{6,4},{8,10},{10,8},{12,14},{14,12},{16,18},{18,... | collective-permute-start | bytes 393224 | tf_op jit(solution)/shard_map/ppermute | solution.py:289
  96.7 9.8 %collective-permute-start.25 = (bf16[4,128,128]{2,1,0:T(8,128)(2,1)S(1)}, bf16[4,128,128]{2,1,0:T(8,128)(2,1)S(1)}, u32[]{:S(2)}, u32[]{:S(2)}) collective-permute-start(bf16[4,128,128]{2,1,0:T(8,128)(2,1)S(1)} %get-tuple-element.97), channel_id=1, source_target_pairs={{0,12},{2,14},{4,8},{6,10},{8,4},{10,6},{12,0},{14,2},{16,28},{18,... | collective-permute-start | bytes 393224 | tf_op jit(solution)/shard_map/ppermute | solution.py:289
  98.0 11.0 %collective-permute-start.31 = (bf16[4,128,128]{2,1,0:T(8,128)(2,1)S(1)}, bf16[4,128,128]{2,1,0:T(8,128)(2,1)S(1)}, u32[]{:S(2)}, u32[]{:S(2)}) collective-permute-start(bf16[4,128,128]{2,1,0:T(8,128)(2,1)S(1)} %pad_maximum_fusion.16), channel_id=1, source_target_pairs={{0,16},{2,18},{4,20},{6,22},{8,24},{10,26},{12,28},{14,30},{16,0},... | collective-permute-start | bytes 393224 | tf_op jit(solution)/shard_map/ppermute | solution.py:289
  98.7 12.6 %collective-permute-start.32 = (bf16[4,128,128]{2,1,0:T(8,128)(2,1)S(1)}, bf16[4,128,128]{2,1,0:T(8,128)(2,1)S(1)}, u32[]{:S(2)}, u32[]{:S(2)}) collective-permute-start(bf16[4,128,128]{2,1,0:T(8,128)(2,1)S(1)} %pad_maximum_fusion.17), channel_id=1, source_target_pairs={{0,18},{2,16},{4,22},{6,20},{8,26},{10,24},{12,30},{14,28},{16,2},... | collective-permute-start | bytes 393224 | tf_op jit(solution)/shard_map/ppermute | solution.py:289
  106.7 8.0 %collective-permute-start.28 = (bf16[4,128,128]{2,1,0:T(8,128)(2,1)S(1)}, bf16[4,128,128]{2,1,0:T(8,128)(2,1)S(1)}, u32[]{:S(2)}, u32[]{:S(2)}) collective-permute-start(bf16[4,128,128]{2,1,0:T(8,128)(2,1)S(1)} %pad_maximum_fusion.13), channel_id=1, source_target_pairs={{0,16},{2,18},{4,20},{6,22},{8,24},{10,26},{12,28},{14,30},{16,0},... | collective-permute-start | bytes 393224 | tf_op jit(solution)/shard_map/ppermute | solution.py:289
  107.1 9.4 %collective-permute-start.29 = (bf16[4,128,128]{2,1,0:T(8,128)(2,1)S(1)}, bf16[4,128,128]{2,1,0:T(8,128)(2,1)S(1)}, u32[]{:S(2)}, u32[]{:S(2)}) collective-permute-start(bf16[4,128,128]{2,1,0:T(8,128)(2,1)S(1)} %pad_maximum_fusion.14), channel_id=1, source_target_pairs={{0,18},{2,16},{4,22},{6,20},{8,26},{10,24},{12,30},{14,28},{16,2},... | collective-permute-start | bytes 393224 | tf_op jit(solution)/shard_map/ppermute | solution.py:289
  108.9 8.5 %collective-permute-start.26 = (bf16[4,128,128]{2,1,0:T(8,128)(2,1)S(1)}, bf16[4,128,128]{2,1,0:T(8,128)(2,1)S(1)}, u32[]{:S(2)}, u32[]{:S(2)}) collective-permute-start(bf16[4,128,128]{2,1,0:T(8,128)(2,1)S(1)} %pad_maximum_fusion.11), channel_id=1, source_target_pairs={{0,12},{2,14},{4,8},{6,10},{8,4},{10,6},{12,0},{14,2},{16,28},{18,... | collective-permute-start | bytes 393224 | tf_op jit(solution)/shard_map/ppermute | solution.py:289
  111.2 11.7 %collective-permute-start.23 = (bf16[4,128,128]{2,1,0:T(8,128)(2,1)S(1)}, bf16[4,128,128]{2,1,0:T(8,128)(2,1)S(1)}, u32[]{:S(2)}, u32[]{:S(2)}) collective-permute-start(bf16[4,128,128]{2,1,0:T(8,128)(2,1)S(1)} %pad_maximum_fusion.10), channel_id=1, source_target_pairs={{0,8},{2,10},{4,12},{6,14},{8,0},{10,2},{12,4},{14,6},{16,24},{18,... | collective-permute-start | bytes 393224 | tf_op jit(solution)/shard_map/ppermute | solution.py:289
  111.3 11.6 %collective-permute-start.20 = (bf16[4,128,128]{2,1,0:T(8,128)(2,1)S(1)}, bf16[4,128,128]{2,1,0:T(8,128)(2,1)S(1)}, u32[]{:S(2)}, u32[]{:S(2)}) collective-permute-start(bf16[4,128,128]{2,1,0:T(8,128)(2,1)S(1)} %pad_maximum_fusion.9), channel_id=1, source_target_pairs={{0,4},{2,6},{4,0},{6,2},{8,12},{10,14},{12,8},{14,10},{16,20},{18,... | collective-permute-start | bytes 393224 | tf_op jit(solution)/shard_map/ppermute | solution.py:289
  (7 other events, 22.0 us)

commit v4 on v2

v4 whole, which is shorter than its diff:
```python
import functools
import math

import jax
import jax.numpy as jnp
from jax import lax
from jax.experimental import pallas as pl
from jax.experimental.pallas import tpu as pltpu
from jax.sharding import PartitionSpec as P


LOOKBACK = 6
NEG_FILL = -1e30
EXTRA = 8
LOG2_E = math.log2(math.e)
SLACK_BYTES = 6 << 20


def stages(devices):
    seats = [0, 1, devices // 2, devices // 2 + 1]
    lanes = [2 * step for step in range(devices // 4)]
    return seats, lanes


def places_of(devices):
    seats, lanes = stages(devices)
    return [(i, j, lane + seat) for i, lane in enumerate(lanes) for j, seat in enumerate(seats)]


def run_all(copies):
    for copy in copies:
        copy.start()
    for copy in copies:
        copy.wait()


def piece(pieces, lanes_first, i, j, devices):
    seats, lanes = stages(devices)
    firsts = len(lanes) if lanes_first else len(seats)
    near, far = (i, j) if lanes_first else (j, i)
    return pieces[firsts + far - 1].at[near] if far else pieces[near].at[0]


def gathered(place, pieces, lanes_first, target, sems):
    devices = target.shape[0]
    return [
        pltpu.make_async_copy(piece(pieces, lanes_first, i, j, devices), target.at[place ^ mask], sems.at[index])
        for index, (i, j, mask) in enumerate(places_of(devices))
    ]


def scattered(place, source, refs, lanes_first, sems):
    devices = source.shape[0]
    return [
        pltpu.make_async_copy(
            source.at[place ^ mask], (refs[i].at[j] if lanes_first else refs[j].at[i]), sems.at[index]
        )
        for index, (i, j, mask) in enumerate(places_of(devices))
    ]


def pack_kernel(copies, lanes_first, place_ref, first_ref, second_ref, *refs):
    sems = refs[-1]
    width = refs[0].shape[-1]
    started = []
    for index, (i, j, mask) in enumerate(places_of(sems.shape[0])):
        head = (place_ref[0] ^ mask) // copies
        columns = pl.ds(pl.multiple_of(head * width, width), width)
        target = refs[i].at[j] if lanes_first else refs[j].at[i]
        for kind, source in enumerate((first_ref, second_ref)):
            started.append(pltpu.make_async_copy(source.at[:, columns], target.at[kind], sems.at[index, kind]))
    run_all(started)


def unpack_kernel(copies, part, place_ref, *refs):
    sems, home, sums = refs[-1], refs[-2], refs[-3]
    outs = refs[-6:-3]
    pieces = refs[:-6] if part == 0 else refs[:-9]
    devices = sems.shape[0]
    width = home.shape[2]
    half = outs[0].shape[0] // 2
    window = pl.ds(part * half, half)
    started = []
    for index, (i, j, mask) in enumerate(places_of(devices)):
        source = piece(pieces, part == 0, i, j, devices)
        other = place_ref[0] ^ mask
        if copies > 1:
            started.append(pltpu.make_async_copy(source, home.at[other], sems.at[index, 0]))
            continue
        columns = pl.ds(pl.multiple_of(other * width, width), width)
        for kind, out in enumerate(outs):
            rows = source.at[pl.ds(kind * half, half)]
            started.append(pltpu.make_async_copy(rows, out.at[window, columns], sems.at[index, kind]))
    run_all(started)
    if copies > 1:
        for head in range(devices // copies):
            columns = pl.ds(head * width, width)
            for kind, out in enumerate(outs):
                rows = pl.ds(kind * half, half)
                value = home[head * copies, rows].astype(jnp.float32)
                for other in range(1, copies):
                    value = value + home[head * copies + other, rows].astype(jnp.float32)
                sums[kind, :, columns] = value.astype(sums.dtype)
        run_all([pltpu.make_async_copy(sums.at[kind], out.at[window], sems.at[0, kind]) for kind, out in enumerate(outs)])


def dot(left, right, contract):
    return lax.dot_general(left, right, (contract, ((), ())), preferred_element_type=jnp.float32)


def fold(tile, op):
    return op(tile.reshape(tile.shape[0] // 8, 8, tile.shape[1]), axis=0)


def pair(ref, block, *kind):
    blocks = ref.shape[0] // 2
    return jnp.concatenate([ref[block, *kind], ref[blocks + block, *kind]], axis=0)


def tile_count(blocks):
    return sum(min(block, LOOKBACK) + 1 for block in range(blocks))


def for_groups(length, rows, blocks, on_group, off_group=None):
    early = min(LOOKBACK, blocks)
    group = 2 if early % 2 == 0 and (blocks - early) % 2 == 0 else 1
    visited = ((length + group * rows - 1) // (group * rows)) * group
    visited = jnp.minimum(visited, blocks)
    for start in range(0, early, group):
        @pl.when(start < visited)
        def _():
            on_group([(block, tile_count(block), block + 1) for block in range(start, start + group)])

        if off_group is not None:
            pl.when(start >= visited)(lambda: off_group([start + k for k in range(group)]))
    if blocks > early:
        def member(block):
            return block, tile_count(LOOKBACK) + (block - LOOKBACK) * (LOOKBACK + 1), LOOKBACK + 1

        def live(step, carried):
            on_group([member(LOOKBACK + step * group + k) for k in range(group)])
            return carried

        def dead(step, carried):
            off_group([LOOKBACK + step * group + k for k in range(group)])
            return carried

        late = jnp.maximum(visited - LOOKBACK, 0) // group
        lax.fori_loop(0, late, live, 0)
        if off_group is not None:
            lax.fori_loop(late, (blocks - early) // group, dead, 0)
    return visited


def stats_kernel(copies, length_ref, place_ref, bias_ref, *refs):
    pieces, (qk_ref, kt_ref, power_ref, inverse_ref, sems) = refs[:-5], refs[-5:]
    devices, _, rows, width = qk_ref.shape
    blocks = devices // 2
    both = 2 * rows
    log2_scale = LOG2_E / math.sqrt(width)
    place = place_ref[0]
    bias = bias_ref[place // copies] * LOG2_E
    part = place % copies
    length = length_ref[0]
    run_all(gathered(place, pieces, True, qk_ref, sems))

    column = lax.broadcasted_iota(jnp.int32, (1, both), 1)
    own = [jnp.where((column // rows) == c, 0.0, bias) for c in range(2)]
    key_row = lax.broadcasted_iota(jnp.int32, (rows, both), 0)
    query_column = lax.broadcasted_iota(jnp.int32, (rows, both), 1) % rows
    for block in range(blocks):
        kt_ref[block] = pair(qk_ref, block, 1).T

    def on_group(members):
        shifts = []
        for block, base, tiles in members:
            queries = pair(qk_ref, block, 0)
            first = block - (tiles - 1)
            peaks = [jnp.full((8, both), NEG_FILL, jnp.float32)] * 2
            for t in range(tiles):
                raw = dot(pair(qk_ref, first + t, 1), queries, ((1,), (1,)))
                for c in range(2):
                    tile = raw[c * rows : (c + 1) * rows]
                    if t == tiles - 1:
                        tile = jnp.where(key_row <= query_column, tile, NEG_FILL)
                    if tiles == LOOKBACK + 1 and t == 0:
                        tile = jnp.where(key_row > query_column, tile, NEG_FILL)
                    power_ref[base + t, c * rows : (c + 1) * rows] = tile
                    peaks[c] = jnp.maximum(peaks[c], fold(tile, jnp.max))
            peaks = [jnp.max(peaks[c], axis=0, keepdims=True) * log2_scale + own[c] for c in range(2)]
            peak = jnp.maximum(peaks[0], peaks[1])
            shifts.append([own[c] - peak for c in range(2)])
        for (block, base, tiles), shift in zip(members, shifts):
            total = jnp.zeros((8, both), jnp.float32)
            for t in range(tiles):
                for c in range(2):
                    window = slice(c * rows, (c + 1) * rows)
                    power = jnp.exp2(power_ref[base + t, window] * log2_scale + shift[c])
                    power_ref[base + t, window] = power
                    total = total + fold(power, jnp.sum)
            total = jnp.sum(total, axis=0, keepdims=True)
            live = block * rows + column % rows < length
            if copies > 1:
                live = live & ((column * copies) // both == part)
            inverse_ref[block] = jnp.broadcast_to(jnp.where(live, 1.0 / total, 0.0), (8, both))

    for_groups(length, rows, blocks, on_group)


def grads_kernel(length_ref, place_ref, qk_ref, kt_ref, power_ref, inverse_ref, *refs):
    arrays, scratch = refs[:-9], refs[-9:]
    gv_ref, low_a, low_b, d_ref, dk_ref, dv_ref, bias_acc, got_sems, send_sems = scratch
    devices, _, rows, width = qk_ref.shape
    seats, lanes = stages(devices)
    count = len(seats) + len(lanes) - 1
    blocks = devices // 2
    both = 2 * rows
    half = rows // 2
    root_scale = 1.0 / math.sqrt(width)
    place = place_ref[0]
    outputs = arrays[count:]
    run_all(gathered(place, arrays[:count], False, gv_ref, got_sems))
    bias_acc[...] = jnp.zeros_like(bias_acc)

    def put(kind, c, block, tile):
        low_a[c * blocks + block, kind * half : (kind + 1) * half] = tile[:half]
        low_b[c * blocks + block, kind * half : (kind + 1) * half] = tile[half:]

    def on_group(members):
        deltas = []
        for k, (block, base, tiles) in enumerate(members):
            grads = pair(gv_ref, block, 0)
            first = block - (tiles - 1)
            moment = jnp.zeros((8, both), jnp.float32)
            for t in range(tiles):
                weight_grad = dot(pair(gv_ref, first + t, 1), grads, ((1,), (1,)))
                d_ref[k, t] = weight_grad
                moment = moment + fold(power_ref[base + t] * weight_grad, jnp.sum)
            deltas.append(jnp.sum(moment, axis=0, keepdims=True) * inverse_ref[block, :1])
        sums = []
        for k, (block, base, tiles) in enumerate(members):
            queries = pair(qk_ref, block, 0)
            grads = pair(gv_ref, block, 0)
            inverse = inverse_ref[block, :1]
            first = block - (tiles - 1)
            query_sum = jnp.zeros((width, both), jnp.float32)
            cross = jnp.zeros((8, rows), jnp.float32)
            for t in range(tiles):
                weights = power_ref[base + t] * inverse
                score_grad = weights * (d_ref[k, t] - deltas[k])
                cross = cross + fold(score_grad[:rows, rows:], jnp.sum) + fold(score_grad[rows:, :rows], jnp.sum)
                score_low = score_grad.astype(jnp.bfloat16)
                value_term = dot(weights.astype(jnp.bfloat16), grads, ((1,), (0,)))
                key_term = dot(score_low, queries, ((1,), (0,)))
                if t == tiles - 1:
                    dv_ref[block] = value_term
                    dk_ref[block] = key_term
                else:
                    dv_ref[first + t] += value_term
                    dk_ref[first + t] += key_term
                query_sum = query_sum + dot(kt_ref[first + t], score_low, ((1,), (0,)))
            bias_acc[...] += cross
            sums.append(query_sum)
        for (block, _, _), query_sum in zip(members, sums):
            query_grad = (query_sum * root_scale).T.astype(low_a.dtype)
            for c in range(2):
                put(0, c, block, query_grad[c * rows : (c + 1) * rows])

    def off_group(members):
        for block in members:
            for c in range(2):
                put(0, c, block, jnp.zeros((rows, width), low_a.dtype))

    visited = for_groups(length_ref[0], rows, blocks, on_group, off_group)

    whole = jnp.sum(jnp.sum(bias_acc[...], axis=0, keepdims=True), axis=1, keepdims=True)
    whole = jnp.broadcast_to(whole, (1, width))
    high = whole.astype(jnp.bfloat16).astype(jnp.float32)
    middle = (whole - high).astype(jnp.bfloat16).astype(jnp.float32)
    low = (whole - high - middle).astype(jnp.bfloat16).astype(jnp.float32)
    lane = lax.broadcasted_iota(jnp.int32, (1, width), 1)
    pieces = jnp.where(lane == 0, high, jnp.where(lane == 1, middle, jnp.where(lane == 2, low, 0.0)))
    pieces = jnp.broadcast_to(pieces, (EXTRA, width)).astype(low_a.dtype)
    for block in range(blocks):
        seen = block < visited
        key_grad = jnp.where(seen, dk_ref[block] * root_scale, 0.0).astype(low_a.dtype)
        value_grad = jnp.where(seen, dv_ref[block], 0.0).astype(low_a.dtype)
        for c in range(2):
            put(1, c, block, key_grad[c * rows : (c + 1) * rows])
            put(2, c, block, value_grad[c * rows : (c + 1) * rows])
            low_a[c * blocks + block, 3 * half : 3 * half + EXTRA] = pieces
    leaving = scattered(place, low_a, outputs[: len(lanes)], True, send_sems.at[0])
    leaving += scattered(place, low_b, outputs[len(lanes) :], False, send_sems.at[1])
    run_all(leaving)


def summed_over(value, axis):
    count = lax.axis_size(axis)
    if count & (count - 1):
        return lax.psum(value, axis)
    step = 1
    while step < count:
        pairs = [(source, source ^ step) for source in range(count)]
        value = value + lax.ppermute(value, axis, pairs)
        step *= 2
    return value


def in_hbm(value):
    return pltpu.with_memory_space_constraint(value, pltpu.HBM)


def moved(value, mask):
    devices = lax.axis_size("chan") * lax.axis_size("seq")
    return lax.ppermute(value, ("chan", "seq"), [(source, source ^ mask) for source in range(devices)])


def exchanged(by_lane, by_seat, devices):
    seats, lanes = stages(devices)
    first_a = [by_lane[0]] + [moved(by_lane[i], lanes[i]) for i in range(1, len(lanes))]
    first_b = [by_seat[0]] + [moved(by_seat[j], seats[j]) for j in range(1, len(seats))]
    last_b = []
    for i in range(1, len(lanes)):
        waiting, first_a[i] = lax.optimization_barrier((jnp.stack([value[i] for value in first_b]), first_a[i]))
        last_b.append(moved(waiting, lanes[i]))
    last_a = [moved(jnp.stack([value[j] for value in first_a]), seats[j]) for j in range(1, len(seats))]
    return first_a + last_a, first_b + last_b


def layer(queries, keys, values, out_grad, cross_bias, lengths):
    rows, features = queries.shape[2:]
    heads = cross_bias.shape[0]
    width = features // heads
    blocks = lax.axis_size("seq")
    devices = lax.axis_size("chan") * blocks
    copies = devices // heads
    seats, lanes = stages(devices)
    place = lax.axis_index("chan") * blocks + lax.axis_index("seq")
    places = place.astype(jnp.int32)[None]
    kind = queries.dtype
    both = 2 * rows
    tiles = min(LOOKBACK + 1, blocks)
    vmem = pl.BlockSpec(memory_space=pltpu.VMEM)
    smem = pl.BlockSpec(memory_space=pltpu.SMEM)
    anywhere = pl.BlockSpec(memory_space=pl.ANY)
    hbm = pl.BlockSpec(memory_space=pltpu.HBM)

    def by_lane(*block):
        return [jax.ShapeDtypeStruct((len(seats),) + block, kind)] * len(lanes)

    def by_seat(*block):
        return [jax.ShapeDtypeStruct((len(lanes),) + block, kind)] * len(seats)

    def size(*shapes):
        return sum(math.prod(shape.shape) * shape.dtype.itemsize for shape in shapes)

    def call(kernel, out_shape, in_specs, out_specs, scratch, grant, matmuls, args):
        flops = 2 * matmuls * tile_count(blocks) * both * both * width
        return pl.pallas_call(
            kernel,
            out_shape=out_shape,
            in_specs=in_specs,
            out_specs=out_specs,
            scratch_shapes=scratch,
            compiler_params=pltpu.CompilerParams(vmem_limit_bytes=grant + SLACK_BYTES),
            cost_estimate=pl.CostEstimate(flops=flops, bytes_accessed=2 << 20, transcendentals=0),
        )(*args)

    def pack(lanes_first, first, second):
        sends = by_lane(2, rows, width) if lanes_first else by_seat(2, rows, width)
        return call(
            functools.partial(pack_kernel, copies, lanes_first),
            sends,
            [smem, hbm, hbm],
            [vmem] * len(sends),
            [pltpu.SemaphoreType.DMA((devices, 2))],
            0,
            0,
            (places, in_hbm(first[0, 0]), in_hbm(second[0, 0])),
        )

    sent_a = pack(True, queries, keys)
    values, out_grad, sent_a = lax.optimization_barrier((values, out_grad, sent_a))
    sent_b = pack(False, out_grad, values)
    arrived_a, arrived_b = exchanged(sent_a, sent_b, devices)

    half = rows // 2
    group = 2
    two_shape = jax.ShapeDtypeStruct((devices, 2, rows, width), kind)
    turned_shape = jax.ShapeDtypeStruct((blocks, width, both), kind)
    power_shape = jax.ShapeDtypeStruct((tile_count(blocks), both, both), jnp.float32)
    inverse_shape = jax.ShapeDtypeStruct((blocks, 8, both), jnp.float32)
    sums_shape = jax.ShapeDtypeStruct((blocks, both, width), jnp.float32)
    low_a, low_b = (
        jax.ShapeDtypeStruct((devices, pay, width), kind) for pay in (3 * half + EXTRA, 3 * half)
    )
    d_shape = jax.ShapeDtypeStruct((group, tiles, both, both), jnp.float32)
    dma = pltpu.SemaphoreType.DMA((devices,))
    made = call(
        functools.partial(stats_kernel, copies),
        (two_shape, turned_shape, power_shape, inverse_shape),
        [smem, smem, smem] + [anywhere] * len(arrived_a),
        [vmem] * 4,
        [dma],
        size(two_shape, turned_shape, power_shape, inverse_shape),
        1,
        (lengths, places, cross_bias, *arrived_a),
    )
    sends = by_lane(*low_a.shape[1:]) + by_seat(*low_b.shape[1:])
    held = (two_shape, low_a, low_b, d_shape, sums_shape, sums_shape)
    back = call(
        grads_kernel,
        sends,
        [smem, smem] + [vmem] * 4 + [anywhere] * len(arrived_b),
        [anywhere] * len(sends),
        [pltpu.VMEM(shape.shape, shape.dtype) for shape in held]
        + [pltpu.VMEM((8, rows), jnp.float32), dma, pltpu.SemaphoreType.DMA((2, devices))],
        size(*held, two_shape, turned_shape, power_shape, inverse_shape),
        4,
        (lengths, places, *made, *arrived_b),
    )
    arrived_a, arrived_b = exchanged(back[: len(lanes)], back[len(lanes) :], devices)

    pieces = [
        (arrived_a[i][0] if j == 0 else arrived_a[len(lanes) + j - 1][i])[3 * half] for i, j, _ in places_of(devices)
    ]
    masks = jnp.array([mask for _, _, mask in places_of(devices)], jnp.int32)
    chosen = (masks ^ place)[None] // copies == jnp.arange(heads, dtype=jnp.int32)[:, None]
    sums = jnp.sum(jnp.stack(pieces).astype(jnp.float32), axis=1)
    bias_out = summed_over(jnp.sum(jnp.where(chosen, sums[None], 0.0), axis=1), "dp")

    def unpack(part, arrived, earlier):
        flat = jax.ShapeDtypeStruct((rows, features), kind)
        alone = copies == 1
        return pl.pallas_call(
            functools.partial(unpack_kernel, copies, part),
            out_shape=(flat, flat, flat),
            in_specs=[smem] + [anywhere] * len(arrived) + [hbm] * len(earlier),
            out_specs=(hbm, hbm, hbm),
            scratch_shapes=[
                pltpu.VMEM((8, 8, 128) if alone else (3, half, features), kind),
                pltpu.VMEM((1, 8, width) if alone else (devices,) + arrived[0].shape[1:], kind),
                pltpu.SemaphoreType.DMA((devices, 3)),
            ],
            input_output_aliases={1 + len(arrived) + i: i for i in range(len(earlier))},
            compiler_params=pltpu.CompilerParams(vmem_limit_bytes=SLACK_BYTES),
            name="unpack_b" if part else "unpack_a",
        )(places, *arrived, *earlier)

    grads = unpack(1, arrived_b, unpack(0, arrived_a, ()))
    return tuple(grad[None, None] for grad in grads) + (bias_out,)


def solution(mesh):
    placed = P("dp", "chan", "seq", None)
    return jax.shard_map(
        layer,
        mesh=mesh,
        in_specs=(placed, placed, placed, placed, P(), P("dp")),
        out_specs=(placed, placed, placed, P()),
        check_vma=False,
    )
```

time: 121 us -> 115 us (0.950)
  starting transfers between devices: 33.4 us -> 24.5 us
  waiting for transfers between devices: 57.3 us -> 62.7 us
  Pallas kernels: 24.1 us -> 22.1 us
    ppermute x30 -> x24, starting transfers between devices: 32.1 us -> 23.2 us  [moved(): lax.ppermute(value, ('chan', 'seq'), [(source, source ^ mask) for source...]
    ppermute x30 -> x24, waiting for transfers between devices: 57 us -> 62.7 us  [moved(): lax.ppermute(value, ('chan', 'seq'), [(source, source ^ mask) for source...]
    pallas_call x8 -> x4, Pallas kernels: 24.1 us -> 19.5 us  [call(): pl.pallas_call(kernel, out_shape=out_shape, in_specs=in_specs, out_specs=...]
    pallas_call x0 -> x2, Pallas kernels: none -> 2.56 us  [unpack(): pl.pallas_call(functools.partial(unpack_kernel, copies, part), out_shape=...]
  transfers between devices with their start and end apart: 31 -> 25, of which waited for: 14 -> 12; matrix products, arithmetic and copies ran while one was open for 1% -> 1% of each run, Pallas kernels for 14% -> 7%
where the time goes in v4:
time: 115 us; the launch traced here: 114 us
  waiting for transfers between devices  62.7 us (55%)
  starting transfers between devices  24.5 us (21%)
  Pallas kernels  22.1 us (19%)
  other arithmetic  1.8 us (2%)
  between operations  1.62 us (1%)
    ppermute x24, waiting for transfers between devices, moved(): lax.ppermute(value, ('chan', 'seq'), [(source, source ^ mask) for source...  62.7 us
    ppermute x24, starting transfers between devices, moved(): lax.ppermute(value, ('chan', 'seq'), [(source, source ^ mask) for source...  23.2 us
    pallas_call x4, Pallas kernels, call(): pl.pallas_call(kernel, out_shape=out_shape, in_specs=in_specs, out_specs=...  19.5 us
    pallas_call x2, Pallas kernels, unpack(): pl.pallas_call(functools.partial(unpack_kernel, copies, part), out_shape=...  2.56 us
  transfers between devices with their start and end apart: 25, of which 12 were waited for; matrix products, arithmetic and copies ran while one was open for 1% of the time, Pallas kernels for 7%

profile of v4, /device:TPU:1, one launch (start us, length us, event | category | flops | bytes accessed | tf_op | source)
XLA Modules:
  0.0 113.6 jit_solution(10083417514585908350)
XLA Ops:
  0.6 1.5 %shard_map.102 = (bf16[4,2,128,128]{3,2,1,0:T(8,128)(2,1)S(1)}, bf16[4,2,128,128]{3,2,1,0:T(8,128)(2,1)S(1)}, bf16[4,2,128,128]{3,2,1,0:T(8,128)(2,1)S(1)}, bf16[4,2,128,128]{3,2,1,0:T(8,128)(2,1)S(1)}) custom-call(s32[1]{0:T(128)} %bitcast.place_ref, bf16[128,2048]{1,0:T(8,128)(2,1)} %bitcast.43, bf16[128,2048]{1,0:T(8,128)(2,1)} %bitcast.44), custom_call_target="tpu_custom_call" | custom-call | bytes 2097152 | tf_op jit(solution)/shard_map/pallas_call | solution.py:359
  2.1 1.5 %shard_map.103 = (bf16[4,2,128,128]{3,2,1,0:T(8,128)(2,1)S(1)}, bf16[4,2,128,128]{3,2,1,0:T(8,128)(2,1)S(1)}, bf16[4,2,128,128]{3,2,1,0:T(8,128)(2,1)S(1)}, bf16[4,2,128,128]{3,2,1,0:T(8,128)(2,1)S(1)}) custom-call(s32[1]{0:T(128)} %bitcast.place_ref, bf16[128,2048]{1,0:T(8,128)(2,1)} %bitcast.45, bf16[128,2048]{1,0:T(8,128)(2,1)} %bitcast.46), custom_call_target="tpu_custom_call" | custom-call | bytes 2097152 | tf_op jit(solution)/shard_map/pallas_call | solution.py:359
  3.7 2.7 %collective-permute-start.1 = (bf16[4,2,128,128]{3,2,1,0:T(8,128)(2,1)S(1)}, bf16[4,2,128,128]{3,2,1,0:T(8,128)(2,1)S(1)}, u32[]{:S(2)}, u32[]{:S(2)}) collective-permute-start(bf16[4,2,128,128]{3,2,1,0:T(8,128)(2,1)S(1)} %get-tuple-element.57), channel_id=1, source_target_pairs={{0,16},{2,18},{4,20},{6,22},{8,24},{10,26},{12,28},{14,30},{16,0},... | collective-permute-start | bytes 786440 | tf_op jit(solution)/shard_map/ppermute | solution.py:315
  6.5 3.7 %collective-permute-start.5 = (bf16[4,2,128,128]{3,2,1,0:T(8,128)(2,1)S(1)}, bf16[4,2,128,128]{3,2,1,0:T(8,128)(2,1)S(1)}, u32[]{:S(2)}, u32[]{:S(2)}) collective-permute-start(bf16[4,2,128,128]{3,2,1,0:T(8,128)(2,1)S(1)} %get-tuple-element.63), channel_id=1, source_target_pairs={{0,12},{2,14},{4,8},{6,10},{8,4},{10,6},{12,0},{14,2},{16,28},{18,... | collective-permute-start | bytes 786440 | tf_op jit(solution)/shard_map/ppermute | solution.py:315
  10.6 2.4 %collective-permute-done.1.refs_2_ = bf16[4,2,128,128]{3,2,1,0:T(8,128)(2,1)S(1)} collective-permute-done((bf16[4,2,128,128]{3,2,1,0:T(8,128)(2,1)S(1)}, bf16[4,2,128,128]{3,2,1,0:T(8,128)(2,1)S(1)}, u32[]{:S(2)}, u32[]{:S(2)}) %collective-permute-start.1) | collective-permute-done | bytes 262176 | tf_op jit(solution)/shard_map/ppermute | solution.py:315
  13.0 5.9 %collective-permute-done.2.refs_3_ = bf16[4,2,128,128]{3,2,1,0:T(8,128)(2,1)S(1)} collective-permute-done((bf16[4,2,128,128]{3,2,1,0:T(8,128)(2,1)S(1)}, bf16[4,2,128,128]{3,2,1,0:T(8,128)(2,1)S(1)}, u32[]{:S(2)}, u32[]{:S(2)}) %collective-permute-start.2) | collective-permute-done | bytes 262176 | tf_op jit(solution)/shard_map/ppermute | solution.py:315
  19.1 13.4 %collective-permute-done.4.refs_2_ = bf16[4,2,128,128]{3,2,1,0:T(8,128)(2,1)S(1)} collective-permute-done((bf16[4,2,128,128]{3,2,1,0:T(8,128)(2,1)S(1)}, bf16[4,2,128,128]{3,2,1,0:T(8,128)(2,1)S(1)}, u32[]{:S(2)}, u32[]{:S(2)}) %collective-permute-start.4) | collective-permute-done | bytes 262176 | tf_op jit(solution)/shard_map/ppermute | solution.py:315
  32.6 2.2 %collective-permute-start.8 = (bf16[4,2,128,128]{3,2,1,0:T(8,128)(2,1)S(1)}, bf16[4,2,128,128]{3,2,1,0:T(8,128)(2,1)S(1)}, u32[]{:S(2)}, u32[]{:S(2)}) collective-permute-start(bf16[4,2,128,128]{3,2,1,0:T(8,128)(2,1)S(1)} %pad_maximum_fusion.5), channel_id=1, source_target_pairs={{0,18},{2,16},{4,22},{6,20},{8,26},{10,24},{12,30},{14,28},{16,2},... | collective-permute-start | bytes 786440 | tf_op jit(solution)/shard_map/ppermute | solution.py:315
  36.0 2.3 %collective-permute-start.11 = (bf16[4,2,128,128]{3,2,1,0:T(8,128)(2,1)S(1)}, bf16[4,2,128,128]{3,2,1,0:T(8,128)(2,1)S(1)}, u32[]{:S(2)}, u32[]{:S(2)}) collective-permute-start(bf16[4,2,128,128]{3,2,1,0:T(8,128)(2,1)S(1)} %pad_maximum_fusion.2), channel_id=1, source_target_pairs={{0,12},{2,14},{4,8},{6,10},{8,4},{10,6},{12,0},{14,2},{16,28},{18,... | collective-permute-start | bytes 786440 | tf_op jit(solution)/shard_map/ppermute | solution.py:315
  38.3 3.6 %collective-permute-done.8.refs_6_ = bf16[4,2,128,128]{3,2,1,0:T(8,128)(2,1)S(1)} collective-permute-done((bf16[4,2,128,128]{3,2,1,0:T(8,128)(2,1)S(1)}, bf16[4,2,128,128]{3,2,1,0:T(8,128)(2,1)S(1)}, u32[]{:S(2)}, u32[]{:S(2)}) %collective-permute-start.8) | collective-permute-done | bytes 262176 | tf_op jit(solution)/shard_map/ppermute | solution.py:315
  41.9 0.7 broadcast_xor_fusion
  42.6 4.8 %collective-permute-done.7.refs_5_ = bf16[4,2,128,128]{3,2,1,0:T(8,128)(2,1)S(1)} collective-permute-done((bf16[4,2,128,128]{3,2,1,0:T(8,128)(2,1)S(1)}, bf16[4,2,128,128]{3,2,1,0:T(8,128)(2,1)S(1)}, u32[]{:S(2)}, u32[]{:S(2)}) %collective-permute-start.7) | collective-permute-done | bytes 262176 | tf_op jit(solution)/shard_map/ppermute | solution.py:315
  47.4 0.7 copy-done
  48.0 5.6 %shard_map.104 = (bf16[16,2,128,128]{3,2,1,0:T(8,128)(2,1)S(1)}, bf16[8,128,256]{2,1,0:T(8,128)(2,1)S(1)}, f32[35,256,256]{2,1,0:T(8,128)S(1)}, f32[8,8,256]{2,1,0:T(8,128)S(1)}) custom-call(s32[1]{0:T(128)S(6)} %copy.17.length_ref, s32[1]{0:T(128)} %bitcast.place_ref, f32[16]{0:T(128)S(1)} %copy-done, ...), custom_call_target="tpu_custom_call" | custom-call | flops 587202560 | bytes 2097152 | tf_op jit(solution)/shard_map/pallas_call | solution.py:359
  53.6 6.0 %collective-permute-done.10.refs_5_ = bf16[4,2,128,128]{3,2,1,0:T(8,128)(2,1)S(1)} collective-permute-done((bf16[4,2,128,128]{3,2,1,0:T(8,128)(2,1)S(1)}, bf16[4,2,128,128]{3,2,1,0:T(8,128)(2,1)S(1)}, u32[]{:S(2)}, u32[]{:S(2)}) %collective-permute-start.10) | collective-permute-done | bytes 262176 | tf_op jit(solution)/shard_map/ppermute | solution.py:315
  59.6 11.0 %shard_map.105 = (bf16[4,200,128]{2,1,0:T(8,128)(2,1)S(1)}, bf16[4,200,128]{2,1,0:T(8,128)(2,1)S(1)}, bf16[4,200,128]{2,1,0:T(8,128)(2,1)S(1)}, bf16[4,200,128]{...) custom-call(s32[1]{0:T(128)S(6)} %copy.17.length_ref, ...), custom_call_target="tpu_custom_call" | custom-call | flops 2348810240 | bytes 2097152 | tf_op jit(solution)/shard_map/pallas_call | solution.py:359
  70.6 1.2 %collective-permute-start.12 = (bf16[4,192,128]{2,1,0:T(8,128)(2,1)S(1)}, bf16[4,192,128]{2,1,0:T(8,128)(2,1)S(1)}, u32[]{:S(2)}, u32[]{:S(2)}) collective-permute-start(bf16[4,192,128]{2,1,0:T(8,128)(2,1)S(1)} %get-tuple-element.73), channel_id=1, source_target_pairs={{0,2},{2,0},{4,6},{6,4},{8,10},{10,8},{12,14},{14,12},{16,18},{18,... | collective-permute-start | bytes 589832 | tf_op jit(solution)/shard_map/ppermute | solution.py:315
  71.8 1.1 collective-permute-start.13
  72.9 0.6 collective-permute-start.14
  73.6 1.1 collective-permute-start.19
  74.7 2.5 %collective-permute-start.15 = (bf16[4,200,128]{2,1,0:T(8,128)(2,1)S(1)}, bf16[4,200,128]{2,1,0:T(8,128)(2,1)S(1)}, u32[]{:S(2)}, u32[]{:S(2)}) collective-permute-start(bf16[4,200,128]{2,1,0:T(8,128)(2,1)S(1)} %get-tuple-element.76), channel_id=1, source_target_pairs={{0,4},{2,6},{4,0},{6,2},{8,12},{10,14},{12,8},{14,10},{16,20},{18,... | collective-permute-start | bytes 614408 | tf_op jit(solution)/shard_map/ppermute | solution.py:315
  77.3 0.9 collective-permute-done.13.refs_2_
  78.2 4.7 %collective-permute-done.14.refs_3_ = bf16[4,192,128]{2,1,0:T(8,128)(2,1)S(1)} collective-permute-done((bf16[4,192,128]{2,1,0:T(8,128)(2,1)S(1)}, bf16[4,192,128]{2,1,0:T(8,128)(2,1)S(1)}, u32[]{:S(2)}, u32[]{:S(2)}) %collective-permute-start.14) | collective-permute-done | bytes 196640 | tf_op jit(solution)/shard_map/ppermute | solution.py:315
  83.1 8.3 %collective-permute-done.17.refs_2_ = bf16[4,200,128]{2,1,0:T(8,128)(2,1)S(1)} collective-permute-done((bf16[4,200,128]{2,1,0:T(8,128)(2,1)S(1)}, bf16[4,200,128]{2,1,0:T(8,128)(2,1)S(1)}, u32[]{:S(2)}, u32[]{:S(2)}) %collective-permute-start.17) | collective-permute-done | bytes 204832 | tf_op jit(solution)/shard_map/ppermute | solution.py:315
  91.5 1.9 %collective-permute-start.23 = (bf16[4,200,128]{2,1,0:T(8,128)(2,1)S(1)}, bf16[4,200,128]{2,1,0:T(8,128)(2,1)S(1)}, u32[]{:S(2)}, u32[]{:S(2)}) collective-permute-start(bf16[4,200,128]{2,1,0:T(8,128)(2,1)S(1)} %pad_maximum_fusion.8), channel_id=1, source_target_pairs={{0,18},{2,16},{4,22},{6,20},{8,26},{10,24},{12,30},{14,28},{16,2},... | collective-permute-start | bytes 614408 | tf_op jit(solution)/shard_map/ppermute | solution.py:315
  94.0 2.2 %collective-permute-start.20 = (bf16[4,192,128]{2,1,0:T(8,128)(2,1)S(1)}, bf16[4,192,128]{2,1,0:T(8,128)(2,1)S(1)}, u32[]{:S(2)}, u32[]{:S(2)}) collective-permute-start(bf16[4,192,128]{2,1,0:T(8,128)(2,1)S(1)} %pad_maximum_fusion.11), channel_id=1, source_target_pairs={{0,12},{2,14},{4,8},{6,10},{8,4},{10,6},{12,0},{14,2},{16,28},{18,... | collective-permute-start | bytes 589832 | tf_op jit(solution)/shard_map/ppermute | solution.py:315
  96.2 3.0 %collective-permute-done.23.refs_6_ = bf16[4,200,128]{2,1,0:T(8,128)(2,1)S(1)} collective-permute-done((bf16[4,200,128]{2,1,0:T(8,128)(2,1)S(1)}, bf16[4,200,128]{2,1,0:T(8,128)(2,1)S(1)}, u32[]{:S(2)}, u32[]{:S(2)}) %collective-permute-start.23) | collective-permute-done | bytes 204832 | tf_op jit(solution)/shard_map/ppermute | solution.py:315
  99.2 4.5 %collective-permute-done.22.refs_5_ = bf16[4,200,128]{2,1,0:T(8,128)(2,1)S(1)} collective-permute-done((bf16[4,200,128]{2,1,0:T(8,128)(2,1)S(1)}, bf16[4,200,128]{2,1,0:T(8,128)(2,1)S(1)}, u32[]{:S(2)}, u32[]{:S(2)}) %collective-permute-start.22) | collective-permute-done | bytes 204832 | tf_op jit(solution)/shard_map/ppermute | solution.py:315
  104.0 1.3 %collective-permute-start.24 = (f32[16]{0:T(128)S(1)}, f32[16]{0:T(128)S(1)}, u32[]{:S(2)}, u32[]{:S(2)}) collective-permute-start(f32[16]{0:T(128)S(1)} %select_reduce_fusion), channel_id=1, source_target_pairs={{0,1},{1,0},{2,3},{3,2},{4,5},{5,4},{6,7},{7,6},{8,9},{9,8},{10,11... | collective-permute-start | bytes 200 | tf_op jit(solution)/shard_map/ppermute | solution.py:304
  105.3 1.3 %unpack_a.1 = (bf16[128,2048]{1,0:T(8,128)(2,1)}, bf16[128,2048]{1,0:T(8,128)(2,1)}, bf16[128,2048]{1,0:T(8,128)(2,1)}) custom-call(s32[1]{0:T(128)} %bitcast.place_ref, bf16[4,200,128]{2,1,0:T(8,128)(2,1)S(1)} %get-tuple-element.82.refs_0_, bf16[4,200,128]{2,1,0:T(8,128)(2,1)S(1)} %collective-permute-done.15.refs_1_, ...), custom_call_target="tpu_custom_call" | custom-call | tf_op jit(solution)/shard_map/unpack_a/pallas_call | solution.py:435
  106.6 5.2 %collective-permute-done.18.refs_5_ = bf16[4,192,128]{2,1,0:T(8,128)(2,1)S(1)} collective-permute-done((bf16[4,192,128]{2,1,0:T(8,128)(2,1)S(1)}, bf16[4,192,128]{2,1,0:T(8,128)(2,1)S(1)}, u32[]{:S(2)}, u32[]{:S(2)}) %collective-permute-start.18) | collective-permute-done | bytes 196640 | tf_op jit(solution)/shard_map/ppermute | solution.py:315
  111.8 1.3 %unpack_b.1 = (bf16[128,2048]{1,0:T(8,128)(2,1)}, bf16[128,2048]{1,0:T(8,128)(2,1)}, bf16[128,2048]{1,0:T(8,128)(2,1)}) custom-call(s32[1]{0:T(128)} %bitcast.place_ref, bf16[4,192,128]{2,1,0:T(8,128)(2,1)S(1)} %get-tuple-element.72.refs_0_, ...), custom_call_target="tpu_custom_call", output_to_operand_aliasing={{0}: (8, {}), {1}: (9, {}), {2}: (10, {})} | custom-call | tf_op jit(solution)/shard_map/unpack_b/pallas_call | solution.py:435
  (66 shorter events, 3.1 us)
Async XLA Ops:
  3.6 6.6 %collective-permute-start = (bf16[4,2,128,128]{3,2,1,0:T(8,128)(2,1)S(1)}, bf16[4,2,128,128]{3,2,1,0:T(8,128)(2,1)S(1)}, u32[]{:S(2)}, u32[]{:S(2)}) collective-permute-start(bf16[4,2,128,128]{3,2,1,0:T(8,128)(2,1)S(1)} %get-tuple-element.56), channel_id=1, source_target_pairs={{0,2},{2,0},{4,6},{6,4},{8,10},{10,8},{12,14},{14,12},{16,18},{18,... | collective-permute-start | bytes 786440 | tf_op jit(solution)/shard_map/ppermute | solution.py:315
  3.7 9.3 %collective-permute-start.1 = (bf16[4,2,128,128]{3,2,1,0:T(8,128)(2,1)S(1)}, bf16[4,2,128,128]{3,2,1,0:T(8,128)(2,1)S(1)}, u32[]{:S(2)}, u32[]{:S(2)}) collective-permute-start(bf16[4,2,128,128]{3,2,1,0:T(8,128)(2,1)S(1)} %get-tuple-element.57), channel_id=1, source_target_pairs={{0,16},{2,18},{4,20},{6,22},{8,24},{10,26},{12,28},{14,30},{16,0},... | collective-permute-start | bytes 786440 | tf_op jit(solution)/shard_map/ppermute | solution.py:315
  6.4 12.5 %collective-permute-start.2 = (bf16[4,2,128,128]{3,2,1,0:T(8,128)(2,1)S(1)}, bf16[4,2,128,128]{3,2,1,0:T(8,128)(2,1)S(1)}, u32[]{:S(2)}, u32[]{:S(2)}) collective-permute-start(bf16[4,2,128,128]{3,2,1,0:T(8,128)(2,1)S(1)} %get-tuple-element.58), channel_id=1, source_target_pairs={{0,18},{2,16},{4,22},{6,20},{8,26},{10,24},{12,30},{14,28},{16,2},... | collective-permute-start | bytes 786440 | tf_op jit(solution)/shard_map/ppermute | solution.py:315
  6.5 12.5 %collective-permute-start.5 = (bf16[4,2,128,128]{3,2,1,0:T(8,128)(2,1)S(1)}, bf16[4,2,128,128]{3,2,1,0:T(8,128)(2,1)S(1)}, u32[]{:S(2)}, u32[]{:S(2)}) collective-permute-start(bf16[4,2,128,128]{3,2,1,0:T(8,128)(2,1)S(1)} %get-tuple-element.63), channel_id=1, source_target_pairs={{0,12},{2,14},{4,8},{6,10},{8,4},{10,6},{12,0},{14,2},{16,28},{18,... | collective-permute-start | bytes 786440 | tf_op jit(solution)/shard_map/ppermute | solution.py:315
  10.2 22.3 %collective-permute-start.4 = (bf16[4,2,128,128]{3,2,1,0:T(8,128)(2,1)S(1)}, bf16[4,2,128,128]{3,2,1,0:T(8,128)(2,1)S(1)}, u32[]{:S(2)}, u32[]{:S(2)}) collective-permute-start(bf16[4,2,128,128]{3,2,1,0:T(8,128)(2,1)S(1)} %get-tuple-element.61), channel_id=1, source_target_pairs={{0,8},{2,10},{4,12},{6,14},{8,0},{10,2},{12,4},{14,6},{16,24},{18,... | collective-permute-start | bytes 786440 | tf_op jit(solution)/shard_map/ppermute | solution.py:315
  10.3 22.2 %collective-permute-start.3 = (bf16[4,2,128,128]{3,2,1,0:T(8,128)(2,1)S(1)}, bf16[4,2,128,128]{3,2,1,0:T(8,128)(2,1)S(1)}, u32[]{:S(2)}, u32[]{:S(2)}) collective-permute-start(bf16[4,2,128,128]{3,2,1,0:T(8,128)(2,1)S(1)} %get-tuple-element.59), channel_id=1, source_target_pairs={{0,4},{2,6},{4,0},{6,2},{8,12},{10,14},{12,8},{14,10},{16,20},{18,... | collective-permute-start | bytes 786440 | tf_op jit(solution)/shard_map/ppermute | solution.py:315
  32.6 9.4 %collective-permute-start.8 = (bf16[4,2,128,128]{3,2,1,0:T(8,128)(2,1)S(1)}, bf16[4,2,128,128]{3,2,1,0:T(8,128)(2,1)S(1)}, u32[]{:S(2)}, u32[]{:S(2)}) collective-permute-start(bf16[4,2,128,128]{3,2,1,0:T(8,128)(2,1)S(1)} %pad_maximum_fusion.5), channel_id=1, source_target_pairs={{0,18},{2,16},{4,22},{6,20},{8,26},{10,24},{12,30},{14,28},{16,2},... | collective-permute-start | bytes 786440 | tf_op jit(solution)/shard_map/ppermute | solution.py:315
  34.8 12.6 %collective-permute-start.7 = (bf16[4,2,128,128]{3,2,1,0:T(8,128)(2,1)S(1)}, bf16[4,2,128,128]{3,2,1,0:T(8,128)(2,1)S(1)}, u32[]{:S(2)}, u32[]{:S(2)}) collective-permute-start(bf16[4,2,128,128]{3,2,1,0:T(8,128)(2,1)S(1)} %pad_maximum_fusion.4), channel_id=1, source_target_pairs={{0,16},{2,18},{4,20},{6,22},{8,24},{10,26},{12,28},{14,30},{16,0},... | collective-permute-start | bytes 786440 | tf_op jit(solution)/shard_map/ppermute | solution.py:315
  35.1 12.3 %collective-permute-start.6 = (bf16[4,2,128,128]{3,2,1,0:T(8,128)(2,1)S(1)}, bf16[4,2,128,128]{3,2,1,0:T(8,128)(2,1)S(1)}, u32[]{:S(2)}, u32[]{:S(2)}) collective-permute-start(bf16[4,2,128,128]{3,2,1,0:T(8,128)(2,1)S(1)} %pad_maximum_fusion.3), channel_id=1, source_target_pairs={{0,2},{2,0},{4,6},{6,4},{8,10},{10,8},{12,14},{14,12},{16,18},{18,... | collective-permute-start | bytes 786440 | tf_op jit(solution)/shard_map/ppermute | solution.py:315
  36.0 17.6 %collective-permute-start.11 = (bf16[4,2,128,128]{3,2,1,0:T(8,128)(2,1)S(1)}, bf16[4,2,128,128]{3,2,1,0:T(8,128)(2,1)S(1)}, u32[]{:S(2)}, u32[]{:S(2)}) collective-permute-start(bf16[4,2,128,128]{3,2,1,0:T(8,128)(2,1)S(1)} %pad_maximum_fusion.2), channel_id=1, source_target_pairs={{0,12},{2,14},{4,8},{6,10},{8,4},{10,6},{12,0},{14,2},{16,28},{18,... | collective-permute-start | bytes 786440 | tf_op jit(solution)/shard_map/ppermute | solution.py:315
  38.3 21.3 %collective-permute-start.10 = (bf16[4,2,128,128]{3,2,1,0:T(8,128)(2,1)S(1)}, bf16[4,2,128,128]{3,2,1,0:T(8,128)(2,1)S(1)}, u32[]{:S(2)}, u32[]{:S(2)}) collective-permute-start(bf16[4,2,128,128]{3,2,1,0:T(8,128)(2,1)S(1)} %pad_maximum_fusion.1), channel_id=1, source_target_pairs={{0,8},{2,10},{4,12},{6,14},{8,0},{10,2},{12,4},{14,6},{16,24},{18,... | collective-permute-start | bytes 786440 | tf_op jit(solution)/shard_map/ppermute | solution.py:315
  41.9 17.7 %collective-permute-start.9 = (bf16[4,2,128,128]{3,2,1,0:T(8,128)(2,1)S(1)}, bf16[4,2,128,128]{3,2,1,0:T(8,128)(2,1)S(1)}, u32[]{:S(2)}, u32[]{:S(2)}) collective-permute-start(bf16[4,2,128,128]{3,2,1,0:T(8,128)(2,1)S(1)} %pad_maximum_fusion), channel_id=1, source_target_pairs={{0,4},{2,6},{4,0},{6,2},{8,12},{10,14},{12,8},{14,10},{16,20},{18,... | collective-permute-start | bytes 786440 | tf_op jit(solution)/shard_map/ppermute | solution.py:315
  47.4 0.7 copy-start
  70.6 4.1 %collective-permute-start.12 = (bf16[4,192,128]{2,1,0:T(8,128)(2,1)S(1)}, bf16[4,192,128]{2,1,0:T(8,128)(2,1)S(1)}, u32[]{:S(2)}, u32[]{:S(2)}) collective-permute-start(bf16[4,192,128]{2,1,0:T(8,128)(2,1)S(1)} %get-tuple-element.73), channel_id=1, source_target_pairs={{0,2},{2,0},{4,6},{6,4},{8,10},{10,8},{12,14},{14,12},{16,18},{18,... | collective-permute-start | bytes 589832 | tf_op jit(solution)/shard_map/ppermute | solution.py:315
  71.8 6.4 %collective-permute-start.13 = (bf16[4,192,128]{2,1,0:T(8,128)(2,1)S(1)}, bf16[4,192,128]{2,1,0:T(8,128)(2,1)S(1)}, u32[]{:S(2)}, u32[]{:S(2)}) collective-permute-start(bf16[4,192,128]{2,1,0:T(8,128)(2,1)S(1)} %get-tuple-element.74), channel_id=1, source_target_pairs={{0,16},{2,18},{4,20},{6,22},{8,24},{10,26},{12,28},{14,30},{16,0},... | collective-permute-start | bytes 589832 | tf_op jit(solution)/shard_map/ppermute | solution.py:315
  72.9 10.1 %collective-permute-start.14 = (bf16[4,192,128]{2,1,0:T(8,128)(2,1)S(1)}, bf16[4,192,128]{2,1,0:T(8,128)(2,1)S(1)}, u32[]{:S(2)}, u32[]{:S(2)}) collective-permute-start(bf16[4,192,128]{2,1,0:T(8,128)(2,1)S(1)} %get-tuple-element.75), channel_id=1, source_target_pairs={{0,18},{2,16},{4,22},{6,20},{8,26},{10,24},{12,30},{14,28},{16,2},... | collective-permute-start | bytes 589832 | tf_op jit(solution)/shard_map/ppermute | solution.py:315
  73.6 9.5 %collective-permute-start.19 = (bf16[4,200,128]{2,1,0:T(8,128)(2,1)S(1)}, bf16[4,200,128]{2,1,0:T(8,128)(2,1)S(1)}, u32[]{:S(2)}, u32[]{:S(2)}) collective-permute-start(bf16[4,200,128]{2,1,0:T(8,128)(2,1)S(1)} %get-tuple-element.80), channel_id=1, source_target_pairs={{0,12},{2,14},{4,8},{6,10},{8,4},{10,6},{12,0},{14,2},{16,28},{18,... | collective-permute-start | bytes 614408 | tf_op jit(solution)/shard_map/ppermute | solution.py:315
  74.7 16.7 %collective-permute-start.17 = (bf16[4,200,128]{2,1,0:T(8,128)(2,1)S(1)}, bf16[4,200,128]{2,1,0:T(8,128)(2,1)S(1)}, u32[]{:S(2)}, u32[]{:S(2)}) collective-permute-start(bf16[4,200,128]{2,1,0:T(8,128)(2,1)S(1)} %get-tuple-element.78), channel_id=1, source_target_pairs={{0,8},{2,10},{4,12},{6,14},{8,0},{10,2},{12,4},{14,6},{16,24},{18,... | collective-permute-start | bytes 614408 | tf_op jit(solution)/shard_map/ppermute | solution.py:315
  74.7 16.7 %collective-permute-start.15 = (bf16[4,200,128]{2,1,0:T(8,128)(2,1)S(1)}, bf16[4,200,128]{2,1,0:T(8,128)(2,1)S(1)}, u32[]{:S(2)}, u32[]{:S(2)}) collective-permute-start(bf16[4,200,128]{2,1,0:T(8,128)(2,1)S(1)} %get-tuple-element.76), channel_id=1, source_target_pairs={{0,4},{2,6},{4,0},{6,2},{8,12},{10,14},{12,8},{14,10},{16,20},{18,... | collective-permute-start | bytes 614408 | tf_op jit(solution)/shard_map/ppermute | solution.py:315
  91.5 7.7 %collective-permute-start.23 = (bf16[4,200,128]{2,1,0:T(8,128)(2,1)S(1)}, bf16[4,200,128]{2,1,0:T(8,128)(2,1)S(1)}, u32[]{:S(2)}, u32[]{:S(2)}) collective-permute-start(bf16[4,200,128]{2,1,0:T(8,128)(2,1)S(1)} %pad_maximum_fusion.8), channel_id=1, source_target_pairs={{0,18},{2,16},{4,22},{6,20},{8,26},{10,24},{12,30},{14,28},{16,2},... | collective-permute-start | bytes 614408 | tf_op jit(solution)/shard_map/ppermute | solution.py:315
  93.4 10.3 %collective-permute-start.22 = (bf16[4,200,128]{2,1,0:T(8,128)(2,1)S(1)}, bf16[4,200,128]{2,1,0:T(8,128)(2,1)S(1)}, u32[]{:S(2)}, u32[]{:S(2)}) collective-permute-start(bf16[4,200,128]{2,1,0:T(8,128)(2,1)S(1)} %pad_maximum_fusion.7), channel_id=1, source_target_pairs={{0,16},{2,18},{4,20},{6,22},{8,24},{10,26},{12,28},{14,30},{16,0},... | collective-permute-start | bytes 614408 | tf_op jit(solution)/shard_map/ppermute | solution.py:315
  93.9 9.8 %collective-permute-start.21 = (bf16[4,200,128]{2,1,0:T(8,128)(2,1)S(1)}, bf16[4,200,128]{2,1,0:T(8,128)(2,1)S(1)}, u32[]{:S(2)}, u32[]{:S(2)}) collective-permute-start(bf16[4,200,128]{2,1,0:T(8,128)(2,1)S(1)} %pad_maximum_fusion.6), channel_id=1, source_target_pairs={{0,2},{2,0},{4,6},{6,4},{8,10},{10,8},{12,14},{14,12},{16,18},{18,... | collective-permute-start | bytes 614408 | tf_op jit(solution)/shard_map/ppermute | solution.py:315
  94.0 12.6 %collective-permute-start.20 = (bf16[4,192,128]{2,1,0:T(8,128)(2,1)S(1)}, bf16[4,192,128]{2,1,0:T(8,128)(2,1)S(1)}, u32[]{:S(2)}, u32[]{:S(2)}) collective-permute-start(bf16[4,192,128]{2,1,0:T(8,128)(2,1)S(1)} %pad_maximum_fusion.11), channel_id=1, source_target_pairs={{0,12},{2,14},{4,8},{6,10},{8,4},{10,6},{12,0},{14,2},{16,28},{18,... | collective-permute-start | bytes 589832 | tf_op jit(solution)/shard_map/ppermute | solution.py:315
  96.2 15.6 %collective-permute-start.18 = (bf16[4,192,128]{2,1,0:T(8,128)(2,1)S(1)}, bf16[4,192,128]{2,1,0:T(8,128)(2,1)S(1)}, u32[]{:S(2)}, u32[]{:S(2)}) collective-permute-start(bf16[4,192,128]{2,1,0:T(8,128)(2,1)S(1)} %pad_maximum_fusion.10), channel_id=1, source_target_pairs={{0,8},{2,10},{4,12},{6,14},{8,0},{10,2},{12,4},{14,6},{16,24},{18,... | collective-permute-start | bytes 589832 | tf_op jit(solution)/shard_map/ppermute | solution.py:315
  99.2 12.6 %collective-permute-start.16 = (bf16[4,192,128]{2,1,0:T(8,128)(2,1)S(1)}, bf16[4,192,128]{2,1,0:T(8,128)(2,1)S(1)}, u32[]{:S(2)}, u32[]{:S(2)}) collective-permute-start(bf16[4,192,128]{2,1,0:T(8,128)(2,1)S(1)} %pad_maximum_fusion.9), channel_id=1, source_target_pairs={{0,4},{2,6},{4,0},{6,2},{8,12},{10,14},{12,8},{14,10},{16,20},{18,... | collective-permute-start | bytes 589832 | tf_op jit(solution)/shard_map/ppermute | solution.py:315
  104.0 9.1 %collective-permute-start.24 = (f32[16]{0:T(128)S(1)}, f32[16]{0:T(128)S(1)}, u32[]{:S(2)}, u32[]{:S(2)}) collective-permute-start(f32[16]{0:T(128)S(1)} %select_reduce_fusion), channel_id=1, source_target_pairs={{0,1},{1,0},{2,3},{3,2},{4,5},{5,4},{6,7},{7,6},{8,9},{9,8},{10,11... | collective-permute-start | bytes 200 | tf_op jit(solution)/shard_map/ppermute | solution.py:304

commit v5 on v4

--- a/solution.py
+++ b/solution.py
@@ -41,34 +41,24 @@
     return pieces[firsts + far - 1].at[near] if far else pieces[near].at[0]
 
 
-def gathered(place, pieces, lanes_first, target, sems):
-    devices = target.shape[0]
-    return [
-        pltpu.make_async_copy(piece(pieces, lanes_first, i, j, devices), target.at[place ^ mask], sems.at[index])
-        for index, (i, j, mask) in enumerate(places_of(devices))
-    ]
-
-
-def scattered(place, source, refs, lanes_first, sems):
-    devices = source.shape[0]
-    return [
-        pltpu.make_async_copy(
-            source.at[place ^ mask], (refs[i].at[j] if lanes_first else refs[j].at[i]), sems.at[index]
-        )
-        for index, (i, j, mask) in enumerate(places_of(devices))
-    ]
-
-
-def pack_kernel(copies, lanes_first, place_ref, first_ref, second_ref, *refs):
+def position(place, other, blocks):
+    mask = place ^ other
+    return lax.rem(mask, blocks) // 2, lax.rem(mask, 2) + 2 * (mask // blocks)
+
+
+def pack_kernel(copies, lanes_first, group, place_ref, first_ref, second_ref, *refs):
     sems = refs[-1]
     width = refs[0].shape[-1]
     started = []
     for index, (i, j, mask) in enumerate(places_of(sems.shape[0])):
+        near, far = (i, j) if lanes_first else (j, i)
+        if near not in group:
+            continue
         head = (place_ref[0] ^ mask) // copies
         columns = pl.ds(pl.multiple_of(head * width, width), width)
-        target = refs[i].at[j] if lanes_first else refs[j].at[i]
         for kind, source in enumerate((first_ref, second_ref)):
-            started.append(pltpu.make_async_copy(source.at[:, columns], target.at[kind], sems.at[index, kind]))
+            target = refs[group.index(near)].at[far, kind]
+            started.append(pltpu.make_async_copy(source.at[:, columns], target, sems.at[index, kind]))
     run_all(started)
 
 
@@ -112,73 +102,79 @@
     return op(tile.reshape(tile.shape[0] // 8, 8, tile.shape[1]), axis=0)
 
 
-def pair(ref, block, *kind):
-    blocks = ref.shape[0] // 2
-    return jnp.concatenate([ref[block, *kind], ref[blocks + block, *kind]], axis=0)
+def pair(ref, place, block, kind, lanes_first):
+    blocks = 2 * ref.shape[1 if not lanes_first else 0]
+    parts = []
+    for c in range(2):
+        i, j = position(place, c * blocks + block, blocks)
+        parts.append(ref[i, j, kind] if lanes_first else ref[j, i, kind])
+    return jnp.concatenate(parts, axis=0)
 
 
 def tile_count(blocks):
     return sum(min(block, LOOKBACK) + 1 for block in range(blocks))
 
 
+def group_size(blocks):
+    early = min(LOOKBACK, blocks)
+    return 2 if early % 2 == 0 and (blocks - early) % 2 == 0 else 1
+
+
 def for_groups(length, rows, blocks, on_group, off_group=None):
     early = min(LOOKBACK, blocks)
-    group = 2 if early % 2 == 0 and (blocks - early) % 2 == 0 else 1
-    visited = ((length + group * rows - 1) // (group * rows)) * group
-    visited = jnp.minimum(visited, blocks)
-    for start in range(0, early, group):
-        @pl.when(start < visited)
-        def _():
-            on_group([(block, tile_count(block), block + 1) for block in range(start, start + group)])
-
+    group = group_size(blocks)
+    visited = jnp.minimum(((length + group * rows - 1) // (group * rows)) * group, blocks)
+
+    def either(members, higher):
+        pl.when(members[0][0] < visited)(lambda: on_group(members, higher))
         if off_group is not None:
-            pl.when(start >= visited)(lambda: off_group([start + k for k in range(group)]))
+            pl.when(members[0][0] >= visited)(lambda: off_group(members, higher))
+
+    def late(start, higher):
+        members = [(start + k, tile_count(LOOKBACK) + (start + k - LOOKBACK) * (LOOKBACK + 1)) for k in range(group)]
+        either([(block, base, LOOKBACK + 1) for block, base in members], higher)
+
+    higher = None
     if blocks > early:
-        def member(block):
-            return block, tile_count(LOOKBACK) + (block - LOOKBACK) * (LOOKBACK + 1), LOOKBACK + 1
-
-        def live(step, carried):
-            on_group([member(LOOKBACK + step * group + k) for k in range(group)])
+        late(blocks - group, None)
+
+        def step(index, carried):
+            start = blocks - (index + 1) * group
+            late(start, [start + group + k for k in range(group)])
             return carried
 
-        def dead(step, carried):
-            off_group([LOOKBACK + step * group + k for k in range(group)])
-            return carried
-
-        late = jnp.maximum(visited - LOOKBACK, 0) // group
-        lax.fori_loop(0, late, live, 0)
-        if off_group is not None:
-            lax.fori_loop(late, (blocks - early) // group, dead, 0)
-    return visited
-
-
-def stats_kernel(copies, length_ref, place_ref, bias_ref, *refs):
-    pieces, (qk_ref, kt_ref, power_ref, inverse_ref, sems) = refs[:-5], refs[-5:]
-    devices, _, rows, width = qk_ref.shape
-    blocks = devices // 2
+        lax.fori_loop(1, (blocks - early) // group, step, 0)
+        higher = [early + k for k in range(group)]
+    for start in range(early - group, -1, -group):
+        either([(block, tile_count(block), block + 1) for block in range(start, start + group)], higher)
+        higher = [start + k for k in range(group)]
+
+
+def stats_kernel(copies, length_ref, place_ref, bias_ref, qk_ref, kt_ref, power_ref, inverse_ref):
+    rows, width = qk_ref.shape[3:]
+    blocks = 2 * qk_ref.shape[1]
     both = 2 * rows
     log2_scale = LOG2_E / math.sqrt(width)
     place = place_ref[0]
     bias = bias_ref[place // copies] * LOG2_E
     part = place % copies
     length = length_ref[0]
-    run_all(gathered(place, pieces, True, qk_ref, sems))
 
     column = lax.broadcasted_iota(jnp.int32, (1, both), 1)
     own = [jnp.where((column // rows) == c, 0.0, bias) for c in range(2)]
     key_row = lax.broadcasted_iota(jnp.int32, (rows, both), 0)
     query_column = lax.broadcasted_iota(jnp.int32, (rows, both), 1) % rows
     for block in range(blocks):
-        kt_ref[block] = pair(qk_ref, block, 1).T
-
-    def on_group(members):
+        kt_ref[block] = pair(qk_ref, place, block, 1, False).T
+
+    def on_group(members, higher):
         shifts = []
         for block, base, tiles in members:
-            queries = pair(qk_ref, block, 0)
+            queries = pair(qk_ref, place, block, 0, False)
             first = block - (tiles - 1)
             peaks = [jnp.full((8, both), NEG_FILL, jnp.float32)] * 2
             for t in range(tiles):
-                raw = dot(pair(qk_ref, first + t, 1), queries, ((1,), (1,)))
+                raw = dot(pair(qk_ref, place, first + t, 1, False), queries, ((1,), (1,)))
                 for c in range(2):
                     tile = raw[c * rows : (c + 1) * rows]
                     if t == tiles - 1:
@@ -207,40 +203,44 @@
     for_groups(length, rows, blocks, on_group)
 
 
-def grads_kernel(length_ref, place_ref, qk_ref, kt_ref, power_ref, inverse_ref, *refs):
-    arrays, scratch = refs[:-9], refs[-9:]
-    gv_ref, low_a, low_b, d_ref, dk_ref, dv_ref, bias_acc, got_sems, send_sems = scratch
-    devices, _, rows, width = qk_ref.shape
-    seats, lanes = stages(devices)
-    count = len(seats) + len(lanes) - 1
-    blocks = devices // 2
+def grads_kernel(length_ref, place_ref, qk_ref, kt_ref, power_ref, inverse_ref, gv_ref, out_a, out_b, d_ref, dk_ref, dv_ref, bias_acc):
+    rows, width = gv_ref.shape[3:]
+    blocks = 2 * gv_ref.shape[0]
     both = 2 * rows
     half = rows // 2
     root_scale = 1.0 / math.sqrt(width)
     place = place_ref[0]
-    outputs = arrays[count:]
-    run_all(gathered(place, arrays[:count], False, gv_ref, got_sems))
     bias_acc[...] = jnp.zeros_like(bias_acc)
-
-    def put(kind, c, block, tile):
-        low_a[c * blocks + block, kind * half : (kind + 1) * half] = tile[:half]
-        low_b[c * blocks + block, kind * half : (kind + 1) * half] = tile[half:]
-
-    def on_group(members):
+    dk_ref[...] = jnp.zeros_like(dk_ref)
+    dv_ref[...] = jnp.zeros_like(dv_ref)
+
+    def put(kind, block, tile):
+        for c in range(2):
+            i, j = position(place, c * blocks + block, blocks)
+            out_a[i, j, kind * half : (kind + 1) * half] = tile[c * rows : c * rows + half]
+            out_b[j, i, kind * half : (kind + 1) * half] = tile[c * rows + half : (c + 1) * rows]
+
+    def key_blocks(members):
+        for block in members or ():
+            put(1, block, (dk_ref[block] * root_scale).astype(out_a.dtype))
+            put(2, block, dv_ref[block].astype(out_a.dtype))
+
+    def on_group(members, higher):
+        key_blocks(higher)
         deltas = []
         for k, (block, base, tiles) in enumerate(members):
-            grads = pair(gv_ref, block, 0)
+            grads = pair(gv_ref, place, block, 0, True)
             first = block - (tiles - 1)
             moment = jnp.zeros((8, both), jnp.float32)
             for t in range(tiles):
-                weight_grad = dot(pair(gv_ref, first + t, 1), grads, ((1,), (1,)))
+                weight_grad = dot(pair(gv_ref, place, first + t, 1, True), grads, ((1,), (1,)))
                 d_ref[k, t] = weight_grad
                 moment = moment + fold(power_ref[base + t] * weight_grad, jnp.sum)
             deltas.append(jnp.sum(moment, axis=0, keepdims=True) * inverse_ref[block, :1])
         sums = []
         for k, (block, base, tiles) in enumerate(members):
-            queries = pair(qk_ref, block, 0)
-            grads = pair(gv_ref, block, 0)
+            queries = pair(qk_ref, place, block, 0, False)
+            grads = pair(gv_ref, place, block, 0, True)
             inverse = inverse_ref[block, :1]
             first = block - (tiles - 1)
             query_sum = jnp.zeros((width, both), jnp.float32)
@@ -250,28 +250,21 @@
                 score_grad = weights * (d_ref[k, t] - deltas[k])
                 cross = cross + fold(score_grad[:rows, rows:], jnp.sum) + fold(score_grad[rows:, :rows], jnp.sum)
                 score_low = score_grad.astype(jnp.bfloat16)
-                value_term = dot(weights.astype(jnp.bfloat16), grads, ((1,), (0,)))
-                key_term = dot(score_low, queries, ((1,), (0,)))
-                if t == tiles - 1:
-                    dv_ref[block] = value_term
-                    dk_ref[block] = key_term
-                else:
-                    dv_ref[first + t] += value_term
-                    dk_ref[first + t] += key_term
+                dv_ref[first + t] += dot(weights.astype(jnp.bfloat16), grads, ((1,), (0,)))
+                dk_ref[first + t] += dot(score_low, queries, ((1,), (0,)))
                 query_sum = query_sum + dot(kt_ref[first + t], score_low, ((1,), (0,)))
             bias_acc[...] += cross
             sums.append(query_sum)
         for (block, _, _), query_sum in zip(members, sums):
-            query_grad = (query_sum * root_scale).T.astype(low_a.dtype)
-            for c in range(2):
-                put(0, c, block, query_grad[c * rows : (c + 1) * rows])
-
-    def off_group(members):
-        for block in members:
-            for c in range(2):
-                put(0, c, block, jnp.zeros((rows, width), low_a.dtype))
-
-    visited = for_groups(length_ref[0], rows, blocks, on_group, off_group)
+            put(0, block, (query_sum * root_scale).T.astype(out_a.dtype))
+
+    def off_group(members, higher):
+        key_blocks(higher)
+        for block, _, _ in members:
+            put(0, block, jnp.zeros((both, width), out_a.dtype))
+
+    for_groups(length_ref[0], rows, blocks, on_group, off_group)
+    key_blocks(range(group_size(blocks)))
 
     whole = jnp.sum(jnp.sum(bias_acc[...], axis=0, keepdims=True), axis=1, keepdims=True)
     whole = jnp.broadcast_to(whole, (1, width))
@@ -280,18 +273,10 @@
     low = (whole - high - middle).astype(jnp.bfloat16).astype(jnp.float32)
     lane = lax.broadcasted_iota(jnp.int32, (1, width), 1)
     pieces = jnp.where(lane == 0, high, jnp.where(lane == 1, middle, jnp.where(lane == 2, low, 0.0)))
-    pieces = jnp.broadcast_to(pieces, (EXTRA, width)).astype(low_a.dtype)
-    for block in range(blocks):
-        seen = block < visited
-        key_grad = jnp.where(seen, dk_ref[block] * root_scale, 0.0).astype(low_a.dtype)
-        value_grad = jnp.where(seen, dv_ref[block], 0.0).astype(low_a.dtype)
-        for c in range(2):
-            put(1, c, block, key_grad[c * rows : (c + 1) * rows])
-            put(2, c, block, value_grad[c * rows : (c + 1) * rows])
-            low_a[c * blocks + block, 3 * half : 3 * half + EXTRA] = pieces
-    leaving = scattered(place, low_a, outputs[: len(lanes)], True, send_sems.at[0])
-    leaving += scattered(place, low_b, outputs[len(lanes) :], False, send_sems.at[1])
-    run_all(leaving)
+    pieces = jnp.broadcast_to(pieces, (EXTRA, width)).astype(out_a.dtype)
+    for i in range(out_a.shape[0]):
+        for j in range(out_a.shape[1]):
+            out_a[i, j, 3 * half : 3 * half + EXTRA] = pieces
 
 
 def summed_over(value, axis):
@@ -315,16 +300,22 @@
     return lax.ppermute(value, ("chan", "seq"), [(source, source ^ mask) for source in range(devices)])
 
 
-def exchanged(by_lane, by_seat, devices):
+def exchanged(by_lane, by_seat, devices, phase):
     seats, lanes = stages(devices)
     first_a = [by_lane[0]] + [moved(by_lane[i], lanes[i]) for i in range(1, len(lanes))]
     first_b = [by_seat[0]] + [moved(by_seat[j], seats[j]) for j in range(1, len(seats))]
     last_b = []
     for i in range(1, len(lanes)):
-        waiting, first_a[i] = lax.optimization_barrier((jnp.stack([value[i] for value in first_b]), first_a[i]))
+        waiting = jnp.stack([value[i] for value in first_b])
+        if phase == "in" or i < len(lanes) - 1:
+            waiting, first_a[i] = lax.optimization_barrier((waiting, first_a[i]))
         last_b.append(moved(waiting, lanes[i]))
     last_a = [moved(jnp.stack([value[j] for value in first_a]), seats[j]) for j in range(1, len(seats))]
     return first_a + last_a, first_b + last_b
+
+
+def arranged(pieces, firsts):
+    return jnp.stack([jnp.stack([value[0] for value in pieces[:firsts]])] + list(pieces[firsts:]))
 
 
 def layer(queries, keys, values, out_grad, cross_bias, lengths):
@@ -366,10 +357,10 @@
             cost_estimate=pl.CostEstimate(flops=flops, bytes_accessed=2 << 20, transcendentals=0),
         )(*args)
 
-    def pack(lanes_first, first, second):
-        sends = by_lane(2, rows, width) if lanes_first else by_seat(2, rows, width)
+    def pack(lanes_first, group, first, second):
+        sends = (by_lane(2, rows, width) if lanes_first else by_seat(2, rows, width))[: len(group)]
         return call(
-            functools.partial(pack_kernel, copies, lanes_first),
+            functools.partial(pack_kernel, copies, lanes_first, group),
             sends,
             [smem, hbm, hbm],
             [vmem] * len(sends),
@@ -379,47 +370,48 @@
             (places, in_hbm(first[0, 0]), in_hbm(second[0, 0])),
         )
 
-    sent_a = pack(True, queries, keys)
-    values, out_grad, sent_a = lax.optimization_barrier((values, out_grad, sent_a))
-    sent_b = pack(False, out_grad, values)
-    arrived_a, arrived_b = exchanged(sent_a, sent_b, devices)
+    middle = len(lanes) // 2
+    far_a = pack(True, list(range(middle, len(lanes))), queries, keys)
+    values, out_grad, far_a = lax.optimization_barrier((values, out_grad, far_a))
+    sent_b = pack(False, list(range(len(seats))), out_grad, values)
+    queries, keys, sent_b = lax.optimization_barrier((queries, keys, sent_b))
+    sent_a = pack(True, list(range(middle)), queries, keys) + far_a
+    arrived_a, arrived_b = exchanged(sent_a, sent_b, devices, "in")
+    qk, gv = arranged(arrived_a, len(lanes)), arranged(arrived_b, len(seats))
 
     half = rows // 2
-    group = 2
-    two_shape = jax.ShapeDtypeStruct((devices, 2, rows, width), kind)
+    group = group_size(blocks)
     turned_shape = jax.ShapeDtypeStruct((blocks, width, both), kind)
     power_shape = jax.ShapeDtypeStruct((tile_count(blocks), both, both), jnp.float32)
     inverse_shape = jax.ShapeDtypeStruct((blocks, 8, both), jnp.float32)
     sums_shape = jax.ShapeDtypeStruct((blocks, both, width), jnp.float32)
-    low_a, low_b = (
-        jax.ShapeDtypeStruct((devices, pay, width), kind) for pay in (3 * half + EXTRA, 3 * half)
-    )
     d_shape = jax.ShapeDtypeStruct((group, tiles, both, both), jnp.float32)
-    dma = pltpu.SemaphoreType.DMA((devices,))
     made = call(
         functools.partial(stats_kernel, copies),
-        (two_shape, turned_shape, power_shape, inverse_shape),
-        [smem, smem, smem] + [anywhere] * len(arrived_a),
-        [vmem] * 4,
-        [dma],
-        size(two_shape, turned_shape, power_shape, inverse_shape),
+        (turned_shape, power_shape, inverse_shape),
+        [smem, smem, smem, vmem],
+        [vmem] * 3,
+        [],
+        size(qk, turned_shape, power_shape, inverse_shape),
         1,
-        (lengths, places, cross_bias, *arrived_a),
+        (lengths, places, cross_bias, qk),
     )
-    sends = by_lane(*low_a.shape[1:]) + by_seat(*low_b.shape[1:])
-    held = (two_shape, low_a, low_b, d_shape, sums_shape, sums_shape)
-    back = call(
+    sends = (
+        jax.ShapeDtypeStruct((len(lanes), len(seats), 3 * half + EXTRA, width), kind),
+        jax.ShapeDtypeStruct((len(seats), len(lanes), 3 * half, width), kind),
+    )
+    held = (d_shape, sums_shape, sums_shape)
+    back_a, back_b = call(
         grads_kernel,
         sends,
-        [smem, smem] + [vmem] * 4 + [anywhere] * len(arrived_b),
-        [anywhere] * len(sends),
-        [pltpu.VMEM(shape.shape, shape.dtype) for shape in held]
-        + [pltpu.VMEM((8, rows), jnp.float32), dma, pltpu.SemaphoreType.DMA((2, devices))],
-        size(*held, two_shape, turned_shape, power_shape, inverse_shape),
+        [smem, smem] + [vmem] * 5,
+        [vmem] * 2,
+        [pltpu.VMEM(shape.shape, shape.dtype) for shape in held] + [pltpu.VMEM((8, rows), jnp.float32)],
+        size(*held, *sends, qk, gv, turned_shape, power_shape, inverse_shape),
         4,
-        (lengths, places, *made, *arrived_b),
+        (lengths, places, qk, *made, gv),
     )
-    arrived_a, arrived_b = exchanged(back[: len(lanes)], back[len(lanes) :], devices)
+    arrived_a, arrived_b = exchanged(list(back_a), list(back_b), devices, "out")
 
     pieces = [
         (arrived_a[i][0] if j == 0 else arrived_a[len(lanes) + j - 1][i])[3 * half] for i, j, _ in places_of(devices)
@@ -447,7 +439,9 @@
             name="unpack_b" if part else "unpack_a",
         )(places, *arrived, *earlier)
 
-    grads = unpack(1, arrived_b, unpack(0, arrived_a, ()))
+    earlier = unpack(0, arrived_a, ())
+    bias_out, *earlier = lax.optimization_barrier((bias_out, *earlier))
+    grads = unpack(1, arrived_b, earlier)
     return tuple(grad[None, None] for grad in grads) + (bias_out,)
 
 

time: 115 us -> 116 us (level)
  starting transfers between devices: 24.5 us -> 49.1 us
  waiting for transfers between devices: 62.7 us -> 45.2 us
  Pallas kernels: 22.1 us -> 17.2 us
    ppermute x24, starting transfers between devices: 23.2 us -> 47.8 us  [moved(): lax.ppermute(value, ('chan', 'seq'), [(source, source ^ mask) for source...]
    ppermute x24, waiting for transfers between devices: 62.7 us -> 44.9 us  [moved(): lax.ppermute(value, ('chan', 'seq'), [(source, source ^ mask) for source...]
    pallas_call x4 -> x5, Pallas kernels: 19.5 us -> 14.7 us  [call(): pl.pallas_call(kernel, out_shape=out_shape, in_specs=in_specs, out_specs=...]
  transfers between devices with their start and end apart: 25 -> 25, of which waited for: 12 -> 13; matrix products, arithmetic and copies ran while one was open for 1% -> 1% of each run, Pallas kernels for 7% -> 6%
where the time goes in v5:
time: 116 us; the launch traced here: 115 us
  starting transfers between devices  49.1 us (42%)
  waiting for transfers between devices  45.2 us (39%)
  Pallas kernels  17.2 us (15%)
  between operations  1.65 us (1%)
  other arithmetic  1.47 us (1%)
    ppermute x24, starting transfers between devices, moved(): lax.ppermute(value, ('chan', 'seq'), [(source, source ^ mask) for source...  47.8 us
    ppermute x24, waiting for transfers between devices, moved(): lax.ppermute(value, ('chan', 'seq'), [(source, source ^ mask) for source...  44.9 us
    pallas_call x5, Pallas kernels, call(): pl.pallas_call(kernel, out_shape=out_shape, in_specs=in_specs, out_specs=...  14.7 us
    pallas_call x2, Pallas kernels, unpack(): pl.pallas_call(functools.partial(unpack_kernel, copies, part), out_shape=...  2.56 us
  transfers between devices with their start and end apart: 25, of which 13 were waited for; matrix products, arithmetic and copies ran while one was open for 1% of the time, Pallas kernels for 6%

profile of v5, /device:TPU:1, one launch (start us, length us, event | category | flops | bytes accessed | tf_op | source)
XLA Modules:
  0.0 115.0 jit_solution(8841428168780684157)
XLA Ops:
  0.7 1.3 %shard_map.102 = (bf16[4,2,128,128]{3,2,1,0:T(8,128)(2,1)S(1)}, bf16[4,2,128,128]{3,2,1,0:T(8,128)(2,1)S(1)}) custom-call(s32[1]{0:T(128)} %bitcast.place_ref, bf16[128,2048]{1,0:T(8,128)(2,1)} %bitcast.80, bf16[128,2048]{1,0:T(8,128)(2,1)} %bitcast.82), custom_call_target="tpu_custom_call" | custom-call | bytes 2097152 | tf_op jit(solution)/shard_map/pallas_call | solution.py:350
  2.0 1.5 %shard_map.103 = (bf16[4,2,128,128]{3,2,1,0:T(8,128)(2,1)S(1)}, bf16[4,2,128,128]{3,2,1,0:T(8,128)(2,1)S(1)}, bf16[4,2,128,128]{3,2,1,0:T(8,128)(2,1)S(1)}, bf16[4,2,128,128]{3,2,1,0:T(8,128)(2,1)S(1)}) custom-call(s32[1]{0:T(128)} %bitcast.place_ref, bf16[128,2048]{1,0:T(8,128)(2,1)} %bitcast.87, bf16[128,2048]{1,0:T(8,128)(2,1)} %bitcast.88), custom_call_target="tpu_custom_call" | custom-call | bytes 2097152 | tf_op jit(solution)/shard_map/pallas_call | solution.py:350
  3.5 2.7 %collective-permute-start.1 = (bf16[4,2,128,128]{3,2,1,0:T(8,128)(2,1)S(1)}, bf16[4,2,128,128]{3,2,1,0:T(8,128)(2,1)S(1)}, u32[]{:S(2)}, u32[]{:S(2)}) collective-permute-start(bf16[4,2,128,128]{3,2,1,0:T(8,128)(2,1)S(1)} %get-tuple-element.60), channel_id=1, source_target_pairs={{0,16},{2,18},{4,20},{6,22},{8,24},{10,26},{12,28},{14,30},{16,0},... | collective-permute-start | bytes 786440 | tf_op jit(solution)/shard_map/ppermute | solution.py:300
  6.3 1.3 %shard_map.104 = (bf16[4,2,128,128]{3,2,1,0:T(8,128)(2,1)S(1)}, bf16[4,2,128,128]{3,2,1,0:T(8,128)(2,1)S(1)}) custom-call(s32[1]{0:T(128)} %bitcast.place_ref, bf16[128,2048]{1,0:T(8,128)(2,1)} %bitcast.81, bf16[128,2048]{1,0:T(8,128)(2,1)} %bitcast.83), custom_call_target="tpu_custom_call" | custom-call | bytes 2097152 | tf_op jit(solution)/shard_map/pallas_call | solution.py:350
  7.6 1.8 %collective-permute-start.3 = (bf16[4,2,128,128]{3,2,1,0:T(8,128)(2,1)S(1)}, bf16[4,2,128,128]{3,2,1,0:T(8,128)(2,1)S(1)}, u32[]{:S(2)}, u32[]{:S(2)}) collective-permute-start(bf16[4,2,128,128]{3,2,1,0:T(8,128)(2,1)S(1)} %get-tuple-element.62), channel_id=1, source_target_pairs={{0,4},{2,6},{4,0},{6,2},{8,12},{10,14},{12,8},{14,10},{16,20},{18,... | collective-permute-start | bytes 786440 | tf_op jit(solution)/shard_map/ppermute | solution.py:300
  9.4 2.3 %collective-permute-start.4 = (bf16[4,2,128,128]{3,2,1,0:T(8,128)(2,1)S(1)}, bf16[4,2,128,128]{3,2,1,0:T(8,128)(2,1)S(1)}, u32[]{:S(2)}, u32[]{:S(2)}) collective-permute-start(bf16[4,2,128,128]{3,2,1,0:T(8,128)(2,1)S(1)} %get-tuple-element.64), channel_id=1, source_target_pairs={{0,8},{2,10},{4,12},{6,14},{8,0},{10,2},{12,4},{14,6},{16,24},{18,... | collective-permute-start | bytes 786440 | tf_op jit(solution)/shard_map/ppermute | solution.py:300
  12.9 5.9 %collective-permute-done.2 = bf16[4,2,128,128]{3,2,1,0:T(8,128)(2,1)S(1)} collective-permute-done((bf16[4,2,128,128]{3,2,1,0:T(8,128)(2,1)S(1)}, bf16[4,2,128,128]{3,2,1,0:T(8,128)(2,1)S(1)}, u32[]{:S(2)}, u32[]{:S(2)}) %collective-permute-start.2) | collective-permute-done | bytes 262176 | tf_op jit(solution)/shard_map/ppermute | solution.py:300
  18.8 2.0 %collective-permute-done.3 = bf16[4,2,128,128]{3,2,1,0:T(8,128)(2,1)S(1)} collective-permute-done((bf16[4,2,128,128]{3,2,1,0:T(8,128)(2,1)S(1)}, bf16[4,2,128,128]{3,2,1,0:T(8,128)(2,1)S(1)}, u32[]{:S(2)}, u32[]{:S(2)}) %collective-permute-start.3) | collective-permute-done | bytes 262176 | tf_op jit(solution)/shard_map/ppermute | solution.py:300
  20.9 8.2 %collective-permute-done.5 = bf16[4,2,128,128]{3,2,1,0:T(8,128)(2,1)S(1)} collective-permute-done((bf16[4,2,128,128]{3,2,1,0:T(8,128)(2,1)S(1)}, bf16[4,2,128,128]{3,2,1,0:T(8,128)(2,1)S(1)}, u32[]{:S(2)}, u32[]{:S(2)}) %collective-permute-start.5) | collective-permute-done | bytes 262176 | tf_op jit(solution)/shard_map/ppermute | solution.py:300
  29.2 2.2 %collective-permute-start.6 = (bf16[4,2,128,128]{3,2,1,0:T(8,128)(2,1)S(1)}, bf16[4,2,128,128]{3,2,1,0:T(8,128)(2,1)S(1)}, u32[]{:S(2)}, u32[]{:S(2)}) collective-permute-start(bf16[4,2,128,128]{3,2,1,0:T(8,128)(2,1)S(1)} %pad_maximum_fusion.5), channel_id=1, source_target_pairs={{0,2},{2,0},{4,6},{6,4},{8,10},{10,8},{12,14},{14,12},{16,18},{18,... | collective-permute-start | bytes 786440 | tf_op jit(solution)/shard_map/ppermute | solution.py:300
  31.5 1.3 %collective-permute-start.7 = (bf16[4,2,128,128]{3,2,1,0:T(8,128)(2,1)S(1)}, bf16[4,2,128,128]{3,2,1,0:T(8,128)(2,1)S(1)}, u32[]{:S(2)}, u32[]{:S(2)}) collective-permute-start(bf16[4,2,128,128]{3,2,1,0:T(8,128)(2,1)S(1)} %pad_maximum_fusion.6), channel_id=1, source_target_pairs={{0,16},{2,18},{4,20},{6,22},{8,24},{10,26},{12,28},{14,30},{16,0},... | collective-permute-start | bytes 786440 | tf_op jit(solution)/shard_map/ppermute | solution.py:300
  33.9 5.0 %collective-permute-start.9 = (bf16[4,2,128,128]{3,2,1,0:T(8,128)(2,1)S(1)}, bf16[4,2,128,128]{3,2,1,0:T(8,128)(2,1)S(1)}, u32[]{:S(2)}, u32[]{:S(2)}) collective-permute-start(bf16[4,2,128,128]{3,2,1,0:T(8,128)(2,1)S(1)} %pad_maximum_fusion.2), channel_id=1, source_target_pairs={{0,4},{2,6},{4,0},{6,2},{8,12},{10,14},{12,8},{14,10},{16,20},{18,... | collective-permute-start | bytes 786440 | tf_op jit(solution)/shard_map/ppermute | solution.py:300
  40.1 1.2 %collective-permute-start.11 = (bf16[4,2,128,128]{3,2,1,0:T(8,128)(2,1)S(1)}, bf16[4,2,128,128]{3,2,1,0:T(8,128)(2,1)S(1)}, u32[]{:S(2)}, u32[]{:S(2)}) collective-permute-start(bf16[4,2,128,128]{3,2,1,0:T(8,128)(2,1)S(1)} %pad_maximum_fusion.4), channel_id=1, source_target_pairs={{0,12},{2,14},{4,8},{6,10},{8,4},{10,6},{12,0},{14,2},{16,28},{18,... | collective-permute-start | bytes 786440 | tf_op jit(solution)/shard_map/ppermute | solution.py:300
  41.3 4.1 %collective-permute-done.8 = bf16[4,2,128,128]{3,2,1,0:T(8,128)(2,1)S(1)} collective-permute-done((bf16[4,2,128,128]{3,2,1,0:T(8,128)(2,1)S(1)}, bf16[4,2,128,128]{3,2,1,0:T(8,128)(2,1)S(1)}, u32[]{:S(2)}, u32[]{:S(2)}) %collective-permute-start.8) | collective-permute-done | bytes 262176 | tf_op jit(solution)/shard_map/ppermute | solution.py:300
  45.6 4.1 %shard_map.105 = (bf16[8,128,256]{2,1,0:T(8,128)(2,1)S(1)}, f32[35,256,256]{2,1,0:T(8,128)S(1)}, f32[8,8,256]{2,1,0:T(8,128)S(1)}) custom-call(s32[1]{0:T(128)S(6)} %copy.17.length_ref, s32[1]{0:T(128)} %bitcast.place_ref, f32[16]{0:T(128)S(1)} %copy-done, bf16[4,4,2,128,128]{4,3,2,1,0:T(8,128)(2,1)S(1)} %pad_maximum_fusion.qk_ref), custom_call_target="tpu_custom_call" | custom-call | flops 587202560 | bytes 2097152 | tf_op jit(solution)/shard_map/pallas_call | solution.py:350
  50.5 8.1 %collective-permute-done.11 = bf16[4,2,128,128]{3,2,1,0:T(8,128)(2,1)S(1)} collective-permute-done((bf16[4,2,128,128]{3,2,1,0:T(8,128)(2,1)S(1)}, bf16[4,2,128,128]{3,2,1,0:T(8,128)(2,1)S(1)}, u32[]{:S(2)}, u32[]{:S(2)}) %collective-permute-start.11) | collective-permute-done | bytes 262176 | tf_op jit(solution)/shard_map/ppermute | solution.py:300
  58.8 6.5 %shard_map.106 = (bf16[4,4,200,128]{3,2,1,0:T(8,128)(2,1)S(1)}, bf16[4,4,192,128]{3,2,1,0:T(8,128)(2,1)S(1)}) custom-call(s32[1]{0:T(128)S(6)} %copy.17.length_ref, s32[1]{0:T(128)} %bitcast.place_ref, bf16[4,4,2,128,128]{4,3,2,1,0:T(8,128)(2,1)S(1)} %pad_maximum_fusion.qk_ref, bf16[8,128,256]{2,1,0:T(8,128)(2,1)S(1)} %get-tuple-element.68.kt_ref, ...), custom_call_target="tpu_custom_call" | custom-call | flops 2348810240 | bytes 2097152 | tf_op jit(solution)/shard_map/pallas_call | solution.py:350
  65.4 2.3 %collective-permute-start.12 = (bf16[4,192,128]{2,1,0:T(8,128)(2,1)S(1)}, bf16[4,192,128]{2,1,0:T(8,128)(2,1)S(1)}, u32[]{:S(2)}, u32[]{:S(2)}) collective-permute-start(bf16[4,192,128]{2,1,0:T(8,128)(2,1)S(1)} %get-tuple-element.102), channel_id=1, source_target_pairs={{0,2},{2,0},{4,6},{6,4},{8,10},{10,8},{12,14},{14,12},{16,18},{18,... | collective-permute-start | bytes 589832 | tf_op jit(solution)/shard_map/ppermute | solution.py:300
  67.7 1.2 %collective-permute-start.13 = (bf16[4,192,128]{2,1,0:T(8,128)(2,1)S(1)}, bf16[4,192,128]{2,1,0:T(8,128)(2,1)S(1)}, u32[]{:S(2)}, u32[]{:S(2)}) collective-permute-start(bf16[4,192,128]{2,1,0:T(8,128)(2,1)S(1)} %get-tuple-element.101), channel_id=1, source_target_pairs={{0,16},{2,18},{4,20},{6,22},{8,24},{10,26},{12,28},{14,30},{16,0},... | collective-permute-start | bytes 589832 | tf_op jit(solution)/shard_map/ppermute | solution.py:300
  69.4 6.0 %collective-permute-start.17 = (bf16[4,200,128]{2,1,0:T(8,128)(2,1)S(1)}, bf16[4,200,128]{2,1,0:T(8,128)(2,1)S(1)}, u32[]{:S(2)}, u32[]{:S(2)}) collective-permute-start(bf16[4,200,128]{2,1,0:T(8,128)(2,1)S(1)} %get-tuple-element.92), channel_id=1, source_target_pairs={{0,8},{2,10},{4,12},{6,14},{8,0},{10,2},{12,4},{14,6},{16,24},{18,... | collective-permute-start | bytes 614408 | tf_op jit(solution)/shard_map/ppermute | solution.py:300
  75.4 1.2 %collective-permute-start.20 = (bf16[4,200,128]{2,1,0:T(8,128)(2,1)S(1)}, bf16[4,200,128]{2,1,0:T(8,128)(2,1)S(1)}, u32[]{:S(2)}, u32[]{:S(2)}) collective-permute-start(bf16[4,200,128]{2,1,0:T(8,128)(2,1)S(1)} %get-tuple-element.91), channel_id=1, source_target_pairs={{0,12},{2,14},{4,8},{6,10},{8,4},{10,6},{12,0},{14,2},{16,28},{18,... | collective-permute-start | bytes 614408 | tf_op jit(solution)/shard_map/ppermute | solution.py:300
  76.6 2.2 %collective-permute-done.14.refs_3_ = bf16[4,192,128]{2,1,0:T(8,128)(2,1)S(1)} collective-permute-done((bf16[4,192,128]{2,1,0:T(8,128)(2,1)S(1)}, bf16[4,192,128]{2,1,0:T(8,128)(2,1)S(1)}, u32[]{:S(2)}, u32[]{:S(2)}) %collective-permute-start.14) | collective-permute-done | bytes 196640 | tf_op jit(solution)/shard_map/ppermute | solution.py:300
  78.9 2.2 %collective-permute-start.19 = (bf16[4,192,128]{2,1,0:T(8,128)(2,1)S(1)}, bf16[4,192,128]{2,1,0:T(8,128)(2,1)S(1)}, u32[]{:S(2)}, u32[]{:S(2)}) collective-permute-start(bf16[4,192,128]{2,1,0:T(8,128)(2,1)S(1)} %pad_maximum_fusion.13), channel_id=1, source_target_pairs={{0,12},{2,14},{4,8},{6,10},{8,4},{10,6},{12,0},{14,2},{16,28},{18,... | collective-permute-start | bytes 589832 | tf_op jit(solution)/shard_map/ppermute | solution.py:300
  81.2 3.9 %collective-permute-done.17.refs_2_ = bf16[4,200,128]{2,1,0:T(8,128)(2,1)S(1)} collective-permute-done((bf16[4,200,128]{2,1,0:T(8,128)(2,1)S(1)}, bf16[4,200,128]{2,1,0:T(8,128)(2,1)S(1)}, u32[]{:S(2)}, u32[]{:S(2)}) %collective-permute-start.17) | collective-permute-done | bytes 204832 | tf_op jit(solution)/shard_map/ppermute | solution.py:300
  85.1 5.1 %collective-permute-done.20.refs_3_ = bf16[4,200,128]{2,1,0:T(8,128)(2,1)S(1)} collective-permute-done((bf16[4,200,128]{2,1,0:T(8,128)(2,1)S(1)}, bf16[4,200,128]{2,1,0:T(8,128)(2,1)S(1)}, u32[]{:S(2)}, u32[]{:S(2)}) %collective-permute-start.20) | collective-permute-done | bytes 204832 | tf_op jit(solution)/shard_map/ppermute | solution.py:300
  90.3 2.9 %collective-permute-start.23 = (bf16[4,200,128]{2,1,0:T(8,128)(2,1)S(1)}, bf16[4,200,128]{2,1,0:T(8,128)(2,1)S(1)}, u32[]{:S(2)}, u32[]{:S(2)}) collective-permute-start(bf16[4,200,128]{2,1,0:T(8,128)(2,1)S(1)} %pad_maximum_fusion.10), channel_id=1, source_target_pairs={{0,18},{2,16},{4,22},{6,20},{8,26},{10,24},{12,30},{14,28},{16,2},... | collective-permute-start | bytes 614408 | tf_op jit(solution)/shard_map/ppermute | solution.py:300
  93.8 7.3 %collective-permute-start.18 = (bf16[4,192,128]{2,1,0:T(8,128)(2,1)S(1)}, bf16[4,192,128]{2,1,0:T(8,128)(2,1)S(1)}, u32[]{:S(2)}, u32[]{:S(2)}) collective-permute-start(bf16[4,192,128]{2,1,0:T(8,128)(2,1)S(1)} %pad_maximum_fusion.12), channel_id=1, source_target_pairs={{0,8},{2,10},{4,12},{6,14},{8,0},{10,2},{12,4},{14,6},{16,24},{18,... | collective-permute-start | bytes 589832 | tf_op jit(solution)/shard_map/ppermute | solution.py:300
  101.1 5.5 %collective-permute-start.16 = (bf16[4,192,128]{2,1,0:T(8,128)(2,1)S(1)}, bf16[4,192,128]{2,1,0:T(8,128)(2,1)S(1)}, u32[]{:S(2)}, u32[]{:S(2)}) collective-permute-start(bf16[4,192,128]{2,1,0:T(8,128)(2,1)S(1)} %pad_maximum_fusion.11), channel_id=1, source_target_pairs={{0,4},{2,6},{4,0},{6,2},{8,12},{10,14},{12,8},{14,10},{16,20},{18,... | collective-permute-start | bytes 589832 | tf_op jit(solution)/shard_map/ppermute | solution.py:300
  106.9 1.3 %collective-permute-start.24 = (f32[16]{0:T(128)S(1)}, f32[16]{0:T(128)S(1)}, u32[]{:S(2)}, u32[]{:S(2)}) collective-permute-start(f32[16]{0:T(128)S(1)} %select_reduce_fusion), channel_id=1, source_target_pairs={{0,1},{1,0},{2,3},{3,2},{4,5},{5,4},{6,7},{7,6},{8,9},{9,8},{10,11... | collective-permute-start | bytes 200 | tf_op jit(solution)/shard_map/ppermute | solution.py:289
  108.2 1.3 %unpack_a.1 = (bf16[128,2048]{1,0:T(8,128)(2,1)}, bf16[128,2048]{1,0:T(8,128)(2,1)}, bf16[128,2048]{1,0:T(8,128)(2,1)}) custom-call(s32[1]{0:T(128)} %bitcast.place_ref, bf16[4,200,128]{2,1,0:T(8,128)(2,1)S(1)} %get-tuple-element.90.refs_0_, bf16[4,200,128]{2,1,0:T(8,128)(2,1)S(1)} %collective-permute-done.15.refs_1_, ...), custom_call_target="tpu_custom_call" | custom-call | tf_op jit(solution)/shard_map/unpack_a/pallas_call | solution.py:427
  110.8 2.9 %collective-permute-done.16.refs_4_ = bf16[4,192,128]{2,1,0:T(8,128)(2,1)S(1)} collective-permute-done((bf16[4,192,128]{2,1,0:T(8,128)(2,1)S(1)}, bf16[4,192,128]{2,1,0:T(8,128)(2,1)S(1)}, u32[]{:S(2)}, u32[]{:S(2)}) %collective-permute-start.16) | collective-permute-done | bytes 196640 | tf_op jit(solution)/shard_map/ppermute | solution.py:300
  113.8 1.3 %unpack_b.1 = (bf16[128,2048]{1,0:T(8,128)(2,1)}, bf16[128,2048]{1,0:T(8,128)(2,1)}, bf16[128,2048]{1,0:T(8,128)(2,1)}) custom-call(s32[1]{0:T(128)} %bitcast.place_ref, bf16[4,192,128]{2,1,0:T(8,128)(2,1)S(1)} %get-tuple-element.103.refs_0_, ...), custom_call_target="tpu_custom_call", output_to_operand_aliasing={{0}: (8, {}), {1}: (9, {}), {2}: (10, {})} | custom-call | tf_op jit(solution)/shard_map/unpack_b/pallas_call | solution.py:427
  (75 shorter events, 7.4 us)
Async XLA Ops:
  0.6 32.7 %copy-start.1 = (s32[16]{0:T(128)S(1)}, s32[16]{0:T(128)}, u32[]{:S(2)}) copy-start(s32[16]{0:T(128)} %constant.27.clone) | copy-start | bytes 196
  0.6 45.0 %copy-start = (f32[16]{0:T(128)S(1)}, f32[16]{0:T(128)}, u32[]{:S(2)}) copy-start(f32[16]{0:T(128)} %bias_ref.1) | copy-start | bytes 196
  3.5 8.3 %collective-permute-start = (bf16[4,2,128,128]{3,2,1,0:T(8,128)(2,1)S(1)}, bf16[4,2,128,128]{3,2,1,0:T(8,128)(2,1)S(1)}, u32[]{:S(2)}, u32[]{:S(2)}) collective-permute-start(bf16[4,2,128,128]{3,2,1,0:T(8,128)(2,1)S(1)} %get-tuple-element.59), channel_id=1, source_target_pairs={{0,2},{2,0},{4,6},{6,4},{8,10},{10,8},{12,14},{14,12},{16,18},{18,... | collective-permute-start | bytes 786440 | tf_op jit(solution)/shard_map/ppermute | solution.py:300
  3.5 9.3 %collective-permute-start.1 = (bf16[4,2,128,128]{3,2,1,0:T(8,128)(2,1)S(1)}, bf16[4,2,128,128]{3,2,1,0:T(8,128)(2,1)S(1)}, u32[]{:S(2)}, u32[]{:S(2)}) collective-permute-start(bf16[4,2,128,128]{3,2,1,0:T(8,128)(2,1)S(1)} %get-tuple-element.60), channel_id=1, source_target_pairs={{0,16},{2,18},{4,20},{6,22},{8,24},{10,26},{12,28},{14,30},{16,0},... | collective-permute-start | bytes 786440 | tf_op jit(solution)/shard_map/ppermute | solution.py:300
  6.3 12.5 %collective-permute-start.2 = (bf16[4,2,128,128]{3,2,1,0:T(8,128)(2,1)S(1)}, bf16[4,2,128,128]{3,2,1,0:T(8,128)(2,1)S(1)}, u32[]{:S(2)}, u32[]{:S(2)}) collective-permute-start(bf16[4,2,128,128]{3,2,1,0:T(8,128)(2,1)S(1)} %get-tuple-element.61), channel_id=1, source_target_pairs={{0,18},{2,16},{4,22},{6,20},{8,26},{10,24},{12,30},{14,28},{16,2},... | collective-permute-start | bytes 786440 | tf_op jit(solution)/shard_map/ppermute | solution.py:300
  7.6 13.2 %collective-permute-start.3 = (bf16[4,2,128,128]{3,2,1,0:T(8,128)(2,1)S(1)}, bf16[4,2,128,128]{3,2,1,0:T(8,128)(2,1)S(1)}, u32[]{:S(2)}, u32[]{:S(2)}) collective-permute-start(bf16[4,2,128,128]{3,2,1,0:T(8,128)(2,1)S(1)} %get-tuple-element.62), channel_id=1, source_target_pairs={{0,4},{2,6},{4,0},{6,2},{8,12},{10,14},{12,8},{14,10},{16,20},{18,... | collective-permute-start | bytes 786440 | tf_op jit(solution)/shard_map/ppermute | solution.py:300
  9.4 11.5 %collective-permute-start.4 = (bf16[4,2,128,128]{3,2,1,0:T(8,128)(2,1)S(1)}, bf16[4,2,128,128]{3,2,1,0:T(8,128)(2,1)S(1)}, u32[]{:S(2)}, u32[]{:S(2)}) collective-permute-start(bf16[4,2,128,128]{3,2,1,0:T(8,128)(2,1)S(1)} %get-tuple-element.64), channel_id=1, source_target_pairs={{0,8},{2,10},{4,12},{6,14},{8,0},{10,2},{12,4},{14,6},{16,24},{18,... | collective-permute-start | bytes 786440 | tf_op jit(solution)/shard_map/ppermute | solution.py:300
  11.8 17.4 %collective-permute-start.5 = (bf16[4,2,128,128]{3,2,1,0:T(8,128)(2,1)S(1)}, bf16[4,2,128,128]{3,2,1,0:T(8,128)(2,1)S(1)}, u32[]{:S(2)}, u32[]{:S(2)}) collective-permute-start(bf16[4,2,128,128]{3,2,1,0:T(8,128)(2,1)S(1)} %get-tuple-element.66), channel_id=1, source_target_pairs={{0,12},{2,14},{4,8},{6,10},{8,4},{10,6},{12,0},{14,2},{16,28},{18,... | collective-permute-start | bytes 786440 | tf_op jit(solution)/shard_map/ppermute | solution.py:300
  29.2 10.9 %collective-permute-start.6 = (bf16[4,2,128,128]{3,2,1,0:T(8,128)(2,1)S(1)}, bf16[4,2,128,128]{3,2,1,0:T(8,128)(2,1)S(1)}, u32[]{:S(2)}, u32[]{:S(2)}) collective-permute-start(bf16[4,2,128,128]{3,2,1,0:T(8,128)(2,1)S(1)} %pad_maximum_fusion.5), channel_id=1, source_target_pairs={{0,2},{2,0},{4,6},{6,4},{8,10},{10,8},{12,14},{14,12},{16,18},{18,... | collective-permute-start | bytes 786440 | tf_op jit(solution)/shard_map/ppermute | solution.py:300
  31.5 9.9 %collective-permute-start.7 = (bf16[4,2,128,128]{3,2,1,0:T(8,128)(2,1)S(1)}, bf16[4,2,128,128]{3,2,1,0:T(8,128)(2,1)S(1)}, u32[]{:S(2)}, u32[]{:S(2)}) collective-permute-start(bf16[4,2,128,128]{3,2,1,0:T(8,128)(2,1)S(1)} %pad_maximum_fusion.6), channel_id=1, source_target_pairs={{0,16},{2,18},{4,20},{6,22},{8,24},{10,26},{12,28},{14,30},{16,0},... | collective-permute-start | bytes 786440 | tf_op jit(solution)/shard_map/ppermute | solution.py:300
  32.8 12.7 %collective-permute-start.8 = (bf16[4,2,128,128]{3,2,1,0:T(8,128)(2,1)S(1)}, bf16[4,2,128,128]{3,2,1,0:T(8,128)(2,1)S(1)}, u32[]{:S(2)}, u32[]{:S(2)}) collective-permute-start(bf16[4,2,128,128]{3,2,1,0:T(8,128)(2,1)S(1)} %pad_maximum_fusion.7), channel_id=1, source_target_pairs={{0,18},{2,16},{4,22},{6,20},{8,26},{10,24},{12,30},{14,28},{16,2},... | collective-permute-start | bytes 786440 | tf_op jit(solution)/shard_map/ppermute | solution.py:300
  33.9 16.6 %collective-permute-start.9 = (bf16[4,2,128,128]{3,2,1,0:T(8,128)(2,1)S(1)}, bf16[4,2,128,128]{3,2,1,0:T(8,128)(2,1)S(1)}, u32[]{:S(2)}, u32[]{:S(2)}) collective-permute-start(bf16[4,2,128,128]{3,2,1,0:T(8,128)(2,1)S(1)} %pad_maximum_fusion.2), channel_id=1, source_target_pairs={{0,4},{2,6},{4,0},{6,2},{8,12},{10,14},{12,8},{14,10},{16,20},{18,... | collective-permute-start | bytes 786440 | tf_op jit(solution)/shard_map/ppermute | solution.py:300
  39.0 11.6 %collective-permute-start.10 = (bf16[4,2,128,128]{3,2,1,0:T(8,128)(2,1)S(1)}, bf16[4,2,128,128]{3,2,1,0:T(8,128)(2,1)S(1)}, u32[]{:S(2)}, u32[]{:S(2)}) collective-permute-start(bf16[4,2,128,128]{3,2,1,0:T(8,128)(2,1)S(1)} %pad_maximum_fusion.3), channel_id=1, source_target_pairs={{0,8},{2,10},{4,12},{6,14},{8,0},{10,2},{12,4},{14,6},{16,24},{18,... | collective-permute-start | bytes 786440 | tf_op jit(solution)/shard_map/ppermute | solution.py:300
  40.1 18.5 %collective-permute-start.11 = (bf16[4,2,128,128]{3,2,1,0:T(8,128)(2,1)S(1)}, bf16[4,2,128,128]{3,2,1,0:T(8,128)(2,1)S(1)}, u32[]{:S(2)}, u32[]{:S(2)}) collective-permute-start(bf16[4,2,128,128]{3,2,1,0:T(8,128)(2,1)S(1)} %pad_maximum_fusion.4), channel_id=1, source_target_pairs={{0,12},{2,14},{4,8},{6,10},{8,4},{10,6},{12,0},{14,2},{16,28},{18,... | collective-permute-start | bytes 786440 | tf_op jit(solution)/shard_map/ppermute | solution.py:300
  65.4 9.9 %collective-permute-start.12 = (bf16[4,192,128]{2,1,0:T(8,128)(2,1)S(1)}, bf16[4,192,128]{2,1,0:T(8,128)(2,1)S(1)}, u32[]{:S(2)}, u32[]{:S(2)}) collective-permute-start(bf16[4,192,128]{2,1,0:T(8,128)(2,1)S(1)} %get-tuple-element.102), channel_id=1, source_target_pairs={{0,2},{2,0},{4,6},{6,4},{8,10},{10,8},{12,14},{14,12},{16,18},{18,... | collective-permute-start | bytes 589832 | tf_op jit(solution)/shard_map/ppermute | solution.py:300
  67.7 8.9 %collective-permute-start.13 = (bf16[4,192,128]{2,1,0:T(8,128)(2,1)S(1)}, bf16[4,192,128]{2,1,0:T(8,128)(2,1)S(1)}, u32[]{:S(2)}, u32[]{:S(2)}) collective-permute-start(bf16[4,192,128]{2,1,0:T(8,128)(2,1)S(1)} %get-tuple-element.101), channel_id=1, source_target_pairs={{0,16},{2,18},{4,20},{6,22},{8,24},{10,26},{12,28},{14,30},{16,0},... | collective-permute-start | bytes 589832 | tf_op jit(solution)/shard_map/ppermute | solution.py:300
  68.9 9.9 %collective-permute-start.14 = (bf16[4,192,128]{2,1,0:T(8,128)(2,1)S(1)}, bf16[4,192,128]{2,1,0:T(8,128)(2,1)S(1)}, u32[]{:S(2)}, u32[]{:S(2)}) collective-permute-start(bf16[4,192,128]{2,1,0:T(8,128)(2,1)S(1)} %get-tuple-element.100), channel_id=1, source_target_pairs={{0,18},{2,16},{4,22},{6,20},{8,26},{10,24},{12,30},{14,28},{16,2},... | collective-permute-start | bytes 589832 | tf_op jit(solution)/shard_map/ppermute | solution.py:300
  69.4 15.7 %collective-permute-start.17 = (bf16[4,200,128]{2,1,0:T(8,128)(2,1)S(1)}, bf16[4,200,128]{2,1,0:T(8,128)(2,1)S(1)}, u32[]{:S(2)}, u32[]{:S(2)}) collective-permute-start(bf16[4,200,128]{2,1,0:T(8,128)(2,1)S(1)} %get-tuple-element.92), channel_id=1, source_target_pairs={{0,8},{2,10},{4,12},{6,14},{8,0},{10,2},{12,4},{14,6},{16,24},{18,... | collective-permute-start | bytes 614408 | tf_op jit(solution)/shard_map/ppermute | solution.py:300
  75.3 9.8 %collective-permute-start.15 = (bf16[4,200,128]{2,1,0:T(8,128)(2,1)S(1)}, bf16[4,200,128]{2,1,0:T(8,128)(2,1)S(1)}, u32[]{:S(2)}, u32[]{:S(2)}) collective-permute-start(bf16[4,200,128]{2,1,0:T(8,128)(2,1)S(1)} %get-tuple-element.93), channel_id=1, source_target_pairs={{0,4},{2,6},{4,0},{6,2},{8,12},{10,14},{12,8},{14,10},{16,20},{18,... | collective-permute-start | bytes 614408 | tf_op jit(solution)/shard_map/ppermute | solution.py:300
  75.4 14.9 %collective-permute-start.20 = (bf16[4,200,128]{2,1,0:T(8,128)(2,1)S(1)}, bf16[4,200,128]{2,1,0:T(8,128)(2,1)S(1)}, u32[]{:S(2)}, u32[]{:S(2)}) collective-permute-start(bf16[4,200,128]{2,1,0:T(8,128)(2,1)S(1)} %get-tuple-element.91), channel_id=1, source_target_pairs={{0,12},{2,14},{4,8},{6,10},{8,4},{10,6},{12,0},{14,2},{16,28},{18,... | collective-permute-start | bytes 614408 | tf_op jit(solution)/shard_map/ppermute | solution.py:300
  78.9 31.4 %collective-permute-start.19 = (bf16[4,192,128]{2,1,0:T(8,128)(2,1)S(1)}, bf16[4,192,128]{2,1,0:T(8,128)(2,1)S(1)}, u32[]{:S(2)}, u32[]{:S(2)}) collective-permute-start(bf16[4,192,128]{2,1,0:T(8,128)(2,1)S(1)} %pad_maximum_fusion.13), channel_id=1, source_target_pairs={{0,12},{2,14},{4,8},{6,10},{8,4},{10,6},{12,0},{14,2},{16,28},{18,... | collective-permute-start | bytes 589832 | tf_op jit(solution)/shard_map/ppermute | solution.py:300
  90.3 10.8 %collective-permute-start.23 = (bf16[4,200,128]{2,1,0:T(8,128)(2,1)S(1)}, bf16[4,200,128]{2,1,0:T(8,128)(2,1)S(1)}, u32[]{:S(2)}, u32[]{:S(2)}) collective-permute-start(bf16[4,200,128]{2,1,0:T(8,128)(2,1)S(1)} %pad_maximum_fusion.10), channel_id=1, source_target_pairs={{0,18},{2,16},{4,22},{6,20},{8,26},{10,24},{12,30},{14,28},{16,2},... | collective-permute-start | bytes 614408 | tf_op jit(solution)/shard_map/ppermute | solution.py:300
  93.2 13.3 %collective-permute-start.22 = (bf16[4,200,128]{2,1,0:T(8,128)(2,1)S(1)}, bf16[4,200,128]{2,1,0:T(8,128)(2,1)S(1)}, u32[]{:S(2)}, u32[]{:S(2)}) collective-permute-start(bf16[4,200,128]{2,1,0:T(8,128)(2,1)S(1)} %pad_maximum_fusion.9), channel_id=1, source_target_pairs={{0,16},{2,18},{4,20},{6,22},{8,24},{10,26},{12,28},{14,30},{16,0},... | collective-permute-start | bytes 614408 | tf_op jit(solution)/shard_map/ppermute | solution.py:300
  93.6 13.0 %collective-permute-start.21 = (bf16[4,200,128]{2,1,0:T(8,128)(2,1)S(1)}, bf16[4,200,128]{2,1,0:T(8,128)(2,1)S(1)}, u32[]{:S(2)}, u32[]{:S(2)}) collective-permute-start(bf16[4,200,128]{2,1,0:T(8,128)(2,1)S(1)} %pad_maximum_fusion.8), channel_id=1, source_target_pairs={{0,2},{2,0},{4,6},{6,4},{8,10},{10,8},{12,14},{14,12},{16,18},{18,... | collective-permute-start | bytes 614408 | tf_op jit(solution)/shard_map/ppermute | solution.py:300
  93.8 17.0 %collective-permute-start.18 = (bf16[4,192,128]{2,1,0:T(8,128)(2,1)S(1)}, bf16[4,192,128]{2,1,0:T(8,128)(2,1)S(1)}, u32[]{:S(2)}, u32[]{:S(2)}) collective-permute-start(bf16[4,192,128]{2,1,0:T(8,128)(2,1)S(1)} %pad_maximum_fusion.12), channel_id=1, source_target_pairs={{0,8},{2,10},{4,12},{6,14},{8,0},{10,2},{12,4},{14,6},{16,24},{18,... | collective-permute-start | bytes 589832 | tf_op jit(solution)/shard_map/ppermute | solution.py:300
  101.1 12.6 %collective-permute-start.16 = (bf16[4,192,128]{2,1,0:T(8,128)(2,1)S(1)}, bf16[4,192,128]{2,1,0:T(8,128)(2,1)S(1)}, u32[]{:S(2)}, u32[]{:S(2)}) collective-permute-start(bf16[4,192,128]{2,1,0:T(8,128)(2,1)S(1)} %pad_maximum_fusion.11), channel_id=1, source_target_pairs={{0,4},{2,6},{4,0},{6,2},{8,12},{10,14},{12,8},{14,10},{16,20},{18,... | collective-permute-start | bytes 589832 | tf_op jit(solution)/shard_map/ppermute | solution.py:300
  106.9 2.8 %collective-permute-start.24 = (f32[16]{0:T(128)S(1)}, f32[16]{0:T(128)S(1)}, u32[]{:S(2)}, u32[]{:S(2)}) collective-permute-start(f32[16]{0:T(128)S(1)} %select_reduce_fusion), channel_id=1, source_target_pairs={{0,1},{1,0},{2,3},{3,2},{4,5},{5,4},{6,7},{7,6},{8,9},{9,8},{10,11... | collective-permute-start | bytes 200 | tf_op jit(solution)/shard_map/ppermute | solution.py:289

commit v6 on v5

--- a/solution.py
+++ b/solution.py
@@ -46,52 +46,52 @@
     return lax.rem(mask, blocks) // 2, lax.rem(mask, 2) + 2 * (mask // blocks)
 
 
-def pack_kernel(copies, lanes_first, group, place_ref, first_ref, second_ref, *refs):
+def pack_kernel(copies, lanes_first, place_ref, first_ref, second_ref, *refs):
     sems = refs[-1]
     width = refs[0].shape[-1]
     started = []
     for index, (i, j, mask) in enumerate(places_of(sems.shape[0])):
-        near, far = (i, j) if lanes_first else (j, i)
-        if near not in group:
-            continue
         head = (place_ref[0] ^ mask) // copies
         columns = pl.ds(pl.multiple_of(head * width, width), width)
+        target = refs[i].at[j] if lanes_first else refs[j].at[i]
         for kind, source in enumerate((first_ref, second_ref)):
-            target = refs[group.index(near)].at[far, kind]
-            started.append(pltpu.make_async_copy(source.at[:, columns], target, sems.at[index, kind]))
+            started.append(pltpu.make_async_copy(source.at[:, columns], target.at[kind], sems.at[index, kind]))
     run_all(started)
 
 
-def unpack_kernel(copies, part, place_ref, *refs):
-    sems, home, sums = refs[-1], refs[-2], refs[-3]
-    outs = refs[-6:-3]
-    pieces = refs[:-6] if part == 0 else refs[:-9]
+def unpack_kernel(copies, counts, place_ref, *refs):
+    sems, home_b, home_a, sums = refs[-1], refs[-2], refs[-3], refs[-4]
+    outs = refs[-7:-4]
     devices = sems.shape[0]
-    width = home.shape[2]
+    width = home_a.shape[2]
     half = outs[0].shape[0] // 2
-    window = pl.ds(part * half, half)
     started = []
-    for index, (i, j, mask) in enumerate(places_of(devices)):
-        source = piece(pieces, part == 0, i, j, devices)
-        other = place_ref[0] ^ mask
-        if copies > 1:
-            started.append(pltpu.make_async_copy(source, home.at[other], sems.at[index, 0]))
-            continue
-        columns = pl.ds(pl.multiple_of(other * width, width), width)
-        for kind, out in enumerate(outs):
-            rows = source.at[pl.ds(kind * half, half)]
-            started.append(pltpu.make_async_copy(rows, out.at[window, columns], sems.at[index, kind]))
+    for part, home in enumerate((home_a, home_b)):
+        pieces = refs[: counts[0]] if part == 0 else refs[counts[0] : counts[0] + counts[1]]
+        window = pl.ds(part * half, half)
+        for index, (i, j, mask) in enumerate(places_of(devices)):
+            source = piece(pieces, part == 0, i, j, devices)
+            other = place_ref[0] ^ mask
+            if copies > 1:
+                started.append(pltpu.make_async_copy(source, home.at[other], sems.at[index, 3 * part]))
+                continue
+            columns = pl.ds(pl.multiple_of(other * width, width), width)
+            for kind, out in enumerate(outs):
+                rows = source.at[pl.ds(kind * half, half)]
+                copy = pltpu.make_async_copy(rows, out.at[window, columns], sems.at[index, 3 * part + kind])
+                started.append(copy)
     run_all(started)
     if copies > 1:
-        for head in range(devices // copies):
-            columns = pl.ds(head * width, width)
-            for kind, out in enumerate(outs):
-                rows = pl.ds(kind * half, half)
-                value = home[head * copies, rows].astype(jnp.float32)
-                for other in range(1, copies):
-                    value = value + home[head * copies + other, rows].astype(jnp.float32)
-                sums[kind, :, columns] = value.astype(sums.dtype)
-        run_all([pltpu.make_async_copy(sums.at[kind], out.at[window], sems.at[0, kind]) for kind, out in enumerate(outs)])
+        for part, home in enumerate((home_a, home_b)):
+            for head in range(devices // copies):
+                columns = pl.ds(head * width, width)
+                for kind in range(3):
+                    rows = pl.ds(kind * half, half)
+                    value = home[head * copies, rows].astype(jnp.float32)
+                    for other in range(1, copies):
+                        value = value + home[head * copies + other, rows].astype(jnp.float32)
+                    sums[kind, part * half : (part + 1) * half, columns] = value.astype(sums.dtype)
+        run_all([pltpu.make_async_copy(sums.at[kind], out, sems.at[0, kind]) for kind, out in enumerate(outs)])
 
 
 def dot(left, right, contract):
@@ -300,15 +300,13 @@
     return lax.ppermute(value, ("chan", "seq"), [(source, source ^ mask) for source in range(devices)])
 
 
-def exchanged(by_lane, by_seat, devices, phase):
+def exchanged(by_lane, by_seat, devices):
     seats, lanes = stages(devices)
     first_a = [by_lane[0]] + [moved(by_lane[i], lanes[i]) for i in range(1, len(lanes))]
     first_b = [by_seat[0]] + [moved(by_seat[j], seats[j]) for j in range(1, len(seats))]
     last_b = []
     for i in range(1, len(lanes)):
-        waiting = jnp.stack([value[i] for value in first_b])
-        if phase == "in" or i < len(lanes) - 1:
-            waiting, first_a[i] = lax.optimization_barrier((waiting, first_a[i]))
+        waiting, first_a[i] = lax.optimization_barrier((jnp.stack([value[i] for value in first_b]), first_a[i]))
         last_b.append(moved(waiting, lanes[i]))
     last_a = [moved(jnp.stack([value[j] for value in first_a]), seats[j]) for j in range(1, len(seats))]
     return first_a + last_a, first_b + last_b
@@ -357,10 +355,10 @@
             cost_estimate=pl.CostEstimate(flops=flops, bytes_accessed=2 << 20, transcendentals=0),
         )(*args)
 
-    def pack(lanes_first, group, first, second):
-        sends = (by_lane(2, rows, width) if lanes_first else by_seat(2, rows, width))[: len(group)]
+    def pack(lanes_first, first, second):
+        sends = by_lane(2, rows, width) if lanes_first else by_seat(2, rows, width)
         return call(
-            functools.partial(pack_kernel, copies, lanes_first, group),
+            functools.partial(pack_kernel, copies, lanes_first),
             sends,
             [smem, hbm, hbm],
             [vmem] * len(sends),
@@ -370,13 +368,10 @@
             (places, in_hbm(first[0, 0]), in_hbm(second[0, 0])),
         )
 
-    middle = len(lanes) // 2
-    far_a = pack(True, list(range(middle, len(lanes))), queries, keys)
-    values, out_grad, far_a = lax.optimization_barrier((values, out_grad, far_a))
-    sent_b = pack(False, list(range(len(seats))), out_grad, values)
-    queries, keys, sent_b = lax.optimization_barrier((queries, keys, sent_b))
-    sent_a = pack(True, list(range(middle)), queries, keys) + far_a
-    arrived_a, arrived_b = exchanged(sent_a, sent_b, devices, "in")
+    sent_a = pack(True, queries, keys)
+    values, out_grad, sent_a = lax.optimization_barrier((values, out_grad, sent_a))
+    sent_b = pack(False, out_grad, values)
+    arrived_a, arrived_b = exchanged(sent_a, sent_b, devices)
     qk, gv = arranged(arrived_a, len(lanes)), arranged(arrived_b, len(seats))
 
     half = rows // 2
@@ -411,7 +406,7 @@
         4,
         (lengths, places, qk, *made, gv),
     )
-    arrived_a, arrived_b = exchanged(list(back_a), list(back_b), devices, "out")
+    arrived_a, arrived_b = exchanged(list(back_a), list(back_b), devices)
 
     pieces = [
         (arrived_a[i][0] if j == 0 else arrived_a[len(lanes) + j - 1][i])[3 * half] for i, j, _ in places_of(devices)
@@ -421,27 +416,23 @@
     sums = jnp.sum(jnp.stack(pieces).astype(jnp.float32), axis=1)
     bias_out = summed_over(jnp.sum(jnp.where(chosen, sums[None], 0.0), axis=1), "dp")
 
-    def unpack(part, arrived, earlier):
-        flat = jax.ShapeDtypeStruct((rows, features), kind)
-        alone = copies == 1
-        return pl.pallas_call(
-            functools.partial(unpack_kernel, copies, part),
-            out_shape=(flat, flat, flat),
-            in_specs=[smem] + [anywhere] * len(arrived) + [hbm] * len(earlier),
-            out_specs=(hbm, hbm, hbm),
-            scratch_shapes=[
-                pltpu.VMEM((8, 8, 128) if alone else (3, half, features), kind),
-                pltpu.VMEM((1, 8, width) if alone else (devices,) + arrived[0].shape[1:], kind),
-                pltpu.SemaphoreType.DMA((devices, 3)),
-            ],
-            input_output_aliases={1 + len(arrived) + i: i for i in range(len(earlier))},
-            compiler_params=pltpu.CompilerParams(vmem_limit_bytes=SLACK_BYTES),
-            name="unpack_b" if part else "unpack_a",
-        )(places, *arrived, *earlier)
-
-    earlier = unpack(0, arrived_a, ())
-    bias_out, *earlier = lax.optimization_barrier((bias_out, *earlier))
-    grads = unpack(1, arrived_b, earlier)
+    flat = jax.ShapeDtypeStruct((rows, features), kind)
+    alone = copies == 1
+    arrived = arrived_a + arrived_b
+    grads = pl.pallas_call(
+        functools.partial(unpack_kernel, copies, (len(arrived_a), len(arrived_b))),
+        out_shape=(flat, flat, flat),
+        in_specs=[smem] + [anywhere] * len(arrived),
+        out_specs=(hbm, hbm, hbm),
+        scratch_shapes=[
+            pltpu.VMEM((3, 16 if alone else rows, features), kind),
+            pltpu.VMEM((1 if alone else devices,) + arrived_a[0].shape[1:], kind),
+            pltpu.VMEM((1 if alone else devices,) + arrived_b[0].shape[1:], kind),
+            pltpu.SemaphoreType.DMA((devices, 6)),
+        ],
+        compiler_params=pltpu.CompilerParams(vmem_limit_bytes=2 * SLACK_BYTES),
+        name="unpack",
+    )(places, *arrived)
     return tuple(grad[None, None] for grad in grads) + (bias_out,)
 
 

time: 116 us -> 115 us (level)
  starting transfers between devices: 49.1 us -> 34.3 us
  waiting for transfers between devices: 45.2 us -> 59.8 us
  Pallas kernels: 17.2 us -> 15.5 us
    ppermute x24, waiting for transfers between devices: 44.9 us -> 59.8 us  [moved(): lax.ppermute(value, ('chan', 'seq'), [(source, source ^ mask) for source...]
    ppermute x24, starting transfers between devices: 47.8 us -> 33 us  [moved(): lax.ppermute(value, ('chan', 'seq'), [(source, source ^ mask) for source...]
    pallas_call x5 -> x4, Pallas kernels: 14.7 us -> 13.5 us  [call(): pl.pallas_call(kernel, out_shape=out_shape, in_specs=in_specs, out_specs=...]
    pallas_call x2 -> x1, Pallas kernels: 2.56 us -> 1.96 us  [layer(): pl.pallas_call(functools.partial(unpack_kernel, copies, (len(arrived_a),...]
  transfers between devices with their start and end apart: 25 -> 25, of which waited for: 13 -> 12; matrix products, arithmetic and copies ran while one was open for 1% -> 1% of each run, Pallas kernels for 6% -> 5%
where the time goes in v6:
time: 115 us; the launch traced here: 113 us
  waiting for transfers between devices  59.8 us (52%)
  starting transfers between devices  34.3 us (30%)
  Pallas kernels  15.5 us (13%)
  between operations  1.65 us (1%)
  other arithmetic  1.48 us (1%)
    ppermute x24, waiting for transfers between devices, moved(): lax.ppermute(value, ('chan', 'seq'), [(source, source ^ mask) for source...  59.8 us
    ppermute x24, starting transfers between devices, moved(): lax.ppermute(value, ('chan', 'seq'), [(source, source ^ mask) for source...  33 us
    pallas_call x4, Pallas kernels, call(): pl.pallas_call(kernel, out_shape=out_shape, in_specs=in_specs, out_specs=...  13.5 us
  transfers between devices with their start and end apart: 25, of which 12 were waited for; matrix products, arithmetic and copies ran while one was open for 1% of the time, Pallas kernels for 5%

profile of v6, /device:TPU:1, one launch (start us, length us, event | category | flops | bytes accessed | tf_op | source)
XLA Modules:
  0.0 113.2 jit_solution(1311539781373437366)
XLA Ops:
  0.7 1.5 %shard_map.102 = (bf16[4,2,128,128]{3,2,1,0:T(8,128)(2,1)S(1)}, bf16[4,2,128,128]{3,2,1,0:T(8,128)(2,1)S(1)}, bf16[4,2,128,128]{3,2,1,0:T(8,128)(2,1)S(1)}, bf16[4,2,128,128]{3,2,1,0:T(8,128)(2,1)S(1)}) custom-call(s32[1]{0:T(128)} %bitcast.place_ref, bf16[128,2048]{1,0:T(8,128)(2,1)} %bitcast.78, bf16[128,2048]{1,0:T(8,128)(2,1)} %bitcast.79), custom_call_target="tpu_custom_call" | custom-call | bytes 2097152 | tf_op jit(solution)/shard_map/pallas_call | solution.py:348
  2.1 1.5 %shard_map.103 = (bf16[4,2,128,128]{3,2,1,0:T(8,128)(2,1)S(1)}, bf16[4,2,128,128]{3,2,1,0:T(8,128)(2,1)S(1)}, bf16[4,2,128,128]{3,2,1,0:T(8,128)(2,1)S(1)}, bf16[4,2,128,128]{3,2,1,0:T(8,128)(2,1)S(1)}) custom-call(s32[1]{0:T(128)} %bitcast.place_ref, bf16[128,2048]{1,0:T(8,128)(2,1)} %bitcast.80, bf16[128,2048]{1,0:T(8,128)(2,1)} %bitcast.81), custom_call_target="tpu_custom_call" | custom-call | bytes 2097152 | tf_op jit(solution)/shard_map/pallas_call | solution.py:348
  3.7 2.7 %collective-permute-start.1 = (bf16[4,2,128,128]{3,2,1,0:T(8,128)(2,1)S(1)}, bf16[4,2,128,128]{3,2,1,0:T(8,128)(2,1)S(1)}, u32[]{:S(2)}, u32[]{:S(2)}) collective-permute-start(bf16[4,2,128,128]{3,2,1,0:T(8,128)(2,1)S(1)} %get-tuple-element.47), channel_id=1, source_target_pairs={{0,16},{2,18},{4,20},{6,22},{8,24},{10,26},{12,28},{14,30},{16,0},... | collective-permute-start | bytes 786440 | tf_op jit(solution)/shard_map/ppermute | solution.py:300
  6.5 1.7 %collective-permute-start.3 = (bf16[4,2,128,128]{3,2,1,0:T(8,128)(2,1)S(1)}, bf16[4,2,128,128]{3,2,1,0:T(8,128)(2,1)S(1)}, u32[]{:S(2)}, u32[]{:S(2)}) collective-permute-start(bf16[4,2,128,128]{3,2,1,0:T(8,128)(2,1)S(1)} %get-tuple-element.49), channel_id=1, source_target_pairs={{0,4},{2,6},{4,0},{6,2},{8,12},{10,14},{12,8},{14,10},{16,20},{18,... | collective-permute-start | bytes 786440 | tf_op jit(solution)/shard_map/ppermute | solution.py:300
  8.2 2.3 %collective-permute-start.4 = (bf16[4,2,128,128]{3,2,1,0:T(8,128)(2,1)S(1)}, bf16[4,2,128,128]{3,2,1,0:T(8,128)(2,1)S(1)}, u32[]{:S(2)}, u32[]{:S(2)}) collective-permute-start(bf16[4,2,128,128]{3,2,1,0:T(8,128)(2,1)S(1)} %get-tuple-element.51), channel_id=1, source_target_pairs={{0,8},{2,10},{4,12},{6,14},{8,0},{10,2},{12,4},{14,6},{16,24},{18,... | collective-permute-start | bytes 786440 | tf_op jit(solution)/shard_map/ppermute | solution.py:300
  10.7 2.4 %collective-permute-done.1 = bf16[4,2,128,128]{3,2,1,0:T(8,128)(2,1)S(1)} collective-permute-done((bf16[4,2,128,128]{3,2,1,0:T(8,128)(2,1)S(1)}, bf16[4,2,128,128]{3,2,1,0:T(8,128)(2,1)S(1)}, u32[]{:S(2)}, u32[]{:S(2)}) %collective-permute-start.1) | collective-permute-done | bytes 262176 | tf_op jit(solution)/shard_map/ppermute | solution.py:300
  13.1 5.9 %collective-permute-done.2 = bf16[4,2,128,128]{3,2,1,0:T(8,128)(2,1)S(1)} collective-permute-done((bf16[4,2,128,128]{3,2,1,0:T(8,128)(2,1)S(1)}, bf16[4,2,128,128]{3,2,1,0:T(8,128)(2,1)S(1)}, u32[]{:S(2)}, u32[]{:S(2)}) %collective-permute-start.2) | collective-permute-done | bytes 262176 | tf_op jit(solution)/shard_map/ppermute | solution.py:300
  19.0 0.6 collective-permute-done.3
  19.7 8.2 %collective-permute-done.5 = bf16[4,2,128,128]{3,2,1,0:T(8,128)(2,1)S(1)} collective-permute-done((bf16[4,2,128,128]{3,2,1,0:T(8,128)(2,1)S(1)}, bf16[4,2,128,128]{3,2,1,0:T(8,128)(2,1)S(1)}, u32[]{:S(2)}, u32[]{:S(2)}) %collective-permute-start.5) | collective-permute-done | bytes 262176 | tf_op jit(solution)/shard_map/ppermute | solution.py:300
  28.1 2.2 %collective-permute-start.6 = (bf16[4,2,128,128]{3,2,1,0:T(8,128)(2,1)S(1)}, bf16[4,2,128,128]{3,2,1,0:T(8,128)(2,1)S(1)}, u32[]{:S(2)}, u32[]{:S(2)}) collective-permute-start(bf16[4,2,128,128]{3,2,1,0:T(8,128)(2,1)S(1)} %pad_maximum_fusion.5), channel_id=1, source_target_pairs={{0,2},{2,0},{4,6},{6,4},{8,10},{10,8},{12,14},{14,12},{16,18},{18,... | collective-permute-start | bytes 786440 | tf_op jit(solution)/shard_map/ppermute | solution.py:300
  30.3 1.3 %collective-permute-start.7 = (bf16[4,2,128,128]{3,2,1,0:T(8,128)(2,1)S(1)}, bf16[4,2,128,128]{3,2,1,0:T(8,128)(2,1)S(1)}, u32[]{:S(2)}, u32[]{:S(2)}) collective-permute-start(bf16[4,2,128,128]{3,2,1,0:T(8,128)(2,1)S(1)} %pad_maximum_fusion.6), channel_id=1, source_target_pairs={{0,16},{2,18},{4,20},{6,22},{8,24},{10,26},{12,28},{14,30},{16,0},... | collective-permute-start | bytes 786440 | tf_op jit(solution)/shard_map/ppermute | solution.py:300
  32.8 5.0 %collective-permute-start.9 = (bf16[4,2,128,128]{3,2,1,0:T(8,128)(2,1)S(1)}, bf16[4,2,128,128]{3,2,1,0:T(8,128)(2,1)S(1)}, u32[]{:S(2)}, u32[]{:S(2)}) collective-permute-start(bf16[4,2,128,128]{3,2,1,0:T(8,128)(2,1)S(1)} %pad_maximum_fusion.2), channel_id=1, source_target_pairs={{0,4},{2,6},{4,0},{6,2},{8,12},{10,14},{12,8},{14,10},{16,20},{18,... | collective-permute-start | bytes 786440 | tf_op jit(solution)/shard_map/ppermute | solution.py:300
  37.8 1.1 collective-permute-start.10
  38.9 1.2 %collective-permute-start.11 = (bf16[4,2,128,128]{3,2,1,0:T(8,128)(2,1)S(1)}, bf16[4,2,128,128]{3,2,1,0:T(8,128)(2,1)S(1)}, u32[]{:S(2)}, u32[]{:S(2)}) collective-permute-start(bf16[4,2,128,128]{3,2,1,0:T(8,128)(2,1)S(1)} %pad_maximum_fusion.4), channel_id=1, source_target_pairs={{0,12},{2,14},{4,8},{6,10},{8,4},{10,6},{12,0},{14,2},{16,28},{18,... | collective-permute-start | bytes 786440 | tf_op jit(solution)/shard_map/ppermute | solution.py:300
  40.1 4.1 %collective-permute-done.8 = bf16[4,2,128,128]{3,2,1,0:T(8,128)(2,1)S(1)} collective-permute-done((bf16[4,2,128,128]{3,2,1,0:T(8,128)(2,1)S(1)}, bf16[4,2,128,128]{3,2,1,0:T(8,128)(2,1)S(1)}, u32[]{:S(2)}, u32[]{:S(2)}) %collective-permute-start.8) | collective-permute-done | bytes 262176 | tf_op jit(solution)/shard_map/ppermute | solution.py:300
  44.4 4.1 %shard_map.104 = (bf16[8,128,256]{2,1,0:T(8,128)(2,1)S(1)}, f32[35,256,256]{2,1,0:T(8,128)S(1)}, f32[8,8,256]{2,1,0:T(8,128)S(1)}) custom-call(s32[1]{0:T(128)S(6)} %copy.11.length_ref, s32[1]{0:T(128)} %bitcast.place_ref, f32[16]{0:T(128)S(1)} %copy-done, bf16[4,4,2,128,128]{4,3,2,1,0:T(8,128)(2,1)S(1)} %pad_maximum_fusion.qk_ref), custom_call_target="tpu_custom_call" | custom-call | flops 587202560 | bytes 2097152 | tf_op jit(solution)/shard_map/pallas_call | solution.py:348
  48.5 0.8 collective-permute-done.9
  49.3 8.1 %collective-permute-done.11 = bf16[4,2,128,128]{3,2,1,0:T(8,128)(2,1)S(1)} collective-permute-done((bf16[4,2,128,128]{3,2,1,0:T(8,128)(2,1)S(1)}, bf16[4,2,128,128]{3,2,1,0:T(8,128)(2,1)S(1)}, u32[]{:S(2)}, u32[]{:S(2)}) %collective-permute-start.11) | collective-permute-done | bytes 262176 | tf_op jit(solution)/shard_map/ppermute | solution.py:300
  57.6 6.5 %shard_map.105 = (bf16[4,4,200,128]{3,2,1,0:T(8,128)(2,1)S(1)}, bf16[4,4,192,128]{3,2,1,0:T(8,128)(2,1)S(1)}) custom-call(s32[1]{0:T(128)S(6)} %copy.11.length_ref, s32[1]{0:T(128)} %bitcast.place_ref, bf16[4,4,2,128,128]{4,3,2,1,0:T(8,128)(2,1)S(1)} %pad_maximum_fusion.qk_ref, bf16[8,128,256]{2,1,0:T(8,128)(2,1)S(1)} %get-tuple-element.55.kt_ref, ...), custom_call_target="tpu_custom_call" | custom-call | flops 2348810240 | bytes 2097152 | tf_op jit(solution)/shard_map/pallas_call | solution.py:348
  64.2 2.3 %collective-permute-start.12 = (bf16[4,192,128]{2,1,0:T(8,128)(2,1)S(1)}, bf16[4,192,128]{2,1,0:T(8,128)(2,1)S(1)}, u32[]{:S(2)}, u32[]{:S(2)}) collective-permute-start(bf16[4,192,128]{2,1,0:T(8,128)(2,1)S(1)} %get-tuple-element.82), channel_id=1, source_target_pairs={{0,2},{2,0},{4,6},{6,4},{8,10},{10,8},{12,14},{14,12},{16,18},{18,... | collective-permute-start | bytes 589832 | tf_op jit(solution)/shard_map/ppermute | solution.py:300
  66.5 1.2 %collective-permute-start.13 = (bf16[4,192,128]{2,1,0:T(8,128)(2,1)S(1)}, bf16[4,192,128]{2,1,0:T(8,128)(2,1)S(1)}, u32[]{:S(2)}, u32[]{:S(2)}) collective-permute-start(bf16[4,192,128]{2,1,0:T(8,128)(2,1)S(1)} %get-tuple-element.81), channel_id=1, source_target_pairs={{0,16},{2,18},{4,20},{6,22},{8,24},{10,26},{12,28},{14,30},{16,0},... | collective-permute-start | bytes 589832 | tf_op jit(solution)/shard_map/ppermute | solution.py:300
  68.2 2.2 %collective-permute-start.17 = (bf16[4,200,128]{2,1,0:T(8,128)(2,1)S(1)}, bf16[4,200,128]{2,1,0:T(8,128)(2,1)S(1)}, u32[]{:S(2)}, u32[]{:S(2)}) collective-permute-start(bf16[4,200,128]{2,1,0:T(8,128)(2,1)S(1)} %get-tuple-element.75), channel_id=1, source_target_pairs={{0,12},{2,14},{4,8},{6,10},{8,4},{10,6},{12,0},{14,2},{16,28},{18,... | collective-permute-start | bytes 614408 | tf_op jit(solution)/shard_map/ppermute | solution.py:300
  70.4 3.9 %collective-permute-start.16 = (bf16[4,200,128]{2,1,0:T(8,128)(2,1)S(1)}, bf16[4,200,128]{2,1,0:T(8,128)(2,1)S(1)}, u32[]{:S(2)}, u32[]{:S(2)}) collective-permute-start(bf16[4,200,128]{2,1,0:T(8,128)(2,1)S(1)} %get-tuple-element.76), channel_id=1, source_target_pairs={{0,8},{2,10},{4,12},{6,14},{8,0},{10,2},{12,4},{14,6},{16,24},{18,... | collective-permute-start | bytes 614408 | tf_op jit(solution)/shard_map/ppermute | solution.py:300
  74.6 2.8 %collective-permute-done.14.refs_10_ = bf16[4,192,128]{2,1,0:T(8,128)(2,1)S(1)} collective-permute-done((bf16[4,192,128]{2,1,0:T(8,128)(2,1)S(1)}, bf16[4,192,128]{2,1,0:T(8,128)(2,1)S(1)}, u32[]{:S(2)}, u32[]{:S(2)}) %collective-permute-start.14) | collective-permute-done | bytes 196640 | tf_op jit(solution)/shard_map/ppermute | solution.py:300
  77.5 12.7 %collective-permute-done.16.refs_2_ = bf16[4,200,128]{2,1,0:T(8,128)(2,1)S(1)} collective-permute-done((bf16[4,200,128]{2,1,0:T(8,128)(2,1)S(1)}, bf16[4,200,128]{2,1,0:T(8,128)(2,1)S(1)}, u32[]{:S(2)}, u32[]{:S(2)}) %collective-permute-start.16) | collective-permute-done | bytes 204832 | tf_op jit(solution)/shard_map/ppermute | solution.py:300
  90.3 1.7 %collective-permute-start.20 = (bf16[4,200,128]{2,1,0:T(8,128)(2,1)S(1)}, bf16[4,200,128]{2,1,0:T(8,128)(2,1)S(1)}, u32[]{:S(2)}, u32[]{:S(2)}) collective-permute-start(bf16[4,200,128]{2,1,0:T(8,128)(2,1)S(1)} %pad_maximum_fusion.10), channel_id=1, source_target_pairs={{0,18},{2,16},{4,22},{6,20},{8,26},{10,24},{12,30},{14,28},{16,2},... | collective-permute-start | bytes 614408 | tf_op jit(solution)/shard_map/ppermute | solution.py:300
  92.7 2.2 %collective-permute-start.23 = (bf16[4,192,128]{2,1,0:T(8,128)(2,1)S(1)}, bf16[4,192,128]{2,1,0:T(8,128)(2,1)S(1)}, u32[]{:S(2)}, u32[]{:S(2)}) collective-permute-start(bf16[4,192,128]{2,1,0:T(8,128)(2,1)S(1)} %pad_maximum_fusion.13), channel_id=1, source_target_pairs={{0,12},{2,14},{4,8},{6,10},{8,4},{10,6},{12,0},{14,2},{16,28},{18,... | collective-permute-start | bytes 589832 | tf_op jit(solution)/shard_map/ppermute | solution.py:300
  94.9 3.1 %collective-permute-done.20.refs_6_ = bf16[4,200,128]{2,1,0:T(8,128)(2,1)S(1)} collective-permute-done((bf16[4,200,128]{2,1,0:T(8,128)(2,1)S(1)}, bf16[4,200,128]{2,1,0:T(8,128)(2,1)S(1)}, u32[]{:S(2)}, u32[]{:S(2)}) %collective-permute-start.20) | collective-permute-done | bytes 204832 | tf_op jit(solution)/shard_map/ppermute | solution.py:300
  98.0 3.9 %collective-permute-done.19.refs_5_ = bf16[4,200,128]{2,1,0:T(8,128)(2,1)S(1)} collective-permute-done((bf16[4,200,128]{2,1,0:T(8,128)(2,1)S(1)}, bf16[4,200,128]{2,1,0:T(8,128)(2,1)S(1)}, u32[]{:S(2)}, u32[]{:S(2)}) %collective-permute-start.19) | collective-permute-done | bytes 204832 | tf_op jit(solution)/shard_map/ppermute | solution.py:300
  102.3 1.3 %collective-permute-start.24 = (f32[16]{0:T(128)S(1)}, f32[16]{0:T(128)S(1)}, u32[]{:S(2)}, u32[]{:S(2)}) collective-permute-start(f32[16]{0:T(128)S(1)} %select_reduce_fusion), channel_id=1, source_target_pairs={{0,1},{1,0},{2,3},{3,2},{4,5},{5,4},{6,7},{7,6},{8,9},{9,8},{10,11... | collective-permute-start | bytes 200 | tf_op jit(solution)/shard_map/ppermute | solution.py:289
  103.6 7.1 %collective-permute-done.22.refs_12_ = bf16[4,192,128]{2,1,0:T(8,128)(2,1)S(1)} collective-permute-done((bf16[4,192,128]{2,1,0:T(8,128)(2,1)S(1)}, bf16[4,192,128]{2,1,0:T(8,128)(2,1)S(1)}, u32[]{:S(2)}, u32[]{:S(2)}) %collective-permute-start.22) | collective-permute-done | bytes 196640 | tf_op jit(solution)/shard_map/ppermute | solution.py:300
  110.7 2.0 %unpack.1 = (bf16[128,2048]{1,0:T(8,128)(2,1)}, bf16[128,2048]{1,0:T(8,128)(2,1)}, bf16[128,2048]{1,0:T(8,128)(2,1)}) custom-call(s32[1]{0:T(128)} %bitcast.place_ref, bf16[4,200,128]{2,1,0:T(8,128)(2,1)S(1)} %get-tuple-element.78.refs_0_, bf16[4,200,128]{2,1,0:T(8,128)(2,1)S(1)} %collective-permute-done.15.refs_1_, ...), custom_call_target="tpu_custom_call" | custom-call | tf_op jit(solution)/shard_map/unpack/pallas_call | solution.py:422
  (73 shorter events, 4.0 us)
Async XLA Ops:
  0.6 31.5 %copy-start.1 = (s32[16]{0:T(128)S(1)}, s32[16]{0:T(128)}, u32[]{:S(2)}) copy-start(s32[16]{0:T(128)} %constant.27.clone) | copy-start | bytes 196
  0.6 43.8 %copy-start = (f32[16]{0:T(128)S(1)}, f32[16]{0:T(128)}, u32[]{:S(2)}) copy-start(f32[16]{0:T(128)} %bias_ref.1) | copy-start | bytes 196
  3.6 6.9 %collective-permute-start = (bf16[4,2,128,128]{3,2,1,0:T(8,128)(2,1)S(1)}, bf16[4,2,128,128]{3,2,1,0:T(8,128)(2,1)S(1)}, u32[]{:S(2)}, u32[]{:S(2)}) collective-permute-start(bf16[4,2,128,128]{3,2,1,0:T(8,128)(2,1)S(1)} %get-tuple-element.46), channel_id=1, source_target_pairs={{0,2},{2,0},{4,6},{6,4},{8,10},{10,8},{12,14},{14,12},{16,18},{18,... | collective-permute-start | bytes 786440 | tf_op jit(solution)/shard_map/ppermute | solution.py:300
  3.7 9.3 %collective-permute-start.1 = (bf16[4,2,128,128]{3,2,1,0:T(8,128)(2,1)S(1)}, bf16[4,2,128,128]{3,2,1,0:T(8,128)(2,1)S(1)}, u32[]{:S(2)}, u32[]{:S(2)}) collective-permute-start(bf16[4,2,128,128]{3,2,1,0:T(8,128)(2,1)S(1)} %get-tuple-element.47), channel_id=1, source_target_pairs={{0,16},{2,18},{4,20},{6,22},{8,24},{10,26},{12,28},{14,30},{16,0},... | collective-permute-start | bytes 786440 | tf_op jit(solution)/shard_map/ppermute | solution.py:300
  6.4 12.5 %collective-permute-start.2 = (bf16[4,2,128,128]{3,2,1,0:T(8,128)(2,1)S(1)}, bf16[4,2,128,128]{3,2,1,0:T(8,128)(2,1)S(1)}, u32[]{:S(2)}, u32[]{:S(2)}) collective-permute-start(bf16[4,2,128,128]{3,2,1,0:T(8,128)(2,1)S(1)} %get-tuple-element.48), channel_id=1, source_target_pairs={{0,18},{2,16},{4,22},{6,20},{8,26},{10,24},{12,30},{14,28},{16,2},... | collective-permute-start | bytes 786440 | tf_op jit(solution)/shard_map/ppermute | solution.py:300
  6.5 13.1 %collective-permute-start.3 = (bf16[4,2,128,128]{3,2,1,0:T(8,128)(2,1)S(1)}, bf16[4,2,128,128]{3,2,1,0:T(8,128)(2,1)S(1)}, u32[]{:S(2)}, u32[]{:S(2)}) collective-permute-start(bf16[4,2,128,128]{3,2,1,0:T(8,128)(2,1)S(1)} %get-tuple-element.49), channel_id=1, source_target_pairs={{0,4},{2,6},{4,0},{6,2},{8,12},{10,14},{12,8},{14,10},{16,20},{18,... | collective-permute-start | bytes 786440 | tf_op jit(solution)/shard_map/ppermute | solution.py:300
  8.2 11.5 %collective-permute-start.4 = (bf16[4,2,128,128]{3,2,1,0:T(8,128)(2,1)S(1)}, bf16[4,2,128,128]{3,2,1,0:T(8,128)(2,1)S(1)}, u32[]{:S(2)}, u32[]{:S(2)}) collective-permute-start(bf16[4,2,128,128]{3,2,1,0:T(8,128)(2,1)S(1)} %get-tuple-element.51), channel_id=1, source_target_pairs={{0,8},{2,10},{4,12},{6,14},{8,0},{10,2},{12,4},{14,6},{16,24},{18,... | collective-permute-start | bytes 786440 | tf_op jit(solution)/shard_map/ppermute | solution.py:300
  10.6 17.4 %collective-permute-start.5 = (bf16[4,2,128,128]{3,2,1,0:T(8,128)(2,1)S(1)}, bf16[4,2,128,128]{3,2,1,0:T(8,128)(2,1)S(1)}, u32[]{:S(2)}, u32[]{:S(2)}) collective-permute-start(bf16[4,2,128,128]{3,2,1,0:T(8,128)(2,1)S(1)} %get-tuple-element.53), channel_id=1, source_target_pairs={{0,12},{2,14},{4,8},{6,10},{8,4},{10,6},{12,0},{14,2},{16,28},{18,... | collective-permute-start | bytes 786440 | tf_op jit(solution)/shard_map/ppermute | solution.py:300
  28.1 10.9 %collective-permute-start.6 = (bf16[4,2,128,128]{3,2,1,0:T(8,128)(2,1)S(1)}, bf16[4,2,128,128]{3,2,1,0:T(8,128)(2,1)S(1)}, u32[]{:S(2)}, u32[]{:S(2)}) collective-permute-start(bf16[4,2,128,128]{3,2,1,0:T(8,128)(2,1)S(1)} %pad_maximum_fusion.5), channel_id=1, source_target_pairs={{0,2},{2,0},{4,6},{6,4},{8,10},{10,8},{12,14},{14,12},{16,18},{18,... | collective-permute-start | bytes 786440 | tf_op jit(solution)/shard_map/ppermute | solution.py:300
  30.3 9.9 %collective-permute-start.7 = (bf16[4,2,128,128]{3,2,1,0:T(8,128)(2,1)S(1)}, bf16[4,2,128,128]{3,2,1,0:T(8,128)(2,1)S(1)}, u32[]{:S(2)}, u32[]{:S(2)}) collective-permute-start(bf16[4,2,128,128]{3,2,1,0:T(8,128)(2,1)S(1)} %pad_maximum_fusion.6), channel_id=1, source_target_pairs={{0,16},{2,18},{4,20},{6,22},{8,24},{10,26},{12,28},{14,30},{16,0},... | collective-permute-start | bytes 786440 | tf_op jit(solution)/shard_map/ppermute | solution.py:300
  31.6 12.7 %collective-permute-start.8 = (bf16[4,2,128,128]{3,2,1,0:T(8,128)(2,1)S(1)}, bf16[4,2,128,128]{3,2,1,0:T(8,128)(2,1)S(1)}, u32[]{:S(2)}, u32[]{:S(2)}) collective-permute-start(bf16[4,2,128,128]{3,2,1,0:T(8,128)(2,1)S(1)} %pad_maximum_fusion.7), channel_id=1, source_target_pairs={{0,18},{2,16},{4,22},{6,20},{8,26},{10,24},{12,30},{14,28},{16,2},... | collective-permute-start | bytes 786440 | tf_op jit(solution)/shard_map/ppermute | solution.py:300
  32.8 16.6 %collective-permute-start.9 = (bf16[4,2,128,128]{3,2,1,0:T(8,128)(2,1)S(1)}, bf16[4,2,128,128]{3,2,1,0:T(8,128)(2,1)S(1)}, u32[]{:S(2)}, u32[]{:S(2)}) collective-permute-start(bf16[4,2,128,128]{3,2,1,0:T(8,128)(2,1)S(1)} %pad_maximum_fusion.2), channel_id=1, source_target_pairs={{0,4},{2,6},{4,0},{6,2},{8,12},{10,14},{12,8},{14,10},{16,20},{18,... | collective-permute-start | bytes 786440 | tf_op jit(solution)/shard_map/ppermute | solution.py:300
  37.8 11.6 %collective-permute-start.10 = (bf16[4,2,128,128]{3,2,1,0:T(8,128)(2,1)S(1)}, bf16[4,2,128,128]{3,2,1,0:T(8,128)(2,1)S(1)}, u32[]{:S(2)}, u32[]{:S(2)}) collective-permute-start(bf16[4,2,128,128]{3,2,1,0:T(8,128)(2,1)S(1)} %pad_maximum_fusion.3), channel_id=1, source_target_pairs={{0,8},{2,10},{4,12},{6,14},{8,0},{10,2},{12,4},{14,6},{16,24},{18,... | collective-permute-start | bytes 786440 | tf_op jit(solution)/shard_map/ppermute | solution.py:300
  38.9 18.5 %collective-permute-start.11 = (bf16[4,2,128,128]{3,2,1,0:T(8,128)(2,1)S(1)}, bf16[4,2,128,128]{3,2,1,0:T(8,128)(2,1)S(1)}, u32[]{:S(2)}, u32[]{:S(2)}) collective-permute-start(bf16[4,2,128,128]{3,2,1,0:T(8,128)(2,1)S(1)} %pad_maximum_fusion.4), channel_id=1, source_target_pairs={{0,12},{2,14},{4,8},{6,10},{8,4},{10,6},{12,0},{14,2},{16,28},{18,... | collective-permute-start | bytes 786440 | tf_op jit(solution)/shard_map/ppermute | solution.py:300
  64.2 10.1 %collective-permute-start.12 = (bf16[4,192,128]{2,1,0:T(8,128)(2,1)S(1)}, bf16[4,192,128]{2,1,0:T(8,128)(2,1)S(1)}, u32[]{:S(2)}, u32[]{:S(2)}) collective-permute-start(bf16[4,192,128]{2,1,0:T(8,128)(2,1)S(1)} %get-tuple-element.82), channel_id=1, source_target_pairs={{0,2},{2,0},{4,6},{6,4},{8,10},{10,8},{12,14},{14,12},{16,18},{18,... | collective-permute-start | bytes 589832 | tf_op jit(solution)/shard_map/ppermute | solution.py:300
  66.5 8.1 %collective-permute-start.13 = (bf16[4,192,128]{2,1,0:T(8,128)(2,1)S(1)}, bf16[4,192,128]{2,1,0:T(8,128)(2,1)S(1)}, u32[]{:S(2)}, u32[]{:S(2)}) collective-permute-start(bf16[4,192,128]{2,1,0:T(8,128)(2,1)S(1)} %get-tuple-element.81), channel_id=1, source_target_pairs={{0,16},{2,18},{4,20},{6,22},{8,24},{10,26},{12,28},{14,30},{16,0},... | collective-permute-start | bytes 589832 | tf_op jit(solution)/shard_map/ppermute | solution.py:300
  67.7 9.6 %collective-permute-start.14 = (bf16[4,192,128]{2,1,0:T(8,128)(2,1)S(1)}, bf16[4,192,128]{2,1,0:T(8,128)(2,1)S(1)}, u32[]{:S(2)}, u32[]{:S(2)}) collective-permute-start(bf16[4,192,128]{2,1,0:T(8,128)(2,1)S(1)} %get-tuple-element.80), channel_id=1, source_target_pairs={{0,18},{2,16},{4,22},{6,20},{8,26},{10,24},{12,30},{14,28},{16,2},... | collective-permute-start | bytes 589832 | tf_op jit(solution)/shard_map/ppermute | solution.py:300
  68.2 9.3 %collective-permute-start.17 = (bf16[4,200,128]{2,1,0:T(8,128)(2,1)S(1)}, bf16[4,200,128]{2,1,0:T(8,128)(2,1)S(1)}, u32[]{:S(2)}, u32[]{:S(2)}) collective-permute-start(bf16[4,200,128]{2,1,0:T(8,128)(2,1)S(1)} %get-tuple-element.75), channel_id=1, source_target_pairs={{0,12},{2,14},{4,8},{6,10},{8,4},{10,6},{12,0},{14,2},{16,28},{18,... | collective-permute-start | bytes 614408 | tf_op jit(solution)/shard_map/ppermute | solution.py:300
  70.4 19.8 %collective-permute-start.16 = (bf16[4,200,128]{2,1,0:T(8,128)(2,1)S(1)}, bf16[4,200,128]{2,1,0:T(8,128)(2,1)S(1)}, u32[]{:S(2)}, u32[]{:S(2)}) collective-permute-start(bf16[4,200,128]{2,1,0:T(8,128)(2,1)S(1)} %get-tuple-element.76), channel_id=1, source_target_pairs={{0,8},{2,10},{4,12},{6,14},{8,0},{10,2},{12,4},{14,6},{16,24},{18,... | collective-permute-start | bytes 614408 | tf_op jit(solution)/shard_map/ppermute | solution.py:300
  74.3 15.9 %collective-permute-start.15 = (bf16[4,200,128]{2,1,0:T(8,128)(2,1)S(1)}, bf16[4,200,128]{2,1,0:T(8,128)(2,1)S(1)}, u32[]{:S(2)}, u32[]{:S(2)}) collective-permute-start(bf16[4,200,128]{2,1,0:T(8,128)(2,1)S(1)} %get-tuple-element.77), channel_id=1, source_target_pairs={{0,4},{2,6},{4,0},{6,2},{8,12},{10,14},{12,8},{14,10},{16,20},{18,... | collective-permute-start | bytes 614408 | tf_op jit(solution)/shard_map/ppermute | solution.py:300
  90.3 7.7 %collective-permute-start.20 = (bf16[4,200,128]{2,1,0:T(8,128)(2,1)S(1)}, bf16[4,200,128]{2,1,0:T(8,128)(2,1)S(1)}, u32[]{:S(2)}, u32[]{:S(2)}) collective-permute-start(bf16[4,200,128]{2,1,0:T(8,128)(2,1)S(1)} %pad_maximum_fusion.10), channel_id=1, source_target_pairs={{0,18},{2,16},{4,22},{6,20},{8,26},{10,24},{12,30},{14,28},{16,2},... | collective-permute-start | bytes 614408 | tf_op jit(solution)/shard_map/ppermute | solution.py:300
  92.0 10.0 %collective-permute-start.19 = (bf16[4,200,128]{2,1,0:T(8,128)(2,1)S(1)}, bf16[4,200,128]{2,1,0:T(8,128)(2,1)S(1)}, u32[]{:S(2)}, u32[]{:S(2)}) collective-permute-start(bf16[4,200,128]{2,1,0:T(8,128)(2,1)S(1)} %pad_maximum_fusion.9), channel_id=1, source_target_pairs={{0,16},{2,18},{4,20},{6,22},{8,24},{10,26},{12,28},{14,30},{16,0},... | collective-permute-start | bytes 614408 | tf_op jit(solution)/shard_map/ppermute | solution.py:300
  92.3 9.7 %collective-permute-start.18 = (bf16[4,200,128]{2,1,0:T(8,128)(2,1)S(1)}, bf16[4,200,128]{2,1,0:T(8,128)(2,1)S(1)}, u32[]{:S(2)}, u32[]{:S(2)}) collective-permute-start(bf16[4,200,128]{2,1,0:T(8,128)(2,1)S(1)} %pad_maximum_fusion.8), channel_id=1, source_target_pairs={{0,2},{2,0},{4,6},{6,4},{8,10},{10,8},{12,14},{14,12},{16,18},{18,... | collective-permute-start | bytes 614408 | tf_op jit(solution)/shard_map/ppermute | solution.py:300
  92.7 10.9 %collective-permute-start.23 = (bf16[4,192,128]{2,1,0:T(8,128)(2,1)S(1)}, bf16[4,192,128]{2,1,0:T(8,128)(2,1)S(1)}, u32[]{:S(2)}, u32[]{:S(2)}) collective-permute-start(bf16[4,192,128]{2,1,0:T(8,128)(2,1)S(1)} %pad_maximum_fusion.13), channel_id=1, source_target_pairs={{0,12},{2,14},{4,8},{6,10},{8,4},{10,6},{12,0},{14,2},{16,28},{18,... | collective-permute-start | bytes 589832 | tf_op jit(solution)/shard_map/ppermute | solution.py:300
  94.9 15.8 %collective-permute-start.22 = (bf16[4,192,128]{2,1,0:T(8,128)(2,1)S(1)}, bf16[4,192,128]{2,1,0:T(8,128)(2,1)S(1)}, u32[]{:S(2)}, u32[]{:S(2)}) collective-permute-start(bf16[4,192,128]{2,1,0:T(8,128)(2,1)S(1)} %pad_maximum_fusion.12), channel_id=1, source_target_pairs={{0,8},{2,10},{4,12},{6,14},{8,0},{10,2},{12,4},{14,6},{16,24},{18,... | collective-permute-start | bytes 589832 | tf_op jit(solution)/shard_map/ppermute | solution.py:300
  98.0 12.7 %collective-permute-start.21 = (bf16[4,192,128]{2,1,0:T(8,128)(2,1)S(1)}, bf16[4,192,128]{2,1,0:T(8,128)(2,1)S(1)}, u32[]{:S(2)}, u32[]{:S(2)}) collective-permute-start(bf16[4,192,128]{2,1,0:T(8,128)(2,1)S(1)} %pad_maximum_fusion.11), channel_id=1, source_target_pairs={{0,4},{2,6},{4,0},{6,2},{8,12},{10,14},{12,8},{14,10},{16,20},{18,... | collective-permute-start | bytes 589832 | tf_op jit(solution)/shard_map/ppermute | solution.py:300
  102.3 10.4 %collective-permute-start.24 = (f32[16]{0:T(128)S(1)}, f32[16]{0:T(128)S(1)}, u32[]{:S(2)}, u32[]{:S(2)}) collective-permute-start(f32[16]{0:T(128)S(1)} %select_reduce_fusion), channel_id=1, source_target_pairs={{0,1},{1,0},{2,3},{3,2},{4,5},{5,4},{6,7},{7,6},{8,9},{9,8},{10,11... | collective-permute-start | bytes 200 | tf_op jit(solution)/shard_map/ppermute | solution.py:289

commit v7 on v6

--- a/solution.py
+++ b/solution.py
@@ -11,7 +11,6 @@
 
 LOOKBACK = 6
 NEG_FILL = -1e30
-EXTRA = 8
 LOG2_E = math.log2(math.e)
 SLACK_BYTES = 6 << 20
 
@@ -203,7 +202,9 @@
     for_groups(length, rows, blocks, on_group)
 
 
-def grads_kernel(length_ref, place_ref, qk_ref, kt_ref, power_ref, inverse_ref, gv_ref, out_a, out_b, d_ref, dk_ref, dv_ref, bias_acc):
+def grads_kernel(
+    copies, length_ref, place_ref, qk_ref, kt_ref, power_ref, inverse_ref, gv_ref, out_a, out_b, bias_ref, d_ref, dk_ref, dv_ref, bias_acc
+):
     rows, width = gv_ref.shape[3:]
     blocks = 2 * gv_ref.shape[0]
     both = 2 * rows
@@ -267,16 +268,8 @@
     key_blocks(range(group_size(blocks)))
 
     whole = jnp.sum(jnp.sum(bias_acc[...], axis=0, keepdims=True), axis=1, keepdims=True)
-    whole = jnp.broadcast_to(whole, (1, width))
-    high = whole.astype(jnp.bfloat16).astype(jnp.float32)
-    middle = (whole - high).astype(jnp.bfloat16).astype(jnp.float32)
-    low = (whole - high - middle).astype(jnp.bfloat16).astype(jnp.float32)
-    lane = lax.broadcasted_iota(jnp.int32, (1, width), 1)
-    pieces = jnp.where(lane == 0, high, jnp.where(lane == 1, middle, jnp.where(lane == 2, low, 0.0)))
-    pieces = jnp.broadcast_to(pieces, (EXTRA, width)).astype(out_a.dtype)
-    for i in range(out_a.shape[0]):
-        for j in range(out_a.shape[1]):
-            out_a[i, j, 3 * half : 3 * half + EXTRA] = pieces
+    lane = lax.broadcasted_iota(jnp.int32, bias_ref.shape, 1)
+    bias_ref[...] = jnp.where(lane == place // copies, whole, 0.0)
 
 
 def summed_over(value, axis):
@@ -392,15 +385,16 @@
         (lengths, places, cross_bias, qk),
     )
     sends = (
-        jax.ShapeDtypeStruct((len(lanes), len(seats), 3 * half + EXTRA, width), kind),
+        jax.ShapeDtypeStruct((len(lanes), len(seats), 3 * half, width), kind),
         jax.ShapeDtypeStruct((len(seats), len(lanes), 3 * half, width), kind),
+        jax.ShapeDtypeStruct((1, heads), jnp.float32),
     )
     held = (d_shape, sums_shape, sums_shape)
-    back_a, back_b = call(
-        grads_kernel,
+    back_a, back_b, bias_sum = call(
+        functools.partial(grads_kernel, copies),
         sends,
         [smem, smem] + [vmem] * 5,
-        [vmem] * 2,
+        [vmem] * 3,
         [pltpu.VMEM(shape.shape, shape.dtype) for shape in held] + [pltpu.VMEM((8, rows), jnp.float32)],
         size(*held, *sends, qk, gv, turned_shape, power_shape, inverse_shape),
         4,
@@ -408,13 +402,11 @@
     )
     arrived_a, arrived_b = exchanged(list(back_a), list(back_b), devices)
 
-    pieces = [
-        (arrived_a[i][0] if j == 0 else arrived_a[len(lanes) + j - 1][i])[3 * half] for i, j, _ in places_of(devices)
-    ]
-    masks = jnp.array([mask for _, _, mask in places_of(devices)], jnp.int32)
-    chosen = (masks ^ place)[None] // copies == jnp.arange(heads, dtype=jnp.int32)[:, None]
-    sums = jnp.sum(jnp.stack(pieces).astype(jnp.float32), axis=1)
-    bias_out = summed_over(jnp.sum(jnp.where(chosen, sums[None], 0.0), axis=1), "dp")
+    bias_out = summed_over(bias_sum[0], "dp")
+    mask = 1
+    while mask < devices:
+        bias_out = bias_out + moved(bias_out, mask)
+        mask *= 2
 
     flat = jax.ShapeDtypeStruct((rows, features), kind)
     alone = copies == 1

time: 115 us -> 120 us (1.043)
  the two profiles are of different devices: /device:TPU:1 before, /device:TPU:8 now
where the time goes in v7:
time: 120 us
  waiting for transfers between devices  70.9 us (59%)
  starting transfers between devices  29.4 us (24%)
  Pallas kernels  15.9 us (13%)
  between operations  1.83 us (2%)
  other arithmetic  1.25 us (1%)
    ppermute x28, waiting for transfers between devices, moved(): lax.ppermute(value, ('chan', 'seq'), [(source, source ^ mask) for source...  68.8 us
    ppermute x28, starting transfers between devices, moved(): lax.ppermute(value, ('chan', 'seq'), [(source, source ^ mask) for source...  27.9 us
    pallas_call x4, Pallas kernels, call(): pl.pallas_call(kernel, out_shape=out_shape, in_specs=in_specs, out_specs=...  13.9 us
  transfers between devices with their start and end apart: 29, of which 16 were waited for; matrix products, arithmetic and copies ran while one was open for 1% of the time, Pallas kernels for 5%

profile of v7, /device:TPU:8, one launch (start us, length us, event | category | flops | bytes accessed | tf_op | source)
XLA Modules:
  0.0 119.6 jit_solution(8499307839046981479)
XLA Ops:
  0.6 1.5 %shard_map.93 = (bf16[4,2,128,128]{3,2,1,0:T(8,128)(2,1)S(1)}, bf16[4,2,128,128]{3,2,1,0:T(8,128)(2,1)S(1)}, bf16[4,2,128,128]{3,2,1,0:T(8,128)(2,1)S(1)}, bf16[4,2,128,128]{3,2,1,0:T(8,128)(2,1)S(1)}) custom-call(s32[1]{0:T(128)} %bitcast.place_ref, bf16[128,2048]{1,0:T(8,128)(2,1)} %bitcast.49, bf16[128,2048]{1,0:T(8,128)(2,1)} %bitcast.50), custom_call_target="tpu_custom_call" | custom-call | bytes 2097152 | tf_op jit(solution)/shard_map/pallas_call | solution.py:341
  2.2 3.0 %collective-permute-start.4 = (bf16[4,2,128,128]{3,2,1,0:T(8,128)(2,1)S(1)}, bf16[4,2,128,128]{3,2,1,0:T(8,128)(2,1)S(1)}, u32[]{:S(2)}, u32[]{:S(2)}) collective-permute-start(bf16[4,2,128,128]{3,2,1,0:T(8,128)(2,1)S(1)} %get-tuple-element.52), channel_id=1, source_target_pairs={{0,8},{2,10},{4,12},{6,14},{8,0},{10,2},{12,4},{14,6},{16,24},{18,... | collective-permute-start | bytes 786440 | tf_op jit(solution)/shard_map/ppermute | solution.py:293
  5.7 1.5 %shard_map.94 = (bf16[4,2,128,128]{3,2,1,0:T(8,128)(2,1)S(1)}, bf16[4,2,128,128]{3,2,1,0:T(8,128)(2,1)S(1)}, bf16[4,2,128,128]{3,2,1,0:T(8,128)(2,1)S(1)}, bf16[4,2,128,128]{3,2,1,0:T(8,128)(2,1)S(1)}) custom-call(s32[1]{0:T(128)} %bitcast.place_ref, bf16[128,2048]{1,0:T(8,128)(2,1)} %bitcast.51, bf16[128,2048]{1,0:T(8,128)(2,1)} %bitcast.52), custom_call_target="tpu_custom_call" | custom-call | bytes 2097152 | tf_op jit(solution)/shard_map/pallas_call | solution.py:341
  7.2 1.6 %collective-permute-start.1 = (bf16[4,2,128,128]{3,2,1,0:T(8,128)(2,1)S(1)}, bf16[4,2,128,128]{3,2,1,0:T(8,128)(2,1)S(1)}, u32[]{:S(2)}, u32[]{:S(2)}) collective-permute-start(bf16[4,2,128,128]{3,2,1,0:T(8,128)(2,1)S(1)} %get-tuple-element.48), channel_id=1, source_target_pairs={{0,16},{2,18},{4,20},{6,22},{8,24},{10,26},{12,28},{14,30},{16,0},... | collective-permute-start | bytes 786440 | tf_op jit(solution)/shard_map/ppermute | solution.py:293
  10.1 6.4 %collective-permute-done.1 = bf16[4,2,128,128]{3,2,1,0:T(8,128)(2,1)S(1)} collective-permute-done((bf16[4,2,128,128]{3,2,1,0:T(8,128)(2,1)S(1)}, bf16[4,2,128,128]{3,2,1,0:T(8,128)(2,1)S(1)}, u32[]{:S(2)}, u32[]{:S(2)}) %collective-permute-start.1) | collective-permute-done | bytes 262176 | tf_op jit(solution)/shard_map/ppermute | solution.py:293
  16.5 4.5 %collective-permute-done.2 = bf16[4,2,128,128]{3,2,1,0:T(8,128)(2,1)S(1)} collective-permute-done((bf16[4,2,128,128]{3,2,1,0:T(8,128)(2,1)S(1)}, bf16[4,2,128,128]{3,2,1,0:T(8,128)(2,1)S(1)}, u32[]{:S(2)}, u32[]{:S(2)}) %collective-permute-start.2) | collective-permute-done | bytes 262176 | tf_op jit(solution)/shard_map/ppermute | solution.py:293
  21.1 7.2 %collective-permute-done.5 = bf16[4,2,128,128]{3,2,1,0:T(8,128)(2,1)S(1)} collective-permute-done((bf16[4,2,128,128]{3,2,1,0:T(8,128)(2,1)S(1)}, bf16[4,2,128,128]{3,2,1,0:T(8,128)(2,1)S(1)}, u32[]{:S(2)}, u32[]{:S(2)}) %collective-permute-start.5) | collective-permute-done | bytes 262176 | tf_op jit(solution)/shard_map/ppermute | solution.py:293
  28.7 1.6 %collective-permute-start.7 = (bf16[4,2,128,128]{3,2,1,0:T(8,128)(2,1)S(1)}, bf16[4,2,128,128]{3,2,1,0:T(8,128)(2,1)S(1)}, u32[]{:S(2)}, u32[]{:S(2)}) collective-permute-start(bf16[4,2,128,128]{3,2,1,0:T(8,128)(2,1)S(1)} %pad_maximum_fusion.6), channel_id=1, source_target_pairs={{0,16},{2,18},{4,20},{6,22},{8,24},{10,26},{12,28},{14,30},{16,0},... | collective-permute-start | bytes 786440 | tf_op jit(solution)/shard_map/ppermute | solution.py:293
  31.4 3.0 %collective-permute-start.10 = (bf16[4,2,128,128]{3,2,1,0:T(8,128)(2,1)S(1)}, bf16[4,2,128,128]{3,2,1,0:T(8,128)(2,1)S(1)}, u32[]{:S(2)}, u32[]{:S(2)}) collective-permute-start(bf16[4,2,128,128]{3,2,1,0:T(8,128)(2,1)S(1)} %pad_maximum_fusion.3), channel_id=1, source_target_pairs={{0,8},{2,10},{4,12},{6,14},{8,0},{10,2},{12,4},{14,6},{16,24},{18,... | collective-permute-start | bytes 786440 | tf_op jit(solution)/shard_map/ppermute | solution.py:293
  35.1 2.9 %collective-permute-done.7 = bf16[4,2,128,128]{3,2,1,0:T(8,128)(2,1)S(1)} collective-permute-done((bf16[4,2,128,128]{3,2,1,0:T(8,128)(2,1)S(1)}, bf16[4,2,128,128]{3,2,1,0:T(8,128)(2,1)S(1)}, u32[]{:S(2)}, u32[]{:S(2)}) %collective-permute-start.7) | collective-permute-done | bytes 262176 | tf_op jit(solution)/shard_map/ppermute | solution.py:293
  37.9 4.7 %collective-permute-done.8 = bf16[4,2,128,128]{3,2,1,0:T(8,128)(2,1)S(1)} collective-permute-done((bf16[4,2,128,128]{3,2,1,0:T(8,128)(2,1)S(1)}, bf16[4,2,128,128]{3,2,1,0:T(8,128)(2,1)S(1)}, u32[]{:S(2)}, u32[]{:S(2)}) %collective-permute-start.8) | collective-permute-done | bytes 262176 | tf_op jit(solution)/shard_map/ppermute | solution.py:293
  42.7 4.1 %shard_map.95 = (bf16[8,128,256]{2,1,0:T(8,128)(2,1)S(1)}, f32[35,256,256]{2,1,0:T(8,128)S(1)}, f32[8,8,256]{2,1,0:T(8,128)S(1)}) custom-call(s32[1]{0:T(128)S(6)} %copy.10.length_ref, s32[1]{0:T(128)} %bitcast.place_ref, f32[16]{0:T(128)S(1)} %copy-done, bf16[4,4,2,128,128]{4,3,2,1,0:T(8,128)(2,1)S(1)} %pad_maximum_fusion.qk_ref), custom_call_target="tpu_custom_call" | custom-call | flops 587202560 | bytes 2097152 | tf_op jit(solution)/shard_map/pallas_call | solution.py:341
  46.9 5.6 %collective-permute-done.10 = bf16[4,2,128,128]{3,2,1,0:T(8,128)(2,1)S(1)} collective-permute-done((bf16[4,2,128,128]{3,2,1,0:T(8,128)(2,1)S(1)}, bf16[4,2,128,128]{3,2,1,0:T(8,128)(2,1)S(1)}, u32[]{:S(2)}, u32[]{:S(2)}) %collective-permute-start.10) | collective-permute-done | bytes 262176 | tf_op jit(solution)/shard_map/ppermute | solution.py:293
  52.4 5.6 %collective-permute-done.11 = bf16[4,2,128,128]{3,2,1,0:T(8,128)(2,1)S(1)} collective-permute-done((bf16[4,2,128,128]{3,2,1,0:T(8,128)(2,1)S(1)}, bf16[4,2,128,128]{3,2,1,0:T(8,128)(2,1)S(1)}, u32[]{:S(2)}, u32[]{:S(2)}) %collective-permute-start.11) | collective-permute-done | bytes 262176 | tf_op jit(solution)/shard_map/ppermute | solution.py:293
  58.1 6.8 %shard_map.96 = (bf16[4,4,192,128]{3,2,1,0:T(8,128)(2,1)S(1)}, bf16[4,4,192,128]{3,2,1,0:T(8,128)(2,1)S(1)}, f32[1,16]{1,0:T(1,128)S(1)}) custom-call(s32[1]{0:T(128)S(6)} %copy.10.length_ref, s32[1]{0:T(128)} %bitcast.place_ref, bf16[4,4,2,128,128]{4,3,2,1,0:T(8,128)(2,1)S(1)} %pad_maximum_fusion.qk_ref, bf16[8,128,256]{2,1,0:T(8,128)(2,1)S(1)} %get-tuple-element.56.kt_ref, ...), custom_call_target="tpu_custom_call" | custom-call | flops 2348810240 | bytes 2097152 | tf_op jit(solution)/shard_map/pallas_call | solution.py:341
  65.1 1.6 %collective-permute-start.24 = (f32[16]{0:T(128)S(1)}, f32[16]{0:T(128)S(1)}, u32[]{:S(2)}, u32[]{:S(2)}) collective-permute-start(f32[16]{0:T(128)S(1)} %bitcast.48), channel_id=1, source_target_pairs={{0,1},{1,0},{2,3},{3,2},{4,5},{5,4},{6,7},{7,6},{8,9},{9,8},{10,11... | collective-permute-start | bytes 200 | tf_op jit(solution)/shard_map/ppermute | solution.py:282
  66.7 2.1 %collective-permute-done.24 = f32[16]{0:T(128)S(1)} collective-permute-done((f32[16]{0:T(128)S(1)}, f32[16]{0:T(128)S(1)}, u32[]{:S(2)}, u32[]{:S(2)}) %collective-permute-start.24) | collective-permute-done | bytes 96 | tf_op jit(solution)/shard_map/ppermute | solution.py:282
  68.8 1.6 %collective-permute-start.17 = (bf16[4,192,128]{2,1,0:T(8,128)(2,1)S(1)}, bf16[4,192,128]{2,1,0:T(8,128)(2,1)S(1)}, u32[]{:S(2)}, u32[]{:S(2)}) collective-permute-start(bf16[4,192,128]{2,1,0:T(8,128)(2,1)S(1)} %get-tuple-element.81), channel_id=1, source_target_pairs={{0,12},{2,14},{4,8},{6,10},{8,4},{10,6},{12,0},{14,2},{16,28},{18,... | collective-permute-start | bytes 589832 | tf_op jit(solution)/shard_map/ppermute | solution.py:293
  70.3 2.6 %collective-permute-start.16 = (bf16[4,192,128]{2,1,0:T(8,128)(2,1)S(1)}, bf16[4,192,128]{2,1,0:T(8,128)(2,1)S(1)}, u32[]{:S(2)}, u32[]{:S(2)}) collective-permute-start(bf16[4,192,128]{2,1,0:T(8,128)(2,1)S(1)} %get-tuple-element.82), channel_id=1, source_target_pairs={{0,8},{2,10},{4,12},{6,14},{8,0},{10,2},{12,4},{14,6},{16,24},{18,... | collective-permute-start | bytes 589832 | tf_op jit(solution)/shard_map/ppermute | solution.py:293
  74.5 2.0 %collective-permute-start.15 = (bf16[4,192,128]{2,1,0:T(8,128)(2,1)S(1)}, bf16[4,192,128]{2,1,0:T(8,128)(2,1)S(1)}, u32[]{:S(2)}, u32[]{:S(2)}) collective-permute-start(bf16[4,192,128]{2,1,0:T(8,128)(2,1)S(1)} %get-tuple-element.83), channel_id=1, source_target_pairs={{0,4},{2,6},{4,0},{6,2},{8,12},{10,14},{12,8},{14,10},{16,20},{18,... | collective-permute-start | bytes 589832 | tf_op jit(solution)/shard_map/ppermute | solution.py:293
  76.5 8.5 %collective-permute-done.27 = f32[16]{0:T(128)S(1)} collective-permute-done((f32[16]{0:T(128)S(1)}, f32[16]{0:T(128)S(1)}, u32[]{:S(2)}, u32[]{:S(2)}) %collective-permute-start.27) | collective-permute-done | bytes 96 | tf_op jit(solution)/shard_map/ppermute | solution.py:293
  85.0 1.5 %collective-permute-start.13 = (bf16[4,192,128]{2,1,0:T(8,128)(2,1)S(1)}, bf16[4,192,128]{2,1,0:T(8,128)(2,1)S(1)}, u32[]{:S(2)}, u32[]{:S(2)}) collective-permute-start(bf16[4,192,128]{2,1,0:T(8,128)(2,1)S(1)} %get-tuple-element.76), channel_id=1, source_target_pairs={{0,16},{2,18},{4,20},{6,22},{8,24},{10,26},{12,28},{14,30},{16,0},... | collective-permute-start | bytes 589832 | tf_op jit(solution)/shard_map/ppermute | solution.py:293
  86.6 5.3 %collective-permute-done.13.refs_9_ = bf16[4,192,128]{2,1,0:T(8,128)(2,1)S(1)} collective-permute-done((bf16[4,192,128]{2,1,0:T(8,128)(2,1)S(1)}, bf16[4,192,128]{2,1,0:T(8,128)(2,1)S(1)}, u32[]{:S(2)}, u32[]{:S(2)}) %collective-permute-start.13) | collective-permute-done | bytes 196640 | tf_op jit(solution)/shard_map/ppermute | solution.py:293
  91.9 1.5 %collective-permute-start.28 = (f32[16]{0:T(128)S(1)}, f32[16]{0:T(128)S(1)}, u32[]{:S(2)}, u32[]{:S(2)}) collective-permute-start(f32[16]{0:T(128)S(1)} %add.22), channel_id=1, source_target_pairs={{0,16},{2,18},{4,20},{6,22},{8,24},{10,26},{12,28},{14,30},{16,0},... | collective-permute-start | bytes 200 | tf_op jit(solution)/shard_map/ppermute | solution.py:293
  94.4 1.4 %collective-permute-start.20 = (bf16[4,192,128]{2,1,0:T(8,128)(2,1)S(1)}, bf16[4,192,128]{2,1,0:T(8,128)(2,1)S(1)}, u32[]{:S(2)}, u32[]{:S(2)}) collective-permute-start(bf16[4,192,128]{2,1,0:T(8,128)(2,1)S(1)} %pad_maximum_fusion.13), channel_id=1, source_target_pairs={{0,18},{2,16},{4,22},{6,20},{8,26},{10,24},{12,30},{14,28},{16,2},... | collective-permute-start | bytes 589832 | tf_op jit(solution)/shard_map/ppermute | solution.py:293
  95.8 2.3 %collective-permute-start.21 = (bf16[4,192,128]{2,1,0:T(8,128)(2,1)S(1)}, bf16[4,192,128]{2,1,0:T(8,128)(2,1)S(1)}, u32[]{:S(2)}, u32[]{:S(2)}) collective-permute-start(bf16[4,192,128]{2,1,0:T(8,128)(2,1)S(1)} %pad_maximum_fusion.8), channel_id=1, source_target_pairs={{0,4},{2,6},{4,0},{6,2},{8,12},{10,14},{12,8},{14,10},{16,20},{18,... | collective-permute-start | bytes 589832 | tf_op jit(solution)/shard_map/ppermute | solution.py:293
  100.3 1.3 %collective-permute-done.19.refs_5_ = bf16[4,192,128]{2,1,0:T(8,128)(2,1)S(1)} collective-permute-done((bf16[4,192,128]{2,1,0:T(8,128)(2,1)S(1)}, bf16[4,192,128]{2,1,0:T(8,128)(2,1)S(1)}, u32[]{:S(2)}, u32[]{:S(2)}) %collective-permute-start.19) | collective-permute-done | bytes 196640 | tf_op jit(solution)/shard_map/ppermute | solution.py:293
  101.6 3.3 %collective-permute-done.20.refs_6_ = bf16[4,192,128]{2,1,0:T(8,128)(2,1)S(1)} collective-permute-done((bf16[4,192,128]{2,1,0:T(8,128)(2,1)S(1)}, bf16[4,192,128]{2,1,0:T(8,128)(2,1)S(1)}, u32[]{:S(2)}, u32[]{:S(2)}) %collective-permute-start.20) | collective-permute-done | bytes 196640 | tf_op jit(solution)/shard_map/ppermute | solution.py:293
  104.9 1.6 %collective-permute-done.21.refs_11_ = bf16[4,192,128]{2,1,0:T(8,128)(2,1)S(1)} collective-permute-done((bf16[4,192,128]{2,1,0:T(8,128)(2,1)S(1)}, bf16[4,192,128]{2,1,0:T(8,128)(2,1)S(1)}, u32[]{:S(2)}, u32[]{:S(2)}) %collective-permute-start.21) | collective-permute-done | bytes 196640 | tf_op jit(solution)/shard_map/ppermute | solution.py:293
  106.5 6.4 %collective-permute-done.22.refs_12_ = bf16[4,192,128]{2,1,0:T(8,128)(2,1)S(1)} collective-permute-done((bf16[4,192,128]{2,1,0:T(8,128)(2,1)S(1)}, bf16[4,192,128]{2,1,0:T(8,128)(2,1)S(1)}, u32[]{:S(2)}, u32[]{:S(2)}) %collective-permute-start.22) | collective-permute-done | bytes 196640 | tf_op jit(solution)/shard_map/ppermute | solution.py:293
  112.9 4.6 %collective-permute-done.23.refs_13_ = bf16[4,192,128]{2,1,0:T(8,128)(2,1)S(1)} collective-permute-done((bf16[4,192,128]{2,1,0:T(8,128)(2,1)S(1)}, bf16[4,192,128]{2,1,0:T(8,128)(2,1)S(1)}, u32[]{:S(2)}, u32[]{:S(2)}) %collective-permute-start.23) | collective-permute-done | bytes 196640 | tf_op jit(solution)/shard_map/ppermute | solution.py:293
  117.5 2.0 %unpack.1 = (bf16[128,2048]{1,0:T(8,128)(2,1)}, bf16[128,2048]{1,0:T(8,128)(2,1)}, bf16[128,2048]{1,0:T(8,128)(2,1)}) custom-call(s32[1]{0:T(128)} %bitcast.place_ref, bf16[4,192,128]{2,1,0:T(8,128)(2,1)S(1)} %get-tuple-element.84.refs_0_, bf16[4,192,128]{2,1,0:T(8,128)(2,1)S(1)} %collective-permute-done.15.refs_1_, ...), custom_call_target="tpu_custom_call" | custom-call | tf_op jit(solution)/shard_map/unpack/pallas_call | solution.py:414
  (71 shorter events, 8.3 us)
Async XLA Ops:
  0.6 42.1 %copy-start = (f32[16]{0:T(128)S(1)}, f32[16]{0:T(128)}, u32[]{:S(2)}) copy-start(f32[16]{0:T(128)} %bias_ref.1) | copy-start | bytes 196
  2.1 26.3 %collective-permute-start.3 = (bf16[4,2,128,128]{3,2,1,0:T(8,128)(2,1)S(1)}, bf16[4,2,128,128]{3,2,1,0:T(8,128)(2,1)S(1)}, u32[]{:S(2)}, u32[]{:S(2)}) collective-permute-start(bf16[4,2,128,128]{3,2,1,0:T(8,128)(2,1)S(1)} %get-tuple-element.50), channel_id=1, source_target_pairs={{0,4},{2,6},{4,0},{6,2},{8,12},{10,14},{12,8},{14,10},{16,20},{18,... | collective-permute-start | bytes 786440 | tf_op jit(solution)/shard_map/ppermute | solution.py:293
  2.2 26.2 %collective-permute-start.4 = (bf16[4,2,128,128]{3,2,1,0:T(8,128)(2,1)S(1)}, bf16[4,2,128,128]{3,2,1,0:T(8,128)(2,1)S(1)}, u32[]{:S(2)}, u32[]{:S(2)}) collective-permute-start(bf16[4,2,128,128]{3,2,1,0:T(8,128)(2,1)S(1)} %get-tuple-element.52), channel_id=1, source_target_pairs={{0,8},{2,10},{4,12},{6,14},{8,0},{10,2},{12,4},{14,6},{16,24},{18,... | collective-permute-start | bytes 786440 | tf_op jit(solution)/shard_map/ppermute | solution.py:293
  5.2 23.1 %collective-permute-start.5 = (bf16[4,2,128,128]{3,2,1,0:T(8,128)(2,1)S(1)}, bf16[4,2,128,128]{3,2,1,0:T(8,128)(2,1)S(1)}, u32[]{:S(2)}, u32[]{:S(2)}) collective-permute-start(bf16[4,2,128,128]{3,2,1,0:T(8,128)(2,1)S(1)} %get-tuple-element.54), channel_id=1, source_target_pairs={{0,12},{2,14},{4,8},{6,10},{8,4},{10,6},{12,0},{14,2},{16,28},{18,... | collective-permute-start | bytes 786440 | tf_op jit(solution)/shard_map/ppermute | solution.py:293
  7.2 1.7 %collective-permute-start = (bf16[4,2,128,128]{3,2,1,0:T(8,128)(2,1)S(1)}, bf16[4,2,128,128]{3,2,1,0:T(8,128)(2,1)S(1)}, u32[]{:S(2)}, u32[]{:S(2)}) collective-permute-start(bf16[4,2,128,128]{3,2,1,0:T(8,128)(2,1)S(1)} %get-tuple-element.47), channel_id=1, source_target_pairs={{0,2},{2,0},{4,6},{6,4},{8,10},{10,8},{12,14},{14,12},{16,18},{18,... | collective-permute-start | bytes 786440 | tf_op jit(solution)/shard_map/ppermute | solution.py:293
  7.2 9.2 %collective-permute-start.1 = (bf16[4,2,128,128]{3,2,1,0:T(8,128)(2,1)S(1)}, bf16[4,2,128,128]{3,2,1,0:T(8,128)(2,1)S(1)}, u32[]{:S(2)}, u32[]{:S(2)}) collective-permute-start(bf16[4,2,128,128]{3,2,1,0:T(8,128)(2,1)S(1)} %get-tuple-element.48), channel_id=1, source_target_pairs={{0,16},{2,18},{4,20},{6,22},{8,24},{10,26},{12,28},{14,30},{16,0},... | collective-permute-start | bytes 786440 | tf_op jit(solution)/shard_map/ppermute | solution.py:293
  8.9 12.1 %collective-permute-start.2 = (bf16[4,2,128,128]{3,2,1,0:T(8,128)(2,1)S(1)}, bf16[4,2,128,128]{3,2,1,0:T(8,128)(2,1)S(1)}, u32[]{:S(2)}, u32[]{:S(2)}) collective-permute-start(bf16[4,2,128,128]{3,2,1,0:T(8,128)(2,1)S(1)} %get-tuple-element.49), channel_id=1, source_target_pairs={{0,18},{2,16},{4,22},{6,20},{8,26},{10,24},{12,30},{14,28},{16,2},... | collective-permute-start | bytes 786440 | tf_op jit(solution)/shard_map/ppermute | solution.py:293
  28.6 5.9 %collective-permute-start.6 = (bf16[4,2,128,128]{3,2,1,0:T(8,128)(2,1)S(1)}, bf16[4,2,128,128]{3,2,1,0:T(8,128)(2,1)S(1)}, u32[]{:S(2)}, u32[]{:S(2)}) collective-permute-start(bf16[4,2,128,128]{3,2,1,0:T(8,128)(2,1)S(1)} %pad_maximum_fusion.5), channel_id=1, source_target_pairs={{0,2},{2,0},{4,6},{6,4},{8,10},{10,8},{12,14},{14,12},{16,18},{18,... | collective-permute-start | bytes 786440 | tf_op jit(solution)/shard_map/ppermute | solution.py:293
  28.7 9.2 %collective-permute-start.7 = (bf16[4,2,128,128]{3,2,1,0:T(8,128)(2,1)S(1)}, bf16[4,2,128,128]{3,2,1,0:T(8,128)(2,1)S(1)}, u32[]{:S(2)}, u32[]{:S(2)}) collective-permute-start(bf16[4,2,128,128]{3,2,1,0:T(8,128)(2,1)S(1)} %pad_maximum_fusion.6), channel_id=1, source_target_pairs={{0,16},{2,18},{4,20},{6,22},{8,24},{10,26},{12,28},{14,30},{16,0},... | collective-permute-start | bytes 786440 | tf_op jit(solution)/shard_map/ppermute | solution.py:293
  30.3 12.3 %collective-permute-start.8 = (bf16[4,2,128,128]{3,2,1,0:T(8,128)(2,1)S(1)}, bf16[4,2,128,128]{3,2,1,0:T(8,128)(2,1)S(1)}, u32[]{:S(2)}, u32[]{:S(2)}) collective-permute-start(bf16[4,2,128,128]{3,2,1,0:T(8,128)(2,1)S(1)} %pad_maximum_fusion.7), channel_id=1, source_target_pairs={{0,18},{2,16},{4,22},{6,20},{8,26},{10,24},{12,30},{14,28},{16,2},... | collective-permute-start | bytes 786440 | tf_op jit(solution)/shard_map/ppermute | solution.py:293
  31.3 15.5 %collective-permute-start.9 = (bf16[4,2,128,128]{3,2,1,0:T(8,128)(2,1)S(1)}, bf16[4,2,128,128]{3,2,1,0:T(8,128)(2,1)S(1)}, u32[]{:S(2)}, u32[]{:S(2)}) collective-permute-start(bf16[4,2,128,128]{3,2,1,0:T(8,128)(2,1)S(1)} %pad_maximum_fusion.2), channel_id=1, source_target_pairs={{0,4},{2,6},{4,0},{6,2},{8,12},{10,14},{12,8},{14,10},{16,20},{18,... | collective-permute-start | bytes 786440 | tf_op jit(solution)/shard_map/ppermute | solution.py:293
  31.4 21.0 %collective-permute-start.10 = (bf16[4,2,128,128]{3,2,1,0:T(8,128)(2,1)S(1)}, bf16[4,2,128,128]{3,2,1,0:T(8,128)(2,1)S(1)}, u32[]{:S(2)}, u32[]{:S(2)}) collective-permute-start(bf16[4,2,128,128]{3,2,1,0:T(8,128)(2,1)S(1)} %pad_maximum_fusion.3), channel_id=1, source_target_pairs={{0,8},{2,10},{4,12},{6,14},{8,0},{10,2},{12,4},{14,6},{16,24},{18,... | collective-permute-start | bytes 786440 | tf_op jit(solution)/shard_map/ppermute | solution.py:293
  34.5 23.5 %collective-permute-start.11 = (bf16[4,2,128,128]{3,2,1,0:T(8,128)(2,1)S(1)}, bf16[4,2,128,128]{3,2,1,0:T(8,128)(2,1)S(1)}, u32[]{:S(2)}, u32[]{:S(2)}) collective-permute-start(bf16[4,2,128,128]{3,2,1,0:T(8,128)(2,1)S(1)} %pad_maximum_fusion.4), channel_id=1, source_target_pairs={{0,12},{2,14},{4,8},{6,10},{8,4},{10,6},{12,0},{14,2},{16,28},{18,... | collective-permute-start | bytes 786440 | tf_op jit(solution)/shard_map/ppermute | solution.py:293
  65.1 3.6 %collective-permute-start.24 = (f32[16]{0:T(128)S(1)}, f32[16]{0:T(128)S(1)}, u32[]{:S(2)}, u32[]{:S(2)}) collective-permute-start(f32[16]{0:T(128)S(1)} %bitcast.48), channel_id=1, source_target_pairs={{0,1},{1,0},{2,3},{3,2},{4,5},{5,4},{6,7},{7,6},{8,9},{9,8},{10,11... | collective-permute-start | bytes 200 | tf_op jit(solution)/shard_map/ppermute | solution.py:282
  66.7 19.9 %collective-permute-start.14 = (bf16[4,192,128]{2,1,0:T(8,128)(2,1)S(1)}, bf16[4,192,128]{2,1,0:T(8,128)(2,1)S(1)}, u32[]{:S(2)}, u32[]{:S(2)}) collective-permute-start(bf16[4,192,128]{2,1,0:T(8,128)(2,1)S(1)} %get-tuple-element.75), channel_id=1, source_target_pairs={{0,18},{2,16},{4,22},{6,20},{8,26},{10,24},{12,30},{14,28},{16,2},... | collective-permute-start | bytes 589832 | tf_op jit(solution)/shard_map/ppermute | solution.py:293
  68.8 1.6 %collective-permute-start.25 = (f32[16]{0:T(128)S(1)}, f32[16]{0:T(128)S(1)}, u32[]{:S(2)}, u32[]{:S(2)}) collective-permute-start(f32[16]{0:T(128)S(1)} %bitcast_add_fusion), channel_id=1, source_target_pairs={{0,2},{2,0},{4,6},{6,4},{8,10},{10,8},{12,14},{14,12},{16,18},{18,... | collective-permute-start | bytes 200 | tf_op jit(solution)/shard_map/ppermute | solution.py:293
  68.8 24.7 %collective-permute-start.17 = (bf16[4,192,128]{2,1,0:T(8,128)(2,1)S(1)}, bf16[4,192,128]{2,1,0:T(8,128)(2,1)S(1)}, u32[]{:S(2)}, u32[]{:S(2)}) collective-permute-start(bf16[4,192,128]{2,1,0:T(8,128)(2,1)S(1)} %get-tuple-element.81), channel_id=1, source_target_pairs={{0,12},{2,14},{4,8},{6,10},{8,4},{10,6},{12,0},{14,2},{16,28},{18,... | collective-permute-start | bytes 589832 | tf_op jit(solution)/shard_map/ppermute | solution.py:293
  70.3 3.6 %collective-permute-start.26 = (f32[16]{0:T(128)S(1)}, f32[16]{0:T(128)S(1)}, u32[]{:S(2)}, u32[]{:S(2)}) collective-permute-start(f32[16]{0:T(128)S(1)} %add.20), channel_id=1, source_target_pairs={{0,4},{2,6},{4,0},{6,2},{8,12},{10,14},{12,8},{14,10},{16,20},{18,... | collective-permute-start | bytes 200 | tf_op jit(solution)/shard_map/ppermute | solution.py:293
  70.3 23.2 %collective-permute-start.16 = (bf16[4,192,128]{2,1,0:T(8,128)(2,1)S(1)}, bf16[4,192,128]{2,1,0:T(8,128)(2,1)S(1)}, u32[]{:S(2)}, u32[]{:S(2)}) collective-permute-start(bf16[4,192,128]{2,1,0:T(8,128)(2,1)S(1)} %get-tuple-element.82), channel_id=1, source_target_pairs={{0,8},{2,10},{4,12},{6,14},{8,0},{10,2},{12,4},{14,6},{16,24},{18,... | collective-permute-start | bytes 589832 | tf_op jit(solution)/shard_map/ppermute | solution.py:293
  73.9 11.1 %collective-permute-start.27 = (f32[16]{0:T(128)S(1)}, f32[16]{0:T(128)S(1)}, u32[]{:S(2)}, u32[]{:S(2)}) collective-permute-start(f32[16]{0:T(128)S(1)} %add.21), channel_id=1, source_target_pairs={{0,8},{2,10},{4,12},{6,14},{8,0},{10,2},{12,4},{14,6},{16,24},{18,... | collective-permute-start | bytes 200 | tf_op jit(solution)/shard_map/ppermute | solution.py:293
  74.5 19.1 %collective-permute-start.15 = (bf16[4,192,128]{2,1,0:T(8,128)(2,1)S(1)}, bf16[4,192,128]{2,1,0:T(8,128)(2,1)S(1)}, u32[]{:S(2)}, u32[]{:S(2)}) collective-permute-start(bf16[4,192,128]{2,1,0:T(8,128)(2,1)S(1)} %get-tuple-element.83), channel_id=1, source_target_pairs={{0,4},{2,6},{4,0},{6,2},{8,12},{10,14},{12,8},{14,10},{16,20},{18,... | collective-permute-start | bytes 589832 | tf_op jit(solution)/shard_map/ppermute | solution.py:293
  85.0 6.8 %collective-permute-start.13 = (bf16[4,192,128]{2,1,0:T(8,128)(2,1)S(1)}, bf16[4,192,128]{2,1,0:T(8,128)(2,1)S(1)}, u32[]{:S(2)}, u32[]{:S(2)}) collective-permute-start(bf16[4,192,128]{2,1,0:T(8,128)(2,1)S(1)} %get-tuple-element.76), channel_id=1, source_target_pairs={{0,16},{2,18},{4,20},{6,22},{8,24},{10,26},{12,28},{14,30},{16,0},... | collective-permute-start | bytes 589832 | tf_op jit(solution)/shard_map/ppermute | solution.py:293
  86.5 6.9 %collective-permute-start.12 = (bf16[4,192,128]{2,1,0:T(8,128)(2,1)S(1)}, bf16[4,192,128]{2,1,0:T(8,128)(2,1)S(1)}, u32[]{:S(2)}, u32[]{:S(2)}) collective-permute-start(bf16[4,192,128]{2,1,0:T(8,128)(2,1)S(1)} %get-tuple-element.77), channel_id=1, source_target_pairs={{0,2},{2,0},{4,6},{6,4},{8,10},{10,8},{12,14},{14,12},{16,18},{18,... | collective-permute-start | bytes 589832 | tf_op jit(solution)/shard_map/ppermute | solution.py:293
  91.9 6.3 %collective-permute-start.28 = (f32[16]{0:T(128)S(1)}, f32[16]{0:T(128)S(1)}, u32[]{:S(2)}, u32[]{:S(2)}) collective-permute-start(f32[16]{0:T(128)S(1)} %add.22), channel_id=1, source_target_pairs={{0,16},{2,18},{4,20},{6,22},{8,24},{10,26},{12,28},{14,30},{16,0},... | collective-permute-start | bytes 200 | tf_op jit(solution)/shard_map/ppermute | solution.py:293
  93.7 5.5 %collective-permute-start.18 = (bf16[4,192,128]{2,1,0:T(8,128)(2,1)S(1)}, bf16[4,192,128]{2,1,0:T(8,128)(2,1)S(1)}, u32[]{:S(2)}, u32[]{:S(2)}) collective-permute-start(bf16[4,192,128]{2,1,0:T(8,128)(2,1)S(1)} %pad_maximum_fusion.11), channel_id=1, source_target_pairs={{0,2},{2,0},{4,6},{6,4},{8,10},{10,8},{12,14},{14,12},{16,18},{18,... | collective-permute-start | bytes 589832 | tf_op jit(solution)/shard_map/ppermute | solution.py:293
  93.8 7.8 %collective-permute-start.19 = (bf16[4,192,128]{2,1,0:T(8,128)(2,1)S(1)}, bf16[4,192,128]{2,1,0:T(8,128)(2,1)S(1)}, u32[]{:S(2)}, u32[]{:S(2)}) collective-permute-start(bf16[4,192,128]{2,1,0:T(8,128)(2,1)S(1)} %pad_maximum_fusion.12), channel_id=1, source_target_pairs={{0,16},{2,18},{4,20},{6,22},{8,24},{10,26},{12,28},{14,30},{16,0},... | collective-permute-start | bytes 589832 | tf_op jit(solution)/shard_map/ppermute | solution.py:293
  94.4 10.5 %collective-permute-start.20 = (bf16[4,192,128]{2,1,0:T(8,128)(2,1)S(1)}, bf16[4,192,128]{2,1,0:T(8,128)(2,1)S(1)}, u32[]{:S(2)}, u32[]{:S(2)}) collective-permute-start(bf16[4,192,128]{2,1,0:T(8,128)(2,1)S(1)} %pad_maximum_fusion.13), channel_id=1, source_target_pairs={{0,18},{2,16},{4,22},{6,20},{8,26},{10,24},{12,30},{14,28},{16,2},... | collective-permute-start | bytes 589832 | tf_op jit(solution)/shard_map/ppermute | solution.py:293
  95.8 10.7 %collective-permute-start.21 = (bf16[4,192,128]{2,1,0:T(8,128)(2,1)S(1)}, bf16[4,192,128]{2,1,0:T(8,128)(2,1)S(1)}, u32[]{:S(2)}, u32[]{:S(2)}) collective-permute-start(bf16[4,192,128]{2,1,0:T(8,128)(2,1)S(1)} %pad_maximum_fusion.8), channel_id=1, source_target_pairs={{0,4},{2,6},{4,0},{6,2},{8,12},{10,14},{12,8},{14,10},{16,20},{18,... | collective-permute-start | bytes 589832 | tf_op jit(solution)/shard_map/ppermute | solution.py:293
  98.1 14.8 %collective-permute-start.22 = (bf16[4,192,128]{2,1,0:T(8,128)(2,1)S(1)}, bf16[4,192,128]{2,1,0:T(8,128)(2,1)S(1)}, u32[]{:S(2)}, u32[]{:S(2)}) collective-permute-start(bf16[4,192,128]{2,1,0:T(8,128)(2,1)S(1)} %pad_maximum_fusion.9), channel_id=1, source_target_pairs={{0,8},{2,10},{4,12},{6,14},{8,0},{10,2},{12,4},{14,6},{16,24},{18,... | collective-permute-start | bytes 589832 | tf_op jit(solution)/shard_map/ppermute | solution.py:293
  99.1 18.3 %collective-permute-start.23 = (bf16[4,192,128]{2,1,0:T(8,128)(2,1)S(1)}, bf16[4,192,128]{2,1,0:T(8,128)(2,1)S(1)}, u32[]{:S(2)}, u32[]{:S(2)}) collective-permute-start(bf16[4,192,128]{2,1,0:T(8,128)(2,1)S(1)} %pad_maximum_fusion.10), channel_id=1, source_target_pairs={{0,12},{2,14},{4,8},{6,10},{8,4},{10,6},{12,0},{14,2},{16,28},{18,... | collective-permute-start | bytes 589832 | tf_op jit(solution)/shard_map/ppermute | solution.py:293

commit v8 on v7

--- a/solution.py
+++ b/solution.py
@@ -212,8 +212,6 @@
     root_scale = 1.0 / math.sqrt(width)
     place = place_ref[0]
     bias_acc[...] = jnp.zeros_like(bias_acc)
-    dk_ref[...] = jnp.zeros_like(dk_ref)
-    dv_ref[...] = jnp.zeros_like(dv_ref)
 
     def put(kind, block, tile):
         for c in range(2):
@@ -226,7 +224,14 @@
             put(1, block, (dk_ref[block] * root_scale).astype(out_a.dtype))
             put(2, block, dv_ref[block].astype(out_a.dtype))
 
+    def cleared(count):
+        for block in range(count):
+            dk_ref[block] = jnp.zeros(dk_ref.shape[1:], dk_ref.dtype)
+            dv_ref[block] = jnp.zeros(dv_ref.shape[1:], dv_ref.dtype)
+
     def on_group(members, higher):
+        if higher is None:
+            cleared(members[0][0] - members[0][2] + 1)
         key_blocks(higher)
         deltas = []
         for k, (block, base, tiles) in enumerate(members):
@@ -251,8 +256,14 @@
                 score_grad = weights * (d_ref[k, t] - deltas[k])
                 cross = cross + fold(score_grad[:rows, rows:], jnp.sum) + fold(score_grad[rows:, :rows], jnp.sum)
                 score_low = score_grad.astype(jnp.bfloat16)
-                dv_ref[first + t] += dot(weights.astype(jnp.bfloat16), grads, ((1,), (0,)))
-                dk_ref[first + t] += dot(score_low, queries, ((1,), (0,)))
+                value_term = dot(weights.astype(jnp.bfloat16), grads, ((1,), (0,)))
+                key_term = dot(score_low, queries, ((1,), (0,)))
+                if higher is None and (k == 0 or t == tiles - 1):
+                    dv_ref[first + t] = value_term
+                    dk_ref[first + t] = key_term
+                else:
+                    dv_ref[first + t] += value_term
+                    dk_ref[first + t] += key_term
                 query_sum = query_sum + dot(kt_ref[first + t], score_low, ((1,), (0,)))
             bias_acc[...] += cross
             sums.append(query_sum)
@@ -260,6 +271,8 @@
             put(0, block, (query_sum * root_scale).T.astype(out_a.dtype))
 
     def off_group(members, higher):
+        if higher is None:
+            cleared(blocks)
         key_blocks(higher)
         for block, _, _ in members:
             put(0, block, jnp.zeros((both, width), out_a.dtype))

time: 120 us -> 120 us (level)
  no operation moved by 1% of the time
where the time goes in v8:
time: 120 us; the launch traced here: 119 us
  waiting for transfers between devices  70.9 us (59%)
  starting transfers between devices  29.4 us (24%)
  Pallas kernels  15.7 us (13%)
  between operations  1.83 us (2%)
  other arithmetic  1.25 us (1%)
    ppermute x28, waiting for transfers between devices, moved(): lax.ppermute(value, ('chan', 'seq'), [(source, source ^ mask) for source...  68.8 us
    ppermute x28, starting transfers between devices, moved(): lax.ppermute(value, ('chan', 'seq'), [(source, source ^ mask) for source...  27.9 us
    pallas_call x4, Pallas kernels, call(): pl.pallas_call(kernel, out_shape=out_shape, in_specs=in_specs, out_specs=...  13.7 us
  transfers between devices with their start and end apart: 29, of which 16 were waited for; matrix products, arithmetic and copies ran while one was open for 1% of the time, Pallas kernels for 5%

profile of v8, /device:TPU:8, one launch (start us, length us, event | category | flops | bytes accessed | tf_op | source)
XLA Modules:
  0.0 119.4 jit_solution(14211104035858188927)
XLA Ops:
  0.6 1.5 %shard_map.93 = (bf16[4,2,128,128]{3,2,1,0:T(8,128)(2,1)S(1)}, bf16[4,2,128,128]{3,2,1,0:T(8,128)(2,1)S(1)}, bf16[4,2,128,128]{3,2,1,0:T(8,128)(2,1)S(1)}, bf16[4,2,128,128]{3,2,1,0:T(8,128)(2,1)S(1)}) custom-call(s32[1]{0:T(128)} %bitcast.place_ref, bf16[128,2048]{1,0:T(8,128)(2,1)} %bitcast.49, bf16[128,2048]{1,0:T(8,128)(2,1)} %bitcast.50), custom_call_target="tpu_custom_call" | custom-call | bytes 2097152 | tf_op jit(solution)/shard_map/pallas_call | solution.py:354
  2.2 3.0 %collective-permute-start.4 = (bf16[4,2,128,128]{3,2,1,0:T(8,128)(2,1)S(1)}, bf16[4,2,128,128]{3,2,1,0:T(8,128)(2,1)S(1)}, u32[]{:S(2)}, u32[]{:S(2)}) collective-permute-start(bf16[4,2,128,128]{3,2,1,0:T(8,128)(2,1)S(1)} %get-tuple-element.52), channel_id=1, source_target_pairs={{0,8},{2,10},{4,12},{6,14},{8,0},{10,2},{12,4},{14,6},{16,24},{18,... | collective-permute-start | bytes 786440 | tf_op jit(solution)/shard_map/ppermute | solution.py:306
  5.7 1.5 %shard_map.94 = (bf16[4,2,128,128]{3,2,1,0:T(8,128)(2,1)S(1)}, bf16[4,2,128,128]{3,2,1,0:T(8,128)(2,1)S(1)}, bf16[4,2,128,128]{3,2,1,0:T(8,128)(2,1)S(1)}, bf16[4,2,128,128]{3,2,1,0:T(8,128)(2,1)S(1)}) custom-call(s32[1]{0:T(128)} %bitcast.place_ref, bf16[128,2048]{1,0:T(8,128)(2,1)} %bitcast.51, bf16[128,2048]{1,0:T(8,128)(2,1)} %bitcast.52), custom_call_target="tpu_custom_call" | custom-call | bytes 2097152 | tf_op jit(solution)/shard_map/pallas_call | solution.py:354
  7.2 1.6 %collective-permute-start.1 = (bf16[4,2,128,128]{3,2,1,0:T(8,128)(2,1)S(1)}, bf16[4,2,128,128]{3,2,1,0:T(8,128)(2,1)S(1)}, u32[]{:S(2)}, u32[]{:S(2)}) collective-permute-start(bf16[4,2,128,128]{3,2,1,0:T(8,128)(2,1)S(1)} %get-tuple-element.48), channel_id=1, source_target_pairs={{0,16},{2,18},{4,20},{6,22},{8,24},{10,26},{12,28},{14,30},{16,0},... | collective-permute-start | bytes 786440 | tf_op jit(solution)/shard_map/ppermute | solution.py:306
  10.1 6.4 %collective-permute-done.1 = bf16[4,2,128,128]{3,2,1,0:T(8,128)(2,1)S(1)} collective-permute-done((bf16[4,2,128,128]{3,2,1,0:T(8,128)(2,1)S(1)}, bf16[4,2,128,128]{3,2,1,0:T(8,128)(2,1)S(1)}, u32[]{:S(2)}, u32[]{:S(2)}) %collective-permute-start.1) | collective-permute-done | bytes 262176 | tf_op jit(solution)/shard_map/ppermute | solution.py:306
  16.5 4.5 %collective-permute-done.2 = bf16[4,2,128,128]{3,2,1,0:T(8,128)(2,1)S(1)} collective-permute-done((bf16[4,2,128,128]{3,2,1,0:T(8,128)(2,1)S(1)}, bf16[4,2,128,128]{3,2,1,0:T(8,128)(2,1)S(1)}, u32[]{:S(2)}, u32[]{:S(2)}) %collective-permute-start.2) | collective-permute-done | bytes 262176 | tf_op jit(solution)/shard_map/ppermute | solution.py:306
  21.1 7.2 %collective-permute-done.5 = bf16[4,2,128,128]{3,2,1,0:T(8,128)(2,1)S(1)} collective-permute-done((bf16[4,2,128,128]{3,2,1,0:T(8,128)(2,1)S(1)}, bf16[4,2,128,128]{3,2,1,0:T(8,128)(2,1)S(1)}, u32[]{:S(2)}, u32[]{:S(2)}) %collective-permute-start.5) | collective-permute-done | bytes 262176 | tf_op jit(solution)/shard_map/ppermute | solution.py:306
  28.7 1.6 %collective-permute-start.7 = (bf16[4,2,128,128]{3,2,1,0:T(8,128)(2,1)S(1)}, bf16[4,2,128,128]{3,2,1,0:T(8,128)(2,1)S(1)}, u32[]{:S(2)}, u32[]{:S(2)}) collective-permute-start(bf16[4,2,128,128]{3,2,1,0:T(8,128)(2,1)S(1)} %pad_maximum_fusion.6), channel_id=1, source_target_pairs={{0,16},{2,18},{4,20},{6,22},{8,24},{10,26},{12,28},{14,30},{16,0},... | collective-permute-start | bytes 786440 | tf_op jit(solution)/shard_map/ppermute | solution.py:306
  31.4 3.0 %collective-permute-start.10 = (bf16[4,2,128,128]{3,2,1,0:T(8,128)(2,1)S(1)}, bf16[4,2,128,128]{3,2,1,0:T(8,128)(2,1)S(1)}, u32[]{:S(2)}, u32[]{:S(2)}) collective-permute-start(bf16[4,2,128,128]{3,2,1,0:T(8,128)(2,1)S(1)} %pad_maximum_fusion.3), channel_id=1, source_target_pairs={{0,8},{2,10},{4,12},{6,14},{8,0},{10,2},{12,4},{14,6},{16,24},{18,... | collective-permute-start | bytes 786440 | tf_op jit(solution)/shard_map/ppermute | solution.py:306
  35.1 2.9 %collective-permute-done.7 = bf16[4,2,128,128]{3,2,1,0:T(8,128)(2,1)S(1)} collective-permute-done((bf16[4,2,128,128]{3,2,1,0:T(8,128)(2,1)S(1)}, bf16[4,2,128,128]{3,2,1,0:T(8,128)(2,1)S(1)}, u32[]{:S(2)}, u32[]{:S(2)}) %collective-permute-start.7) | collective-permute-done | bytes 262176 | tf_op jit(solution)/shard_map/ppermute | solution.py:306
  37.9 4.7 %collective-permute-done.8 = bf16[4,2,128,128]{3,2,1,0:T(8,128)(2,1)S(1)} collective-permute-done((bf16[4,2,128,128]{3,2,1,0:T(8,128)(2,1)S(1)}, bf16[4,2,128,128]{3,2,1,0:T(8,128)(2,1)S(1)}, u32[]{:S(2)}, u32[]{:S(2)}) %collective-permute-start.8) | collective-permute-done | bytes 262176 | tf_op jit(solution)/shard_map/ppermute | solution.py:306
  42.7 4.1 %shard_map.95 = (bf16[8,128,256]{2,1,0:T(8,128)(2,1)S(1)}, f32[35,256,256]{2,1,0:T(8,128)S(1)}, f32[8,8,256]{2,1,0:T(8,128)S(1)}) custom-call(s32[1]{0:T(128)S(6)} %copy.10.length_ref, s32[1]{0:T(128)} %bitcast.place_ref, f32[16]{0:T(128)S(1)} %copy-done, bf16[4,4,2,128,128]{4,3,2,1,0:T(8,128)(2,1)S(1)} %pad_maximum_fusion.qk_ref), custom_call_target="tpu_custom_call" | custom-call | flops 587202560 | bytes 2097152 | tf_op jit(solution)/shard_map/pallas_call | solution.py:354
  46.9 5.6 %collective-permute-done.10 = bf16[4,2,128,128]{3,2,1,0:T(8,128)(2,1)S(1)} collective-permute-done((bf16[4,2,128,128]{3,2,1,0:T(8,128)(2,1)S(1)}, bf16[4,2,128,128]{3,2,1,0:T(8,128)(2,1)S(1)}, u32[]{:S(2)}, u32[]{:S(2)}) %collective-permute-start.10) | collective-permute-done | bytes 262176 | tf_op jit(solution)/shard_map/ppermute | solution.py:306
  52.4 5.6 %collective-permute-done.11 = bf16[4,2,128,128]{3,2,1,0:T(8,128)(2,1)S(1)} collective-permute-done((bf16[4,2,128,128]{3,2,1,0:T(8,128)(2,1)S(1)}, bf16[4,2,128,128]{3,2,1,0:T(8,128)(2,1)S(1)}, u32[]{:S(2)}, u32[]{:S(2)}) %collective-permute-start.11) | collective-permute-done | bytes 262176 | tf_op jit(solution)/shard_map/ppermute | solution.py:306
  58.1 6.7 %shard_map.96 = (bf16[4,4,192,128]{3,2,1,0:T(8,128)(2,1)S(1)}, bf16[4,4,192,128]{3,2,1,0:T(8,128)(2,1)S(1)}, f32[1,16]{1,0:T(1,128)S(1)}) custom-call(s32[1]{0:T(128)S(6)} %copy.10.length_ref, s32[1]{0:T(128)} %bitcast.place_ref, bf16[4,4,2,128,128]{4,3,2,1,0:T(8,128)(2,1)S(1)} %pad_maximum_fusion.qk_ref, bf16[8,128,256]{2,1,0:T(8,128)(2,1)S(1)} %get-tuple-element.56.kt_ref, ...), custom_call_target="tpu_custom_call" | custom-call | flops 2348810240 | bytes 2097152 | tf_op jit(solution)/shard_map/pallas_call | solution.py:354
  64.9 1.6 %collective-permute-start.24 = (f32[16]{0:T(128)S(1)}, f32[16]{0:T(128)S(1)}, u32[]{:S(2)}, u32[]{:S(2)}) collective-permute-start(f32[16]{0:T(128)S(1)} %bitcast.48), channel_id=1, source_target_pairs={{0,1},{1,0},{2,3},{3,2},{4,5},{5,4},{6,7},{7,6},{8,9},{9,8},{10,11... | collective-permute-start | bytes 200 | tf_op jit(solution)/shard_map/ppermute | solution.py:295
  66.5 2.1 %collective-permute-done.24 = f32[16]{0:T(128)S(1)} collective-permute-done((f32[16]{0:T(128)S(1)}, f32[16]{0:T(128)S(1)}, u32[]{:S(2)}, u32[]{:S(2)}) %collective-permute-start.24) | collective-permute-done | bytes 96 | tf_op jit(solution)/shard_map/ppermute | solution.py:295
  68.6 1.6 %collective-permute-start.17 = (bf16[4,192,128]{2,1,0:T(8,128)(2,1)S(1)}, bf16[4,192,128]{2,1,0:T(8,128)(2,1)S(1)}, u32[]{:S(2)}, u32[]{:S(2)}) collective-permute-start(bf16[4,192,128]{2,1,0:T(8,128)(2,1)S(1)} %get-tuple-element.81), channel_id=1, source_target_pairs={{0,12},{2,14},{4,8},{6,10},{8,4},{10,6},{12,0},{14,2},{16,28},{18,... | collective-permute-start | bytes 589832 | tf_op jit(solution)/shard_map/ppermute | solution.py:306
  70.2 2.6 %collective-permute-start.16 = (bf16[4,192,128]{2,1,0:T(8,128)(2,1)S(1)}, bf16[4,192,128]{2,1,0:T(8,128)(2,1)S(1)}, u32[]{:S(2)}, u32[]{:S(2)}) collective-permute-start(bf16[4,192,128]{2,1,0:T(8,128)(2,1)S(1)} %get-tuple-element.82), channel_id=1, source_target_pairs={{0,8},{2,10},{4,12},{6,14},{8,0},{10,2},{12,4},{14,6},{16,24},{18,... | collective-permute-start | bytes 589832 | tf_op jit(solution)/shard_map/ppermute | solution.py:306
  74.4 2.0 %collective-permute-start.15 = (bf16[4,192,128]{2,1,0:T(8,128)(2,1)S(1)}, bf16[4,192,128]{2,1,0:T(8,128)(2,1)S(1)}, u32[]{:S(2)}, u32[]{:S(2)}) collective-permute-start(bf16[4,192,128]{2,1,0:T(8,128)(2,1)S(1)} %get-tuple-element.83), channel_id=1, source_target_pairs={{0,4},{2,6},{4,0},{6,2},{8,12},{10,14},{12,8},{14,10},{16,20},{18,... | collective-permute-start | bytes 589832 | tf_op jit(solution)/shard_map/ppermute | solution.py:306
  76.4 8.5 %collective-permute-done.27 = f32[16]{0:T(128)S(1)} collective-permute-done((f32[16]{0:T(128)S(1)}, f32[16]{0:T(128)S(1)}, u32[]{:S(2)}, u32[]{:S(2)}) %collective-permute-start.27) | collective-permute-done | bytes 96 | tf_op jit(solution)/shard_map/ppermute | solution.py:306
  84.9 1.5 %collective-permute-start.13 = (bf16[4,192,128]{2,1,0:T(8,128)(2,1)S(1)}, bf16[4,192,128]{2,1,0:T(8,128)(2,1)S(1)}, u32[]{:S(2)}, u32[]{:S(2)}) collective-permute-start(bf16[4,192,128]{2,1,0:T(8,128)(2,1)S(1)} %get-tuple-element.76), channel_id=1, source_target_pairs={{0,16},{2,18},{4,20},{6,22},{8,24},{10,26},{12,28},{14,30},{16,0},... | collective-permute-start | bytes 589832 | tf_op jit(solution)/shard_map/ppermute | solution.py:306
  86.4 5.3 %collective-permute-done.13.refs_9_ = bf16[4,192,128]{2,1,0:T(8,128)(2,1)S(1)} collective-permute-done((bf16[4,192,128]{2,1,0:T(8,128)(2,1)S(1)}, bf16[4,192,128]{2,1,0:T(8,128)(2,1)S(1)}, u32[]{:S(2)}, u32[]{:S(2)}) %collective-permute-start.13) | collective-permute-done | bytes 196640 | tf_op jit(solution)/shard_map/ppermute | solution.py:306
  91.7 1.5 %collective-permute-start.28 = (f32[16]{0:T(128)S(1)}, f32[16]{0:T(128)S(1)}, u32[]{:S(2)}, u32[]{:S(2)}) collective-permute-start(f32[16]{0:T(128)S(1)} %add.22), channel_id=1, source_target_pairs={{0,16},{2,18},{4,20},{6,22},{8,24},{10,26},{12,28},{14,30},{16,0},... | collective-permute-start | bytes 200 | tf_op jit(solution)/shard_map/ppermute | solution.py:306
  94.2 1.4 %collective-permute-start.20 = (bf16[4,192,128]{2,1,0:T(8,128)(2,1)S(1)}, bf16[4,192,128]{2,1,0:T(8,128)(2,1)S(1)}, u32[]{:S(2)}, u32[]{:S(2)}) collective-permute-start(bf16[4,192,128]{2,1,0:T(8,128)(2,1)S(1)} %pad_maximum_fusion.13), channel_id=1, source_target_pairs={{0,18},{2,16},{4,22},{6,20},{8,26},{10,24},{12,30},{14,28},{16,2},... | collective-permute-start | bytes 589832 | tf_op jit(solution)/shard_map/ppermute | solution.py:306
  95.6 2.3 %collective-permute-start.21 = (bf16[4,192,128]{2,1,0:T(8,128)(2,1)S(1)}, bf16[4,192,128]{2,1,0:T(8,128)(2,1)S(1)}, u32[]{:S(2)}, u32[]{:S(2)}) collective-permute-start(bf16[4,192,128]{2,1,0:T(8,128)(2,1)S(1)} %pad_maximum_fusion.8), channel_id=1, source_target_pairs={{0,4},{2,6},{4,0},{6,2},{8,12},{10,14},{12,8},{14,10},{16,20},{18,... | collective-permute-start | bytes 589832 | tf_op jit(solution)/shard_map/ppermute | solution.py:306
  100.1 1.3 %collective-permute-done.19.refs_5_ = bf16[4,192,128]{2,1,0:T(8,128)(2,1)S(1)} collective-permute-done((bf16[4,192,128]{2,1,0:T(8,128)(2,1)S(1)}, bf16[4,192,128]{2,1,0:T(8,128)(2,1)S(1)}, u32[]{:S(2)}, u32[]{:S(2)}) %collective-permute-start.19) | collective-permute-done | bytes 196640 | tf_op jit(solution)/shard_map/ppermute | solution.py:306
  101.5 3.3 %collective-permute-done.20.refs_6_ = bf16[4,192,128]{2,1,0:T(8,128)(2,1)S(1)} collective-permute-done((bf16[4,192,128]{2,1,0:T(8,128)(2,1)S(1)}, bf16[4,192,128]{2,1,0:T(8,128)(2,1)S(1)}, u32[]{:S(2)}, u32[]{:S(2)}) %collective-permute-start.20) | collective-permute-done | bytes 196640 | tf_op jit(solution)/shard_map/ppermute | solution.py:306
  104.7 1.6 %collective-permute-done.21.refs_11_ = bf16[4,192,128]{2,1,0:T(8,128)(2,1)S(1)} collective-permute-done((bf16[4,192,128]{2,1,0:T(8,128)(2,1)S(1)}, bf16[4,192,128]{2,1,0:T(8,128)(2,1)S(1)}, u32[]{:S(2)}, u32[]{:S(2)}) %collective-permute-start.21) | collective-permute-done | bytes 196640 | tf_op jit(solution)/shard_map/ppermute | solution.py:306
  106.4 6.4 %collective-permute-done.22.refs_12_ = bf16[4,192,128]{2,1,0:T(8,128)(2,1)S(1)} collective-permute-done((bf16[4,192,128]{2,1,0:T(8,128)(2,1)S(1)}, bf16[4,192,128]{2,1,0:T(8,128)(2,1)S(1)}, u32[]{:S(2)}, u32[]{:S(2)}) %collective-permute-start.22) | collective-permute-done | bytes 196640 | tf_op jit(solution)/shard_map/ppermute | solution.py:306
  112.8 4.6 %collective-permute-done.23.refs_13_ = bf16[4,192,128]{2,1,0:T(8,128)(2,1)S(1)} collective-permute-done((bf16[4,192,128]{2,1,0:T(8,128)(2,1)S(1)}, bf16[4,192,128]{2,1,0:T(8,128)(2,1)S(1)}, u32[]{:S(2)}, u32[]{:S(2)}) %collective-permute-start.23) | collective-permute-done | bytes 196640 | tf_op jit(solution)/shard_map/ppermute | solution.py:306
  117.3 2.0 %unpack.1 = (bf16[128,2048]{1,0:T(8,128)(2,1)}, bf16[128,2048]{1,0:T(8,128)(2,1)}, bf16[128,2048]{1,0:T(8,128)(2,1)}) custom-call(s32[1]{0:T(128)} %bitcast.place_ref, bf16[4,192,128]{2,1,0:T(8,128)(2,1)S(1)} %get-tuple-element.84.refs_0_, bf16[4,192,128]{2,1,0:T(8,128)(2,1)S(1)} %collective-permute-done.15.refs_1_, ...), custom_call_target="tpu_custom_call" | custom-call | tf_op jit(solution)/shard_map/unpack/pallas_call | solution.py:427
  (71 shorter events, 8.3 us)
Async XLA Ops:
  0.6 42.1 %copy-start = (f32[16]{0:T(128)S(1)}, f32[16]{0:T(128)}, u32[]{:S(2)}) copy-start(f32[16]{0:T(128)} %bias_ref.1) | copy-start | bytes 196
  2.1 26.3 %collective-permute-start.3 = (bf16[4,2,128,128]{3,2,1,0:T(8,128)(2,1)S(1)}, bf16[4,2,128,128]{3,2,1,0:T(8,128)(2,1)S(1)}, u32[]{:S(2)}, u32[]{:S(2)}) collective-permute-start(bf16[4,2,128,128]{3,2,1,0:T(8,128)(2,1)S(1)} %get-tuple-element.50), channel_id=1, source_target_pairs={{0,4},{2,6},{4,0},{6,2},{8,12},{10,14},{12,8},{14,10},{16,20},{18,... | collective-permute-start | bytes 786440 | tf_op jit(solution)/shard_map/ppermute | solution.py:306
  2.2 26.2 %collective-permute-start.4 = (bf16[4,2,128,128]{3,2,1,0:T(8,128)(2,1)S(1)}, bf16[4,2,128,128]{3,2,1,0:T(8,128)(2,1)S(1)}, u32[]{:S(2)}, u32[]{:S(2)}) collective-permute-start(bf16[4,2,128,128]{3,2,1,0:T(8,128)(2,1)S(1)} %get-tuple-element.52), channel_id=1, source_target_pairs={{0,8},{2,10},{4,12},{6,14},{8,0},{10,2},{12,4},{14,6},{16,24},{18,... | collective-permute-start | bytes 786440 | tf_op jit(solution)/shard_map/ppermute | solution.py:306
  5.2 23.1 %collective-permute-start.5 = (bf16[4,2,128,128]{3,2,1,0:T(8,128)(2,1)S(1)}, bf16[4,2,128,128]{3,2,1,0:T(8,128)(2,1)S(1)}, u32[]{:S(2)}, u32[]{:S(2)}) collective-permute-start(bf16[4,2,128,128]{3,2,1,0:T(8,128)(2,1)S(1)} %get-tuple-element.54), channel_id=1, source_target_pairs={{0,12},{2,14},{4,8},{6,10},{8,4},{10,6},{12,0},{14,2},{16,28},{18,... | collective-permute-start | bytes 786440 | tf_op jit(solution)/shard_map/ppermute | solution.py:306
  7.2 1.7 %collective-permute-start = (bf16[4,2,128,128]{3,2,1,0:T(8,128)(2,1)S(1)}, bf16[4,2,128,128]{3,2,1,0:T(8,128)(2,1)S(1)}, u32[]{:S(2)}, u32[]{:S(2)}) collective-permute-start(bf16[4,2,128,128]{3,2,1,0:T(8,128)(2,1)S(1)} %get-tuple-element.47), channel_id=1, source_target_pairs={{0,2},{2,0},{4,6},{6,4},{8,10},{10,8},{12,14},{14,12},{16,18},{18,... | collective-permute-start | bytes 786440 | tf_op jit(solution)/shard_map/ppermute | solution.py:306
  7.2 9.2 %collective-permute-start.1 = (bf16[4,2,128,128]{3,2,1,0:T(8,128)(2,1)S(1)}, bf16[4,2,128,128]{3,2,1,0:T(8,128)(2,1)S(1)}, u32[]{:S(2)}, u32[]{:S(2)}) collective-permute-start(bf16[4,2,128,128]{3,2,1,0:T(8,128)(2,1)S(1)} %get-tuple-element.48), channel_id=1, source_target_pairs={{0,16},{2,18},{4,20},{6,22},{8,24},{10,26},{12,28},{14,30},{16,0},... | collective-permute-start | bytes 786440 | tf_op jit(solution)/shard_map/ppermute | solution.py:306
  8.9 12.1 %collective-permute-start.2 = (bf16[4,2,128,128]{3,2,1,0:T(8,128)(2,1)S(1)}, bf16[4,2,128,128]{3,2,1,0:T(8,128)(2,1)S(1)}, u32[]{:S(2)}, u32[]{:S(2)}) collective-permute-start(bf16[4,2,128,128]{3,2,1,0:T(8,128)(2,1)S(1)} %get-tuple-element.49), channel_id=1, source_target_pairs={{0,18},{2,16},{4,22},{6,20},{8,26},{10,24},{12,30},{14,28},{16,2},... | collective-permute-start | bytes 786440 | tf_op jit(solution)/shard_map/ppermute | solution.py:306
  28.6 5.9 %collective-permute-start.6 = (bf16[4,2,128,128]{3,2,1,0:T(8,128)(2,1)S(1)}, bf16[4,2,128,128]{3,2,1,0:T(8,128)(2,1)S(1)}, u32[]{:S(2)}, u32[]{:S(2)}) collective-permute-start(bf16[4,2,128,128]{3,2,1,0:T(8,128)(2,1)S(1)} %pad_maximum_fusion.5), channel_id=1, source_target_pairs={{0,2},{2,0},{4,6},{6,4},{8,10},{10,8},{12,14},{14,12},{16,18},{18,... | collective-permute-start | bytes 786440 | tf_op jit(solution)/shard_map/ppermute | solution.py:306
  28.7 9.2 %collective-permute-start.7 = (bf16[4,2,128,128]{3,2,1,0:T(8,128)(2,1)S(1)}, bf16[4,2,128,128]{3,2,1,0:T(8,128)(2,1)S(1)}, u32[]{:S(2)}, u32[]{:S(2)}) collective-permute-start(bf16[4,2,128,128]{3,2,1,0:T(8,128)(2,1)S(1)} %pad_maximum_fusion.6), channel_id=1, source_target_pairs={{0,16},{2,18},{4,20},{6,22},{8,24},{10,26},{12,28},{14,30},{16,0},... | collective-permute-start | bytes 786440 | tf_op jit(solution)/shard_map/ppermute | solution.py:306
  30.3 12.3 %collective-permute-start.8 = (bf16[4,2,128,128]{3,2,1,0:T(8,128)(2,1)S(1)}, bf16[4,2,128,128]{3,2,1,0:T(8,128)(2,1)S(1)}, u32[]{:S(2)}, u32[]{:S(2)}) collective-permute-start(bf16[4,2,128,128]{3,2,1,0:T(8,128)(2,1)S(1)} %pad_maximum_fusion.7), channel_id=1, source_target_pairs={{0,18},{2,16},{4,22},{6,20},{8,26},{10,24},{12,30},{14,28},{16,2},... | collective-permute-start | bytes 786440 | tf_op jit(solution)/shard_map/ppermute | solution.py:306
  31.3 15.5 %collective-permute-start.9 = (bf16[4,2,128,128]{3,2,1,0:T(8,128)(2,1)S(1)}, bf16[4,2,128,128]{3,2,1,0:T(8,128)(2,1)S(1)}, u32[]{:S(2)}, u32[]{:S(2)}) collective-permute-start(bf16[4,2,128,128]{3,2,1,0:T(8,128)(2,1)S(1)} %pad_maximum_fusion.2), channel_id=1, source_target_pairs={{0,4},{2,6},{4,0},{6,2},{8,12},{10,14},{12,8},{14,10},{16,20},{18,... | collective-permute-start | bytes 786440 | tf_op jit(solution)/shard_map/ppermute | solution.py:306
  31.4 21.0 %collective-permute-start.10 = (bf16[4,2,128,128]{3,2,1,0:T(8,128)(2,1)S(1)}, bf16[4,2,128,128]{3,2,1,0:T(8,128)(2,1)S(1)}, u32[]{:S(2)}, u32[]{:S(2)}) collective-permute-start(bf16[4,2,128,128]{3,2,1,0:T(8,128)(2,1)S(1)} %pad_maximum_fusion.3), channel_id=1, source_target_pairs={{0,8},{2,10},{4,12},{6,14},{8,0},{10,2},{12,4},{14,6},{16,24},{18,... | collective-permute-start | bytes 786440 | tf_op jit(solution)/shard_map/ppermute | solution.py:306
  34.5 23.5 %collective-permute-start.11 = (bf16[4,2,128,128]{3,2,1,0:T(8,128)(2,1)S(1)}, bf16[4,2,128,128]{3,2,1,0:T(8,128)(2,1)S(1)}, u32[]{:S(2)}, u32[]{:S(2)}) collective-permute-start(bf16[4,2,128,128]{3,2,1,0:T(8,128)(2,1)S(1)} %pad_maximum_fusion.4), channel_id=1, source_target_pairs={{0,12},{2,14},{4,8},{6,10},{8,4},{10,6},{12,0},{14,2},{16,28},{18,... | collective-permute-start | bytes 786440 | tf_op jit(solution)/shard_map/ppermute | solution.py:306
  64.9 3.6 %collective-permute-start.24 = (f32[16]{0:T(128)S(1)}, f32[16]{0:T(128)S(1)}, u32[]{:S(2)}, u32[]{:S(2)}) collective-permute-start(f32[16]{0:T(128)S(1)} %bitcast.48), channel_id=1, source_target_pairs={{0,1},{1,0},{2,3},{3,2},{4,5},{5,4},{6,7},{7,6},{8,9},{9,8},{10,11... | collective-permute-start | bytes 200 | tf_op jit(solution)/shard_map/ppermute | solution.py:295
  66.5 19.9 %collective-permute-start.14 = (bf16[4,192,128]{2,1,0:T(8,128)(2,1)S(1)}, bf16[4,192,128]{2,1,0:T(8,128)(2,1)S(1)}, u32[]{:S(2)}, u32[]{:S(2)}) collective-permute-start(bf16[4,192,128]{2,1,0:T(8,128)(2,1)S(1)} %get-tuple-element.75), channel_id=1, source_target_pairs={{0,18},{2,16},{4,22},{6,20},{8,26},{10,24},{12,30},{14,28},{16,2},... | collective-permute-start | bytes 589832 | tf_op jit(solution)/shard_map/ppermute | solution.py:306
  68.6 1.6 %collective-permute-start.25 = (f32[16]{0:T(128)S(1)}, f32[16]{0:T(128)S(1)}, u32[]{:S(2)}, u32[]{:S(2)}) collective-permute-start(f32[16]{0:T(128)S(1)} %bitcast_add_fusion), channel_id=1, source_target_pairs={{0,2},{2,0},{4,6},{6,4},{8,10},{10,8},{12,14},{14,12},{16,18},{18,... | collective-permute-start | bytes 200 | tf_op jit(solution)/shard_map/ppermute | solution.py:306
  68.6 24.7 %collective-permute-start.17 = (bf16[4,192,128]{2,1,0:T(8,128)(2,1)S(1)}, bf16[4,192,128]{2,1,0:T(8,128)(2,1)S(1)}, u32[]{:S(2)}, u32[]{:S(2)}) collective-permute-start(bf16[4,192,128]{2,1,0:T(8,128)(2,1)S(1)} %get-tuple-element.81), channel_id=1, source_target_pairs={{0,12},{2,14},{4,8},{6,10},{8,4},{10,6},{12,0},{14,2},{16,28},{18,... | collective-permute-start | bytes 589832 | tf_op jit(solution)/shard_map/ppermute | solution.py:306
  70.2 3.6 %collective-permute-start.26 = (f32[16]{0:T(128)S(1)}, f32[16]{0:T(128)S(1)}, u32[]{:S(2)}, u32[]{:S(2)}) collective-permute-start(f32[16]{0:T(128)S(1)} %add.20), channel_id=1, source_target_pairs={{0,4},{2,6},{4,0},{6,2},{8,12},{10,14},{12,8},{14,10},{16,20},{18,... | collective-permute-start | bytes 200 | tf_op jit(solution)/shard_map/ppermute | solution.py:306
  70.2 23.2 %collective-permute-start.16 = (bf16[4,192,128]{2,1,0:T(8,128)(2,1)S(1)}, bf16[4,192,128]{2,1,0:T(8,128)(2,1)S(1)}, u32[]{:S(2)}, u32[]{:S(2)}) collective-permute-start(bf16[4,192,128]{2,1,0:T(8,128)(2,1)S(1)} %get-tuple-element.82), channel_id=1, source_target_pairs={{0,8},{2,10},{4,12},{6,14},{8,0},{10,2},{12,4},{14,6},{16,24},{18,... | collective-permute-start | bytes 589832 | tf_op jit(solution)/shard_map/ppermute | solution.py:306
  73.8 11.1 %collective-permute-start.27 = (f32[16]{0:T(128)S(1)}, f32[16]{0:T(128)S(1)}, u32[]{:S(2)}, u32[]{:S(2)}) collective-permute-start(f32[16]{0:T(128)S(1)} %add.21), channel_id=1, source_target_pairs={{0,8},{2,10},{4,12},{6,14},{8,0},{10,2},{12,4},{14,6},{16,24},{18,... | collective-permute-start | bytes 200 | tf_op jit(solution)/shard_map/ppermute | solution.py:306
  74.4 19.1 %collective-permute-start.15 = (bf16[4,192,128]{2,1,0:T(8,128)(2,1)S(1)}, bf16[4,192,128]{2,1,0:T(8,128)(2,1)S(1)}, u32[]{:S(2)}, u32[]{:S(2)}) collective-permute-start(bf16[4,192,128]{2,1,0:T(8,128)(2,1)S(1)} %get-tuple-element.83), channel_id=1, source_target_pairs={{0,4},{2,6},{4,0},{6,2},{8,12},{10,14},{12,8},{14,10},{16,20},{18,... | collective-permute-start | bytes 589832 | tf_op jit(solution)/shard_map/ppermute | solution.py:306
  84.9 6.8 %collective-permute-start.13 = (bf16[4,192,128]{2,1,0:T(8,128)(2,1)S(1)}, bf16[4,192,128]{2,1,0:T(8,128)(2,1)S(1)}, u32[]{:S(2)}, u32[]{:S(2)}) collective-permute-start(bf16[4,192,128]{2,1,0:T(8,128)(2,1)S(1)} %get-tuple-element.76), channel_id=1, source_target_pairs={{0,16},{2,18},{4,20},{6,22},{8,24},{10,26},{12,28},{14,30},{16,0},... | collective-permute-start | bytes 589832 | tf_op jit(solution)/shard_map/ppermute | solution.py:306
  86.4 6.9 %collective-permute-start.12 = (bf16[4,192,128]{2,1,0:T(8,128)(2,1)S(1)}, bf16[4,192,128]{2,1,0:T(8,128)(2,1)S(1)}, u32[]{:S(2)}, u32[]{:S(2)}) collective-permute-start(bf16[4,192,128]{2,1,0:T(8,128)(2,1)S(1)} %get-tuple-element.77), channel_id=1, source_target_pairs={{0,2},{2,0},{4,6},{6,4},{8,10},{10,8},{12,14},{14,12},{16,18},{18,... | collective-permute-start | bytes 589832 | tf_op jit(solution)/shard_map/ppermute | solution.py:306
  91.7 6.3 %collective-permute-start.28 = (f32[16]{0:T(128)S(1)}, f32[16]{0:T(128)S(1)}, u32[]{:S(2)}, u32[]{:S(2)}) collective-permute-start(f32[16]{0:T(128)S(1)} %add.22), channel_id=1, source_target_pairs={{0,16},{2,18},{4,20},{6,22},{8,24},{10,26},{12,28},{14,30},{16,0},... | collective-permute-start | bytes 200 | tf_op jit(solution)/shard_map/ppermute | solution.py:306
  93.5 5.5 %collective-permute-start.18 = (bf16[4,192,128]{2,1,0:T(8,128)(2,1)S(1)}, bf16[4,192,128]{2,1,0:T(8,128)(2,1)S(1)}, u32[]{:S(2)}, u32[]{:S(2)}) collective-permute-start(bf16[4,192,128]{2,1,0:T(8,128)(2,1)S(1)} %pad_maximum_fusion.11), channel_id=1, source_target_pairs={{0,2},{2,0},{4,6},{6,4},{8,10},{10,8},{12,14},{14,12},{16,18},{18,... | collective-permute-start | bytes 589832 | tf_op jit(solution)/shard_map/ppermute | solution.py:306
  93.6 7.8 %collective-permute-start.19 = (bf16[4,192,128]{2,1,0:T(8,128)(2,1)S(1)}, bf16[4,192,128]{2,1,0:T(8,128)(2,1)S(1)}, u32[]{:S(2)}, u32[]{:S(2)}) collective-permute-start(bf16[4,192,128]{2,1,0:T(8,128)(2,1)S(1)} %pad_maximum_fusion.12), channel_id=1, source_target_pairs={{0,16},{2,18},{4,20},{6,22},{8,24},{10,26},{12,28},{14,30},{16,0},... | collective-permute-start | bytes 589832 | tf_op jit(solution)/shard_map/ppermute | solution.py:306
  94.2 10.5 %collective-permute-start.20 = (bf16[4,192,128]{2,1,0:T(8,128)(2,1)S(1)}, bf16[4,192,128]{2,1,0:T(8,128)(2,1)S(1)}, u32[]{:S(2)}, u32[]{:S(2)}) collective-permute-start(bf16[4,192,128]{2,1,0:T(8,128)(2,1)S(1)} %pad_maximum_fusion.13), channel_id=1, source_target_pairs={{0,18},{2,16},{4,22},{6,20},{8,26},{10,24},{12,30},{14,28},{16,2},... | collective-permute-start | bytes 589832 | tf_op jit(solution)/shard_map/ppermute | solution.py:306
  95.6 10.7 %collective-permute-start.21 = (bf16[4,192,128]{2,1,0:T(8,128)(2,1)S(1)}, bf16[4,192,128]{2,1,0:T(8,128)(2,1)S(1)}, u32[]{:S(2)}, u32[]{:S(2)}) collective-permute-start(bf16[4,192,128]{2,1,0:T(8,128)(2,1)S(1)} %pad_maximum_fusion.8), channel_id=1, source_target_pairs={{0,4},{2,6},{4,0},{6,2},{8,12},{10,14},{12,8},{14,10},{16,20},{18,... | collective-permute-start | bytes 589832 | tf_op jit(solution)/shard_map/ppermute | solution.py:306
  98.0 14.8 %collective-permute-start.22 = (bf16[4,192,128]{2,1,0:T(8,128)(2,1)S(1)}, bf16[4,192,128]{2,1,0:T(8,128)(2,1)S(1)}, u32[]{:S(2)}, u32[]{:S(2)}) collective-permute-start(bf16[4,192,128]{2,1,0:T(8,128)(2,1)S(1)} %pad_maximum_fusion.9), channel_id=1, source_target_pairs={{0,8},{2,10},{4,12},{6,14},{8,0},{10,2},{12,4},{14,6},{16,24},{18,... | collective-permute-start | bytes 589832 | tf_op jit(solution)/shard_map/ppermute | solution.py:306
  99.0 18.3 %collective-permute-start.23 = (bf16[4,192,128]{2,1,0:T(8,128)(2,1)S(1)}, bf16[4,192,128]{2,1,0:T(8,128)(2,1)S(1)}, u32[]{:S(2)}, u32[]{:S(2)}) collective-permute-start(bf16[4,192,128]{2,1,0:T(8,128)(2,1)S(1)} %pad_maximum_fusion.10), channel_id=1, source_target_pairs={{0,12},{2,14},{4,8},{6,10},{8,4},{10,6},{12,0},{14,2},{16,28},{18,... | collective-permute-start | bytes 589832 | tf_op jit(solution)/shard_map/ppermute | solution.py:306
